TPU v7x, 32 devices: a whole 2x2x4 slice. The times are simulated.
32 devices in a mesh: groups: 2 (over y), context: 4 (over x, core), tensor: 4 (over z).
Axes of the slice: x: 2, y: 2, z: 4, core: 2. Of those that a mesh axis runs over, the one named last changes fastest.
Arguments:
- tokens: bfloat16 [4096, 4096], P(('groups', 'context', 'tensor')), parts along dimension 0, may hold values from -1000 to 1000
- norm_gain: bfloat16 [4096], replicated, may hold values from 0.099609375 to 1.8984375
- w_in: bfloat16 [4096, 3, 4096], P('context', None, 'tensor'), may hold values from -0.09375 to 0.09375
- short_filter: float32 [3, 3, 4096], P(None, None, 'tensor'), may hold values from -3.6 to 3.6
- medium_filter: float32 [128, 4096], P(None, 'tensor'), may hold values from -0.9 to 0.9
- decay: float32 [4096], P('tensor'), may hold values from 0.004 to 0.12
- w_out: bfloat16 [4096, 4096], P('context', 'tensor'), may hold values from -0.09375 to 0.09375
Outputs:
- mixer_out: bfloat16 [4096, 4096], P(('groups', 'context', 'tensor')), parts along dimension 0
There are 2 independent parts, one for each index of `groups`. A program takes and returns all parts, laid end to end along the dimension named above; an argument that names none is the same for every part. Nothing has to cross between parts.
All inputs are finite; a program needn't handle non-finite values.
Results may differ from a plain program's by a relative error of at most 0.01.
Values may be sent and summed in bfloat16 or wider, within the bound.
No kernel may reach another device: no remote copies, remote signals or barrier semaphores. Data moves between devices by JAX's collectives and lax.ppermute only.
A program may use at most 128 MiB of HBM per device.

v0:
```python
import functools
import jax
import jax.numpy as jnp
import ml_dtypes
import numpy as np
from jax import lax
from jax.experimental import pallas as pl
from jax.experimental.pallas import tpu as pltpu
from jax.sharding import PartitionSpec as P

norm_epsilon = 1e-06
axes = ("groups", "context", "tensor")
edge = 16
f32 = jnp.float32
bf16 = jnp.bfloat16


def split_parts(matrix):
    high = matrix.astype(ml_dtypes.bfloat16)
    low = (matrix - high.astype(np.float64)).astype(ml_dtypes.bfloat16)
    return high, low


def fourier_tables(taps):
    size = 2 * taps
    freq = np.arange(taps)[:, None]
    time = np.arange(size)[None, :]
    angle = 2 * np.pi * ((freq * time) % size) / size
    cosine, sine = np.cos(angle), np.sin(angle)
    sine[0] = 1.0 - 2.0 * (np.arange(size) % 2)
    forward = np.concatenate([cosine, sine], axis=0)
    weight = np.full((2 * taps, 1), 2.0 / size)
    weight[0] = weight[taps] = 1.0 / size
    inverse = (forward * weight)[:, taps:].T
    fh, fl = split_parts(forward[:, :taps])
    ih, il = split_parts(inverse)
    return np.concatenate([fh, fl], axis=0), np.concatenate([ih, ih, il], axis=1)


def short_sum(s, taps_ref, branch, slab):
    total = None
    for lag in range(taps_ref.shape[0]):
        term = taps_ref[lag, branch][None] * s[edge - lag : edge - lag + slab]
        total = term if total is None else total + term
    return total


def product(at_ref, x_ref, pieces):
    total = None
    for n, piece in enumerate(pieces):
        depth = piece.shape[-2]
        step = min(depth, 256)
        part = x_ref[:, pl.ds(pl.multiple_of(at_ref[n], step), depth)]
        term = jnp.dot(part, piece[...], preferred_element_type=f32)
        total = term if total is None else total + term
    return total.astype(bf16).astype(f32)


def gate_kernel(counts, at_ref, x_ref, taps_ref, *rest):
    slab = x_ref.shape[0]
    pieces = [rest[: counts[0]], rest[counts[0] : sum(counts)]]
    gated_ref, head_ref, tail_ref, s = rest[sum(counts) :]
    feats = []
    for k in range(2):
        s[0:edge] = jnp.zeros((edge, s.shape[1]), f32)
        s[edge : edge + slab] = product(at_ref, x_ref, pieces[k])
        head_ref[k] = s[edge : 2 * edge].astype(bf16)
        tail_ref[k] = s[slab : slab + edge].astype(bf16)
        feats.append(short_sum(s, taps_ref, k + 1, slab))
    gated_ref[...] = (feats[0] * feats[1]).astype(bf16)


def piece_specs(pieces, width):
    specs = []
    for array, branch, _ in pieces:
        if branch is None:
            specs.append(pl.BlockSpec((array.shape[0], width), lambda i, at: (0, i)))
        else:
            specs.append(
                pl.BlockSpec((None, array.shape[1], width), lambda i, at, b=branch: (b, 0, i))
            )
    return specs


def offsets(pieces):
    return jnp.stack([jnp.asarray(p[2], jnp.int32) for p in pieces])


def gate(x, one, two, short_filter, width):
    slab = x.shape[0]
    channels = short_filter.shape[-1]
    grid_spec = pltpu.PrefetchScalarGridSpec(
        num_scalar_prefetch=1,
        grid=(channels // width,),
        in_specs=[
            pl.BlockSpec(x.shape, lambda i, at: (0, 0)),
            pl.BlockSpec(short_filter.shape[:2] + (width,), lambda i, at: (0, 0, i)),
        ]
        + piece_specs(one, width)
        + piece_specs(two, width),
        out_specs=[
            pl.BlockSpec((slab, width), lambda i, at: (0, i)),
            pl.BlockSpec((2, edge, width), lambda i, at: (0, 0, i)),
            pl.BlockSpec((2, edge, width), lambda i, at: (0, 0, i)),
        ],
        scratch_shapes=[pltpu.VMEM((slab + edge, width), f32)],
    )
    return pl.pallas_call(
        functools.partial(gate_kernel, (len(one), len(two))),
        grid_spec=grid_spec,
        out_shape=[
            jax.ShapeDtypeStruct((slab, channels), bf16),
            jax.ShapeDtypeStruct((2, edge, channels), bf16),
            jax.ShapeDtypeStruct((2, edge, channels), bf16),
        ],
        compiler_params=pltpu.CompilerParams(vmem_limit_bytes=50 << 20),
        name="gate",
    )(offsets(one), x, short_filter, *[p[0] for p in one + two])


def query_kernel(at_ref, x_ref, before_ref, taps_ref, *rest):
    slab = x_ref.shape[0]
    *pieces, out_ref, s = rest
    s[0:edge] = product(at_ref, before_ref, pieces)
    s[edge : edge + slab] = product(at_ref, x_ref, pieces)
    out_ref[...] = short_sum(s, taps_ref, 0, slab)


def query(x, before, pieces, short_filter, width):
    slab = x.shape[0]
    channels = short_filter.shape[-1]
    grid_spec = pltpu.PrefetchScalarGridSpec(
        num_scalar_prefetch=1,
        grid=(channels // width,),
        in_specs=[
            pl.BlockSpec(x.shape, lambda i, at: (0, 0)),
            pl.BlockSpec(before.shape, lambda i, at: (0, 0)),
            pl.BlockSpec(short_filter.shape[:2] + (width,), lambda i, at: (0, 0, i)),
        ]
        + piece_specs(pieces, width),
        out_specs=pl.BlockSpec((slab, width), lambda i, at: (0, i)),
        scratch_shapes=[pltpu.VMEM((slab + edge, width), f32)],
    )
    return pl.pallas_call(
        query_kernel,
        grid_spec=grid_spec,
        out_shape=jax.ShapeDtypeStruct((slab, channels), f32),
        compiler_params=pltpu.CompilerParams(vmem_limit_bytes=50 << 20),
        name="query",
    )(offsets(pieces), x, before, short_filter, *[p[0] for p in pieces])


def mix_kernel(
    gated_ref, before_ref, head_ref, edge_ref, short_ref, taps_ref, query_ref, fwd_ref, inv_ref, out_ref, s
):
    taps = taps_ref.shape[0]
    blocks = gated_ref.shape[0] // taps
    feats = []
    for k in range(2):
        s[0:edge] = edge_ref[k].astype(f32)
        s[edge : 2 * edge] = head_ref[k].astype(f32)
        total = None
        for lag in range(short_ref.shape[0]):
            term = short_ref[lag, k + 1][None] * s[edge - lag : 2 * edge - lag]
            total = term if total is None else total + term
        feats.append(total)
    first = (feats[0] * feats[1]).astype(bf16)

    def transform(block):
        both = jnp.dot(fwd_ref[...], block, preferred_element_type=f32)
        return both[: 2 * taps] + both[2 * taps :]

    row = lax.broadcasted_iota(jnp.int32, (2 * taps, 1), 0)
    sign = jnp.where(row % 2 == 0, 1.0, -1.0).astype(f32)
    is_zero = lax.broadcasted_iota(jnp.int32, (taps, 1), 0) == 0
    response = transform(taps_ref[...])
    h_cos, h_sin = response[:taps], response[taps:]
    h_low = jnp.where(is_zero, h_sin, h_cos)
    h_sin = jnp.where(is_zero, 0.0, h_sin)
    last = transform(before_ref[...])
    for b in range(blocks):
        if b == 0:
            block = jnp.concatenate([first, gated_ref[edge:taps]], axis=0)
        else:
            block = gated_ref[b * taps : (b + 1) * taps]
        now = transform(block)
        x = last + sign * now
        last = now
        x_cos, x_sin = x[:taps], x[taps:]
        y = jnp.concatenate([x_cos * h_cos - x_sin * h_sin, x_sin * h_low + x_cos * h_sin], axis=0)
        high = y.astype(bf16)
        low = (y - high.astype(f32)).astype(bf16)
        mixed = jnp.dot(
            inv_ref[...], jnp.concatenate([high, low, high], axis=0), preferred_element_type=f32
        )
        at = slice(b * taps, (b + 1) * taps)
        out_ref[at] = (query_ref[at] * mixed).astype(bf16)


def mix(gated, before, head, edge_rows, short_filter, taps, query_rows, width):
    slab, channels = gated.shape
    count = taps.shape[0]
    forward, inverse = fourier_tables(count)
    col = lambda rows: pl.BlockSpec((rows, width), lambda i: (0, i))
    cube = lambda a, b: pl.BlockSpec((a, b, width), lambda i: (0, 0, i))
    return pl.pallas_call(
        mix_kernel,
        grid=(channels // width,),
        in_specs=[
            col(slab),
            col(count),
            cube(2, edge),
            cube(2, edge),
            cube(*short_filter.shape[:2]),
            col(count),
            col(slab),
            pl.BlockSpec(forward.shape, lambda i: (0, 0)),
            pl.BlockSpec(inverse.shape, lambda i: (0, 0)),
        ],
        out_specs=col(slab),
        out_shape=jax.ShapeDtypeStruct((slab, channels), bf16),
        scratch_shapes=[pltpu.VMEM((2 * edge, width), f32)],
        compiler_params=pltpu.CompilerParams(vmem_limit_bytes=40 << 20),
        name="mix",
    )(gated, before, head, edge_rows, short_filter, taps, query_rows, forward, inverse)


def local(tokens, norm_gain, w_in, short_filter, medium_filter, decay, w_out):
    groups, contexts, count = (lax.axis_size(a) for a in axes)
    g, c, z = (lax.axis_index(a) for a in axes)
    length, features = tokens.shape
    rows, branches, channels = w_in.shape
    slab = length * count
    width = min(channels, 256)
    paired = contexts == 4 and groups == 2

    def move(value, target):
        pairs = []
        for i in range(groups):
            for j in range(contexts):
                for k in range(count):
                    to = target(i, j, k)
                    if 0 <= to[1] < contexts and 0 <= to[2] < count:
                        pairs.append(
                            ((i * contexts + j) * count + k, (to[0] * contexts + to[1]) * count + to[2])
                        )
        return lax.ppermute(value, axes, pairs)

    to_chip = lambda v: move(v, lambda i, j, k: (i, j ^ 2, k))
    to_core = lambda v: move(v, lambda i, j, k: (i, j ^ 1, k))
    to_group = lambda v: move(v, lambda i, j, k: (1 - i, j, k))
    to_next = lambda v: move(v, lambda i, j, k: (i, j + 1, k))
    send = lambda v, pairs: move(v, lambda i, j, k: (i, j, pairs.get(k, -1)))
    to_up = lambda v: move(v, lambda i, j, k: (i, j, k + 1))
    to_down = lambda v: move(v, lambda i, j, k: (i, j, k - 1))

    def after(value, *earlier):
        return lax.optimization_barrier((value, *earlier))[0]

    values = tokens.astype(f32)
    inverse_rms = lax.rsqrt(jnp.mean(values * values, axis=1, keepdims=True) + norm_epsilon)
    normed = (values * inverse_rms * norm_gain.astype(f32)[None, :]).astype(bf16)

    weights = jnp.transpose(w_in, (1, 0, 2))
    half = rows // 2
    fine = half // 2
    order = (1, 2, 0)
    out_rows = w_out.shape[0]
    out_half = out_rows // 2
    if paired:
        first_half, other_half = g * half, (1 - g) * half
        peer = to_core(weights)
        pieces = {b: [(weights, b, c * rows), (peer, b, (c ^ 1) * rows)] for b in order}
        nears = []
        for b in order:
            for u in range(half // fine):
                mine = lax.dynamic_slice(weights[b], (first_half + u * fine, 0), (fine, channels))
                if len(nears) >= 2:
                    mine = after(mine, nears[-2])
                near = to_chip(mine)
                far = to_group(near)
                nears.append(near)
                pieces[b] += [
                    (near, None, (c ^ 2) * rows + first_half + u * fine),
                    (to_core(near), None, (c ^ 3) * rows + first_half + u * fine),
                    (far, None, (c ^ 2) * rows + other_half + u * fine),
                    (to_core(far), None, (c ^ 3) * rows + other_half + u * fine),
                ]
        mine = lax.dynamic_slice(w_out, (g * out_half, 0), (out_half, channels))
        near = to_chip(after(mine, nears[-2]))
        far = to_group(near)
        out_peer = to_core(after(w_out, nears[-2]))
        sets = [[w_out], [out_peer], [near, far], [to_core(near), to_core(far)]]
    else:
        full = lax.all_gather(weights, "context", axis=1, tiled=True)
        pieces = {b: [(full, b, 0)] for b in order}
        sets = [[lax.all_gather(w_out, "context", axis=0, tiled=True)]]

    gathered = lax.all_gather(normed, "tensor", axis=0, tiled=True)
    before_rows = to_next(gathered[slab - edge :])

    medium_count = medium_filter.shape[0]
    lag_index = jnp.arange(medium_count, dtype=f32)
    taps = (medium_filter * jnp.exp(-decay[None, :] * lag_index[:, None])).astype(bf16)
    gated, head, tail = gate(gathered, pieces[1], pieces[2], short_filter, width)
    before = to_next(gated[slab - medium_count :])
    edge_rows = to_next(tail)
    query_rows = query(gathered, before_rows, pieces[0], short_filter, width)
    combined = mix(gated, before, head, edge_rows, short_filter, taps, query_rows, width)

    results = []
    for parts in sets:
        partial = [
            lax.dot_general(
                combined, part, (((1,), (1,)), ((), ())), preferred_element_type=f32
            ).astype(bf16)
            for part in parts
        ]

        def block(index, blocks=1):
            index = jnp.clip(index, 0, count - blocks)
            return jnp.concatenate(
                [
                    lax.dynamic_slice(p, (index * length, 0), (blocks * length, p.shape[1]))
                    for p in partial
                ],
                1,
            )

        def plus(*terms):
            total = terms[0].astype(f32)
            for term in terms[1:]:
                total = total + term.astype(f32)
            return total.astype(bf16)

        if count == 4:
            far_pair = block(jnp.where(z < 2, 2, 0), 2)
            got = send(far_pair, {0: 1, 3: 2})
            got = send(plus(far_pair, got), {1: 2, 2: 1})
            low, high = got[:length], got[length:]
            odd = z % 2 == 1
            got_own = jnp.where(odd, high, low)
            got_peer = jnp.where(odd, low, high)
            last = send(plus(block(z ^ 1), got_peer), {0: 1, 1: 0, 2: 3, 3: 2})
            results.append(plus(block(z), got_own, last))
        else:
            up = down = None
            for s in range(1, count):
                rising = block(count + z - s)
                falling = block(z - count + s)
                if up is not None:
                    rising, falling = plus(rising, up), plus(falling, down)
                up, down = to_up(rising), to_down(falling)
            results.append(plus(block(z), up, down))
    if not paired:
        return results[0]
    swap = lambda test, a, b: (jnp.where(test, b, a), jnp.where(test, a, b))
    e0, e1, e2, e3 = results
    e2 = jnp.concatenate(swap(g == 1, e2[:, :out_half], e2[:, out_half:]), 1)
    e3 = jnp.concatenate(swap(g == 1, e3[:, :out_half], e3[:, out_half:]), 1)
    odd = c % 2 == 1
    low = jnp.concatenate(swap(odd, e0, e1), 1)
    high = jnp.concatenate(swap(odd, e2, e3), 1)
    return jnp.concatenate(swap(c >= 2, low, high), 1)


def solution(mesh):
    in_specs = (
        P(axes, None),
        P(),
        P("context", None, "tensor"),
        P(None, None, "tensor"),
        P(None, "tensor"),
        P("tensor"),
        P("context", "tensor"),
    )
    return jax.shard_map(
        local, mesh=mesh, in_specs=in_specs, out_specs=P(axes, None), check_vma=False
    )
```

profile of v0, /device:TPU:0, one launch (start us, length us, event | category | flops | bytes accessed | tf_op | source)
XLA Modules:
  0.0 266.9 jit_solution(4257620666041192860)
XLA Ops:
  7.0 0.7 convert_element_type.151
  7.7 1.5 fusion
  9.2 2.5 fusion.2
  11.8 3.6 %fusion.3 = (bf16[1,1024,1024]{2,1,0:T(8,128)(2,1)S(1)}, bf16[1,1024,1024]{2,1,0:T(8,128)(2,1)S(1)}, bf16[1,1024,1024]{2,1,0:T(8,128)(2,1)S(1)}) fusion(bf16[3,1024,1024]{2,1,0:T(8,128)(2,1)} %bitcast.36), kind=kLoop, calls=%fused_computation.63 | loop fusion | bytes 12582912 | tf_op jit(solution)/shard_map/slice | solution.py:277
  15.4 2.6 collective-permute-start.1
  18.1 12.7 %collective-permute-done.1.rest_2_ = bf16[256,1024]{1,0:T(8,128)(2,1)S(1)} collective-permute-done((bf16[256,1024]{1,0:T(8,128)(2,1)S(1)}, bf16[256,1024]{1,0:T(8,128)(2,1)S(1)}, u32[]{:S(2)}, u32[]{:S(2)}) %collective-permute-start.1) | collective-permute-done | bytes 524320 | tf_op jit(solution)/shard_map/ppermute | solution.py:247
  30.8 2.0 collective-permute-start.3
  32.7 9.1 %collective-permute-done.5.rest_6_ = bf16[256,1024]{1,0:T(8,128)(2,1)S(1)} collective-permute-done((bf16[256,1024]{1,0:T(8,128)(2,1)S(1)}, bf16[256,1024]{1,0:T(8,128)(2,1)S(1)}, u32[]{:S(2)}, u32[]{:S(2)}) %collective-permute-start.5) | collective-permute-done | bytes 524320 | tf_op jit(solution)/shard_map/ppermute | solution.py:247
  41.9 1.7 collective-permute-start.7
  43.7 1.6 collective-permute-start.9
  45.6 1.8 collective-permute-start.13
  47.4 9.2 %collective-permute-done.7.rest_8_ = bf16[256,1024]{1,0:T(8,128)(2,1)S(1)} collective-permute-done((bf16[256,1024]{1,0:T(8,128)(2,1)S(1)}, bf16[256,1024]{1,0:T(8,128)(2,1)S(1)}, u32[]{:S(2)}, u32[]{:S(2)}) %collective-permute-start.7) | collective-permute-done | bytes 524320 | tf_op jit(solution)/shard_map/ppermute | solution.py:247
  56.6 1.9 collective-permute-done.9.rest_12_
  58.5 10.5 %collective-permute-done.13.rest_16_ = bf16[256,1024]{1,0:T(8,128)(2,1)S(1)} collective-permute-done((bf16[256,1024]{1,0:T(8,128)(2,1)S(1)}, bf16[256,1024]{1,0:T(8,128)(2,1)S(1)}, u32[]{:S(2)}, u32[]{:S(2)}) %collective-permute-start.13) | collective-permute-done | bytes 524320 | tf_op jit(solution)/shard_map/ppermute | solution.py:247
  69.4 0.8 copy-done.2
  70.2 1.7 collective-permute-start.20
  72.0 1.6 collective-permute-start.15
  73.6 10.3 %collective-permute-done.11.rest_14_ = bf16[256,1024]{1,0:T(8,128)(2,1)S(1)} collective-permute-done((bf16[256,1024]{1,0:T(8,128)(2,1)S(1)}, bf16[256,1024]{1,0:T(8,128)(2,1)S(1)}, u32[]{:S(2)}, u32[]{:S(2)}) %collective-permute-start.11) | collective-permute-done | bytes 524320 | tf_op jit(solution)/shard_map/ppermute | solution.py:247
  83.9 1.5 collective-permute-start.24
  85.4 1.5 constant_dynamic-slice_fusion.14
  87.5 6.1 %collective-permute-done.15.rest_18_ = bf16[256,1024]{1,0:T(8,128)(2,1)S(1)} collective-permute-done((bf16[256,1024]{1,0:T(8,128)(2,1)S(1)}, bf16[256,1024]{1,0:T(8,128)(2,1)S(1)}, u32[]{:S(2)}, u32[]{:S(2)}) %collective-permute-start.15) | collective-permute-done | bytes 524320 | tf_op jit(solution)/shard_map/ppermute | solution.py:247
  93.6 5.2 %collective-permute-done.24.rest_6_ = bf16[256,1024]{1,0:T(8,128)(2,1)} collective-permute-done((bf16[256,1024]{1,0:T(8,128)(2,1)S(1)}, bf16[256,1024]{1,0:T(8,128)(2,1)}, u32[]{:S(2)}, u32[]{:S(2)}) %collective-permute-start.24) | collective-permute-done | bytes 524320 | tf_op jit(solution)/shard_map/ppermute | solution.py:247
  99.4 1.4 collective-permute-done.16.rest_19_
  101.5 0.9 copy-done.6
  102.4 1.3 collective-permute-start.26
  103.7 13.8 %collective-permute-done.28 = bf16[512,1024]{1,0:T(8,128)(2,1)} collective-permute-done((bf16[512,1024]{1,0:T(8,128)(2,1)S(1)}, bf16[512,1024]{1,0:T(8,128)(2,1)}, u32[]{:S(2)}, u32[]{:S(2)}) %collective-permute-start.28) | collective-permute-done | bytes 1048608 | tf_op jit(solution)/shard_map/ppermute | solution.py:247
  117.5 1.4 collective-permute-start.30
  118.9 8.0 %collective-permute-done.26.rest_8_ = bf16[256,1024]{1,0:T(8,128)(2,1)} collective-permute-done((bf16[256,1024]{1,0:T(8,128)(2,1)}, bf16[256,1024]{1,0:T(8,128)(2,1)}, u32[]{:S(2)}, u32[]{:S(2)}) %collective-permute-start.26) | collective-permute-done | bytes 524320 | tf_op jit(solution)/shard_map/ppermute | solution.py:247
  127.6 1.0 copy-done.3
  128.7 15.6 %gate.1 = (bf16[512,1024]{1,0:T(8,128)(2,1)}, bf16[2,16,1024]{2,1,0:T(8,128)(2,1)S(1)}, bf16[2,16,1024]{2,1,0:T(8,128)(2,1)S(1)}) custom-call(s32[10]{0:T(128)S(1)} %stack.54.at_ref, bf16[512,4096]{1,0:T(8,128)(2,1)} %all-gather.2.cloned.1.call-done.x_ref, f32[3,3,1024]{2,1,0:T(4,128)S(1)} %copy-done.8, bf16[3,1024,1024]{2,1,0:T(8,128)(2,1)} %bitcast.37, ...), custom_call_target="tpu_custom_call" | custom-call | tf_op jit(solution)/shard_map/gate/pallas_call | solution.py:108
  144.3 1.0 slice.56
  145.3 2.0 collective-permute-start.17
  147.3 0.9 slice.73
  148.2 3.5 %collective-permute-start.18 = (bf16[2,16,1024]{2,1,0:T(8,128)(2,1)S(1)}, bf16[2,16,1024]{2,1,0:T(8,128)(2,1)S(1)}, u32[]{:S(2)}, u32[]{:S(2)}) collective-permute-start(bf16[2,16,1024]{2,1,0:T(8,128)(2,1)S(1)} %get-tuple-element.18), channel_id=1, source_target_pairs={{0,4},{1,5},{2,6},{3,7},{4,8},{5,9},{6,10},{7,11},{8,12},{9,13},{1... | collective-permute-start | bytes 196616 | tf_op jit(solution)/shard_map/ppermute | solution.py:247
  151.7 2.0 collective-permute-start.19
  153.9 0.7 collective-permute-done.19.before_ref
  154.6 1.0 collective-permute-start.31
  155.6 1.0 copy-done.5
  156.6 1.0 copy-done.7
  157.7 10.8 %query.1.query_ref = f32[512,1024]{1,0:T(8,128)} custom-call(s32[10]{0:T(128)S(1)} %stack.54.at_ref, bf16[512,4096]{1,0:T(8,128)(2,1)} %all-gather.2.cloned.1.call-done.x_ref, bf16[16,4096]{1,0:T(8,128)(2,1)S(1)} %collective-permute-done.19.before_ref, f32[3,3,1024]{2,1,0:T(4,128)S(1)} %copy-done.8, bf16[3,1024,1024]{2,1,0:T(8,128)(2,1)} %bitcast.39, ...), custom_call_target="tpu_custom_call" | custom-call | tf_op jit(solution)/shard_map/query/pallas_call | solution.py:144
  168.5 1.6 copy-done
  170.1 7.8 %mix.1 = bf16[512,1024]{1,0:T(8,128)(2,1)S(1)} custom-call(bf16[512,1024]{1,0:T(8,128)(2,1)S(1)} %copy-done.1, bf16[128,1024]{1,0:T(8,128)(2,1)S(1)} %collective-permute-done.17.before_ref, bf16[2,16,1024]{2,1,0:T(8,128)(2,1)S(1)} %get-tuple-element.17.head_ref, bf16[2,16,1024]{2,1,0:T(8,128)(2,1)S(1)} %collective-permute-done.18.edge_ref, ...), custom_call_target="tpu_custom_call" | custom-call | tf_op jit(solution)/shard_map/mix/pallas_call | solution.py:206
  178.0 2.9 %convolution_convert_fusion.1 = bf16[512,1024]{0,1:T(8,128)(2,1)S(1)} fusion(bf16[512,1024]{1,0:T(8,128)(2,1)S(1)} %mix.1, bf16[1024,1024]{1,0:T(8,128)(2,1)} %collective-permute-done.38), kind=kOutput, calls=%fused_computation.6 | convolution fusion | flops 1074266112 | bytes 4194304 | tf_op jit(solution)/shard_map/dot_general | solution.py:314
  180.9 3.7 %collective-permute-start.39 = (bf16[256,1024]{0,1:T(8,128)(2,1)S(1)}, bf16[256,1024]{0,1:T(8,128)(2,1)S(1)}, u32[]{:S(2)}, u32[]{:S(2)}) collective-permute-start(bf16[256,1024]{0,1:T(8,128)(2,1)S(1)} %constant_dynamic-slice_fusion.1), channel_id=1, source_target_pairs={{0,1},{3,2},{4,5},{7,6},{8,9},{11,10},{12,13},{15,14},{16,17},{19,... | collective-permute-start | bytes 1572872 | tf_op jit(solution)/shard_map/ppermute | solution.py:247
  184.6 2.0 convolution_convert_fusion.2
  186.6 2.0 convolution_convert_fusion.3
  188.7 1.3 collective-permute-start.35
  190.0 0.7 convolution_convert_fusion.5
  190.9 2.9 %convolution_convert_fusion = bf16[512,1024]{0,1:T(8,128)(2,1)S(1)} fusion(bf16[512,1024]{1,0:T(8,128)(2,1)S(1)} %mix.1, bf16[1024,1024]{1,0:T(8,128)(2,1)} %param.15), kind=kOutput, calls=%fused_computation.5 | convolution fusion | flops 1074266112 | bytes 4194304 | tf_op jit(solution)/shard_map/dot_general | solution.py:314
  193.8 0.7 convolution_convert_fusion.4
  194.7 1.3 collective-permute-start.32
  196.1 1.3 collective-permute-start.42
  197.6 0.7 collective-permute-start.40
  198.3 9.6 %collective-permute-done.35 = bf16[256,1024]{0,1:T(8,128)(2,1)S(1)} collective-permute-done((bf16[256,1024]{0,1:T(8,128)(2,1)S(1)}, bf16[256,1024]{0,1:T(8,128)(2,1)S(1)}, u32[]{:S(2)}, u32[]{:S(2)}) %collective-permute-start.35) | collective-permute-done | bytes 524320 | tf_op jit(solution)/shard_map/ppermute | solution.py:247
  208.1 0.7 collective-permute-start.36
  208.8 10.4 %collective-permute-done.32 = bf16[256,1024]{0,1:T(8,128)(2,1)S(1)} collective-permute-done((bf16[256,1024]{0,1:T(8,128)(2,1)S(1)}, bf16[256,1024]{0,1:T(8,128)(2,1)S(1)}, u32[]{:S(2)}, u32[]{:S(2)}) %collective-permute-start.32) | collective-permute-done | bytes 524320 | tf_op jit(solution)/shard_map/ppermute | solution.py:247
  220.0 9.4 %collective-permute-done.42 = bf16[256,1024]{0,1:T(8,128)(2,1)S(1)} collective-permute-done((bf16[256,1024]{0,1:T(8,128)(2,1)S(1)}, bf16[256,1024]{0,1:T(8,128)(2,1)S(1)}, u32[]{:S(2)}, u32[]{:S(2)}) %collective-permute-start.42) | collective-permute-done | bytes 524320 | tf_op jit(solution)/shard_map/ppermute | solution.py:247
  230.4 5.4 %collective-permute-start.41 = (bf16[128,1024]{0,1:T(8,128)(2,1)S(1)}, bf16[128,1024]{0,1:T(8,128)(2,1)S(1)}, u32[]{:S(2)}, u32[]{:S(2)}) collective-permute-start(bf16[128,1024]{0,1:T(8,128)(2,1)S(1)} %add_convert_fusion.7), channel_id=1, source_target_pairs={{0,1},{1,0},{2,3},{3,2},{4,5},{5,4},{6,7},{7,6},{8,9},{9,8},{10,11... | collective-permute-start | bytes 786440 | tf_op jit(solution)/shard_map/ppermute | solution.py:247
  236.1 2.1 collective-permute-start.34
  238.3 8.8 %collective-permute-start.44 = (bf16[128,1024]{0,1:T(8,128)(2,1)S(1)}, bf16[128,1024]{0,1:T(8,128)(2,1)S(1)}, u32[]{:S(2)}, u32[]{:S(2)}) collective-permute-start(bf16[128,1024]{0,1:T(8,128)(2,1)S(1)} %add_convert_fusion.5), channel_id=1, source_target_pairs={{0,1},{1,0},{2,3},{3,2},{4,5},{5,4},{6,7},{7,6},{8,9},{9,8},{10,11... | collective-permute-start | bytes 786440 | tf_op jit(solution)/shard_map/ppermute | solution.py:247
  247.1 1.5 collective-permute-done.37
  248.8 5.5 %collective-permute-done.34 = bf16[128,1024]{0,1:T(8,128)(2,1)S(1)} collective-permute-done((bf16[128,1024]{0,1:T(8,128)(2,1)S(1)}, bf16[128,1024]{0,1:T(8,128)(2,1)S(1)}, u32[]{:S(2)}, u32[]{:S(2)}) %collective-permute-start.34) | collective-permute-done | bytes 262176 | tf_op jit(solution)/shard_map/ppermute | solution.py:247
  254.5 3.5 %collective-permute-done.44 = bf16[128,1024]{0,1:T(8,128)(2,1)S(1)} collective-permute-done((bf16[128,1024]{0,1:T(8,128)(2,1)S(1)}, bf16[128,1024]{0,1:T(8,128)(2,1)S(1)}, u32[]{:S(2)}, u32[]{:S(2)}) %collective-permute-start.44) | collective-permute-done | bytes 262176 | tf_op jit(solution)/shard_map/ppermute | solution.py:247
  258.7 1.3 copy.12
  (125 shorter events, 8.3 us)
Async XLA Ops:
  6.5 121.1 %all-gather.2.cloned.1.call-start = ((), (), s32[]{:S(2)}) async-start(), calls=%async_computation | async-start | bytes 5242880 | tf_op jit(solution)/shard_map/all_gather | solution.py:299
  6.5 120.4 %collective-permute-start = (bf16[3,1024,1024]{2,1,0:T(8,128)(2,1)}, bf16[3,1024,1024]{2,1,0:T(8,128)(2,1)}, u32[]{:S(2)}, u32[]{:S(2)}) collective-permute-start(bf16[3,1024,1024]{2,1,0:T(8,128)(2,1)} %bitcast.35), channel_id=1, source_target_pairs={{0,4},{1,5},{2,6},{3,7},{4,0},{5,1},{6,2},{7,3},{8,12},{9,13},{10,... | collective-permute-start | bytes 18874376 | tf_op jit(solution)/shard_map/ppermute | solution.py:247
  15.4 15.3 %collective-permute-start.1 = (bf16[256,1024]{1,0:T(8,128)(2,1)S(1)}, bf16[256,1024]{1,0:T(8,128)(2,1)S(1)}, u32[]{:S(2)}, u32[]{:S(2)}) collective-permute-start(bf16[256,1024]{1,0:T(8,128)(2,1)S(1)} %get-tuple-element.34), channel_id=1, source_target_pairs={{0,8},{1,9},{2,10},{3,11},{4,12},{5,13},{6,14},{7,15},{8,0},{9,1},... | collective-permute-start | bytes 1572872 | tf_op jit(solution)/shard_map/ppermute | solution.py:247
  18.0 23.8 %collective-permute-start.5 = (bf16[256,1024]{1,0:T(8,128)(2,1)S(1)}, bf16[256,1024]{1,0:T(8,128)(2,1)S(1)}, u32[]{:S(2)}, u32[]{:S(2)}) collective-permute-start(bf16[256,1024]{1,0:T(8,128)(2,1)S(1)} %get-tuple-element.33), channel_id=1, source_target_pairs={{0,8},{1,9},{2,10},{3,11},{4,12},{5,13},{6,14},{7,15},{8,0},{9,1},... | collective-permute-start | bytes 1572872 | tf_op jit(solution)/shard_map/ppermute | solution.py:247
  30.8 12.9 %collective-permute-start.2 = (bf16[256,1024]{1,0:T(8,128)(2,1)S(1)}, bf16[256,1024]{1,0:T(8,128)(2,1)S(1)}, u32[]{:S(2)}, u32[]{:S(2)}) collective-permute-start(bf16[256,1024]{1,0:T(8,128)(2,1)S(1)} %collective-permute-done.1.rest_2_), channel_id=1, source_target_pairs={{0,4},{1,5},{2,6},{3,7},{4,0},{5,1},{6,2},{7,3},{8,12},{9,13},{10,... | collective-permute-start | bytes 1572872 | tf_op jit(solution)/shard_map/ppermute | solution.py:247
  30.8 14.8 %collective-permute-start.3 = (bf16[256,1024]{1,0:T(8,128)(2,1)S(1)}, bf16[256,1024]{1,0:T(8,128)(2,1)S(1)}, u32[]{:S(2)}, u32[]{:S(2)}) collective-permute-start(bf16[256,1024]{1,0:T(8,128)(2,1)S(1)} %collective-permute-done.1.rest_2_), channel_id=1, source_target_pairs={{0,16},{1,17},{2,18},{3,19},{4,20},{5,21},{6,22},{7,23},{8,24},{9,... | collective-permute-start | bytes 1572872 | tf_op jit(solution)/shard_map/ppermute | solution.py:247
  41.8 5.5 %collective-permute-start.6 = (bf16[256,1024]{1,0:T(8,128)(2,1)S(1)}, bf16[256,1024]{1,0:T(8,128)(2,1)S(1)}, u32[]{:S(2)}, u32[]{:S(2)}) collective-permute-start(bf16[256,1024]{1,0:T(8,128)(2,1)S(1)} %collective-permute-done.5.rest_6_), channel_id=1, source_target_pairs={{0,4},{1,5},{2,6},{3,7},{4,0},{5,1},{6,2},{7,3},{8,12},{9,13},{10,... | collective-permute-start | bytes 1572872 | tf_op jit(solution)/shard_map/ppermute | solution.py:247
  41.9 14.7 %collective-permute-start.7 = (bf16[256,1024]{1,0:T(8,128)(2,1)S(1)}, bf16[256,1024]{1,0:T(8,128)(2,1)S(1)}, u32[]{:S(2)}, u32[]{:S(2)}) collective-permute-start(bf16[256,1024]{1,0:T(8,128)(2,1)S(1)} %collective-permute-done.5.rest_6_), channel_id=1, source_target_pairs={{0,16},{1,17},{2,18},{3,19},{4,20},{5,21},{6,22},{7,23},{8,24},{9,... | collective-permute-start | bytes 1572872 | tf_op jit(solution)/shard_map/ppermute | solution.py:247
  43.7 14.8 %collective-permute-start.9 = (bf16[256,1024]{1,0:T(8,128)(2,1)S(1)}, bf16[256,1024]{1,0:T(8,128)(2,1)S(1)}, u32[]{:S(2)}, u32[]{:S(2)}) collective-permute-start(bf16[256,1024]{1,0:T(8,128)(2,1)S(1)} %get-tuple-element.14), channel_id=1, source_target_pairs={{0,8},{1,9},{2,10},{3,11},{4,12},{5,13},{6,14},{7,15},{8,0},{9,1},... | collective-permute-start | bytes 1572872 | tf_op jit(solution)/shard_map/ppermute | solution.py:247
  45.6 23.5 %collective-permute-start.13 = (bf16[256,1024]{1,0:T(8,128)(2,1)S(1)}, bf16[256,1024]{1,0:T(8,128)(2,1)S(1)}, u32[]{:S(2)}, u32[]{:S(2)}) collective-permute-start(bf16[256,1024]{1,0:T(8,128)(2,1)S(1)} %get-tuple-element.15), channel_id=1, source_target_pairs={{0,8},{1,9},{2,10},{3,11},{4,12},{5,13},{6,14},{7,15},{8,0},{9,1},... | collective-permute-start | bytes 1572872 | tf_op jit(solution)/shard_map/ppermute | solution.py:247
  47.4 22.0 %collective-permute-start.4 = (bf16[256,1024]{1,0:T(8,128)(2,1)S(1)}, bf16[256,1024]{1,0:T(8,128)(2,1)S(1)}, u32[]{:S(2)}, u32[]{:S(2)}) collective-permute-start(bf16[256,1024]{1,0:T(8,128)(2,1)S(1)} %collective-permute-done.3.rest_4_), channel_id=1, source_target_pairs={{0,4},{1,5},{2,6},{3,7},{4,0},{5,1},{6,2},{7,3},{8,12},{9,13},{10,... | collective-permute-start | bytes 1572872 | tf_op jit(solution)/shard_map/ppermute | solution.py:247
  56.6 15.4 %collective-permute-start.8 = (bf16[256,1024]{1,0:T(8,128)(2,1)S(1)}, bf16[256,1024]{1,0:T(8,128)(2,1)S(1)}, u32[]{:S(2)}, u32[]{:S(2)}) collective-permute-start(bf16[256,1024]{1,0:T(8,128)(2,1)S(1)} %collective-permute-done.7.rest_8_), channel_id=1, source_target_pairs={{0,4},{1,5},{2,6},{3,7},{4,0},{5,1},{6,2},{7,3},{8,12},{9,13},{10,... | collective-permute-start | bytes 1572872 | tf_op jit(solution)/shard_map/ppermute | solution.py:247
  58.5 28.4 %copy-start.11 = (bf16[256,1024]{1,0:T(8,128)(2,1)}, bf16[256,1024]{1,0:T(8,128)(2,1)S(1)}, u32[]{:S(2)}) copy-start(bf16[256,1024]{1,0:T(8,128)(2,1)S(1)} %collective-permute-done.9.rest_12_) | copy-start | bytes 1572868
  58.5 13.5 %collective-permute-start.10 = (bf16[256,1024]{1,0:T(8,128)(2,1)S(1)}, bf16[256,1024]{1,0:T(8,128)(2,1)S(1)}, u32[]{:S(2)}, u32[]{:S(2)}) collective-permute-start(bf16[256,1024]{1,0:T(8,128)(2,1)S(1)} %collective-permute-done.9.rest_12_), channel_id=1, source_target_pairs={{0,4},{1,5},{2,6},{3,7},{4,0},{5,1},{6,2},{7,3},{8,12},{9,13},{10,... | collective-permute-start | bytes 1572872 | tf_op jit(solution)/shard_map/ppermute | solution.py:247
  69.0 17.9 %copy-start.12 = (bf16[256,1024]{1,0:T(8,128)(2,1)}, bf16[256,1024]{1,0:T(8,128)(2,1)S(1)}, u32[]{:S(2)}) copy-start(bf16[256,1024]{1,0:T(8,128)(2,1)S(1)} %collective-permute-done.13.rest_16_) | copy-start | bytes 1572868
  69.0 14.9 %collective-permute-start.11 = (bf16[256,1024]{1,0:T(8,128)(2,1)S(1)}, bf16[256,1024]{1,0:T(8,128)(2,1)S(1)}, u32[]{:S(2)}, u32[]{:S(2)}) collective-permute-start(bf16[256,1024]{1,0:T(8,128)(2,1)S(1)} %collective-permute-done.9.rest_12_), channel_id=1, source_target_pairs={{0,16},{1,17},{2,18},{3,19},{4,20},{5,21},{6,22},{7,23},{8,24},{9,... | collective-permute-start | bytes 1572872 | tf_op jit(solution)/shard_map/ppermute | solution.py:247
  69.3 58.3 %copy-start.8 = (f32[3,3,1024]{2,1,0:T(4,128)S(1)}, f32[3,3,1024]{2,1,0:T(4,128)}, u32[]{:S(2)}) copy-start(f32[3,3,1024]{2,1,0:T(4,128)} %short_ref.1) | copy-start | bytes 110596
  70.2 15.2 %collective-permute-start.20 = (bf16[256,1024]{1,0:T(8,128)(2,1)S(1)}, bf16[256,1024]{1,0:T(8,128)(2,1)S(1)}, u32[]{:S(2)}, u32[]{:S(2)}) collective-permute-start(bf16[256,1024]{1,0:T(8,128)(2,1)S(1)} %get-tuple-element.19), channel_id=1, source_target_pairs={{0,8},{1,9},{2,10},{3,11},{4,12},{5,13},{6,14},{7,15},{8,0},{9,1},... | collective-permute-start | bytes 1572872 | tf_op jit(solution)/shard_map/ppermute | solution.py:247
  72.0 46.9 %copy-start.13 = (bf16[256,1024]{1,0:T(8,128)(2,1)}, bf16[256,1024]{1,0:T(8,128)(2,1)S(1)}, u32[]{:S(2)}) copy-start(bf16[256,1024]{1,0:T(8,128)(2,1)S(1)} %collective-permute-done.8.rest_9_) | copy-start | bytes 1572868
  72.0 14.9 %collective-permute-start.14 = (bf16[256,1024]{1,0:T(8,128)(2,1)S(1)}, bf16[256,1024]{1,0:T(8,128)(2,1)S(1)}, u32[]{:S(2)}, u32[]{:S(2)}) collective-permute-start(bf16[256,1024]{1,0:T(8,128)(2,1)S(1)} %collective-permute-done.13.rest_16_), channel_id=1, source_target_pairs={{0,4},{1,5},{2,6},{3,7},{4,0},{5,1},{6,2},{7,3},{8,12},{9,13},{10,... | collective-permute-start | bytes 1572872 | tf_op jit(solution)/shard_map/ppermute | solution.py:247
  72.0 46.9 %copy-start.14 = (bf16[256,1024]{1,0:T(8,128)(2,1)}, bf16[256,1024]{1,0:T(8,128)(2,1)S(1)}, u32[]{:S(2)}) copy-start(bf16[256,1024]{1,0:T(8,128)(2,1)S(1)} %collective-permute-done.10.rest_13_) | copy-start | bytes 1572868
  72.0 21.6 %collective-permute-start.15 = (bf16[256,1024]{1,0:T(8,128)(2,1)S(1)}, bf16[256,1024]{1,0:T(8,128)(2,1)S(1)}, u32[]{:S(2)}, u32[]{:S(2)}) collective-permute-start(bf16[256,1024]{1,0:T(8,128)(2,1)S(1)} %collective-permute-done.13.rest_16_), channel_id=1, source_target_pairs={{0,16},{1,17},{2,18},{3,19},{4,20},{5,21},{6,22},{7,23},{8,24},{9,... | collective-permute-start | bytes 1572872 | tf_op jit(solution)/shard_map/ppermute | solution.py:247
  83.9 43.0 %copy-start.15 = (bf16[256,1024]{1,0:T(8,128)(2,1)}, bf16[256,1024]{1,0:T(8,128)(2,1)S(1)}, u32[]{:S(2)}) copy-start(bf16[256,1024]{1,0:T(8,128)(2,1)S(1)} %collective-permute-done.11.rest_14_) | copy-start | bytes 1572868
  83.9 15.0 %collective-permute-start.24 = (bf16[256,1024]{1,0:T(8,128)(2,1)S(1)}, bf16[256,1024]{1,0:T(8,128)(2,1)}, u32[]{:S(2)}, u32[]{:S(2)}) collective-permute-start(bf16[256,1024]{1,0:T(8,128)(2,1)S(1)} %get-tuple-element.20), channel_id=1, source_target_pairs={{0,8},{1,9},{2,10},{3,11},{4,12},{5,13},{6,14},{7,15},{8,0},{9,1},... | collective-permute-start | bytes 1572872 | tf_op jit(solution)/shard_map/ppermute | solution.py:247
  85.4 15.4 %copy-start.4 = (bf16[256,1024]{1,0:T(8,128)(2,1)}, bf16[256,1024]{1,0:T(8,128)(2,1)S(1)}, u32[]{:S(2)}) copy-start(bf16[256,1024]{1,0:T(8,128)(2,1)S(1)} %collective-permute-done.20.rest_2_) | copy-start | bytes 1572868
  85.4 13.5 %collective-permute-start.12 = (bf16[256,1024]{1,0:T(8,128)(2,1)S(1)}, bf16[256,1024]{1,0:T(8,128)(2,1)S(1)}, u32[]{:S(2)}, u32[]{:S(2)}) collective-permute-start(bf16[256,1024]{1,0:T(8,128)(2,1)S(1)} %collective-permute-done.11.rest_14_), channel_id=1, source_target_pairs={{0,4},{1,5},{2,6},{3,7},{4,0},{5,1},{6,2},{7,3},{8,12},{9,13},{10,... | collective-permute-start | bytes 1572872 | tf_op jit(solution)/shard_map/ppermute | solution.py:247
  86.9 40.0 %copy-start.16 = (bf16[256,1024]{1,0:T(8,128)(2,1)}, bf16[256,1024]{1,0:T(8,128)(2,1)S(1)}, u32[]{:S(2)}) copy-start(bf16[256,1024]{1,0:T(8,128)(2,1)S(1)} %collective-permute-done.14.rest_17_) | copy-start | bytes 1572868
  86.9 30.6 %collective-permute-start.28 = (bf16[512,1024]{1,0:T(8,128)(2,1)S(1)}, bf16[512,1024]{1,0:T(8,128)(2,1)}, u32[]{:S(2)}, u32[]{:S(2)}) collective-permute-start(bf16[512,1024]{1,0:T(8,128)(2,1)S(1)} %constant_dynamic-slice_fusion.14), channel_id=1, source_target_pairs={{0,8},{1,9},{2,10},{3,11},{4,12},{5,13},{6,14},{7,15},{8,0},{9,1},... | collective-permute-start | bytes 3145736 | tf_op jit(solution)/shard_map/ppermute | solution.py:247
  93.6 33.3 %copy-start.17 = (bf16[256,1024]{1,0:T(8,128)(2,1)}, bf16[256,1024]{1,0:T(8,128)(2,1)S(1)}, u32[]{:S(2)}) copy-start(bf16[256,1024]{1,0:T(8,128)(2,1)S(1)} %collective-permute-done.15.rest_18_) | copy-start | bytes 1572868
  93.6 84.3 %collective-permute-start.38 = (bf16[1024,1024]{1,0:T(8,128)(2,1)}, bf16[1024,1024]{1,0:T(8,128)(2,1)}, u32[]{:S(2)}, u32[]{:S(2)}) collective-permute-start(bf16[1024,1024]{1,0:T(8,128)(2,1)} %param.15), channel_id=1, source_target_pairs={{0,4},{1,5},{2,6},{3,7},{4,0},{5,1},{6,2},{7,3},{8,12},{9,13},{10,... | collective-permute-start | bytes 6291464 | tf_op jit(solution)/shard_map/ppermute | solution.py:247
  98.9 1.9 collective-permute-start.16
  98.9 28.1 %copy-start.18 = (bf16[256,1024]{1,0:T(8,128)(2,1)}, bf16[256,1024]{1,0:T(8,128)(2,1)S(1)}, u32[]{:S(2)}) copy-start(bf16[256,1024]{1,0:T(8,128)(2,1)S(1)} %collective-permute-done.12.rest_15_) | copy-start | bytes 1572868
  98.9 2.6 collective-permute-start.21
  100.8 26.2 %copy-start.19 = (bf16[256,1024]{1,0:T(8,128)(2,1)}, bf16[256,1024]{1,0:T(8,128)(2,1)S(1)}, u32[]{:S(2)}) copy-start(bf16[256,1024]{1,0:T(8,128)(2,1)S(1)} %collective-permute-done.16.rest_19_) | copy-start | bytes 1572868
  100.8 18.1 %collective-permute-start.22 = (bf16[256,1024]{1,0:T(8,128)(2,1)S(1)}, bf16[256,1024]{1,0:T(8,128)(2,1)}, u32[]{:S(2)}, u32[]{:S(2)}) collective-permute-start(bf16[256,1024]{1,0:T(8,128)(2,1)S(1)} %collective-permute-done.20.rest_2_), channel_id=1, source_target_pairs={{0,16},{1,17},{2,18},{3,19},{4,20},{5,21},{6,22},{7,23},{8,24},{9,... | collective-permute-start | bytes 1572872 | tf_op jit(solution)/shard_map/ppermute | solution.py:247
  102.4 24.5 %collective-permute-start.26 = (bf16[256,1024]{1,0:T(8,128)(2,1)}, bf16[256,1024]{1,0:T(8,128)(2,1)}, u32[]{:S(2)}, u32[]{:S(2)}) collective-permute-start(bf16[256,1024]{1,0:T(8,128)(2,1)} %collective-permute-done.24.rest_6_), channel_id=1, source_target_pairs={{0,16},{1,17},{2,18},{3,19},{4,20},{5,21},{6,22},{7,23},{8,24},{9,... | collective-permute-start | bytes 1572872 | tf_op jit(solution)/shard_map/ppermute | solution.py:247
  117.5 36.3 %collective-permute-start.30 = (bf16[512,1024]{1,0:T(8,128)(2,1)}, bf16[512,1024]{1,0:T(8,128)(2,1)}, u32[]{:S(2)}, u32[]{:S(2)}) collective-permute-start(bf16[512,1024]{1,0:T(8,128)(2,1)} %collective-permute-done.28), channel_id=1, source_target_pairs={{0,16},{1,17},{2,18},{3,19},{4,20},{5,21},{6,22},{7,23},{8,24},{9,... | collective-permute-start | bytes 3145736 | tf_op jit(solution)/shard_map/ppermute | solution.py:247
  118.9 26.4 %collective-permute-start.25 = (bf16[256,1024]{1,0:T(8,128)(2,1)}, bf16[256,1024]{1,0:T(8,128)(2,1)}, u32[]{:S(2)}, u32[]{:S(2)}) collective-permute-start(bf16[256,1024]{1,0:T(8,128)(2,1)} %collective-permute-done.24.rest_6_), channel_id=1, source_target_pairs={{0,4},{1,5},{2,6},{3,7},{4,0},{5,1},{6,2},{7,3},{8,12},{9,13},{10,... | collective-permute-start | bytes 1572872 | tf_op jit(solution)/shard_map/ppermute | solution.py:247
  126.9 21.3 %collective-permute-start.23 = (bf16[256,1024]{1,0:T(8,128)(2,1)}, bf16[256,1024]{1,0:T(8,128)(2,1)}, u32[]{:S(2)}, u32[]{:S(2)}) collective-permute-start(bf16[256,1024]{1,0:T(8,128)(2,1)} %collective-permute-done.22.rest_4_), channel_id=1, source_target_pairs={{0,4},{1,5},{2,6},{3,7},{4,0},{5,1},{6,2},{7,3},{8,12},{9,13},{10,... | collective-permute-start | bytes 1572872 | tf_op jit(solution)/shard_map/ppermute | solution.py:247
  126.9 24.7 %collective-permute-start.27 = (bf16[256,1024]{1,0:T(8,128)(2,1)}, bf16[256,1024]{1,0:T(8,128)(2,1)}, u32[]{:S(2)}, u32[]{:S(2)}) collective-permute-start(bf16[256,1024]{1,0:T(8,128)(2,1)} %collective-permute-done.26.rest_8_), channel_id=1, source_target_pairs={{0,4},{1,5},{2,6},{3,7},{4,0},{5,1},{6,2},{7,3},{8,12},{9,13},{10,... | collective-permute-start | bytes 1572872 | tf_op jit(solution)/shard_map/ppermute | solution.py:247
  127.6 1.0 copy-start.3
  128.7 18.6 %copy-start.21 = (f32[1024]{0:T(1024)S(1)}, f32[1024]{0:T(1024)}, u32[]{:S(2)}) copy-start(f32[1024]{0:T(1024)} %param.14) | copy-start | bytes 12292
  128.7 25.0 %copy-start.20 = (f32[128,1024]{1,0:T(8,128)S(1)}, f32[128,1024]{1,0:T(8,128)}, u32[]{:S(2)}) copy-start(f32[128,1024]{1,0:T(8,128)} %param.13) | copy-start | bytes 1572868
  145.3 23.2 %collective-permute-start.17 = (bf16[128,1024]{1,0:T(8,128)(2,1)S(1)}, bf16[128,1024]{1,0:T(8,128)(2,1)S(1)}, u32[]{:S(2)}, u32[]{:S(2)}) collective-permute-start(bf16[128,1024]{1,0:T(8,128)(2,1)S(1)} %slice.56), channel_id=1, source_target_pairs={{0,4},{1,5},{2,6},{3,7},{4,8},{5,9},{6,10},{7,11},{8,12},{9,13},{1... | collective-permute-start | bytes 786440 | tf_op jit(solution)/shard_map/ppermute | solution.py:247
  148.2 20.3 %collective-permute-start.18 = (bf16[2,16,1024]{2,1,0:T(8,128)(2,1)S(1)}, bf16[2,16,1024]{2,1,0:T(8,128)(2,1)S(1)}, u32[]{:S(2)}, u32[]{:S(2)}) collective-permute-start(bf16[2,16,1024]{2,1,0:T(8,128)(2,1)S(1)} %get-tuple-element.18), channel_id=1, source_target_pairs={{0,4},{1,5},{2,6},{3,7},{4,8},{5,9},{6,10},{7,11},{8,12},{9,13},{1... | collective-permute-start | bytes 196616 | tf_op jit(solution)/shard_map/ppermute | solution.py:247
  151.7 2.9 %collective-permute-start.19 = (bf16[16,4096]{1,0:T(8,128)(2,1)S(1)}, bf16[16,4096]{1,0:T(8,128)(2,1)S(1)}, u32[]{:S(2)}, u32[]{:S(2)}) collective-permute-start(bf16[16,4096]{1,0:T(8,128)(2,1)S(1)} %slice.73), channel_id=1, source_target_pairs={{0,4},{1,5},{2,6},{3,7},{4,8},{5,9},{6,10},{7,11},{8,12},{9,13},{1... | collective-permute-start | bytes 393224 | tf_op jit(solution)/shard_map/ppermute | solution.py:247
  153.8 14.7 %copy-start.1 = (bf16[512,1024]{1,0:T(8,128)(2,1)S(1)}, bf16[512,1024]{1,0:T(8,128)(2,1)}, u32[]{:S(2)}) copy-start(bf16[512,1024]{1,0:T(8,128)(2,1)} %get-tuple-element.16.gated_ref) | copy-start | bytes 3145732
  153.8 36.2 %collective-permute-start.29 = (bf16[512,1024]{1,0:T(8,128)(2,1)}, bf16[512,1024]{1,0:T(8,128)(2,1)S(1)}, u32[]{:S(2)}, u32[]{:S(2)}) collective-permute-start(bf16[512,1024]{1,0:T(8,128)(2,1)} %collective-permute-done.28), channel_id=1, source_target_pairs={{0,4},{1,5},{2,6},{3,7},{4,0},{5,1},{6,2},{7,3},{8,12},{9,13},{10,... | collective-permute-start | bytes 3145736 | tf_op jit(solution)/shard_map/ppermute | solution.py:247
  154.6 39.2 %collective-permute-start.31 = (bf16[512,1024]{1,0:T(8,128)(2,1)}, bf16[512,1024]{1,0:T(8,128)(2,1)S(1)}, u32[]{:S(2)}, u32[]{:S(2)}) collective-permute-start(bf16[512,1024]{1,0:T(8,128)(2,1)} %collective-permute-done.30), channel_id=1, source_target_pairs={{0,4},{1,5},{2,6},{3,7},{4,0},{5,1},{6,2},{7,3},{8,12},{9,13},{10,... | collective-permute-start | bytes 3145736 | tf_op jit(solution)/shard_map/ppermute | solution.py:247
  157.7 10.9 %copy-start.9 = (bf16[128,768]{1,0:T(8,128)(2,1)S(1)}, bf16[128,768]{1,0:T(8,128)(2,1)}, u32[]{:S(2)}) copy-start(bf16[128,768]{1,0:T(8,128)(2,1)} %constant.68.clone.inv_ref) | copy-start | bytes 589828
  157.7 10.9 %copy-start.10 = (bf16[512,128]{1,0:T(8,128)(2,1)S(1)}, bf16[512,128]{1,0:T(8,128)(2,1)}, u32[]{:S(2)}) copy-start(bf16[512,128]{1,0:T(8,128)(2,1)} %constant.67.clone.fwd_ref) | copy-start | bytes 393220
  168.5 1.6 copy-start
  180.9 16.5 %collective-permute-start.39 = (bf16[256,1024]{0,1:T(8,128)(2,1)S(1)}, bf16[256,1024]{0,1:T(8,128)(2,1)S(1)}, u32[]{:S(2)}, u32[]{:S(2)}) collective-permute-start(bf16[256,1024]{0,1:T(8,128)(2,1)S(1)} %constant_dynamic-slice_fusion.1), channel_id=1, source_target_pairs={{0,1},{3,2},{4,5},{7,6},{8,9},{11,10},{12,13},{15,14},{16,17},{19,... | collective-permute-start | bytes 1572872 | tf_op jit(solution)/shard_map/ppermute | solution.py:247
  188.7 19.3 %collective-permute-start.35 = (bf16[256,1024]{0,1:T(8,128)(2,1)S(1)}, bf16[256,1024]{0,1:T(8,128)(2,1)S(1)}, u32[]{:S(2)}, u32[]{:S(2)}) collective-permute-start(bf16[256,1024]{0,1:T(8,128)(2,1)S(1)} %pad_maximum_fusion.2), channel_id=1, source_target_pairs={{0,1},{3,2},{4,5},{7,6},{8,9},{11,10},{12,13},{15,14},{16,17},{19,... | collective-permute-start | bytes 1572872 | tf_op jit(solution)/shard_map/ppermute | solution.py:247
  194.7 24.5 %collective-permute-start.32 = (bf16[256,1024]{0,1:T(8,128)(2,1)S(1)}, bf16[256,1024]{0,1:T(8,128)(2,1)S(1)}, u32[]{:S(2)}, u32[]{:S(2)}) collective-permute-start(bf16[256,1024]{0,1:T(8,128)(2,1)S(1)} %pad_maximum_fusion.1), channel_id=1, source_target_pairs={{0,1},{3,2},{4,5},{7,6},{8,9},{11,10},{12,13},{15,14},{16,17},{19,... | collective-permute-start | bytes 1572872 | tf_op jit(solution)/shard_map/ppermute | solution.py:247
  196.1 33.3 %collective-permute-start.42 = (bf16[256,1024]{0,1:T(8,128)(2,1)S(1)}, bf16[256,1024]{0,1:T(8,128)(2,1)S(1)}, u32[]{:S(2)}, u32[]{:S(2)}) collective-permute-start(bf16[256,1024]{0,1:T(8,128)(2,1)S(1)} %constant_dynamic-slice_fusion), channel_id=1, source_target_pairs={{0,1},{3,2},{4,5},{7,6},{8,9},{11,10},{12,13},{15,14},{16,17},{19,... | collective-permute-start | bytes 1572872 | tf_op jit(solution)/shard_map/ppermute | solution.py:247
  197.6 32.7 %collective-permute-start.40 = (bf16[256,1024]{0,1:T(8,128)(2,1)S(1)}, bf16[256,1024]{0,1:T(8,128)(2,1)S(1)}, u32[]{:S(2)}, u32[]{:S(2)}) collective-permute-start(bf16[256,1024]{0,1:T(8,128)(2,1)S(1)} %add_convert_fusion.1), channel_id=1, source_target_pairs={{1,2},{2,1},{5,6},{6,5},{9,10},{10,9},{13,14},{14,13},{17,18},{18,... | collective-permute-start | bytes 1572872 | tf_op jit(solution)/shard_map/ppermute | solution.py:247
  208.1 27.7 %collective-permute-start.36 = (bf16[256,1024]{0,1:T(8,128)(2,1)S(1)}, bf16[256,1024]{0,1:T(8,128)(2,1)S(1)}, u32[]{:S(2)}, u32[]{:S(2)}) collective-permute-start(bf16[256,1024]{0,1:T(8,128)(2,1)S(1)} %add_convert_fusion.2), channel_id=1, source_target_pairs={{1,2},{2,1},{5,6},{6,5},{9,10},{10,9},{13,14},{14,13},{17,18},{18,... | collective-permute-start | bytes 1572872 | tf_op jit(solution)/shard_map/ppermute | solution.py:247
  219.3 16.7 %collective-permute-start.33 = (bf16[256,1024]{0,1:T(8,128)(2,1)S(1)}, bf16[256,1024]{0,1:T(8,128)(2,1)S(1)}, u32[]{:S(2)}, u32[]{:S(2)}) collective-permute-start(bf16[256,1024]{0,1:T(8,128)(2,1)S(1)} %add_convert_fusion.3), channel_id=1, source_target_pairs={{1,2},{2,1},{5,6},{6,5},{9,10},{10,9},{13,14},{14,13},{17,18},{18,... | collective-permute-start | bytes 1572872 | tf_op jit(solution)/shard_map/ppermute | solution.py:247
  229.6 8.6 %collective-permute-start.43 = (bf16[256,1024]{0,1:T(8,128)(2,1)S(1)}, bf16[256,1024]{0,1:T(8,128)(2,1)S(1)}, u32[]{:S(2)}, u32[]{:S(2)}) collective-permute-start(bf16[256,1024]{0,1:T(8,128)(2,1)S(1)} %add_convert_fusion), channel_id=1, source_target_pairs={{1,2},{2,1},{5,6},{6,5},{9,10},{10,9},{13,14},{14,13},{17,18},{18,... | collective-permute-start | bytes 1572872 | tf_op jit(solution)/shard_map/ppermute | solution.py:247
  230.4 24.0 %collective-permute-start.41 = (bf16[128,1024]{0,1:T(8,128)(2,1)S(1)}, bf16[128,1024]{0,1:T(8,128)(2,1)S(1)}, u32[]{:S(2)}, u32[]{:S(2)}) collective-permute-start(bf16[128,1024]{0,1:T(8,128)(2,1)S(1)} %add_convert_fusion.7), channel_id=1, source_target_pairs={{0,1},{1,0},{2,3},{3,2},{4,5},{5,4},{6,7},{7,6},{8,9},{9,8},{10,11... | collective-permute-start | bytes 786440 | tf_op jit(solution)/shard_map/ppermute | solution.py:247
  235.9 12.7 %collective-permute-start.37 = (bf16[128,1024]{0,1:T(8,128)(2,1)S(1)}, bf16[128,1024]{0,1:T(8,128)(2,1)S(1)}, u32[]{:S(2)}, u32[]{:S(2)}) collective-permute-start(bf16[128,1024]{0,1:T(8,128)(2,1)S(1)} %add_convert_fusion.9), channel_id=1, source_target_pairs={{0,1},{1,0},{2,3},{3,2},{4,5},{5,4},{6,7},{7,6},{8,9},{9,8},{10,11... | collective-permute-start | bytes 786440 | tf_op jit(solution)/shard_map/ppermute | solution.py:247
  236.1 18.1 %collective-permute-start.34 = (bf16[128,1024]{0,1:T(8,128)(2,1)S(1)}, bf16[128,1024]{0,1:T(8,128)(2,1)S(1)}, u32[]{:S(2)}, u32[]{:S(2)}) collective-permute-start(bf16[128,1024]{0,1:T(8,128)(2,1)S(1)} %add_convert_fusion.11), channel_id=1, source_target_pairs={{0,1},{1,0},{2,3},{3,2},{4,5},{5,4},{6,7},{7,6},{8,9},{9,8},{10,11... | collective-permute-start | bytes 786440 | tf_op jit(solution)/shard_map/ppermute | solution.py:247
  238.3 19.7 %collective-permute-start.44 = (bf16[128,1024]{0,1:T(8,128)(2,1)S(1)}, bf16[128,1024]{0,1:T(8,128)(2,1)S(1)}, u32[]{:S(2)}, u32[]{:S(2)}) collective-permute-start(bf16[128,1024]{0,1:T(8,128)(2,1)S(1)} %add_convert_fusion.5), channel_id=1, source_target_pairs={{0,1},{1,0},{2,3},{3,2},{4,5},{5,4},{6,7},{7,6},{8,9},{9,8},{10,11... | collective-permute-start | bytes 786440 | tf_op jit(solution)/shard_map/ppermute | solution.py:247
  (4 other events, 3.8 us)
Sparse Core Ops, SparseCore 0:
  11.9 83.1 all-gather.1
where the time goes:
time: 268 us; the launch traced here: 267 us
  waiting for transfers between devices  130 us (49%)
  starting transfers between devices  55.1 us (21%)
  Pallas kernels  34.3 us (13%)
  local copies, waits for them, and re-layouts  15.4 us (6%)
  between operations  14.1 us (5%)
  matrix products  11.2 us (4%)
  other arithmetic  7.03 us (3%)
    ppermute x45, waiting for transfers between devices, move(): return lax.ppermute(value, axes, pairs)  130 us
    ppermute x45, starting transfers between devices, move(): return lax.ppermute(value, axes, pairs)  55.1 us
    pallas_call x1, Pallas kernels, gate(): pl.pallas_call(functools.partial(gate_kernel, (len(one), len(two))), grid...  15.6 us
    dot_general x6, matrix products, local(): lax.dot_general(combined, part, (((1,), (1,)), ((), ())), preferred_eleme...  11.2 us
    pallas_call x1, Pallas kernels, query(): pl.pallas_call(query_kernel, grid_spec=grid_spec, out_shape=jax.ShapeDtyp...  10.8 us
    pallas_call x1, Pallas kernels, mix(): pl.pallas_call(mix_kernel, grid=(channels // width,), in_specs=[col(slab)...  7.83 us
    unnamed x44, local copies, waits for them, and re-layouts  6.43 us
  transfers between devices with their start and end apart: 46, of which 20 were waited for; matrix products, arithmetic and copies ran while one was open for 9% of the time, Pallas kernels for 13%

commit v1 on v0

--- a/solution.py
+++ b/solution.py
@@ -34,7 +34,7 @@
     inverse = (forward * weight)[:, taps:].T
     fh, fl = split_parts(forward[:, :taps])
     ih, il = split_parts(inverse)
-    return np.concatenate([fh, fl], axis=0), np.concatenate([ih, ih, il], axis=1)
+    return np.concatenate([fh, fl], axis=1), np.concatenate([ih, ih, il], axis=1)
 
 
 def short_sum(s, taps_ref, branch, slab):
@@ -45,41 +45,79 @@
     return total
 
 
-def product(at_ref, x_ref, pieces):
-    total = None
-    for n, piece in enumerate(pieces):
-        depth = piece.shape[-2]
-        step = min(depth, 256)
-        part = x_ref[:, pl.ds(pl.multiple_of(at_ref[n], step), depth)]
-        term = jnp.dot(part, piece[...], preferred_element_type=f32)
-        total = term if total is None else total + term
-    return total.astype(bf16).astype(f32)
-
-
-def gate_kernel(counts, at_ref, x_ref, taps_ref, *rest):
+def norm_kernel(x_ref, gain_ref, out_ref):
+    values = x_ref[...].astype(f32)
+    mean = jnp.mean(values * values, axis=1, keepdims=True)
+    scaled = values * lax.rsqrt(mean + norm_epsilon)
+    out_ref[...] = (scaled * gain_ref[...].astype(f32)).astype(bf16)
+
+
+def norm(tokens, gain):
+    length, features = tokens.shape
+    rows = min(length, 32)
+    return pl.pallas_call(
+        norm_kernel,
+        grid=(length // rows,),
+        in_specs=[
+            pl.BlockSpec((rows, features), lambda i: (i, 0)),
+            pl.BlockSpec((1, features), lambda i: (0, 0)),
+        ],
+        out_specs=pl.BlockSpec((rows, features), lambda i: (i, 0)),
+        out_shape=jax.ShapeDtypeStruct((length, features), bf16),
+        name="norm",
+    )(tokens, gain.reshape(1, features))
+
+
+def fetch(kinds, at_ref, arrays, buffer, sems, step, slot, width):
+    copies = []
+    columns = pl.ds(pl.multiple_of(step * width, width), width)
+    for n, ((place, branch, depth), array) in enumerate(zip(kinds, arrays)):
+        source = array.at[:, columns] if branch is None else array.at[branch, :, columns]
+        at = at_ref[n % at_ref.shape[0]]
+        rows = pl.ds(pl.multiple_of(at, min(depth, 256)), depth)
+        copies.append(
+            pltpu.make_async_copy(source, buffer.at[slot, place, rows], sems.at[slot, n])
+        )
+    return copies
+
+
+def rotate(kinds, at_ref, arrays, buffer, sems, width):
+    step, steps = pl.program_id(0), pl.num_programs(0)
+    slot = lax.rem(step, 2)
+
+    @pl.when(step == 0)
+    def _():
+        for copy in fetch(kinds, at_ref, arrays, buffer, sems, 0, 0, width):
+            copy.start()
+
+    @pl.when(step + 1 < steps)
+    def _():
+        for copy in fetch(kinds, at_ref, arrays, buffer, sems, step + 1, 1 - slot, width):
+            copy.start()
+
+    for copy in fetch(kinds, at_ref, arrays, buffer, sems, step, slot, width):
+        copy.wait()
+    return slot
+
+
+def gate_kernel(kinds, width, at_ref, x_ref, taps_ref, *rest):
     slab = x_ref.shape[0]
-    pieces = [rest[: counts[0]], rest[counts[0] : sum(counts)]]
-    gated_ref, head_ref, tail_ref, s = rest[sum(counts) :]
+    arrays = rest[: len(kinds)]
+    gated_ref, head_ref, tail_ref, s, buffer, sems = rest[len(kinds) :]
+    slot = rotate(kinds, at_ref, arrays, buffer, sems, width)
     feats = []
     for k in range(2):
-        s[0:edge] = jnp.zeros((edge, s.shape[1]), f32)
-        s[edge : edge + slab] = product(at_ref, x_ref, pieces[k])
+        s[0:edge] = jnp.zeros((edge, width), f32)
+        term = jnp.dot(x_ref[...], buffer[slot, k], preferred_element_type=f32)
+        s[edge : edge + slab] = term.astype(bf16).astype(f32)
         head_ref[k] = s[edge : 2 * edge].astype(bf16)
         tail_ref[k] = s[slab : slab + edge].astype(bf16)
         feats.append(short_sum(s, taps_ref, k + 1, slab))
     gated_ref[...] = (feats[0] * feats[1]).astype(bf16)
 
 
-def piece_specs(pieces, width):
-    specs = []
-    for array, branch, _ in pieces:
-        if branch is None:
-            specs.append(pl.BlockSpec((array.shape[0], width), lambda i, at: (0, i)))
-        else:
-            specs.append(
-                pl.BlockSpec((None, array.shape[1], width), lambda i, at, b=branch: (b, 0, i))
-            )
-    return specs
+def kinds_of(pieces, place):
+    return tuple((place, branch, array.shape[-2]) for array, branch, _ in pieces)
 
 
 def offsets(pieces):
@@ -87,73 +125,122 @@
 
 
 def gate(x, one, two, short_filter, width):
-    slab = x.shape[0]
+    slab, features = x.shape
     channels = short_filter.shape[-1]
+    kinds = kinds_of(one, 0) + kinds_of(two, 1)
     grid_spec = pltpu.PrefetchScalarGridSpec(
         num_scalar_prefetch=1,
         grid=(channels // width,),
         in_specs=[
-            pl.BlockSpec(x.shape, lambda i, at: (0, 0)),
+            pl.BlockSpec(x.shape, lambda i, at: (0, 0), pipeline_mode=pl.Buffered(1)),
             pl.BlockSpec(short_filter.shape[:2] + (width,), lambda i, at: (0, 0, i)),
         ]
-        + piece_specs(one, width)
-        + piece_specs(two, width),
+        + [pl.BlockSpec(memory_space=pl.ANY)] * len(kinds),
         out_specs=[
             pl.BlockSpec((slab, width), lambda i, at: (0, i)),
             pl.BlockSpec((2, edge, width), lambda i, at: (0, 0, i)),
             pl.BlockSpec((2, edge, width), lambda i, at: (0, 0, i)),
         ],
-        scratch_shapes=[pltpu.VMEM((slab + edge, width), f32)],
+        scratch_shapes=[
+            pltpu.VMEM((slab + edge, width), f32),
+            pltpu.VMEM((2, 2, features, width), bf16),
+            pltpu.SemaphoreType.DMA((2, len(kinds))),
+        ],
     )
     return pl.pallas_call(
-        functools.partial(gate_kernel, (len(one), len(two))),
+        functools.partial(gate_kernel, kinds, width),
         grid_spec=grid_spec,
         out_shape=[
             jax.ShapeDtypeStruct((slab, channels), bf16),
             jax.ShapeDtypeStruct((2, edge, channels), bf16),
             jax.ShapeDtypeStruct((2, edge, channels), bf16),
         ],
-        compiler_params=pltpu.CompilerParams(vmem_limit_bytes=50 << 20),
+        compiler_params=pltpu.CompilerParams(vmem_limit_bytes=40 << 20),
         name="gate",
     )(offsets(one), x, short_filter, *[p[0] for p in one + two])
 
 
-def query_kernel(at_ref, x_ref, before_ref, taps_ref, *rest):
+def query_kernel(kinds, width, at_ref, x_ref, before_ref, taps_ref, *rest):
     slab = x_ref.shape[0]
-    *pieces, out_ref, s = rest
-    s[0:edge] = product(at_ref, before_ref, pieces)
-    s[edge : edge + slab] = product(at_ref, x_ref, pieces)
+    arrays = rest[: len(kinds)]
+    out_ref, s, full, buffer, sems = rest[len(kinds) :]
+
+    @pl.when(pl.program_id(0) == 0)
+    def _():
+        full[0:edge] = before_ref[...]
+        full[edge : edge + slab] = x_ref[...]
+
+    slot = rotate(kinds, at_ref, arrays, buffer, sems, width)
+    term = jnp.dot(full[...], buffer[slot, 0], preferred_element_type=f32)
+    s[...] = term.astype(bf16).astype(f32)
     out_ref[...] = short_sum(s, taps_ref, 0, slab)
 
 
 def query(x, before, pieces, short_filter, width):
-    slab = x.shape[0]
+    slab, features = x.shape
     channels = short_filter.shape[-1]
+    kinds = kinds_of(pieces, 0)
     grid_spec = pltpu.PrefetchScalarGridSpec(
         num_scalar_prefetch=1,
         grid=(channels // width,),
         in_specs=[
-            pl.BlockSpec(x.shape, lambda i, at: (0, 0)),
-            pl.BlockSpec(before.shape, lambda i, at: (0, 0)),
+            pl.BlockSpec(x.shape, lambda i, at: (0, 0), pipeline_mode=pl.Buffered(1)),
+            pl.BlockSpec(before.shape, lambda i, at: (0, 0), pipeline_mode=pl.Buffered(1)),
             pl.BlockSpec(short_filter.shape[:2] + (width,), lambda i, at: (0, 0, i)),
         ]
-        + piece_specs(pieces, width),
+        + [pl.BlockSpec(memory_space=pl.ANY)] * len(kinds),
         out_specs=pl.BlockSpec((slab, width), lambda i, at: (0, i)),
-        scratch_shapes=[pltpu.VMEM((slab + edge, width), f32)],
+        scratch_shapes=[
+            pltpu.VMEM((slab + edge, width), f32),
+            pltpu.VMEM((slab + edge, features), bf16),
+            pltpu.VMEM((2, 1, features, width), bf16),
+            pltpu.SemaphoreType.DMA((2, len(kinds))),
+        ],
     )
     return pl.pallas_call(
-        query_kernel,
+        functools.partial(query_kernel, kinds, width),
         grid_spec=grid_spec,
         out_shape=jax.ShapeDtypeStruct((slab, channels), f32),
-        compiler_params=pltpu.CompilerParams(vmem_limit_bytes=50 << 20),
+        compiler_params=pltpu.CompilerParams(vmem_limit_bytes=40 << 20),
         name="query",
     )(offsets(pieces), x, before, short_filter, *[p[0] for p in pieces])
 
 
+def transform(fwd_ref, block):
+    return jnp.dot(fwd_ref[...], jnp.concatenate([block, block], axis=0), preferred_element_type=f32)
+
+
+def respond_kernel(filter_ref, decay_ref, fwd_ref, out_ref):
+    taps = filter_ref.shape[0]
+    lag = lax.broadcasted_iota(jnp.int32, (taps, 1), 0)
+    faded = filter_ref[...] * jnp.exp(-decay_ref[...] * lag.astype(f32))
+    response = transform(fwd_ref, faded.astype(bf16))
+    h_cos, h_sin = response[:taps], response[taps:]
+    out_ref[0] = h_cos
+    out_ref[1] = jnp.where(lag == 0, 0.0, h_sin)
+    out_ref[2] = jnp.where(lag == 0, h_sin, h_cos)
+
+
+def respond(medium_filter, decay, forward, width):
+    taps, channels = medium_filter.shape
+    return pl.pallas_call(
+        respond_kernel,
+        grid=(channels // width,),
+        in_specs=[
+            pl.BlockSpec((taps, width), lambda i: (0, i)),
+            pl.BlockSpec((1, width), lambda i: (0, i)),
+            pl.BlockSpec(forward.shape, lambda i: (0, 0)),
+        ],
+        out_specs=pl.BlockSpec((3, taps, width), lambda i: (0, 0, i)),
+        out_shape=jax.ShapeDtypeStruct((3, taps, channels), f32),
+        name="respond",
+    )(medium_filter, decay.reshape(1, channels), forward)
+
+
 def mix_kernel(
-    gated_ref, before_ref, head_ref, edge_ref, short_ref, taps_ref, query_ref, fwd_ref, inv_ref, out_ref, s
+    gated_ref, before_ref, head_ref, edge_ref, short_ref, response_ref, query_ref, fwd_ref, inv_ref, out_ref, s
 ):
-    taps = taps_ref.shape[0]
+    taps = response_ref.shape[1]
     blocks = gated_ref.shape[0] // taps
     feats = []
     for k in range(2):
@@ -166,24 +253,16 @@
         feats.append(total)
     first = (feats[0] * feats[1]).astype(bf16)
 
-    def transform(block):
-        both = jnp.dot(fwd_ref[...], block, preferred_element_type=f32)
-        return both[: 2 * taps] + both[2 * taps :]
-
     row = lax.broadcasted_iota(jnp.int32, (2 * taps, 1), 0)
     sign = jnp.where(row % 2 == 0, 1.0, -1.0).astype(f32)
-    is_zero = lax.broadcasted_iota(jnp.int32, (taps, 1), 0) == 0
-    response = transform(taps_ref[...])
-    h_cos, h_sin = response[:taps], response[taps:]
-    h_low = jnp.where(is_zero, h_sin, h_cos)
-    h_sin = jnp.where(is_zero, 0.0, h_sin)
-    last = transform(before_ref[...])
+    h_cos, h_sin, h_low = response_ref[0], response_ref[1], response_ref[2]
+    last = transform(fwd_ref, before_ref[...])
     for b in range(blocks):
         if b == 0:
             block = jnp.concatenate([first, gated_ref[edge:taps]], axis=0)
         else:
             block = gated_ref[b * taps : (b + 1) * taps]
-        now = transform(block)
+        now = transform(fwd_ref, block)
         x = last + sign * now
         last = now
         x_cos, x_sin = x[:taps], x[taps:]
@@ -197,10 +276,10 @@
         out_ref[at] = (query_ref[at] * mixed).astype(bf16)
 
 
-def mix(gated, before, head, edge_rows, short_filter, taps, query_rows, width):
+def mix(gated, before, head, edge_rows, short_filter, response, query_rows, tables, width):
     slab, channels = gated.shape
-    count = taps.shape[0]
-    forward, inverse = fourier_tables(count)
+    count = response.shape[1]
+    forward, inverse = tables
     col = lambda rows: pl.BlockSpec((rows, width), lambda i: (0, i))
     cube = lambda a, b: pl.BlockSpec((a, b, width), lambda i: (0, 0, i))
     return pl.pallas_call(
@@ -212,7 +291,7 @@
             cube(2, edge),
             cube(2, edge),
             cube(*short_filter.shape[:2]),
-            col(count),
+            cube(3, count),
             col(slab),
             pl.BlockSpec(forward.shape, lambda i: (0, 0)),
             pl.BlockSpec(inverse.shape, lambda i: (0, 0)),
@@ -222,7 +301,7 @@
         scratch_shapes=[pltpu.VMEM((2 * edge, width), f32)],
         compiler_params=pltpu.CompilerParams(vmem_limit_bytes=40 << 20),
         name="mix",
-    )(gated, before, head, edge_rows, short_filter, taps, query_rows, forward, inverse)
+    )(gated, before, head, edge_rows, short_filter, response, query_rows, forward, inverse)
 
 
 def local(tokens, norm_gain, w_in, short_filter, medium_filter, decay, w_out):
@@ -257,10 +336,6 @@
     def after(value, *earlier):
         return lax.optimization_barrier((value, *earlier))[0]
 
-    values = tokens.astype(f32)
-    inverse_rms = lax.rsqrt(jnp.mean(values * values, axis=1, keepdims=True) + norm_epsilon)
-    normed = (values * inverse_rms * norm_gain.astype(f32)[None, :]).astype(bf16)
-
     weights = jnp.transpose(w_in, (1, 0, 2))
     half = rows // 2
     fine = half // 2
@@ -271,10 +346,14 @@
         first_half, other_half = g * half, (1 - g) * half
         peer = to_core(weights)
         pieces = {b: [(weights, b, c * rows), (peer, b, (c ^ 1) * rows)] for b in order}
-        nears = []
+        nears, far_cores = [], {}
         for b in order:
             for u in range(half // fine):
-                mine = lax.dynamic_slice(weights[b], (first_half + u * fine, 0), (fine, channels))
+                mine = lax.dynamic_slice(
+                    weights, (b, first_half + u * fine, 0), (1, fine, channels)
+                ).reshape(fine, channels)
+                if len(nears) < 2:
+                    tokens = after(tokens, mine)
                 if len(nears) >= 2:
                     mine = after(mine, nears[-2])
                 near = to_chip(mine)
@@ -284,31 +363,41 @@
                     (near, None, (c ^ 2) * rows + first_half + u * fine),
                     (to_core(near), None, (c ^ 3) * rows + first_half + u * fine),
                     (far, None, (c ^ 2) * rows + other_half + u * fine),
-                    (to_core(far), None, (c ^ 3) * rows + other_half + u * fine),
+                    (far if b == 0 else to_core(far), None, (c ^ 3) * rows + other_half + u * fine),
                 ]
+                if b == 0:
+                    far_cores[len(pieces[b]) - 1] = far
         mine = lax.dynamic_slice(w_out, (g * out_half, 0), (out_half, channels))
-        near = to_chip(after(mine, nears[-2]))
-        far = to_group(near)
-        out_peer = to_core(after(w_out, nears[-2]))
-        sets = [[w_out], [out_peer], [near, far], [to_core(near), to_core(far)]]
+        near_out = to_chip(after(mine, nears[-1]))
     else:
         full = lax.all_gather(weights, "context", axis=1, tiled=True)
         pieces = {b: [(full, b, 0)] for b in order}
-        sets = [[lax.all_gather(w_out, "context", axis=0, tiled=True)]]
-
+
+    normed = norm(tokens, norm_gain)
     gathered = lax.all_gather(normed, "tensor", axis=0, tiled=True)
     before_rows = to_next(gathered[slab - edge :])
 
     medium_count = medium_filter.shape[0]
-    lag_index = jnp.arange(medium_count, dtype=f32)
-    taps = (medium_filter * jnp.exp(-decay[None, :] * lag_index[:, None])).astype(bf16)
-    gated, head, tail = gate(gathered, pieces[1], pieces[2], short_filter, width)
+    tables = fourier_tables(medium_count)
+    response = respond(medium_filter, decay, tables[0], width)
+    gate_taps = after(short_filter, response)
+    gated, head, tail = gate(gathered, pieces[1], pieces[2], gate_taps, width)
+    if paired:
+        near_out = after(near_out, gated)
+        far_out = to_group(near_out)
+        out_peer = to_core(after(w_out, gated))
+        sets = [[w_out], [out_peer], [near_out, far_out], [to_core(near_out), to_core(far_out)]]
+        for n, p in enumerate(pieces[0]):
+            if n in far_cores:
+                pieces[0][n] = (to_core(after(far_cores[n], gated)), p[1], p[2])
+    else:
+        sets = [[lax.all_gather(w_out, "context", axis=0, tiled=True)]]
     before = to_next(gated[slab - medium_count :])
     edge_rows = to_next(tail)
     query_rows = query(gathered, before_rows, pieces[0], short_filter, width)
-    combined = mix(gated, before, head, edge_rows, short_filter, taps, query_rows, width)
-
-    results = []
+    combined = mix(gated, before, head, edge_rows, short_filter, response, query_rows, tables, width)
+
+    results, firsts = [], []
     for parts in sets:
         partial = [
             lax.dot_general(
@@ -335,7 +424,10 @@
 
         if count == 4:
             far_pair = block(jnp.where(z < 2, 2, 0), 2)
+            if len(firsts) >= 2:
+                far_pair = after(far_pair, firsts[-2])
             got = send(far_pair, {0: 1, 3: 2})
+            firsts.append(got)
             got = send(plus(far_pair, got), {1: 2, 2: 1})
             low, high = got[:length], got[length:]
             odd = z % 2 == 1

time: 268 us -> 278 us (1.037)
  local copies, waits for them, and re-layouts: 15.4 us -> 34.4 us
  waiting for transfers between devices: 130 us -> 122 us
  starting transfers between devices: 55.1 us -> 61.9 us
  other arithmetic: 7.03 us -> 2.14 us
  matrix products: 11.2 us -> 8.12 us
    unnamed x44 -> x64, local copies, waits for them, and re-layouts: 6.43 us -> 26.5 us
    ppermute x45, waiting for transfers between devices: 130 us -> 122 us  [move(): return lax.ppermute(value, axes, pairs)]
    ppermute x45, starting transfers between devices: 55.1 us -> 61.9 us  [move(): return lax.ppermute(value, axes, pairs)]
    reshape x0 -> x2, local copies, waits for them, and re-layouts: none -> 3.89 us  [the longest x1 3.27 us: local(): mine = lax.dynamic_slice(weights, (b, first_half + u * fine, 0), (1, fine...]
    pallas_call x2 -> x4, Pallas kernels: 26.5 us -> 30.1 us  [the longest x1 14.1 us: gate(): pl.pallas_call(functools.partial(gate_kernel, kinds, width), grid_spec=gr...]
    slice x1 -> x0, local copies, waits for them, and re-layouts: 3.57 us -> none  [local(): weights[b]]
    convert_element_type x3 -> x0, other arithmetic: 3.33 us -> none  [the longest x1 2.53 us: local(): (values * inverse_rms * norm_gain.astype(f32)[None, :]).astype(bf16)]
    pallas_call x1, Pallas kernels: 7.83 us -> 4.52 us  [mix(): pl.pallas_call(mix_kernel, grid=(channels // width,), in_specs=[col(slab)...]
  transfers between devices with their start and end apart: 46 -> 46, of which waited for: 20 -> 16; matrix products, arithmetic and copies ran while one was open for 9% -> 6% of each run, Pallas kernels for 13% -> 12%
where the time goes in v1:
time: 278 us; the launch traced here: 277 us
  waiting for transfers between devices  122 us (44%)
  starting transfers between devices  61.9 us (22%)
  Pallas kernels  34.6 us (12%)
  local copies, waits for them, and re-layouts  34.4 us (12%)
  between operations  14 us (5%)
  matrix products  8.12 us (3%)
    ppermute x45, waiting for transfers between devices, move(): return lax.ppermute(value, axes, pairs)  122 us
    ppermute x45, starting transfers between devices, move(): return lax.ppermute(value, axes, pairs)  61.9 us
    unnamed x64, local copies, waits for them, and re-layouts  26.5 us
    pallas_call x1, Pallas kernels, gate(): pl.pallas_call(functools.partial(gate_kernel, kinds, width), grid_spec=gr...  14.1 us
    pallas_call x1, Pallas kernels, query(): pl.pallas_call(functools.partial(query_kernel, kinds, width), grid_spec=g...  8.45 us
    dot_general x6, matrix products, local(): lax.dot_general(combined, part, (((1,), (1,)), ((), ())), preferred_eleme...  8.12 us
  transfers between devices with their start and end apart: 46, of which 16 were waited for; matrix products, arithmetic and copies ran while one was open for 6% of the time, Pallas kernels for 12%

profile of v1, /device:TPU:0, one launch (start us, length us, event | category | flops | bytes accessed | tf_op | source)
XLA Modules:
  0.0 276.8 jit_solution(7694686607472126448)
XLA Ops:
  7.0 3.3 %dynamic-slice_bitcast_fusion = (bf16[256,1024]{1,0:T(8,128)(2,1)}, bf16[256,1024]{1,0:T(8,128)(2,1)S(1)}, bf16[256,1024]{1,0:T(8,128)(2,1)}, bf16[256,1024]{1,0...) fusion(bf16[1024,3,1024]{2,0,1:T(8,128)(2,1)} %param.11, s32[]{:T(128)S(6)} %select_n.150, ...), kind=kLoop, calls=%fused_computation.23 | loop fusion | bytes 6291464 | tf_op jit(solution)/shard_map/reshape | solution.py:354
  10.9 3.7 %norm.1 = bf16[128,4096]{1,0:T(8,128)(2,1)} custom-call(bf16[128,4096]{1,0:T(8,128)(2,1)} %x_ref, bf16[1,4096]{1,0:T(2,128)(2,1)} %reshape.38.gain_ref), custom_call_target="tpu_custom_call" | custom-call | tf_op jit(solution)/shard_map/norm/pallas_call | solution.py:58
  14.6 2.6 collective-permute-start.1
  17.2 12.7 %collective-permute-done.1.rest_2_ = bf16[256,1024]{1,0:T(8,128)(2,1)S(1)} collective-permute-done((bf16[256,1024]{1,0:T(8,128)(2,1)S(1)}, bf16[256,1024]{1,0:T(8,128)(2,1)S(1)}, u32[]{:S(2)}, u32[]{:S(2)}) %collective-permute-start.1) | collective-permute-done | bytes 524320 | tf_op jit(solution)/shard_map/ppermute | solution.py:326
  29.9 1.9 collective-permute-start.9
  31.8 9.3 %collective-permute-done.5.rest_6_ = bf16[256,1024]{1,0:T(8,128)(2,1)S(1)} collective-permute-done((bf16[256,1024]{1,0:T(8,128)(2,1)S(1)}, bf16[256,1024]{1,0:T(8,128)(2,1)S(1)}, u32[]{:S(2)}, u32[]{:S(2)}) %collective-permute-start.5) | collective-permute-done | bytes 524320 | tf_op jit(solution)/shard_map/ppermute | solution.py:326
  41.1 1.9 collective-permute-start.13
  43.1 1.5 collective-permute-start.3
  45.1 7.3 %collective-permute-done.9.rest_12_ = bf16[256,1024]{1,0:T(8,128)(2,1)S(1)} collective-permute-done((bf16[256,1024]{1,0:T(8,128)(2,1)}, bf16[256,1024]{1,0:T(8,128)(2,1)S(1)}, u32[]{:S(2)}, u32[]{:S(2)}) %collective-permute-start.9) | collective-permute-done | bytes 524320 | tf_op jit(solution)/shard_map/ppermute | solution.py:326
  52.4 11.1 %collective-permute-done.13.rest_16_ = bf16[256,1024]{1,0:T(8,128)(2,1)S(1)} collective-permute-done((bf16[256,1024]{1,0:T(8,128)(2,1)S(1)}, bf16[256,1024]{1,0:T(8,128)(2,1)S(1)}, u32[]{:S(2)}, u32[]{:S(2)}) %collective-permute-start.13) | collective-permute-done | bytes 524320 | tf_op jit(solution)/shard_map/ppermute | solution.py:326
  63.5 1.7 collective-permute-start.11
  65.2 2.9 %collective-permute-done.7.rest_8_ = bf16[256,1024]{1,0:T(8,128)(2,1)S(1)} collective-permute-done((bf16[256,1024]{1,0:T(8,128)(2,1)S(1)}, bf16[256,1024]{1,0:T(8,128)(2,1)S(1)}, u32[]{:S(2)}, u32[]{:S(2)}) %collective-permute-start.7) | collective-permute-done | bytes 524320 | tf_op jit(solution)/shard_map/ppermute | solution.py:326
  68.1 1.2 collective-permute-start.15
  71.4 7.9 %collective-permute-done.11.rest_14_ = bf16[256,1024]{1,0:T(8,128)(2,1)S(1)} collective-permute-done((bf16[256,1024]{1,0:T(8,128)(2,1)S(1)}, bf16[256,1024]{1,0:T(8,128)(2,1)S(1)}, u32[]{:S(2)}, u32[]{:S(2)}) %collective-permute-start.11) | collective-permute-done | bytes 524320 | tf_op jit(solution)/shard_map/ppermute | solution.py:326
  80.1 9.7 %collective-permute-done.15.rest_18_ = bf16[256,1024]{1,0:T(8,128)(2,1)S(1)} collective-permute-done((bf16[256,1024]{1,0:T(8,128)(2,1)S(1)}, bf16[256,1024]{1,0:T(8,128)(2,1)S(1)}, u32[]{:S(2)}, u32[]{:S(2)}) %collective-permute-start.15) | collective-permute-done | bytes 524320 | tf_op jit(solution)/shard_map/ppermute | solution.py:326
  89.8 0.9 collective-permute-start.24
  93.2 1.1 collective-permute-start.20
  96.1 8.9 %collective-permute-done.24.rest_6_ = bf16[256,1024]{1,0:T(8,128)(2,1)} collective-permute-done((bf16[256,1024]{1,0:T(8,128)(2,1)}, bf16[256,1024]{1,0:T(8,128)(2,1)}, u32[]{:S(2)}, u32[]{:S(2)}) %collective-permute-start.24) | collective-permute-done | bytes 524320 | tf_op jit(solution)/shard_map/ppermute | solution.py:326
  105.8 2.3 constant_dynamic-slice_fusion.14
  108.9 0.9 collective-permute-start.28
  109.7 6.5 %collective-permute-done.20.rest_2_ = bf16[256,1024]{1,0:T(8,128)(2,1)} collective-permute-done((bf16[256,1024]{1,0:T(8,128)(2,1)}, bf16[256,1024]{1,0:T(8,128)(2,1)}, u32[]{:S(2)}, u32[]{:S(2)}) %collective-permute-start.20) | collective-permute-done | bytes 524320 | tf_op jit(solution)/shard_map/ppermute | solution.py:326
  116.2 1.5 collective-permute-start.26
  120.4 3.9 %respond.1.response_ref = f32[3,128,1024]{2,1,0:T(8,128)} custom-call(f32[128,1024]{1,0:T(8,128)} %filter_ref.1, f32[1,1024]{1,0:T(1,128)} %bitcast.40, bf16[256,256]{1,0:T(8,128)(2,1)} %constant.54.clone.fwd_ref), custom_call_target="tpu_custom_call" | custom-call | tf_op jit(solution)/shard_map/respond/pallas_call | solution.py:226
  124.3 2.2 copy-done
  126.5 1.0 copy-done.4
  127.6 1.0 copy-done.6
  128.6 1.0 copy-done.8
  129.7 1.0 copy-done.10
  130.7 1.0 copy-done.12
  131.7 1.0 copy-done.14
  132.8 1.0 copy-done.16
  133.8 1.0 copy-done.18
  134.9 1.0 copy-done.20
  135.9 1.0 copy-done.22
  137.0 1.0 copy-done.24
  138.0 1.0 copy-done.26
  139.0 14.1 %gate.1 = (bf16[512,1024]{1,0:T(8,128)(2,1)S(1)}, bf16[2,16,1024]{2,1,0:T(8,128)(2,1)S(1)}, bf16[2,16,1024]{2,1,0:T(8,128)(2,1)S(1)}) custom-call(s32[10]{0:T(128)S(1)} %stack.54.at_ref, bf16[512,4096]{1,0:T(8,128)(2,1)S(1)} %copy-done, f32[3,3,1024]{2,1,0:T(4,128)S(1)} %copy-done.28, bf16[3,1024,1024]{2,1,0:T(8,128)(2,1)} %bitcast.37, ...), custom_call_target="tpu_custom_call" | custom-call | tf_op jit(solution)/shard_map/gate/pallas_call | solution.py:150
  153.8 2.0 collective-permute-start.17
  155.8 2.8 %collective-permute-start.19 = (bf16[16,4096]{1,0:T(8,128)(2,1)S(1)}, bf16[16,4096]{1,0:T(8,128)(2,1)S(1)}, u32[]{:S(2)}, u32[]{:S(2)}) collective-permute-start(bf16[16,4096]{1,0:T(8,128)(2,1)S(1)} %slice.56), channel_id=1, source_target_pairs={{0,4},{1,5},{2,6},{3,7},{4,8},{5,9},{6,10},{7,11},{8,12},{9,13},{1... | collective-permute-start | bytes 393224 | tf_op jit(solution)/shard_map/ppermute | solution.py:326
  158.7 2.0 collective-permute-start.18
  160.7 1.6 collective-permute-start.30
  162.8 2.2 copy-done.1
  164.9 8.4 %query.1.query_ref = f32[512,1024]{1,0:T(8,128)S(1)} custom-call(s32[10]{0:T(128)S(1)} %stack.54.at_ref, bf16[512,4096]{1,0:T(8,128)(2,1)S(1)} %copy-done.1, bf16[16,4096]{1,0:T(8,128)(2,1)S(1)} %collective-permute-done.19.before_ref, f32[3,3,1024]{2,1,0:T(4,128)S(1)} %copy-done.28, bf16[3,1024,1024]{2,1,0:T(8,128)(2,1)} %bitcast.39, ...), custom_call_target="tpu_custom_call" | custom-call | tf_op jit(solution)/shard_map/query/pallas_call | solution.py:200
  173.5 4.5 %mix.1 = bf16[512,1024]{1,0:T(8,128)(2,1)S(1)} custom-call(bf16[512,1024]{1,0:T(8,128)(2,1)S(1)} %get-tuple-element.27.gated_ref, bf16[128,1024]{1,0:T(8,128)(2,1)S(1)} %collective-permute-done.17.before_ref, bf16[2,16,1024]{2,1,0:T(8,128)(2,1)S(1)} %get-tuple-element.28.head_ref, bf16[2,16,1024]{2,1,0:T(8,128)(2,1)S(1)} %collective-permute-done.18.edge_ref, ...), custom_call_target="tpu_custom_call" | custom-call | tf_op jit(solution)/shard_map/mix/pallas_call | solution.py:285
  178.0 2.1 convolution_convert_fusion.3
  180.1 1.3 convolution_convert_fusion
  181.5 3.5 %collective-permute-start.37 = (bf16[256,1024]{0,1:T(8,128)(2,1)S(1)}, bf16[256,1024]{0,1:T(8,128)(2,1)S(1)}, u32[]{:S(2)}, u32[]{:S(2)}) collective-permute-start(bf16[256,1024]{0,1:T(8,128)(2,1)S(1)} %constant_dynamic-slice_fusion.2), channel_id=1, source_target_pairs={{0,1},{3,2},{4,5},{7,6},{8,9},{11,10},{12,13},{15,14},{16,17},{19,... | collective-permute-start | bytes 1572872 | tf_op jit(solution)/shard_map/ppermute | solution.py:326
  185.1 1.7 collective-permute-done.30
  186.8 2.0 convolution_convert_fusion.2
  188.8 7.9 %collective-permute-done.37 = bf16[256,1024]{0,1:T(8,128)(2,1)S(1)} collective-permute-done((bf16[256,1024]{0,1:T(8,128)(2,1)S(1)}, bf16[256,1024]{0,1:T(8,128)(2,1)S(1)}, u32[]{:S(2)}, u32[]{:S(2)}) %collective-permute-start.37) | collective-permute-done | bytes 524320 | tf_op jit(solution)/shard_map/ppermute | solution.py:326
  196.7 4.6 %collective-permute-start.38 = (bf16[256,1024]{0,1:T(8,128)(2,1)S(1)}, bf16[256,1024]{0,1:T(8,128)(2,1)S(1)}, u32[]{:S(2)}, u32[]{:S(2)}) collective-permute-start(bf16[256,1024]{0,1:T(8,128)(2,1)S(1)} %pad_maximum_fusion.2), channel_id=1, source_target_pairs={{0,1},{3,2},{4,5},{7,6},{8,9},{11,10},{12,13},{15,14},{16,17},{19,... | collective-permute-start | bytes 1572872 | tf_op jit(solution)/shard_map/ppermute | solution.py:326
  203.1 8.9 %collective-permute-done.38 = bf16[256,1024]{0,1:T(8,128)(2,1)S(1)} collective-permute-done((bf16[256,1024]{0,1:T(8,128)(2,1)S(1)}, bf16[256,1024]{0,1:T(8,128)(2,1)S(1)}, u32[]{:S(2)}, u32[]{:S(2)}) %collective-permute-start.38) | collective-permute-done | bytes 524320 | tf_op jit(solution)/shard_map/ppermute | solution.py:326
  212.9 5.3 %collective-permute-start.44 = (bf16[128,1024]{0,1:T(8,128)(2,1)S(1)}, bf16[128,1024]{0,1:T(8,128)(2,1)S(1)}, u32[]{:S(2)}, u32[]{:S(2)}) collective-permute-start(bf16[128,1024]{0,1:T(8,128)(2,1)S(1)} %add_convert_fusion.5), channel_id=1, source_target_pairs={{0,1},{1,0},{2,3},{3,2},{4,5},{5,4},{6,7},{7,6},{8,9},{9,8},{10,11... | collective-permute-start | bytes 786440 | tf_op jit(solution)/shard_map/ppermute | solution.py:326
  218.3 1.3 convolution_convert_fusion.1
  219.6 2.0 collective-permute-start.33
  222.4 11.2 %collective-permute-done.33 = bf16[256,1024]{0,1:T(8,128)(2,1)S(1)} collective-permute-done((bf16[256,1024]{0,1:T(8,128)(2,1)S(1)}, bf16[256,1024]{0,1:T(8,128)(2,1)S(1)}, u32[]{:S(2)}, u32[]{:S(2)}) %collective-permute-start.33) | collective-permute-done | bytes 524320 | tf_op jit(solution)/shard_map/ppermute | solution.py:326
  233.6 4.4 %collective-permute-start.34 = (bf16[256,1024]{0,1:T(8,128)(2,1)S(1)}, bf16[256,1024]{0,1:T(8,128)(2,1)S(1)}, u32[]{:S(2)}, u32[]{:S(2)}) collective-permute-start(bf16[256,1024]{0,1:T(8,128)(2,1)S(1)} %pad_maximum_fusion.1), channel_id=1, source_target_pairs={{0,1},{3,2},{4,5},{7,6},{8,9},{11,10},{12,13},{15,14},{16,17},{19,... | collective-permute-start | bytes 1572872 | tf_op jit(solution)/shard_map/ppermute | solution.py:326
  239.1 1.1 collective-permute-start.40
  240.2 9.7 %collective-permute-done.34 = bf16[256,1024]{0,1:T(8,128)(2,1)S(1)} collective-permute-done((bf16[256,1024]{0,1:T(8,128)(2,1)S(1)}, bf16[256,1024]{0,1:T(8,128)(2,1)S(1)}, u32[]{:S(2)}, u32[]{:S(2)}) %collective-permute-start.34) | collective-permute-done | bytes 524320 | tf_op jit(solution)/shard_map/ppermute | solution.py:326
  250.7 2.2 collective-permute-done.40
  253.1 2.5 collective-permute-start.42
  255.8 7.9 %collective-permute-start.36 = (bf16[128,1024]{0,1:T(8,128)(2,1)S(1)}, bf16[128,1024]{0,1:T(8,128)(2,1)S(1)}, u32[]{:S(2)}, u32[]{:S(2)}) collective-permute-start(bf16[128,1024]{0,1:T(8,128)(2,1)S(1)} %add_convert_fusion.11), channel_id=1, source_target_pairs={{0,1},{1,0},{2,3},{3,2},{4,5},{5,4},{6,7},{7,6},{8,9},{9,8},{10,11... | collective-permute-start | bytes 786440 | tf_op jit(solution)/shard_map/ppermute | solution.py:326
  264.1 4.0 %collective-permute-done.36 = bf16[128,1024]{0,1:T(8,128)(2,1)S(1)} collective-permute-done((bf16[128,1024]{0,1:T(8,128)(2,1)S(1)}, bf16[128,1024]{0,1:T(8,128)(2,1)S(1)}, u32[]{:S(2)}, u32[]{:S(2)}) %collective-permute-start.36) | collective-permute-done | bytes 262176 | tf_op jit(solution)/shard_map/ppermute | solution.py:326
  268.7 1.3 copy.12
  (140 shorter events, 21.3 us)
Async XLA Ops:
  6.5 117.8 %all-gather.2.cloned.1.call-start = ((), (), s32[]{:S(2)}) async-start(), calls=%async_computation | async-start | bytes 5242880 | tf_op jit(solution)/shard_map/all_gather | solution.py:377
  6.5 113.3 %collective-permute-start = (bf16[3,1024,1024]{2,1,0:T(8,128)(2,1)}, bf16[3,1024,1024]{2,1,0:T(8,128)(2,1)}, u32[]{:S(2)}, u32[]{:S(2)}) collective-permute-start(bf16[3,1024,1024]{2,1,0:T(8,128)(2,1)} %bitcast.36), channel_id=1, source_target_pairs={{0,4},{1,5},{2,6},{3,7},{4,0},{5,1},{6,2},{7,3},{8,12},{9,13},{10,... | collective-permute-start | bytes 18874376 | tf_op jit(solution)/shard_map/ppermute | solution.py:326
  7.0 3.3 %copy-start.31 = (bf16[4096]{0:T(1024)(128)(2,1)S(1)}, bf16[4096]{0:T(1024)(128)(2,1)}, u32[]{:S(2)}) copy-start(bf16[4096]{0:T(1024)(128)(2,1)} %param.10) | copy-start | bytes 24580
  14.6 15.3 %collective-permute-start.1 = (bf16[256,1024]{1,0:T(8,128)(2,1)S(1)}, bf16[256,1024]{1,0:T(8,128)(2,1)S(1)}, u32[]{:S(2)}, u32[]{:S(2)}) collective-permute-start(bf16[256,1024]{1,0:T(8,128)(2,1)S(1)} %get-tuple-element.46), channel_id=1, source_target_pairs={{0,8},{1,9},{2,10},{3,11},{4,12},{5,13},{6,14},{7,15},{8,0},{9,1},... | collective-permute-start | bytes 1572872 | tf_op jit(solution)/shard_map/ppermute | solution.py:326
  17.1 24.0 %collective-permute-start.5 = (bf16[256,1024]{1,0:T(8,128)(2,1)S(1)}, bf16[256,1024]{1,0:T(8,128)(2,1)S(1)}, u32[]{:S(2)}, u32[]{:S(2)}) collective-permute-start(bf16[256,1024]{1,0:T(8,128)(2,1)S(1)} %get-tuple-element.45), channel_id=1, source_target_pairs={{0,8},{1,9},{2,10},{3,11},{4,12},{5,13},{6,14},{7,15},{8,0},{9,1},... | collective-permute-start | bytes 1572872 | tf_op jit(solution)/shard_map/ppermute | solution.py:326
  29.9 22.5 %collective-permute-start.9 = (bf16[256,1024]{1,0:T(8,128)(2,1)}, bf16[256,1024]{1,0:T(8,128)(2,1)S(1)}, u32[]{:S(2)}, u32[]{:S(2)}) collective-permute-start(bf16[256,1024]{1,0:T(8,128)(2,1)} %get-tuple-element.25), channel_id=1, source_target_pairs={{0,8},{1,9},{2,10},{3,11},{4,12},{5,13},{6,14},{7,15},{8,0},{9,1},... | collective-permute-start | bytes 1572872 | tf_op jit(solution)/shard_map/ppermute | solution.py:326
  41.1 22.3 %collective-permute-start.13 = (bf16[256,1024]{1,0:T(8,128)(2,1)S(1)}, bf16[256,1024]{1,0:T(8,128)(2,1)S(1)}, u32[]{:S(2)}, u32[]{:S(2)}) collective-permute-start(bf16[256,1024]{1,0:T(8,128)(2,1)S(1)} %get-tuple-element.26), channel_id=1, source_target_pairs={{0,8},{1,9},{2,10},{3,11},{4,12},{5,13},{6,14},{7,15},{8,0},{9,1},... | collective-permute-start | bytes 1572872 | tf_op jit(solution)/shard_map/ppermute | solution.py:326
  43.1 20.4 %collective-permute-start.3 = (bf16[256,1024]{1,0:T(8,128)(2,1)S(1)}, bf16[256,1024]{1,0:T(8,128)(2,1)S(1)}, u32[]{:S(2)}, u32[]{:S(2)}) collective-permute-start(bf16[256,1024]{1,0:T(8,128)(2,1)S(1)} %collective-permute-done.1.rest_2_), channel_id=1, source_target_pairs={{0,16},{1,17},{2,18},{3,19},{4,20},{5,21},{6,22},{7,23},{8,24},{9,... | collective-permute-start | bytes 1572872 | tf_op jit(solution)/shard_map/ppermute | solution.py:326
  44.6 23.5 %collective-permute-start.7 = (bf16[256,1024]{1,0:T(8,128)(2,1)S(1)}, bf16[256,1024]{1,0:T(8,128)(2,1)S(1)}, u32[]{:S(2)}, u32[]{:S(2)}) collective-permute-start(bf16[256,1024]{1,0:T(8,128)(2,1)S(1)} %collective-permute-done.5.rest_6_), channel_id=1, source_target_pairs={{0,16},{1,17},{2,18},{3,19},{4,20},{5,21},{6,22},{7,23},{8,24},{9,... | collective-permute-start | bytes 1572872 | tf_op jit(solution)/shard_map/ppermute | solution.py:326
  52.4 16.9 %collective-permute-start.2 = (bf16[256,1024]{1,0:T(8,128)(2,1)S(1)}, bf16[256,1024]{1,0:T(8,128)(2,1)S(1)}, u32[]{:S(2)}, u32[]{:S(2)}) collective-permute-start(bf16[256,1024]{1,0:T(8,128)(2,1)S(1)} %collective-permute-done.1.rest_2_), channel_id=1, source_target_pairs={{0,4},{1,5},{2,6},{3,7},{4,0},{5,1},{6,2},{7,3},{8,12},{9,13},{10,... | collective-permute-start | bytes 1572872 | tf_op jit(solution)/shard_map/ppermute | solution.py:326
  63.4 6.7 %collective-permute-start.6 = (bf16[256,1024]{1,0:T(8,128)(2,1)S(1)}, bf16[256,1024]{1,0:T(8,128)(2,1)S(1)}, u32[]{:S(2)}, u32[]{:S(2)}) collective-permute-start(bf16[256,1024]{1,0:T(8,128)(2,1)S(1)} %collective-permute-done.5.rest_6_), channel_id=1, source_target_pairs={{0,4},{1,5},{2,6},{3,7},{4,0},{5,1},{6,2},{7,3},{8,12},{9,13},{10,... | collective-permute-start | bytes 1572872 | tf_op jit(solution)/shard_map/ppermute | solution.py:326
  63.5 15.8 %collective-permute-start.11 = (bf16[256,1024]{1,0:T(8,128)(2,1)S(1)}, bf16[256,1024]{1,0:T(8,128)(2,1)S(1)}, u32[]{:S(2)}, u32[]{:S(2)}) collective-permute-start(bf16[256,1024]{1,0:T(8,128)(2,1)S(1)} %collective-permute-done.9.rest_12_), channel_id=1, source_target_pairs={{0,16},{1,17},{2,18},{3,19},{4,20},{5,21},{6,22},{7,23},{8,24},{9,... | collective-permute-start | bytes 1572872 | tf_op jit(solution)/shard_map/ppermute | solution.py:326
  68.1 21.8 %collective-permute-start.15 = (bf16[256,1024]{1,0:T(8,128)(2,1)S(1)}, bf16[256,1024]{1,0:T(8,128)(2,1)S(1)}, u32[]{:S(2)}, u32[]{:S(2)}) collective-permute-start(bf16[256,1024]{1,0:T(8,128)(2,1)S(1)} %collective-permute-done.13.rest_16_), channel_id=1, source_target_pairs={{0,16},{1,17},{2,18},{3,19},{4,20},{5,21},{6,22},{7,23},{8,24},{9,... | collective-permute-start | bytes 1572872 | tf_op jit(solution)/shard_map/ppermute | solution.py:326
  70.1 20.7 %collective-permute-start.10 = (bf16[256,1024]{1,0:T(8,128)(2,1)S(1)}, bf16[256,1024]{1,0:T(8,128)(2,1)S(1)}, u32[]{:S(2)}, u32[]{:S(2)}) collective-permute-start(bf16[256,1024]{1,0:T(8,128)(2,1)S(1)} %collective-permute-done.9.rest_12_), channel_id=1, source_target_pairs={{0,4},{1,5},{2,6},{3,7},{4,0},{5,1},{6,2},{7,3},{8,12},{9,13},{10,... | collective-permute-start | bytes 1572872 | tf_op jit(solution)/shard_map/ppermute | solution.py:326
  70.9 21.5 %collective-permute-start.14 = (bf16[256,1024]{1,0:T(8,128)(2,1)S(1)}, bf16[256,1024]{1,0:T(8,128)(2,1)S(1)}, u32[]{:S(2)}, u32[]{:S(2)}) collective-permute-start(bf16[256,1024]{1,0:T(8,128)(2,1)S(1)} %collective-permute-done.13.rest_16_), channel_id=1, source_target_pairs={{0,4},{1,5},{2,6},{3,7},{4,0},{5,1},{6,2},{7,3},{8,12},{9,13},{10,... | collective-permute-start | bytes 1572872 | tf_op jit(solution)/shard_map/ppermute | solution.py:326
  79.3 15.0 %collective-permute-start.4 = (bf16[256,1024]{1,0:T(8,128)(2,1)S(1)}, bf16[256,1024]{1,0:T(8,128)(2,1)S(1)}, u32[]{:S(2)}, u32[]{:S(2)}) collective-permute-start(bf16[256,1024]{1,0:T(8,128)(2,1)S(1)} %collective-permute-done.3.rest_4_), channel_id=1, source_target_pairs={{0,4},{1,5},{2,6},{3,7},{4,0},{5,1},{6,2},{7,3},{8,12},{9,13},{10,... | collective-permute-start | bytes 1572872 | tf_op jit(solution)/shard_map/ppermute | solution.py:326
  89.8 15.2 %collective-permute-start.24 = (bf16[256,1024]{1,0:T(8,128)(2,1)}, bf16[256,1024]{1,0:T(8,128)(2,1)}, u32[]{:S(2)}, u32[]{:S(2)}) collective-permute-start(bf16[256,1024]{1,0:T(8,128)(2,1)} %get-tuple-element.32), channel_id=1, source_target_pairs={{0,8},{1,9},{2,10},{3,11},{4,12},{5,13},{6,14},{7,15},{8,0},{9,1},... | collective-permute-start | bytes 1572872 | tf_op jit(solution)/shard_map/ppermute | solution.py:326
  91.6 16.5 %collective-permute-start.8 = (bf16[256,1024]{1,0:T(8,128)(2,1)S(1)}, bf16[256,1024]{1,0:T(8,128)(2,1)S(1)}, u32[]{:S(2)}, u32[]{:S(2)}) collective-permute-start(bf16[256,1024]{1,0:T(8,128)(2,1)S(1)} %collective-permute-done.7.rest_8_), channel_id=1, source_target_pairs={{0,4},{1,5},{2,6},{3,7},{4,0},{5,1},{6,2},{7,3},{8,12},{9,13},{10,... | collective-permute-start | bytes 1572872 | tf_op jit(solution)/shard_map/ppermute | solution.py:326
  92.4 32.0 %copy-start.28 = (f32[3,3,1024]{2,1,0:T(4,128)S(1)}, f32[3,3,1024]{2,1,0:T(4,128)}, u32[]{:S(2)}) copy-start(f32[3,3,1024]{2,1,0:T(4,128)} %short_ref.1) | copy-start | bytes 110596
  93.2 23.1 %collective-permute-start.20 = (bf16[256,1024]{1,0:T(8,128)(2,1)}, bf16[256,1024]{1,0:T(8,128)(2,1)}, u32[]{:S(2)}, u32[]{:S(2)}) collective-permute-start(bf16[256,1024]{1,0:T(8,128)(2,1)} %get-tuple-element.30), channel_id=1, source_target_pairs={{0,8},{1,9},{2,10},{3,11},{4,12},{5,13},{6,14},{7,15},{8,0},{9,1},... | collective-permute-start | bytes 1572872 | tf_op jit(solution)/shard_map/ppermute | solution.py:326
  95.1 22.6 %collective-permute-start.12 = (bf16[256,1024]{1,0:T(8,128)(2,1)S(1)}, bf16[256,1024]{1,0:T(8,128)(2,1)S(1)}, u32[]{:S(2)}, u32[]{:S(2)}) collective-permute-start(bf16[256,1024]{1,0:T(8,128)(2,1)S(1)} %collective-permute-done.11.rest_14_), channel_id=1, source_target_pairs={{0,4},{1,5},{2,6},{3,7},{4,0},{5,1},{6,2},{7,3},{8,12},{9,13},{10,... | collective-permute-start | bytes 1572872 | tf_op jit(solution)/shard_map/ppermute | solution.py:326
  105.0 14.1 %collective-permute-start.16 = (bf16[256,1024]{1,0:T(8,128)(2,1)S(1)}, bf16[256,1024]{1,0:T(8,128)(2,1)S(1)}, u32[]{:S(2)}, u32[]{:S(2)}) collective-permute-start(bf16[256,1024]{1,0:T(8,128)(2,1)S(1)} %collective-permute-done.15.rest_18_), channel_id=1, source_target_pairs={{0,4},{1,5},{2,6},{3,7},{4,0},{5,1},{6,2},{7,3},{8,12},{9,13},{10,... | collective-permute-start | bytes 1572872 | tf_op jit(solution)/shard_map/ppermute | solution.py:326
  108.9 49.8 %collective-permute-start.28 = (bf16[512,1024]{1,0:T(8,128)(2,1)}, bf16[512,1024]{1,0:T(8,128)(2,1)}, u32[]{:S(2)}, u32[]{:S(2)}) collective-permute-start(bf16[512,1024]{1,0:T(8,128)(2,1)} %constant_dynamic-slice_fusion.14), channel_id=1, source_target_pairs={{0,8},{1,9},{2,10},{3,11},{4,12},{5,13},{6,14},{7,15},{8,0},{9,1},... | collective-permute-start | bytes 3145736 | tf_op jit(solution)/shard_map/ppermute | solution.py:326
  116.2 36.9 %collective-permute-start.26 = (bf16[256,1024]{1,0:T(8,128)(2,1)}, bf16[256,1024]{1,0:T(8,128)(2,1)}, u32[]{:S(2)}, u32[]{:S(2)}) collective-permute-start(bf16[256,1024]{1,0:T(8,128)(2,1)} %collective-permute-done.24.rest_6_), channel_id=1, source_target_pairs={{0,16},{1,17},{2,18},{3,19},{4,20},{5,21},{6,22},{7,23},{8,24},{9,... | collective-permute-start | bytes 1572872 | tf_op jit(solution)/shard_map/ppermute | solution.py:326
  118.5 34.8 %collective-permute-start.22 = (bf16[256,1024]{1,0:T(8,128)(2,1)}, bf16[256,1024]{1,0:T(8,128)(2,1)}, u32[]{:S(2)}, u32[]{:S(2)}) collective-permute-start(bf16[256,1024]{1,0:T(8,128)(2,1)} %collective-permute-done.20.rest_2_), channel_id=1, source_target_pairs={{0,16},{1,17},{2,18},{3,19},{4,20},{5,21},{6,22},{7,23},{8,24},{9,... | collective-permute-start | bytes 1572872 | tf_op jit(solution)/shard_map/ppermute | solution.py:326
  119.9 33.9 %collective-permute-start.25 = (bf16[256,1024]{1,0:T(8,128)(2,1)}, bf16[256,1024]{1,0:T(8,128)(2,1)}, u32[]{:S(2)}, u32[]{:S(2)}) collective-permute-start(bf16[256,1024]{1,0:T(8,128)(2,1)} %collective-permute-done.24.rest_6_), channel_id=1, source_target_pairs={{0,4},{1,5},{2,6},{3,7},{4,0},{5,1},{6,2},{7,3},{8,12},{9,13},{10,... | collective-permute-start | bytes 1572872 | tf_op jit(solution)/shard_map/ppermute | solution.py:326
  119.9 35.9 %collective-permute-start.21 = (bf16[256,1024]{1,0:T(8,128)(2,1)}, bf16[256,1024]{1,0:T(8,128)(2,1)}, u32[]{:S(2)}, u32[]{:S(2)}) collective-permute-start(bf16[256,1024]{1,0:T(8,128)(2,1)} %collective-permute-done.20.rest_2_), channel_id=1, source_target_pairs={{0,4},{1,5},{2,6},{3,7},{4,0},{5,1},{6,2},{7,3},{8,12},{9,13},{10,... | collective-permute-start | bytes 1572872 | tf_op jit(solution)/shard_map/ppermute | solution.py:326
  124.3 2.2 copy-start
  126.5 1.0 copy-start.4
  127.6 1.0 copy-start.6
  128.6 1.0 copy-start.8
  129.7 1.0 copy-start.10
  130.7 1.0 copy-start.12
  131.7 1.0 copy-start.14
  133.8 1.0 copy-start.18
  134.9 1.0 copy-start.20
  135.9 1.0 copy-start.22
  136.9 1.0 copy-start.24
  153.2 9.1 %collective-permute-start.27 = (bf16[256,1024]{1,0:T(8,128)(2,1)}, bf16[256,1024]{1,0:T(8,128)(2,1)S(1)}, u32[]{:S(2)}, u32[]{:S(2)}) collective-permute-start(bf16[256,1024]{1,0:T(8,128)(2,1)} %collective-permute-done.26.rest_8_), channel_id=1, source_target_pairs={{0,4},{1,5},{2,6},{3,7},{4,0},{5,1},{6,2},{7,3},{8,12},{9,13},{10,... | collective-permute-start | bytes 1572872 | tf_op jit(solution)/shard_map/ppermute | solution.py:326
  153.3 9.4 %collective-permute-start.23 = (bf16[256,1024]{1,0:T(8,128)(2,1)}, bf16[256,1024]{1,0:T(8,128)(2,1)S(1)}, u32[]{:S(2)}, u32[]{:S(2)}) collective-permute-start(bf16[256,1024]{1,0:T(8,128)(2,1)} %collective-permute-done.22.rest_4_), channel_id=1, source_target_pairs={{0,4},{1,5},{2,6},{3,7},{4,0},{5,1},{6,2},{7,3},{8,12},{9,13},{10,... | collective-permute-start | bytes 1572872 | tf_op jit(solution)/shard_map/ppermute | solution.py:326
  153.8 19.6 %collective-permute-start.17 = (bf16[128,1024]{1,0:T(8,128)(2,1)S(1)}, bf16[128,1024]{1,0:T(8,128)(2,1)S(1)}, u32[]{:S(2)}, u32[]{:S(2)}) collective-permute-start(bf16[128,1024]{1,0:T(8,128)(2,1)S(1)} %slice.42), channel_id=1, source_target_pairs={{0,4},{1,5},{2,6},{3,7},{4,8},{5,9},{6,10},{7,11},{8,12},{9,13},{1... | collective-permute-start | bytes 786440 | tf_op jit(solution)/shard_map/ppermute | solution.py:326
  155.8 4.8 %collective-permute-start.19 = (bf16[16,4096]{1,0:T(8,128)(2,1)S(1)}, bf16[16,4096]{1,0:T(8,128)(2,1)S(1)}, u32[]{:S(2)}, u32[]{:S(2)}) collective-permute-start(bf16[16,4096]{1,0:T(8,128)(2,1)S(1)} %slice.56), channel_id=1, source_target_pairs={{0,4},{1,5},{2,6},{3,7},{4,8},{5,9},{6,10},{7,11},{8,12},{9,13},{1... | collective-permute-start | bytes 393224 | tf_op jit(solution)/shard_map/ppermute | solution.py:326
  158.7 14.7 %collective-permute-start.18 = (bf16[2,16,1024]{2,1,0:T(8,128)(2,1)S(1)}, bf16[2,16,1024]{2,1,0:T(8,128)(2,1)S(1)}, u32[]{:S(2)}, u32[]{:S(2)}) collective-permute-start(bf16[2,16,1024]{2,1,0:T(8,128)(2,1)S(1)} %get-tuple-element.29), channel_id=1, source_target_pairs={{0,4},{1,5},{2,6},{3,7},{4,8},{5,9},{6,10},{7,11},{8,12},{9,13},{1... | collective-permute-start | bytes 196616 | tf_op jit(solution)/shard_map/ppermute | solution.py:326
  160.7 26.1 %collective-permute-start.30 = (bf16[512,1024]{1,0:T(8,128)(2,1)}, bf16[512,1024]{1,0:T(8,128)(2,1)}, u32[]{:S(2)}, u32[]{:S(2)}) collective-permute-start(bf16[512,1024]{1,0:T(8,128)(2,1)} %collective-permute-done.28), channel_id=1, source_target_pairs={{0,16},{1,17},{2,18},{3,19},{4,20},{5,21},{6,22},{7,23},{8,24},{9,... | collective-permute-start | bytes 3145736 | tf_op jit(solution)/shard_map/ppermute | solution.py:326
  162.2 39.9 %collective-permute-start.29 = (bf16[512,1024]{1,0:T(8,128)(2,1)}, bf16[512,1024]{1,0:T(8,128)(2,1)S(1)}, u32[]{:S(2)}, u32[]{:S(2)}) collective-permute-start(bf16[512,1024]{1,0:T(8,128)(2,1)} %collective-permute-done.28), channel_id=1, source_target_pairs={{0,4},{1,5},{2,6},{3,7},{4,0},{5,1},{6,2},{7,3},{8,12},{9,13},{10,... | collective-permute-start | bytes 3145736 | tf_op jit(solution)/shard_map/ppermute | solution.py:326
  162.6 55.6 %collective-permute-start.32 = (bf16[1024,1024]{1,0:T(8,128)(2,1)}, bf16[1024,1024]{1,0:T(8,128)(2,1)S(1)}, u32[]{:S(2)}, u32[]{:S(2)}) collective-permute-start(bf16[1024,1024]{1,0:T(8,128)(2,1)} %param.15), channel_id=1, source_target_pairs={{0,4},{1,5},{2,6},{3,7},{4,0},{5,1},{6,2},{7,3},{8,12},{9,13},{10,... | collective-permute-start | bytes 6291464 | tf_op jit(solution)/shard_map/ppermute | solution.py:326
  162.8 2.2 copy-start.1
  164.9 8.5 %copy-start.2 = (f32[3,128,1024]{2,1,0:T(8,128)S(1)}, f32[3,128,1024]{2,1,0:T(8,128)}, u32[]{:S(2)}) copy-start(f32[3,128,1024]{2,1,0:T(8,128)} %respond.1.response_ref) | copy-start | bytes 4718596
  164.9 8.5 %copy-start.27 = (bf16[256,256]{1,0:T(8,128)(2,1)S(1)}, bf16[256,256]{1,0:T(8,128)(2,1)}, u32[]{:S(2)}) copy-start(bf16[256,256]{1,0:T(8,128)(2,1)} %constant.54.clone.fwd_ref) | copy-start | bytes 393220
  164.9 8.5 %copy-start.29 = (bf16[128,768]{1,0:T(8,128)(2,1)S(1)}, bf16[128,768]{1,0:T(8,128)(2,1)}, u32[]{:S(2)}) copy-start(bf16[128,768]{1,0:T(8,128)(2,1)} %constant.55.clone.inv_ref) | copy-start | bytes 589828
  178.0 2.1 copy-start.30
  181.5 15.2 %collective-permute-start.37 = (bf16[256,1024]{0,1:T(8,128)(2,1)S(1)}, bf16[256,1024]{0,1:T(8,128)(2,1)S(1)}, u32[]{:S(2)}, u32[]{:S(2)}) collective-permute-start(bf16[256,1024]{0,1:T(8,128)(2,1)S(1)} %constant_dynamic-slice_fusion.2), channel_id=1, source_target_pairs={{0,1},{3,2},{4,5},{7,6},{8,9},{11,10},{12,13},{15,14},{16,17},{19,... | collective-permute-start | bytes 1572872 | tf_op jit(solution)/shard_map/ppermute | solution.py:326
  196.7 15.3 %collective-permute-start.38 = (bf16[256,1024]{0,1:T(8,128)(2,1)S(1)}, bf16[256,1024]{0,1:T(8,128)(2,1)S(1)}, u32[]{:S(2)}, u32[]{:S(2)}) collective-permute-start(bf16[256,1024]{0,1:T(8,128)(2,1)S(1)} %pad_maximum_fusion.2), channel_id=1, source_target_pairs={{0,1},{3,2},{4,5},{7,6},{8,9},{11,10},{12,13},{15,14},{16,17},{19,... | collective-permute-start | bytes 1572872 | tf_op jit(solution)/shard_map/ppermute | solution.py:326
  201.4 11.4 %collective-permute-start.43 = (bf16[256,1024]{0,1:T(8,128)(2,1)S(1)}, bf16[256,1024]{0,1:T(8,128)(2,1)S(1)}, u32[]{:S(2)}, u32[]{:S(2)}) collective-permute-start(bf16[256,1024]{0,1:T(8,128)(2,1)S(1)} %add_convert_fusion), channel_id=1, source_target_pairs={{1,2},{2,1},{5,6},{6,5},{9,10},{10,9},{13,14},{14,13},{17,18},{18,... | collective-permute-start | bytes 1572872 | tf_op jit(solution)/shard_map/ppermute | solution.py:326
  202.9 18.7 %collective-permute-start.31 = (bf16[512,1024]{1,0:T(8,128)(2,1)}, bf16[512,1024]{1,0:T(8,128)(2,1)S(1)}, u32[]{:S(2)}, u32[]{:S(2)}) collective-permute-start(bf16[512,1024]{1,0:T(8,128)(2,1)} %collective-permute-done.30), channel_id=1, source_target_pairs={{0,4},{1,5},{2,6},{3,7},{4,0},{5,1},{6,2},{7,3},{8,12},{9,13},{10,... | collective-permute-start | bytes 3145736 | tf_op jit(solution)/shard_map/ppermute | solution.py:326
  212.1 26.8 %collective-permute-start.39 = (bf16[256,1024]{0,1:T(8,128)(2,1)S(1)}, bf16[256,1024]{0,1:T(8,128)(2,1)S(1)}, u32[]{:S(2)}, u32[]{:S(2)}) collective-permute-start(bf16[256,1024]{0,1:T(8,128)(2,1)S(1)} %add_convert_fusion.2), channel_id=1, source_target_pairs={{1,2},{2,1},{5,6},{6,5},{9,10},{10,9},{13,14},{14,13},{17,18},{18,... | collective-permute-start | bytes 1572872 | tf_op jit(solution)/shard_map/ppermute | solution.py:326
  212.9 50.8 %collective-permute-start.44 = (bf16[128,1024]{0,1:T(8,128)(2,1)S(1)}, bf16[128,1024]{0,1:T(8,128)(2,1)S(1)}, u32[]{:S(2)}, u32[]{:S(2)}) collective-permute-start(bf16[128,1024]{0,1:T(8,128)(2,1)S(1)} %add_convert_fusion.5), channel_id=1, source_target_pairs={{0,1},{1,0},{2,3},{3,2},{4,5},{5,4},{6,7},{7,6},{8,9},{9,8},{10,11... | collective-permute-start | bytes 786440 | tf_op jit(solution)/shard_map/ppermute | solution.py:326
  219.6 14.0 %collective-permute-start.33 = (bf16[256,1024]{0,1:T(8,128)(2,1)S(1)}, bf16[256,1024]{0,1:T(8,128)(2,1)S(1)}, u32[]{:S(2)}, u32[]{:S(2)}) collective-permute-start(bf16[256,1024]{0,1:T(8,128)(2,1)S(1)} %constant_dynamic-slice_fusion.9), channel_id=1, source_target_pairs={{0,1},{3,2},{4,5},{7,6},{8,9},{11,10},{12,13},{15,14},{16,17},{19,... | collective-permute-start | bytes 1572872 | tf_op jit(solution)/shard_map/ppermute | solution.py:326
  233.6 16.2 %collective-permute-start.34 = (bf16[256,1024]{0,1:T(8,128)(2,1)S(1)}, bf16[256,1024]{0,1:T(8,128)(2,1)S(1)}, u32[]{:S(2)}, u32[]{:S(2)}) collective-permute-start(bf16[256,1024]{0,1:T(8,128)(2,1)S(1)} %pad_maximum_fusion.1), channel_id=1, source_target_pairs={{0,1},{3,2},{4,5},{7,6},{8,9},{11,10},{12,13},{15,14},{16,17},{19,... | collective-permute-start | bytes 1572872 | tf_op jit(solution)/shard_map/ppermute | solution.py:326
  238.2 14.8 %collective-permute-start.41 = (bf16[256,1024]{0,1:T(8,128)(2,1)S(1)}, bf16[256,1024]{0,1:T(8,128)(2,1)S(1)}, u32[]{:S(2)}, u32[]{:S(2)}) collective-permute-start(bf16[256,1024]{0,1:T(8,128)(2,1)S(1)} %add_convert_fusion.1), channel_id=1, source_target_pairs={{1,2},{2,1},{5,6},{6,5},{9,10},{10,9},{13,14},{14,13},{17,18},{18,... | collective-permute-start | bytes 1572872 | tf_op jit(solution)/shard_map/ppermute | solution.py:326
  239.1 13.8 %collective-permute-start.40 = (bf16[128,1024]{0,1:T(8,128)(2,1)S(1)}, bf16[128,1024]{0,1:T(8,128)(2,1)S(1)}, u32[]{:S(2)}, u32[]{:S(2)}) collective-permute-start(bf16[128,1024]{0,1:T(8,128)(2,1)S(1)} %add_convert_fusion.9), channel_id=1, source_target_pairs={{0,1},{1,0},{2,3},{3,2},{4,5},{5,4},{6,7},{7,6},{8,9},{9,8},{10,11... | collective-permute-start | bytes 786440 | tf_op jit(solution)/shard_map/ppermute | solution.py:326
  250.0 5.7 %collective-permute-start.35 = (bf16[256,1024]{0,1:T(8,128)(2,1)S(1)}, bf16[256,1024]{0,1:T(8,128)(2,1)S(1)}, u32[]{:S(2)}, u32[]{:S(2)}) collective-permute-start(bf16[256,1024]{0,1:T(8,128)(2,1)S(1)} %add_convert_fusion.3), channel_id=1, source_target_pairs={{1,2},{2,1},{5,6},{6,5},{9,10},{10,9},{13,14},{14,13},{17,18},{18,... | collective-permute-start | bytes 1572872 | tf_op jit(solution)/shard_map/ppermute | solution.py:326
  253.1 10.6 %collective-permute-start.42 = (bf16[128,1024]{0,1:T(8,128)(2,1)S(1)}, bf16[128,1024]{0,1:T(8,128)(2,1)S(1)}, u32[]{:S(2)}, u32[]{:S(2)}) collective-permute-start(bf16[128,1024]{0,1:T(8,128)(2,1)S(1)} %add_convert_fusion.7), channel_id=1, source_target_pairs={{0,1},{1,0},{2,3},{3,2},{4,5},{5,4},{6,7},{7,6},{8,9},{9,8},{10,11... | collective-permute-start | bytes 786440 | tf_op jit(solution)/shard_map/ppermute | solution.py:326
  255.8 12.2 %collective-permute-start.36 = (bf16[128,1024]{0,1:T(8,128)(2,1)S(1)}, bf16[128,1024]{0,1:T(8,128)(2,1)S(1)}, u32[]{:S(2)}, u32[]{:S(2)}) collective-permute-start(bf16[128,1024]{0,1:T(8,128)(2,1)S(1)} %add_convert_fusion.11), channel_id=1, source_target_pairs={{0,1},{1,0},{2,3},{3,2},{4,5},{5,4},{6,7},{7,6},{8,9},{9,8},{10,11... | collective-permute-start | bytes 786440 | tf_op jit(solution)/shard_map/ppermute | solution.py:326
  (14 other events, 11.7 us)
Sparse Core Ops, SparseCore 0:
  14.7 83.1 all-gather.1

commit v2 on v1

--- a/solution.py
+++ b/solution.py
@@ -81,12 +81,14 @@
     return copies
 
 
-def rotate(kinds, at_ref, arrays, buffer, sems, width):
+def rotate(kinds, at_ref, arrays, buffer, sems, width, more):
     step, steps = pl.program_id(0), pl.num_programs(0)
     slot = lax.rem(step, 2)
 
     @pl.when(step == 0)
     def _():
+        for copy in more:
+            copy.start()
         for copy in fetch(kinds, at_ref, arrays, buffer, sems, 0, 0, width):
             copy.start()
 
@@ -95,25 +97,40 @@
         for copy in fetch(kinds, at_ref, arrays, buffer, sems, step + 1, 1 - slot, width):
             copy.start()
 
-    for copy in fetch(kinds, at_ref, arrays, buffer, sems, step, slot, width):
-        copy.wait()
-    return slot
+    @pl.when(step == 0)
+    def _():
+        for copy in more:
+            copy.wait()
+
+    copies = fetch(kinds, at_ref, arrays, buffer, sems, step, slot, width)
+
+    def ready(place):
+        for kind, copy in zip(kinds, copies):
+            if kind[0] == place:
+                copy.wait()
+
+    return slot, ready
 
 
 def gate_kernel(kinds, width, at_ref, x_ref, taps_ref, *rest):
     slab = x_ref.shape[0]
     arrays = rest[: len(kinds)]
-    gated_ref, head_ref, tail_ref, s, buffer, sems = rest[len(kinds) :]
-    slot = rotate(kinds, at_ref, arrays, buffer, sems, width)
+    gated_ref, head_ref, halo_ref, s, full, buffer, sems, x_sem = rest[len(kinds) :]
+    count = halo_ref.shape[0] - 2 * edge
+    load = [pltpu.make_async_copy(x_ref, full, x_sem.at[0])]
+    slot, ready = rotate(kinds, at_ref, arrays, buffer, sems, width, load)
     feats = []
     for k in range(2):
+        ready(k)
         s[0:edge] = jnp.zeros((edge, width), f32)
-        term = jnp.dot(x_ref[...], buffer[slot, k], preferred_element_type=f32)
+        term = jnp.dot(full[...], buffer[slot, k], preferred_element_type=f32)
         s[edge : edge + slab] = term.astype(bf16).astype(f32)
         head_ref[k] = s[edge : 2 * edge].astype(bf16)
-        tail_ref[k] = s[slab : slab + edge].astype(bf16)
+        halo_ref[count + k * edge : count + (k + 1) * edge] = s[slab : slab + edge].astype(bf16)
         feats.append(short_sum(s, taps_ref, k + 1, slab))
-    gated_ref[...] = (feats[0] * feats[1]).astype(bf16)
+    gated = (feats[0] * feats[1]).astype(bf16)
+    gated_ref[...] = gated
+    halo_ref[0:count] = gated[slab - count :]
 
 
 def kinds_of(pieces, place):
@@ -124,7 +141,14 @@
     return jnp.stack([jnp.asarray(p[2], jnp.int32) for p in pieces])
 
 
-def gate(x, one, two, short_filter, width):
+def hold(array):
+    return pltpu.with_memory_space_constraint(array, pltpu.MemorySpace.HBM)
+
+
+in_hbm = pl.BlockSpec(memory_space=pltpu.MemorySpace.HBM)
+
+
+def gate(x, one, two, short_filter, taps, width):
     slab, features = x.shape
     channels = short_filter.shape[-1]
     kinds = kinds_of(one, 0) + kinds_of(two, 1)
@@ -132,19 +156,21 @@
         num_scalar_prefetch=1,
         grid=(channels // width,),
         in_specs=[
-            pl.BlockSpec(x.shape, lambda i, at: (0, 0), pipeline_mode=pl.Buffered(1)),
+            in_hbm,
             pl.BlockSpec(short_filter.shape[:2] + (width,), lambda i, at: (0, 0, i)),
         ]
-        + [pl.BlockSpec(memory_space=pl.ANY)] * len(kinds),
+        + [in_hbm] * len(kinds),
         out_specs=[
             pl.BlockSpec((slab, width), lambda i, at: (0, i)),
             pl.BlockSpec((2, edge, width), lambda i, at: (0, 0, i)),
-            pl.BlockSpec((2, edge, width), lambda i, at: (0, 0, i)),
+            pl.BlockSpec((taps + 2 * edge, width), lambda i, at: (0, i)),
         ],
         scratch_shapes=[
             pltpu.VMEM((slab + edge, width), f32),
+            pltpu.VMEM((slab, features), bf16),
             pltpu.VMEM((2, 2, features, width), bf16),
             pltpu.SemaphoreType.DMA((2, len(kinds))),
+            pltpu.SemaphoreType.DMA((1,)),
         ],
     )
     return pl.pallas_call(
@@ -153,24 +179,23 @@
         out_shape=[
             jax.ShapeDtypeStruct((slab, channels), bf16),
             jax.ShapeDtypeStruct((2, edge, channels), bf16),
-            jax.ShapeDtypeStruct((2, edge, channels), bf16),
+            jax.ShapeDtypeStruct((taps + 2 * edge, channels), bf16),
         ],
         compiler_params=pltpu.CompilerParams(vmem_limit_bytes=40 << 20),
         name="gate",
-    )(offsets(one), x, short_filter, *[p[0] for p in one + two])
+    )(offsets(one), hold(x), short_filter, *[hold(p[0]) for p in one + two])
 
 
 def query_kernel(kinds, width, at_ref, x_ref, before_ref, taps_ref, *rest):
     slab = x_ref.shape[0]
     arrays = rest[: len(kinds)]
-    out_ref, s, full, buffer, sems = rest[len(kinds) :]
-
-    @pl.when(pl.program_id(0) == 0)
-    def _():
-        full[0:edge] = before_ref[...]
-        full[edge : edge + slab] = x_ref[...]
-
-    slot = rotate(kinds, at_ref, arrays, buffer, sems, width)
+    out_ref, s, full, buffer, sems, x_sem = rest[len(kinds) :]
+    load = [
+        pltpu.make_async_copy(x_ref, full.at[edge : edge + slab], x_sem.at[0]),
+        pltpu.make_async_copy(before_ref, full.at[0:edge], x_sem.at[1]),
+    ]
+    slot, ready = rotate(kinds, at_ref, arrays, buffer, sems, width, load)
+    ready(0)
     term = jnp.dot(full[...], buffer[slot, 0], preferred_element_type=f32)
     s[...] = term.astype(bf16).astype(f32)
     out_ref[...] = short_sum(s, taps_ref, 0, slab)
@@ -184,17 +209,18 @@
         num_scalar_prefetch=1,
         grid=(channels // width,),
         in_specs=[
-            pl.BlockSpec(x.shape, lambda i, at: (0, 0), pipeline_mode=pl.Buffered(1)),
-            pl.BlockSpec(before.shape, lambda i, at: (0, 0), pipeline_mode=pl.Buffered(1)),
+            in_hbm,
+            in_hbm,
             pl.BlockSpec(short_filter.shape[:2] + (width,), lambda i, at: (0, 0, i)),
         ]
-        + [pl.BlockSpec(memory_space=pl.ANY)] * len(kinds),
+        + [in_hbm] * len(kinds),
         out_specs=pl.BlockSpec((slab, width), lambda i, at: (0, i)),
         scratch_shapes=[
             pltpu.VMEM((slab + edge, width), f32),
             pltpu.VMEM((slab + edge, features), bf16),
             pltpu.VMEM((2, 1, features, width), bf16),
             pltpu.SemaphoreType.DMA((2, len(kinds))),
+            pltpu.SemaphoreType.DMA((2,)),
         ],
     )
     return pl.pallas_call(
@@ -203,7 +229,7 @@
         out_shape=jax.ShapeDtypeStruct((slab, channels), f32),
         compiler_params=pltpu.CompilerParams(vmem_limit_bytes=40 << 20),
         name="query",
-    )(offsets(pieces), x, before, short_filter, *[p[0] for p in pieces])
+    )(offsets(pieces), hold(x), hold(before), short_filter, *[hold(p[0]) for p in pieces])
 
 
 def transform(fwd_ref, block):
@@ -238,13 +264,13 @@
 
 
 def mix_kernel(
-    gated_ref, before_ref, head_ref, edge_ref, short_ref, response_ref, query_ref, fwd_ref, inv_ref, out_ref, s
+    gated_ref, halo_ref, head_ref, short_ref, response_ref, query_ref, fwd_ref, inv_ref, out_ref, s
 ):
     taps = response_ref.shape[1]
     blocks = gated_ref.shape[0] // taps
     feats = []
     for k in range(2):
-        s[0:edge] = edge_ref[k].astype(f32)
+        s[0:edge] = halo_ref[taps + k * edge : taps + (k + 1) * edge].astype(f32)
         s[edge : 2 * edge] = head_ref[k].astype(f32)
         total = None
         for lag in range(short_ref.shape[0]):
@@ -256,7 +282,7 @@
     row = lax.broadcasted_iota(jnp.int32, (2 * taps, 1), 0)
     sign = jnp.where(row % 2 == 0, 1.0, -1.0).astype(f32)
     h_cos, h_sin, h_low = response_ref[0], response_ref[1], response_ref[2]
-    last = transform(fwd_ref, before_ref[...])
+    last = transform(fwd_ref, halo_ref[0:taps])
     for b in range(blocks):
         if b == 0:
             block = jnp.concatenate([first, gated_ref[edge:taps]], axis=0)
@@ -276,7 +302,7 @@
         out_ref[at] = (query_ref[at] * mixed).astype(bf16)
 
 
-def mix(gated, before, head, edge_rows, short_filter, response, query_rows, tables, width):
+def mix(gated, halo, head, short_filter, response, query_rows, tables, width):
     slab, channels = gated.shape
     count = response.shape[1]
     forward, inverse = tables
@@ -287,8 +313,7 @@
         grid=(channels // width,),
         in_specs=[
             col(slab),
-            col(count),
-            cube(2, edge),
+            col(count + 2 * edge),
             cube(2, edge),
             cube(*short_filter.shape[:2]),
             cube(3, count),
@@ -301,7 +326,7 @@
         scratch_shapes=[pltpu.VMEM((2 * edge, width), f32)],
         compiler_params=pltpu.CompilerParams(vmem_limit_bytes=40 << 20),
         name="mix",
-    )(gated, before, head, edge_rows, short_filter, response, query_rows, forward, inverse)
+    )(gated, halo, head, short_filter, response, query_rows, forward, inverse)
 
 
 def local(tokens, norm_gain, w_in, short_filter, medium_filter, decay, w_out):
@@ -338,26 +363,27 @@
 
     weights = jnp.transpose(w_in, (1, 0, 2))
     half = rows // 2
-    fine = half // 2
+    fine = half
     order = (1, 2, 0)
     out_rows = w_out.shape[0]
-    out_half = out_rows // 2
     if paired:
         first_half, other_half = g * half, (1 - g) * half
         peer = to_core(weights)
         pieces = {b: [(weights, b, c * rows), (peer, b, (c ^ 1) * rows)] for b in order}
-        nears, far_cores = [], {}
+        nears, fars, far_cores = [], [], {}
         for b in order:
             for u in range(half // fine):
+                source = after(weights, normed) if nears else weights
                 mine = lax.dynamic_slice(
-                    weights, (b, first_half + u * fine, 0), (1, fine, channels)
+                    source, (b, first_half + u * fine, 0), (1, fine, channels)
                 ).reshape(fine, channels)
-                if len(nears) < 2:
-                    tokens = after(tokens, mine)
-                if len(nears) >= 2:
-                    mine = after(mine, nears[-2])
+                if not nears:
+                    normed = norm(after(tokens, mine), norm_gain)
+                if nears:
+                    mine = after(mine, nears[-1])
                 near = to_chip(mine)
-                far = to_group(near)
+                far = to_group(after(near, fars[-1]) if fars else near)
+                fars.append(far)
                 nears.append(near)
                 pieces[b] += [
                     (near, None, (c ^ 2) * rows + first_half + u * fine),
@@ -367,13 +393,11 @@
                 ]
                 if b == 0:
                     far_cores[len(pieces[b]) - 1] = far
-        mine = lax.dynamic_slice(w_out, (g * out_half, 0), (out_half, channels))
-        near_out = to_chip(after(mine, nears[-1]))
     else:
         full = lax.all_gather(weights, "context", axis=1, tiled=True)
         pieces = {b: [(full, b, 0)] for b in order}
-
-    normed = norm(tokens, norm_gain)
+        normed = norm(tokens, norm_gain)
+
     gathered = lax.all_gather(normed, "tensor", axis=0, tiled=True)
     before_rows = to_next(gathered[slab - edge :])
 
@@ -381,23 +405,24 @@
     tables = fourier_tables(medium_count)
     response = respond(medium_filter, decay, tables[0], width)
     gate_taps = after(short_filter, response)
-    gated, head, tail = gate(gathered, pieces[1], pieces[2], gate_taps, width)
+    gated, head, edges = gate(
+        gathered, pieces[1], pieces[2], gate_taps, medium_count, width
+    )
+    halo = to_next(edges)
     if paired:
-        near_out = after(near_out, gated)
-        far_out = to_group(near_out)
+        for n, far in far_cores.items():
+            pieces[0][n] = (to_core(after(far, gated)), *pieces[0][n][1:])
+    query_rows = query(gathered, before_rows, pieces[0], short_filter, width)
+    combined = mix(gated, halo, head, short_filter, response, query_rows, tables, width)
+    if paired:
+        out_full = lax.all_gather(after(w_out, nears[0]), "context", axis=0, tiled=True)
         out_peer = to_core(after(w_out, gated))
-        sets = [[w_out], [out_peer], [near_out, far_out], [to_core(near_out), to_core(far_out)]]
-        for n, p in enumerate(pieces[0]):
-            if n in far_cores:
-                pieces[0][n] = (to_core(after(far_cores[n], gated)), p[1], p[2])
+        part = lambda i: lax.dynamic_slice(out_full, ((c ^ i) * out_rows, 0), (out_rows, channels))
+        sets = [[w_out], [out_peer], [part(2)], [part(3)]]
     else:
         sets = [[lax.all_gather(w_out, "context", axis=0, tiled=True)]]
-    before = to_next(gated[slab - medium_count :])
-    edge_rows = to_next(tail)
-    query_rows = query(gathered, before_rows, pieces[0], short_filter, width)
-    combined = mix(gated, before, head, edge_rows, short_filter, response, query_rows, tables, width)
-
-    results, firsts = [], []
+
+    results = []
     for parts in sets:
         partial = [
             lax.dot_general(
@@ -405,6 +430,7 @@
             ).astype(bf16)
             for part in parts
         ]
+        combined = after(combined, *partial)
 
         def block(index, blocks=1):
             index = jnp.clip(index, 0, count - blocks)
@@ -424,10 +450,7 @@
 
         if count == 4:
             far_pair = block(jnp.where(z < 2, 2, 0), 2)
-            if len(firsts) >= 2:
-                far_pair = after(far_pair, firsts[-2])
             got = send(far_pair, {0: 1, 3: 2})
-            firsts.append(got)
             got = send(plus(far_pair, got), {1: 2, 2: 1})
             low, high = got[:length], got[length:]
             odd = z % 2 == 1
@@ -448,8 +471,6 @@
         return results[0]
     swap = lambda test, a, b: (jnp.where(test, b, a), jnp.where(test, a, b))
     e0, e1, e2, e3 = results
-    e2 = jnp.concatenate(swap(g == 1, e2[:, :out_half], e2[:, out_half:]), 1)
-    e3 = jnp.concatenate(swap(g == 1, e3[:, :out_half], e3[:, out_half:]), 1)
     odd = c % 2 == 1
     low = jnp.concatenate(swap(odd, e0, e1), 1)
     high = jnp.concatenate(swap(odd, e2, e3), 1)

time: 278 us -> 233 us (0.84)
  the two profiles are of different devices: /device:TPU:0 before, /device:TPU:10 now
where the time goes in v2:
time: 233 us
  waiting for transfers between devices  113 us (48%)
  Pallas kernels  47.9 us (21%)
  starting transfers between devices  35.3 us (15%)
  between operations  14 us (6%)
  matrix products  10.1 us (4%)
  local copies, waits for them, and re-layouts  9.43 us (4%)
  other arithmetic  3.41 us (1%)
    ppermute x28, waiting for transfers between devices, move(): return lax.ppermute(value, axes, pairs)  113 us
    ppermute x28, starting transfers between devices, move(): return lax.ppermute(value, axes, pairs)  35.3 us
    pallas_call x1, Pallas kernels, gate(): pl.pallas_call(functools.partial(gate_kernel, kinds, width), grid_spec=gr...  25.7 us
    dot_general x4, matrix products, local(): lax.dot_general(combined, part, (((1,), (1,)), ((), ())), preferred_eleme...  10.1 us
    pallas_call x1, Pallas kernels, query(): pl.pallas_call(functools.partial(query_kernel, kinds, width), grid_spec=g...  10.1 us
  transfers between devices with their start and end apart: 30, of which 14 were waited for; matrix products, arithmetic and copies ran while one was open for 7% of the time, Pallas kernels for 19%

profile of v2, /device:TPU:10, one launch (start us, length us, event | category | flops | bytes accessed | tf_op | source)
XLA Modules:
  0.0 232.7 jit_solution(5254239007441154048)
XLA Ops:
  6.5 1.3 dynamic-slice_bitcast_fusion.2
  7.9 0.6 reshape.18.gain_ref
  8.5 3.7 %norm.1 = bf16[128,4096]{1,0:T(8,128)(2,1)} custom-call(bf16[128,4096]{1,0:T(8,128)(2,1)} %x_ref, bf16[1,4096]{1,0:T(2,128)(2,1)} %reshape.18.gain_ref), custom_call_target="tpu_custom_call" | custom-call | tf_op jit(solution)/shard_map/norm/pallas_call | solution.py:58
  12.2 0.6 collective-permute-start.1
  12.8 24.4 %collective-permute-done.1.rest_2_ = bf16[512,1024]{1,0:T(8,128)(2,1)S(1)} collective-permute-done((bf16[512,1024]{1,0:T(8,128)(2,1)S(1)}, bf16[512,1024]{1,0:T(8,128)(2,1)S(1)}, u32[]{:S(2)}, u32[]{:S(2)}) %collective-permute-start.1) | collective-permute-done | bytes 1048608 | tf_op jit(solution)/shard_map/ppermute | solution.py:351
  37.3 2.0 dynamic-slice_bitcast_fusion
  39.3 0.6 collective-permute-start.5
  39.9 1.5 collective-permute-start.3
  41.4 23.3 %collective-permute-done.5.rest_8_ = bf16[512,1024]{1,0:T(8,128)(2,1)} collective-permute-done((bf16[512,1024]{1,0:T(8,128)(2,1)S(1)}, bf16[512,1024]{1,0:T(8,128)(2,1)}, u32[]{:S(2)}, u32[]{:S(2)}) %collective-permute-start.5) | collective-permute-done | bytes 1048608 | tf_op jit(solution)/shard_map/ppermute | solution.py:351
  64.7 0.3 collective-permute-done.3.rest_4_
  65.0 1.5 collective-permute-start.7
  66.5 1.5 collective-permute-start.11
  68.0 0.5 collective-permute-start.6
  68.5 21.0 %collective-permute-done.7.rest_10_ = bf16[512,1024]{1,0:T(8,128)(2,1)} collective-permute-done((bf16[512,1024]{1,0:T(8,128)(2,1)}, bf16[512,1024]{1,0:T(8,128)(2,1)}, u32[]{:S(2)}, u32[]{:S(2)}) %collective-permute-start.7) | collective-permute-done | bytes 1048608 | tf_op jit(solution)/shard_map/ppermute | solution.py:351
  89.5 0.9 collective-permute-done.11.rest_2_
  90.5 1.1 copy-done.9
  91.5 1.0 collective-permute-start.13
  92.6 3.9 %respond.1.response_ref = f32[3,128,1024]{2,1,0:T(8,128)} custom-call(f32[128,1024]{1,0:T(8,128)} %filter_ref.1, f32[1,1024]{1,0:T(1,128)} %bitcast.25, bf16[256,256]{1,0:T(8,128)(2,1)} %constant.52.clone.fwd_ref), custom_call_target="tpu_custom_call" | custom-call | tf_op jit(solution)/shard_map/respond/pallas_call | solution.py:252
  96.7 25.7 %gate.1 = (bf16[512,1024]{1,0:T(8,128)(2,1)S(1)}, bf16[2,16,1024]{2,1,0:T(8,128)(2,1)S(1)}, bf16[160,1024]{1,0:T(8,128)(2,1)S(1)}) custom-call(s32[6]{0:T(128)S(1)} %stack.34.at_ref, bf16[512,4096]{1,0:T(8,128)(2,1)} %all-gather.3.cloned.1.call-done.x_ref, f32[3,3,1024]{2,1,0:T(4,128)S(1)} %copy-done.2, bf16[3,1024,1024]{2,1,0:T(8,128)(2,1)} %bitcast.22, ...), custom_call_target="tpu_custom_call" | custom-call | tf_op jit(solution)/shard_map/gate/pallas_call | solution.py:176
  122.5 0.5 collective-permute-start.12
  123.1 2.3 collective-permute-start.9
  125.4 0.9 slice.36
  126.3 1.9 collective-permute-start.10
  128.3 14.5 %collective-permute-done.10.before_ref = bf16[16,4096]{1,0:T(8,128)(2,1)S(1)} collective-permute-done((bf16[16,4096]{1,0:T(8,128)(2,1)S(1)}, bf16[16,4096]{1,0:T(8,128)(2,1)S(1)}, u32[]{:S(2)}, u32[]{:S(2)}) %collective-permute-start.10) | collective-permute-done | bytes 131104 | tf_op jit(solution)/shard_map/ppermute | solution.py:351
  142.8 0.7 copy-done.10
  143.5 10.1 %query.1.query_ref = f32[512,1024]{1,0:T(8,128)S(1)} custom-call(s32[6]{0:T(128)S(1)} %stack.34.at_ref, bf16[512,4096]{1,0:T(8,128)(2,1)} %all-gather.3.cloned.1.call-done.x_ref, bf16[16,4096]{1,0:T(8,128)(2,1)} %copy-done.10, f32[3,3,1024]{2,1,0:T(4,128)S(1)} %copy-done.2, bf16[3,1024,1024]{2,1,0:T(8,128)(2,1)} %bitcast.24, ...), custom_call_target="tpu_custom_call" | custom-call | tf_op jit(solution)/shard_map/query/pallas_call | solution.py:226
  153.6 4.5 %mix.1 = bf16[512,1024]{1,0:T(8,128)(2,1)S(1)} custom-call(bf16[512,1024]{1,0:T(8,128)(2,1)S(1)} %get-tuple-element.26.gated_ref, bf16[160,1024]{1,0:T(8,128)(2,1)S(1)} %collective-permute-done.9.halo_ref, bf16[2,16,1024]{2,1,0:T(8,128)(2,1)S(1)} %get-tuple-element.28.head_ref, f32[3,3,1024]{2,1,0:T(4,128)S(1)} %copy-done.2, f32[3,128,1024]{2,1,0:T(8,128)S(1)} %copy-done, ...), custom_call_target="tpu_custom_call" | custom-call | tf_op jit(solution)/shard_map/mix/pallas_call | solution.py:311
  158.1 1.3 convolution_convert_fusion.1
  159.4 0.8 constant_dynamic-slice_fusion
  160.3 1.3 collective-permute-start.25
  161.6 2.9 %convolution_convert_fusion = bf16[512,1024]{1,0:T(8,128)(2,1)S(1)} fusion(bf16[512,1024]{1,0:T(8,128)(2,1)S(1)} %mix.1, bf16[1024,1024]{1,0:T(8,128)(2,1)} %collective-permute-done.15), kind=kOutput, calls=%fused_computation.6 | convolution fusion | flops 1074266112 | bytes 4194304 | tf_op jit(solution)/shard_map/dot_general | solution.py:428
  164.5 1.0 copy-done.4
  165.5 0.8 constant_dynamic-slice_fusion.1
  166.3 1.3 collective-permute-start.22
  167.6 2.9 %fusion.4 = bf16[512,1024]{1,0:T(8,128)(2,1)S(1)} fusion(bf16[512,1024]{1,0:T(8,128)(2,1)S(1)} %mix.1, bf16[4096,1024]{1,0:T(8,128)(2,1)} %all-gather.5.cloned.1.call-done, s32[]{:T(128)S(6)} %select_n.123), kind=kOutput, calls=%fused_computation.4 | convolution fusion | flops 1074266112 | bytes 4194308 | tf_op jit(solution)/shard_map/dot_general | solution.py:428
  170.6 1.3 collective-permute-start.19
  171.9 2.9 %fusion.7 = bf16[512,1024]{1,0:T(8,128)(2,1)S(1)} fusion(bf16[512,1024]{1,0:T(8,128)(2,1)S(1)} %mix.1, bf16[4096,1024]{1,0:T(8,128)(2,1)} %all-gather.5.cloned.1.call-done, s32[]{:T(128)S(6)} %select_n.124), kind=kOutput, calls=%fused_computation.5 | convolution fusion | flops 1074266112 | bytes 4194308 | tf_op jit(solution)/shard_map/dot_general | solution.py:428
  174.9 1.6 collective-permute-start.16
  176.5 0.7 collective-permute-done.25
  177.2 0.2 add_convert_fusion
  177.4 3.6 %collective-permute-start.26 = (bf16[256,1024]{1,0:T(8,128)(2,1)S(1)}, bf16[256,1024]{1,0:T(8,128)(2,1)S(1)}, u32[]{:S(2)}, u32[]{:S(2)}) collective-permute-start(bf16[256,1024]{1,0:T(8,128)(2,1)S(1)} %add_convert_fusion), channel_id=1, source_target_pairs={{1,2},{2,1},{5,6},{6,5},{9,10},{10,9},{13,14},{14,13},{17,18},{18,... | collective-permute-start | bytes 1572872 | tf_op jit(solution)/shard_map/ppermute | solution.py:351
  181.0 6.0 %collective-permute-done.22 = bf16[256,1024]{1,0:T(8,128)(2,1)S(1)} collective-permute-done((bf16[256,1024]{1,0:T(8,128)(2,1)}, bf16[256,1024]{1,0:T(8,128)(2,1)S(1)}, u32[]{:S(2)}, u32[]{:S(2)}) %collective-permute-start.22) | collective-permute-done | bytes 524320 | tf_op jit(solution)/shard_map/ppermute | solution.py:351
  187.1 0.2 add_convert_fusion.1
  187.3 3.4 %collective-permute-start.23 = (bf16[256,1024]{1,0:T(8,128)(2,1)S(1)}, bf16[256,1024]{1,0:T(8,128)(2,1)S(1)}, u32[]{:S(2)}, u32[]{:S(2)}) collective-permute-start(bf16[256,1024]{1,0:T(8,128)(2,1)S(1)} %add_convert_fusion.1), channel_id=1, source_target_pairs={{1,2},{2,1},{5,6},{6,5},{9,10},{10,9},{13,14},{14,13},{17,18},{18,... | collective-permute-start | bytes 1572872 | tf_op jit(solution)/shard_map/ppermute | solution.py:351
  190.7 2.9 %collective-permute-done.19 = bf16[256,1024]{1,0:T(8,128)(2,1)S(1)} collective-permute-done((bf16[256,1024]{1,0:T(8,128)(2,1)S(1)}, bf16[256,1024]{1,0:T(8,128)(2,1)S(1)}, u32[]{:S(2)}, u32[]{:S(2)}) %collective-permute-start.19) | collective-permute-done | bytes 524320 | tf_op jit(solution)/shard_map/ppermute | solution.py:351
  193.6 0.2 add_convert_fusion.2
  193.8 4.1 %collective-permute-start.20 = (bf16[256,1024]{1,0:T(8,128)(2,1)S(1)}, bf16[256,1024]{1,0:T(8,128)(2,1)S(1)}, u32[]{:S(2)}, u32[]{:S(2)}) collective-permute-start(bf16[256,1024]{1,0:T(8,128)(2,1)S(1)} %add_convert_fusion.2), channel_id=1, source_target_pairs={{1,2},{2,1},{5,6},{6,5},{9,10},{10,9},{13,14},{14,13},{17,18},{18,... | collective-permute-start | bytes 1572872 | tf_op jit(solution)/shard_map/ppermute | solution.py:351
  197.9 6.9 %collective-permute-done.16 = bf16[256,1024]{1,0:T(8,128)(2,1)S(1)} collective-permute-done((bf16[256,1024]{1,0:T(8,128)(2,1)S(1)}, bf16[256,1024]{1,0:T(8,128)(2,1)S(1)}, u32[]{:S(2)}, u32[]{:S(2)}) %collective-permute-start.16) | collective-permute-done | bytes 524320 | tf_op jit(solution)/shard_map/ppermute | solution.py:351
  204.8 0.2 add_convert_fusion.3
  205.0 4.1 %collective-permute-start.17 = (bf16[256,1024]{1,0:T(8,128)(2,1)S(1)}, bf16[256,1024]{1,0:T(8,128)(2,1)S(1)}, u32[]{:S(2)}, u32[]{:S(2)}) collective-permute-start(bf16[256,1024]{1,0:T(8,128)(2,1)S(1)} %add_convert_fusion.3), channel_id=1, source_target_pairs={{1,2},{2,1},{5,6},{6,5},{9,10},{10,9},{13,14},{14,13},{17,18},{18,... | collective-permute-start | bytes 1572872 | tf_op jit(solution)/shard_map/ppermute | solution.py:351
  209.2 0.1 add_convert_fusion.5
  209.4 0.1 add_convert_fusion.7
  209.5 2.1 collective-permute-start.24
  211.6 0.1 add_convert_fusion.9
  211.7 0.1 collective-permute-start.21
  211.8 4.5 %collective-permute-done.17 = bf16[256,1024]{1,0:T(8,128)(2,1)S(1)} collective-permute-done((bf16[256,1024]{1,0:T(8,128)(2,1)S(1)}, bf16[256,1024]{1,0:T(8,128)(2,1)S(1)}, u32[]{:S(2)}, u32[]{:S(2)}) %collective-permute-start.17) | collective-permute-done | bytes 524320 | tf_op jit(solution)/shard_map/ppermute | solution.py:351
  216.3 0.1 add_convert_fusion.11
  216.5 2.0 collective-permute-done.24
  218.6 0.4 broadcast_select_fusion.3
  219.0 2.4 %collective-permute-done.21 = bf16[128,1024]{1,0:T(8,128)(2,1)S(1)} collective-permute-done((bf16[128,1024]{1,0:T(8,128)(2,1)S(1)}, bf16[128,1024]{1,0:T(8,128)(2,1)S(1)}, u32[]{:S(2)}, u32[]{:S(2)}) %collective-permute-start.21) | collective-permute-done | bytes 262176 | tf_op jit(solution)/shard_map/ppermute | solution.py:351
  221.4 2.8 %collective-permute-done.18 = bf16[128,1024]{1,0:T(8,128)(2,1)S(1)} collective-permute-done((bf16[128,1024]{1,0:T(8,128)(2,1)S(1)}, bf16[128,1024]{1,0:T(8,128)(2,1)S(1)}, u32[]{:S(2)}, u32[]{:S(2)}) %collective-permute-start.18) | collective-permute-done | bytes 262176 | tf_op jit(solution)/shard_map/ppermute | solution.py:351
  224.2 0.4 broadcast_select_fusion.5
  224.6 0.2 broadcast_select_fusion.1
  224.8 1.1 pad_maximum_fusion
  (54 shorter events, 0.8 us)
Async XLA Ops:
  6.5 1.3 copy-start.11
  6.5 90.1 %all-gather.3.cloned.1.call-start = ((), (), s32[]{:S(2)}) async-start(), calls=%async_computation | async-start | bytes 5242880 | tf_op jit(solution)/shard_map/all_gather | solution.py:401
  12.2 155.5 %all-gather.5.cloned.1.call-start = ((), (), s32[]{:S(2)}) async-start(), calls=%async_computation.1 | async-start | bytes 10485760 | tf_op jit(solution)/shard_map/all_gather | solution.py:418
  12.2 25.0 %collective-permute-start.1 = (bf16[512,1024]{1,0:T(8,128)(2,1)S(1)}, bf16[512,1024]{1,0:T(8,128)(2,1)S(1)}, u32[]{:S(2)}, u32[]{:S(2)}) collective-permute-start(bf16[512,1024]{1,0:T(8,128)(2,1)S(1)} %dynamic-slice_bitcast_fusion.2), channel_id=1, source_target_pairs={{0,8},{1,9},{2,10},{3,11},{4,12},{5,13},{6,14},{7,15},{8,0},{9,1},... | collective-permute-start | bytes 3145736 | tf_op jit(solution)/shard_map/ppermute | solution.py:351
  37.2 30.8 %copy-start.8 = (bf16[512,1024]{1,0:T(8,128)(2,1)}, bf16[512,1024]{1,0:T(8,128)(2,1)S(1)}, u32[]{:S(2)}) copy-start(bf16[512,1024]{1,0:T(8,128)(2,1)S(1)} %collective-permute-done.1.rest_2_) | copy-start | bytes 3145732
  37.2 59.4 %collective-permute-start = (bf16[3,1024,1024]{2,1,0:T(8,128)(2,1)}, bf16[3,1024,1024]{2,1,0:T(8,128)(2,1)}, u32[]{:S(2)}, u32[]{:S(2)}) collective-permute-start(bf16[3,1024,1024]{2,1,0:T(8,128)(2,1)} %bitcast.20), channel_id=1, source_target_pairs={{0,4},{1,5},{2,6},{3,7},{4,0},{5,1},{6,2},{7,3},{8,12},{9,13},{10,... | collective-permute-start | bytes 18874376 | tf_op jit(solution)/shard_map/ppermute | solution.py:351
  39.3 57.4 %copy-start.2 = (f32[3,3,1024]{2,1,0:T(4,128)S(1)}, f32[3,3,1024]{2,1,0:T(4,128)}, u32[]{:S(2)}) copy-start(f32[3,3,1024]{2,1,0:T(4,128)} %short_ref.1) | copy-start | bytes 110596
  39.3 25.4 %collective-permute-start.5 = (bf16[512,1024]{1,0:T(8,128)(2,1)S(1)}, bf16[512,1024]{1,0:T(8,128)(2,1)}, u32[]{:S(2)}, u32[]{:S(2)}) collective-permute-start(bf16[512,1024]{1,0:T(8,128)(2,1)S(1)} %get-tuple-element.24), channel_id=1, source_target_pairs={{0,8},{1,9},{2,10},{3,11},{4,12},{5,13},{6,14},{7,15},{8,0},{9,1},... | collective-permute-start | bytes 3145736 | tf_op jit(solution)/shard_map/ppermute | solution.py:351
  39.9 25.1 %collective-permute-start.3 = (bf16[512,1024]{1,0:T(8,128)(2,1)S(1)}, bf16[512,1024]{1,0:T(8,128)(2,1)}, u32[]{:S(2)}, u32[]{:S(2)}) collective-permute-start(bf16[512,1024]{1,0:T(8,128)(2,1)S(1)} %collective-permute-done.1.rest_2_), channel_id=1, source_target_pairs={{0,16},{1,17},{2,18},{3,19},{4,20},{5,21},{6,22},{7,23},{8,24},{9,... | collective-permute-start | bytes 3145736 | tf_op jit(solution)/shard_map/ppermute | solution.py:351
  65.0 24.5 %collective-permute-start.7 = (bf16[512,1024]{1,0:T(8,128)(2,1)}, bf16[512,1024]{1,0:T(8,128)(2,1)}, u32[]{:S(2)}, u32[]{:S(2)}) collective-permute-start(bf16[512,1024]{1,0:T(8,128)(2,1)} %collective-permute-done.5.rest_8_), channel_id=1, source_target_pairs={{0,16},{1,17},{2,18},{3,19},{4,20},{5,21},{6,22},{7,23},{8,24},{9,... | collective-permute-start | bytes 3145736 | tf_op jit(solution)/shard_map/ppermute | solution.py:351
  66.5 23.9 %collective-permute-start.11 = (bf16[512,1024]{1,0:T(8,128)(2,1)S(1)}, bf16[512,1024]{1,0:T(8,128)(2,1)S(1)}, u32[]{:S(2)}, u32[]{:S(2)}) collective-permute-start(bf16[512,1024]{1,0:T(8,128)(2,1)S(1)} %get-tuple-element.29), channel_id=1, source_target_pairs={{0,8},{1,9},{2,10},{3,11},{4,12},{5,13},{6,14},{7,15},{8,0},{9,1},... | collective-permute-start | bytes 3145736 | tf_op jit(solution)/shard_map/ppermute | solution.py:351
  68.0 22.4 %collective-permute-start.2 = (bf16[512,1024]{1,0:T(8,128)(2,1)S(1)}, bf16[512,1024]{1,0:T(8,128)(2,1)S(1)}, u32[]{:S(2)}, u32[]{:S(2)}) collective-permute-start(bf16[512,1024]{1,0:T(8,128)(2,1)S(1)} %collective-permute-done.1.rest_2_), channel_id=1, source_target_pairs={{0,4},{1,5},{2,6},{3,7},{4,0},{5,1},{6,2},{7,3},{8,12},{9,13},{10,... | collective-permute-start | bytes 3145736 | tf_op jit(solution)/shard_map/ppermute | solution.py:351
  68.0 28.6 %collective-permute-start.6 = (bf16[512,1024]{1,0:T(8,128)(2,1)}, bf16[512,1024]{1,0:T(8,128)(2,1)}, u32[]{:S(2)}, u32[]{:S(2)}) collective-permute-start(bf16[512,1024]{1,0:T(8,128)(2,1)} %collective-permute-done.5.rest_8_), channel_id=1, source_target_pairs={{0,4},{1,5},{2,6},{3,7},{4,0},{5,1},{6,2},{7,3},{8,12},{9,13},{10,... | collective-permute-start | bytes 3145736 | tf_op jit(solution)/shard_map/ppermute | solution.py:351
  89.5 7.1 %collective-permute-start.4 = (bf16[512,1024]{1,0:T(8,128)(2,1)}, bf16[512,1024]{1,0:T(8,128)(2,1)}, u32[]{:S(2)}, u32[]{:S(2)}) collective-permute-start(bf16[512,1024]{1,0:T(8,128)(2,1)} %collective-permute-done.3.rest_4_), channel_id=1, source_target_pairs={{0,4},{1,5},{2,6},{3,7},{4,0},{5,1},{6,2},{7,3},{8,12},{9,13},{10,... | collective-permute-start | bytes 3145736 | tf_op jit(solution)/shard_map/ppermute | solution.py:351
  90.4 32.0 %copy-start.7 = (bf16[512,1024]{1,0:T(8,128)(2,1)}, bf16[512,1024]{1,0:T(8,128)(2,1)S(1)}, u32[]{:S(2)}) copy-start(bf16[512,1024]{1,0:T(8,128)(2,1)S(1)} %collective-permute-done.11.rest_2_) | copy-start | bytes 3145732
  90.4 6.2 %collective-permute-start.8 = (bf16[512,1024]{1,0:T(8,128)(2,1)}, bf16[512,1024]{1,0:T(8,128)(2,1)}, u32[]{:S(2)}, u32[]{:S(2)}) collective-permute-start(bf16[512,1024]{1,0:T(8,128)(2,1)} %collective-permute-done.7.rest_10_), channel_id=1, source_target_pairs={{0,4},{1,5},{2,6},{3,7},{4,0},{5,1},{6,2},{7,3},{8,12},{9,13},{10,... | collective-permute-start | bytes 3145736 | tf_op jit(solution)/shard_map/ppermute | solution.py:351
  90.4 1.1 copy-start.9
  91.5 31.4 %collective-permute-start.13 = (bf16[512,1024]{1,0:T(8,128)(2,1)S(1)}, bf16[512,1024]{1,0:T(8,128)(2,1)}, u32[]{:S(2)}, u32[]{:S(2)}) collective-permute-start(bf16[512,1024]{1,0:T(8,128)(2,1)S(1)} %collective-permute-done.11.rest_2_), channel_id=1, source_target_pairs={{0,16},{1,17},{2,18},{3,19},{4,20},{5,21},{6,22},{7,23},{8,24},{9,... | collective-permute-start | bytes 3145736 | tf_op jit(solution)/shard_map/ppermute | solution.py:351
  122.4 39.2 %collective-permute-start.15 = (bf16[1024,1024]{1,0:T(8,128)(2,1)}, bf16[1024,1024]{1,0:T(8,128)(2,1)}, u32[]{:S(2)}, u32[]{:S(2)}) collective-permute-start(bf16[1024,1024]{1,0:T(8,128)(2,1)} %param.15), channel_id=1, source_target_pairs={{0,4},{1,5},{2,6},{3,7},{4,0},{5,1},{6,2},{7,3},{8,12},{9,13},{10,... | collective-permute-start | bytes 6291464 | tf_op jit(solution)/shard_map/ppermute | solution.py:351
  122.5 5.8 %collective-permute-start.12 = (bf16[512,1024]{1,0:T(8,128)(2,1)S(1)}, bf16[512,1024]{1,0:T(8,128)(2,1)}, u32[]{:S(2)}, u32[]{:S(2)}) collective-permute-start(bf16[512,1024]{1,0:T(8,128)(2,1)S(1)} %collective-permute-done.11.rest_2_), channel_id=1, source_target_pairs={{0,4},{1,5},{2,6},{3,7},{4,0},{5,1},{6,2},{7,3},{8,12},{9,13},{10,... | collective-permute-start | bytes 3145736 | tf_op jit(solution)/shard_map/ppermute | solution.py:351
  123.0 19.8 %collective-permute-start.14 = (bf16[512,1024]{1,0:T(8,128)(2,1)}, bf16[512,1024]{1,0:T(8,128)(2,1)}, u32[]{:S(2)}, u32[]{:S(2)}) collective-permute-start(bf16[512,1024]{1,0:T(8,128)(2,1)} %collective-permute-done.13.rest_4_), channel_id=1, source_target_pairs={{0,4},{1,5},{2,6},{3,7},{4,0},{5,1},{6,2},{7,3},{8,12},{9,13},{10,... | collective-permute-start | bytes 3145736 | tf_op jit(solution)/shard_map/ppermute | solution.py:351
  123.1 30.5 %collective-permute-start.9 = (bf16[160,1024]{1,0:T(8,128)(2,1)S(1)}, bf16[160,1024]{1,0:T(8,128)(2,1)S(1)}, u32[]{:S(2)}, u32[]{:S(2)}) collective-permute-start(bf16[160,1024]{1,0:T(8,128)(2,1)S(1)} %get-tuple-element.27), channel_id=1, source_target_pairs={{0,4},{1,5},{2,6},{3,7},{4,8},{5,9},{6,10},{7,11},{8,12},{9,13},{1... | collective-permute-start | bytes 983048 | tf_op jit(solution)/shard_map/ppermute | solution.py:351
  126.3 16.5 %collective-permute-start.10 = (bf16[16,4096]{1,0:T(8,128)(2,1)S(1)}, bf16[16,4096]{1,0:T(8,128)(2,1)S(1)}, u32[]{:S(2)}, u32[]{:S(2)}) collective-permute-start(bf16[16,4096]{1,0:T(8,128)(2,1)S(1)} %slice.36), channel_id=1, source_target_pairs={{0,4},{1,5},{2,6},{3,7},{4,8},{5,9},{6,10},{7,11},{8,12},{9,13},{1... | collective-permute-start | bytes 393224 | tf_op jit(solution)/shard_map/ppermute | solution.py:351
  128.3 25.2 %copy-start = (f32[3,128,1024]{2,1,0:T(8,128)S(1)}, f32[3,128,1024]{2,1,0:T(8,128)}, u32[]{:S(2)}) copy-start(f32[3,128,1024]{2,1,0:T(8,128)} %respond.1.response_ref) | copy-start | bytes 4718596
  128.3 25.2 %copy-start.1 = (bf16[256,256]{1,0:T(8,128)(2,1)S(1)}, bf16[256,256]{1,0:T(8,128)(2,1)}, u32[]{:S(2)}) copy-start(bf16[256,256]{1,0:T(8,128)(2,1)} %constant.52.clone.fwd_ref) | copy-start | bytes 393220
  128.3 25.2 %copy-start.3 = (bf16[128,768]{1,0:T(8,128)(2,1)S(1)}, bf16[128,768]{1,0:T(8,128)(2,1)}, u32[]{:S(2)}) copy-start(bf16[128,768]{1,0:T(8,128)(2,1)} %constant.53.clone.inv_ref) | copy-start | bytes 589828
  142.8 0.7 copy-start.10
  153.6 4.5 %copy-start.6 = (bf16[1024,1024]{1,0:T(8,128)(2,1)S(1)}, bf16[1024,1024]{1,0:T(8,128)(2,1)}, u32[]{:S(2)}) copy-start(bf16[1024,1024]{1,0:T(8,128)(2,1)} %param.15) | copy-start | bytes 6291460
  160.3 17.0 %collective-permute-start.25 = (bf16[256,1024]{1,0:T(8,128)(2,1)}, bf16[256,1024]{1,0:T(8,128)(2,1)S(1)}, u32[]{:S(2)}, u32[]{:S(2)}) collective-permute-start(bf16[256,1024]{1,0:T(8,128)(2,1)} %constant_dynamic-slice_fusion), channel_id=1, source_target_pairs={{0,1},{3,2},{4,5},{7,6},{8,9},{11,10},{12,13},{15,14},{16,17},{19,... | collective-permute-start | bytes 1572872 | tf_op jit(solution)/shard_map/ppermute | solution.py:351
  164.5 1.0 copy-start.4
  166.3 20.8 %collective-permute-start.22 = (bf16[256,1024]{1,0:T(8,128)(2,1)}, bf16[256,1024]{1,0:T(8,128)(2,1)S(1)}, u32[]{:S(2)}, u32[]{:S(2)}) collective-permute-start(bf16[256,1024]{1,0:T(8,128)(2,1)} %constant_dynamic-slice_fusion.1), channel_id=1, source_target_pairs={{0,1},{3,2},{4,5},{7,6},{8,9},{11,10},{12,13},{15,14},{16,17},{19,... | collective-permute-start | bytes 1572872 | tf_op jit(solution)/shard_map/ppermute | solution.py:351
  170.6 23.0 %collective-permute-start.19 = (bf16[256,1024]{1,0:T(8,128)(2,1)S(1)}, bf16[256,1024]{1,0:T(8,128)(2,1)S(1)}, u32[]{:S(2)}, u32[]{:S(2)}) collective-permute-start(bf16[256,1024]{1,0:T(8,128)(2,1)S(1)} %constant_dynamic-slice_fusion.2), channel_id=1, source_target_pairs={{0,1},{3,2},{4,5},{7,6},{8,9},{11,10},{12,13},{15,14},{16,17},{19,... | collective-permute-start | bytes 1572872 | tf_op jit(solution)/shard_map/ppermute | solution.py:351
  174.8 12.2 %copy-start.5 = (bf16[512,1024]{1,0:T(8,128)(2,1)S(1)}, bf16[512,1024]{1,0:T(8,128)(2,1)}, u32[]{:S(2)}) copy-start(bf16[512,1024]{1,0:T(8,128)(2,1)} %copy-done.4) | copy-start | bytes 3145732
  174.9 29.9 %collective-permute-start.16 = (bf16[256,1024]{1,0:T(8,128)(2,1)S(1)}, bf16[256,1024]{1,0:T(8,128)(2,1)S(1)}, u32[]{:S(2)}, u32[]{:S(2)}) collective-permute-start(bf16[256,1024]{1,0:T(8,128)(2,1)S(1)} %constant_dynamic-slice_fusion.3), channel_id=1, source_target_pairs={{0,1},{3,2},{4,5},{7,6},{8,9},{11,10},{12,13},{15,14},{16,17},{19,... | collective-permute-start | bytes 1572872 | tf_op jit(solution)/shard_map/ppermute | solution.py:351
  177.4 31.7 %collective-permute-start.26 = (bf16[256,1024]{1,0:T(8,128)(2,1)S(1)}, bf16[256,1024]{1,0:T(8,128)(2,1)S(1)}, u32[]{:S(2)}, u32[]{:S(2)}) collective-permute-start(bf16[256,1024]{1,0:T(8,128)(2,1)S(1)} %add_convert_fusion), channel_id=1, source_target_pairs={{1,2},{2,1},{5,6},{6,5},{9,10},{10,9},{13,14},{14,13},{17,18},{18,... | collective-permute-start | bytes 1572872 | tf_op jit(solution)/shard_map/ppermute | solution.py:351
  187.3 22.1 %collective-permute-start.23 = (bf16[256,1024]{1,0:T(8,128)(2,1)S(1)}, bf16[256,1024]{1,0:T(8,128)(2,1)S(1)}, u32[]{:S(2)}, u32[]{:S(2)}) collective-permute-start(bf16[256,1024]{1,0:T(8,128)(2,1)S(1)} %add_convert_fusion.1), channel_id=1, source_target_pairs={{1,2},{2,1},{5,6},{6,5},{9,10},{10,9},{13,14},{14,13},{17,18},{18,... | collective-permute-start | bytes 1572872 | tf_op jit(solution)/shard_map/ppermute | solution.py:351
  193.8 17.8 %collective-permute-start.20 = (bf16[256,1024]{1,0:T(8,128)(2,1)S(1)}, bf16[256,1024]{1,0:T(8,128)(2,1)S(1)}, u32[]{:S(2)}, u32[]{:S(2)}) collective-permute-start(bf16[256,1024]{1,0:T(8,128)(2,1)S(1)} %add_convert_fusion.2), channel_id=1, source_target_pairs={{1,2},{2,1},{5,6},{6,5},{9,10},{10,9},{13,14},{14,13},{17,18},{18,... | collective-permute-start | bytes 1572872 | tf_op jit(solution)/shard_map/ppermute | solution.py:351
  205.0 11.3 %collective-permute-start.17 = (bf16[256,1024]{1,0:T(8,128)(2,1)S(1)}, bf16[256,1024]{1,0:T(8,128)(2,1)S(1)}, u32[]{:S(2)}, u32[]{:S(2)}) collective-permute-start(bf16[256,1024]{1,0:T(8,128)(2,1)S(1)} %add_convert_fusion.3), channel_id=1, source_target_pairs={{1,2},{2,1},{5,6},{6,5},{9,10},{10,9},{13,14},{14,13},{17,18},{18,... | collective-permute-start | bytes 1572872 | tf_op jit(solution)/shard_map/ppermute | solution.py:351
  209.3 7.2 %collective-permute-start.27 = (bf16[128,1024]{1,0:T(8,128)(2,1)S(1)}, bf16[128,1024]{1,0:T(8,128)(2,1)S(1)}, u32[]{:S(2)}, u32[]{:S(2)}) collective-permute-start(bf16[128,1024]{1,0:T(8,128)(2,1)S(1)} %add_convert_fusion.5), channel_id=1, source_target_pairs={{0,1},{1,0},{2,3},{3,2},{4,5},{5,4},{6,7},{7,6},{8,9},{9,8},{10,11... | collective-permute-start | bytes 786440 | tf_op jit(solution)/shard_map/ppermute | solution.py:351
  209.5 9.0 %collective-permute-start.24 = (bf16[128,1024]{1,0:T(8,128)(2,1)S(1)}, bf16[128,1024]{1,0:T(8,128)(2,1)S(1)}, u32[]{:S(2)}, u32[]{:S(2)}) collective-permute-start(bf16[128,1024]{1,0:T(8,128)(2,1)S(1)} %add_convert_fusion.7), channel_id=1, source_target_pairs={{0,1},{1,0},{2,3},{3,2},{4,5},{5,4},{6,7},{7,6},{8,9},{9,8},{10,11... | collective-permute-start | bytes 786440 | tf_op jit(solution)/shard_map/ppermute | solution.py:351
  211.7 9.6 %collective-permute-start.21 = (bf16[128,1024]{1,0:T(8,128)(2,1)S(1)}, bf16[128,1024]{1,0:T(8,128)(2,1)S(1)}, u32[]{:S(2)}, u32[]{:S(2)}) collective-permute-start(bf16[128,1024]{1,0:T(8,128)(2,1)S(1)} %add_convert_fusion.9), channel_id=1, source_target_pairs={{0,1},{1,0},{2,3},{3,2},{4,5},{5,4},{6,7},{7,6},{8,9},{9,8},{10,11... | collective-permute-start | bytes 786440 | tf_op jit(solution)/shard_map/ppermute | solution.py:351
  216.4 7.7 %collective-permute-start.18 = (bf16[128,1024]{1,0:T(8,128)(2,1)S(1)}, bf16[128,1024]{1,0:T(8,128)(2,1)S(1)}, u32[]{:S(2)}, u32[]{:S(2)}) collective-permute-start(bf16[128,1024]{1,0:T(8,128)(2,1)S(1)} %add_convert_fusion.11), channel_id=1, source_target_pairs={{0,1},{1,0},{2,3},{3,2},{4,5},{5,4},{6,7},{7,6},{8,9},{9,8},{10,11... | collective-permute-start | bytes 786440 | tf_op jit(solution)/shard_map/ppermute | solution.py:351
Sparse Core Ops, SparseCore 0:
  12.3 79.4 all-gather.2
  93.3 63.2 all-gather.4

commit v3 on v2

v3 whole, which is shorter than its diff:
```python
import functools
import jax
import jax.numpy as jnp
import ml_dtypes
import numpy as np
from jax import lax
from jax.experimental import pallas as pl
from jax.experimental.pallas import tpu as pltpu
from jax.sharding import PartitionSpec as P

norm_epsilon = 1e-06
axes = ("groups", "context", "tensor")
edge = 16
f32 = jnp.float32
bf16 = jnp.bfloat16


def split_parts(matrix):
    high = matrix.astype(ml_dtypes.bfloat16)
    low = (matrix - high.astype(np.float64)).astype(ml_dtypes.bfloat16)
    return high, low


def fourier_tables(taps):
    size = 2 * taps
    freq = np.arange(taps)[:, None]
    time = np.arange(size)[None, :]
    angle = 2 * np.pi * ((freq * time) % size) / size
    cosine, sine = np.cos(angle), np.sin(angle)
    sine[0] = 1.0 - 2.0 * (np.arange(size) % 2)
    forward = np.concatenate([cosine, sine], axis=0)
    weight = np.full((2 * taps, 1), 2.0 / size)
    weight[0] = weight[taps] = 1.0 / size
    inverse = (forward * weight)[:, taps:].T
    fh, fl = split_parts(forward[:, :taps])
    ih, il = split_parts(inverse)
    return np.concatenate([fh, fl], axis=1), np.concatenate([ih, ih, il], axis=1)


def short_sum(s, taps_ref, branch, slab):
    total = None
    for lag in range(taps_ref.shape[0]):
        term = taps_ref[lag, branch][None] * s[edge - lag : edge - lag + slab]
        total = term if total is None else total + term
    return total


def norm_kernel(x_ref, gain_ref, out_ref):
    values = x_ref[...].astype(f32)
    mean = jnp.mean(values * values, axis=1, keepdims=True)
    scaled = values * lax.rsqrt(mean + norm_epsilon)
    out_ref[...] = (scaled * gain_ref[...].astype(f32)).astype(bf16)


def norm(tokens, gain):
    length, features = tokens.shape
    rows = min(length, 32)
    return pl.pallas_call(
        norm_kernel,
        grid=(length // rows,),
        in_specs=[
            pl.BlockSpec((rows, features), lambda i: (i, 0)),
            pl.BlockSpec((1, features), lambda i: (0, 0)),
        ],
        out_specs=pl.BlockSpec((rows, features), lambda i: (i, 0)),
        out_shape=jax.ShapeDtypeStruct((length, features), bf16),
        compiler_params=pltpu.CompilerParams(vmem_limit_bytes=8 << 20),
        name="norm",
    )(tokens, gain.reshape(1, features))


in_hbm = pl.BlockSpec(memory_space=pltpu.MemorySpace.HBM)
in_vmem = pl.BlockSpec(memory_space=pltpu.MemorySpace.VMEM)
in_smem = pl.BlockSpec(memory_space=pltpu.MemorySpace.SMEM)


def hold(array):
    return pltpu.with_memory_space_constraint(array, pltpu.MemorySpace.HBM)


def pack_kernel(kinds, at_ref, *rest):
    arrays = rest[: len(kinds)]
    out_ref, sems = rest[-2:]
    copies = []
    for n, ((branch, depth), array) in enumerate(zip(kinds, arrays)):
        source = array if branch is None else array.at[branch]
        rows = pl.ds(pl.multiple_of(at_ref[n], min(depth, 256)), depth)
        copies.append(pltpu.make_async_copy(source, out_ref.at[rows], sems.at[n]))
    for copy in copies:
        copy.start()
    for copy in copies:
        copy.wait()


def pack(pieces, features, base=None):
    channels = pieces[0][0].shape[-1]
    kinds = tuple((branch, array.shape[-2]) for array, branch, _ in pieces)
    at = jnp.stack([jnp.asarray(p[2], jnp.int32) for p in pieces])
    operands = [at] + [hold(p[0]) for p in pieces] + ([] if base is None else [base])
    specs = [in_smem] + [in_hbm] * len(pieces) + ([] if base is None else [in_vmem])
    return pl.pallas_call(
        functools.partial(pack_kernel, kinds),
        in_specs=specs,
        out_specs=in_vmem,
        out_shape=pltpu.VMEM((features, channels), bf16),
        scratch_shapes=[pltpu.SemaphoreType.DMA((len(pieces),))],
        input_output_aliases={} if base is None else {len(operands) - 1: 0},
        compiler_params=pltpu.CompilerParams(vmem_limit_bytes=1 << 20),
        name="pack",
    )(*operands)


def gate_kernel(width, x_ref, one_ref, two_ref, taps_ref, gated_ref, head_ref, halo_ref, full, s, sem):
    slab, channels = gated_ref.shape
    count = halo_ref.shape[0] - 2 * edge
    load = pltpu.make_async_copy(x_ref, full, sem.at[0])
    load.start()
    load.wait()
    for i in range(channels // width):
        columns = slice(i * width, (i + 1) * width)
        taps = taps_ref[:, :, columns]
        feats = []
        for k, weight in enumerate((one_ref, two_ref)):
            s[k, 0:edge] = jnp.zeros((edge, width), f32)
            term = jnp.dot(full[...], weight[:, columns], preferred_element_type=f32)
            s[k, edge : edge + slab] = term.astype(bf16).astype(f32)
            head_ref[k, :, columns] = s[k, edge : 2 * edge].astype(bf16)
            rows = slice(count + k * edge, count + (k + 1) * edge)
            halo_ref[rows, columns] = s[k, slab : slab + edge].astype(bf16)
            feats.append(short_sum(s.at[k], taps, k + 1, slab))
        gated = (feats[0] * feats[1]).astype(bf16)
        gated_ref[:, columns] = gated
        halo_ref[0:count, columns] = gated[slab - count :]


def gate(x, one, two, short_filter, taps, width):
    slab, features = x.shape
    channels = short_filter.shape[-1]
    return pl.pallas_call(
        functools.partial(gate_kernel, width),
        in_specs=[in_hbm, in_vmem, in_vmem, in_vmem],
        out_specs=[in_vmem] * 3,
        out_shape=[
            jax.ShapeDtypeStruct((slab, channels), bf16),
            jax.ShapeDtypeStruct((2, edge, channels), bf16),
            jax.ShapeDtypeStruct((taps + 2 * edge, channels), bf16),
        ],
        scratch_shapes=[
            pltpu.VMEM((slab, features), bf16),
            pltpu.VMEM((2, slab + edge, width), f32),
            pltpu.SemaphoreType.DMA((1,)),
        ],
        compiler_params=pltpu.CompilerParams(vmem_limit_bytes=16 << 20),
        name="gate",
    )(hold(x), one, two, short_filter)


def query_kernel(width, x_ref, before_ref, weight_ref, taps_ref, out_ref, full, s, sem):
    slab, channels = out_ref.shape
    loads = [
        pltpu.make_async_copy(before_ref, full.at[0:edge], sem.at[0]),
        pltpu.make_async_copy(x_ref, full.at[edge : edge + slab], sem.at[1]),
    ]
    for load in loads:
        load.start()
    for load in loads:
        load.wait()
    for i in range(channels // width):
        columns = slice(i * width, (i + 1) * width)
        term = jnp.dot(full[...], weight_ref[:, columns], preferred_element_type=f32)
        s[...] = term.astype(bf16).astype(f32)
        out_ref[:, columns] = short_sum(s, taps_ref[:, :, columns], 0, slab)


def query(x, before, weight, short_filter, width):
    slab, features = x.shape
    channels = short_filter.shape[-1]
    return pl.pallas_call(
        functools.partial(query_kernel, width),
        in_specs=[in_hbm, in_hbm, in_vmem, in_vmem],
        out_specs=in_vmem,
        out_shape=jax.ShapeDtypeStruct((slab, channels), f32),
        scratch_shapes=[
            pltpu.VMEM((slab + edge, features), bf16),
            pltpu.VMEM((slab + edge, width), f32),
            pltpu.SemaphoreType.DMA((2,)),
        ],
        compiler_params=pltpu.CompilerParams(vmem_limit_bytes=16 << 20),
        name="query",
    )(hold(x), hold(before), weight, short_filter)


def transform(fwd_ref, block):
    return jnp.dot(fwd_ref[...], jnp.concatenate([block, block], axis=0), preferred_element_type=f32)


def respond_kernel(filter_ref, decay_ref, fwd_ref, out_ref):
    taps = filter_ref.shape[0]
    lag = lax.broadcasted_iota(jnp.int32, (taps, 1), 0)
    faded = filter_ref[...] * jnp.exp(-decay_ref[...] * lag.astype(f32))
    response = transform(fwd_ref, faded.astype(bf16))
    h_cos, h_sin = response[:taps], response[taps:]
    out_ref[0] = h_cos
    out_ref[1] = jnp.where(lag == 0, 0.0, h_sin)
    out_ref[2] = jnp.where(lag == 0, h_sin, h_cos)


def respond(medium_filter, decay, forward, width):
    taps, channels = medium_filter.shape
    return pl.pallas_call(
        respond_kernel,
        grid=(channels // width,),
        in_specs=[
            pl.BlockSpec((taps, width), lambda i: (0, i)),
            pl.BlockSpec((1, width), lambda i: (0, i)),
            pl.BlockSpec(forward.shape, lambda i: (0, 0)),
        ],
        out_specs=pl.BlockSpec((3, taps, width), lambda i: (0, 0, i)),
        out_shape=jax.ShapeDtypeStruct((3, taps, channels), f32),
        compiler_params=pltpu.CompilerParams(vmem_limit_bytes=8 << 20),
        name="respond",
    )(medium_filter, decay.reshape(1, channels), forward)


def mix_kernel(
    gated_ref, halo_ref, head_ref, short_ref, response_ref, query_ref, fwd_ref, inv_ref, out_ref, s
):
    taps = response_ref.shape[1]
    blocks = gated_ref.shape[0] // taps
    feats = []
    for k in range(2):
        s[0:edge] = halo_ref[taps + k * edge : taps + (k + 1) * edge].astype(f32)
        s[edge : 2 * edge] = head_ref[k].astype(f32)
        total = None
        for lag in range(short_ref.shape[0]):
            term = short_ref[lag, k + 1][None] * s[edge - lag : 2 * edge - lag]
            total = term if total is None else total + term
        feats.append(total)
    first = (feats[0] * feats[1]).astype(bf16)

    row = lax.broadcasted_iota(jnp.int32, (2 * taps, 1), 0)
    sign = jnp.where(row % 2 == 0, 1.0, -1.0).astype(f32)
    h_cos, h_sin, h_low = response_ref[0], response_ref[1], response_ref[2]
    last = transform(fwd_ref, halo_ref[0:taps])
    for b in range(blocks):
        if b == 0:
            block = jnp.concatenate([first, gated_ref[edge:taps]], axis=0)
        else:
            block = gated_ref[b * taps : (b + 1) * taps]
        now = transform(fwd_ref, block)
        x = last + sign * now
        last = now
        x_cos, x_sin = x[:taps], x[taps:]
        y = jnp.concatenate([x_cos * h_cos - x_sin * h_sin, x_sin * h_low + x_cos * h_sin], axis=0)
        high = y.astype(bf16)
        low = (y - high.astype(f32)).astype(bf16)
        mixed = jnp.dot(
            inv_ref[...], jnp.concatenate([high, low, high], axis=0), preferred_element_type=f32
        )
        at = slice(b * taps, (b + 1) * taps)
        out_ref[at] = (query_ref[at] * mixed).astype(bf16)


def mix(gated, halo, head, short_filter, response, query_rows, tables, width):
    slab, channels = gated.shape
    count = response.shape[1]
    forward, inverse = tables
    col = lambda rows: pl.BlockSpec((rows, width), lambda i: (0, i))
    cube = lambda a, b: pl.BlockSpec((a, b, width), lambda i: (0, 0, i))
    return pl.pallas_call(
        mix_kernel,
        grid=(channels // width,),
        in_specs=[
            col(slab),
            col(count + 2 * edge),
            cube(2, edge),
            cube(*short_filter.shape[:2]),
            cube(3, count),
            col(slab),
            pl.BlockSpec(forward.shape, lambda i: (0, 0)),
            pl.BlockSpec(inverse.shape, lambda i: (0, 0)),
        ],
        out_specs=col(slab),
        out_shape=jax.ShapeDtypeStruct((slab, channels), bf16),
        scratch_shapes=[pltpu.VMEM((2 * edge, width), f32)],
        compiler_params=pltpu.CompilerParams(vmem_limit_bytes=16 << 20),
        name="mix",
    )(gated, halo, head, short_filter, response, query_rows, forward, inverse)


def local(tokens, norm_gain, w_in, short_filter, medium_filter, decay, w_out):
    groups, contexts, count = (lax.axis_size(a) for a in axes)
    g, c, z = (lax.axis_index(a) for a in axes)
    length, features = tokens.shape
    rows, branches, channels = w_in.shape
    slab = length * count
    width = min(channels, 256)
    paired = contexts == 4 and groups == 2

    def move(value, target):
        pairs = []
        for i in range(groups):
            for j in range(contexts):
                for k in range(count):
                    to = target(i, j, k)
                    if 0 <= to[1] < contexts and 0 <= to[2] < count:
                        pairs.append(
                            ((i * contexts + j) * count + k, (to[0] * contexts + to[1]) * count + to[2])
                        )
        return lax.ppermute(value, axes, pairs)

    to_chip = lambda v: move(v, lambda i, j, k: (i, j ^ 2, k))
    to_core = lambda v: move(v, lambda i, j, k: (i, j ^ 1, k))
    to_group = lambda v: move(v, lambda i, j, k: (1 - i, j, k))
    to_next = lambda v: move(v, lambda i, j, k: (i, j + 1, k))
    send = lambda v, pairs: move(v, lambda i, j, k: (i, j, pairs.get(k, -1)))
    to_up = lambda v: move(v, lambda i, j, k: (i, j, k + 1))
    to_down = lambda v: move(v, lambda i, j, k: (i, j, k - 1))

    def after(value, *earlier):
        return lax.optimization_barrier((value, *earlier))[0]

    def spread_last(value):
        value = move(
            value, lambda i, j, k: (i, j + 1, k) if k == count - 1 else (i, -1, k)
        )
        held = 1
        while held < count:
            first, last = max(0, count - 2 * held), count - held
            value = value + move(
                value,
                lambda i, j, k: (i, j, k - held) if k - held >= first and k >= last else (i, j, -1),
            )
            held += last - first
        return value

    medium_count = medium_filter.shape[0]
    tables = fourier_tables(medium_count)
    weights = jnp.transpose(w_in, (1, 0, 2))
    half = rows // 2
    out_rows = w_out.shape[0]
    out_half = out_rows // 2
    if paired:
        first_half, other_half = g * half, (1 - g) * half
        peer = to_core(weights)
        near, far, packed = {}, {}, {}
        order = (1, 2, 0)
        for n, b in enumerate(order):
            source = after(weights, normed) if n else weights
            mine = lax.dynamic_slice(source, (b, first_half, 0), (1, half, channels))
            mine = mine.reshape(half, channels)
            if n == 0:
                normed = norm(after(tokens, mine), norm_gain)
                response = respond(medium_filter, decay, tables[0], width)
                before_rows = spread_last(normed[length - edge :])
            else:
                mine = after(mine, near[order[n - 1]])
            near[b] = to_chip(mine)
            if n == 0:
                ready = near[b]
            elif n == 1:
                ready = after(near[b], far[1], response, before_rows)
            else:
                ready = after(near[b], far[2], packed[1])
            far[b] = to_group(ready)
            packed[b] = pack(
                [
                    (weights, b, c * rows),
                    (peer, b, (c ^ 1) * rows),
                    (near[b], None, (c ^ 2) * rows + first_half),
                    (to_core(near[b]), None, (c ^ 3) * rows + first_half),
                ],
                features,
            )
            if b == 1:
                packed[b] = pack(
                    [
                        (far[b], None, (c ^ 2) * rows + other_half),
                        (to_core(far[b]), None, (c ^ 3) * rows + other_half),
                    ],
                    features,
                    packed[b],
                )
        far_two = after(far[2], packed[2])
        packed[2] = pack(
            [
                (far_two, None, (c ^ 2) * rows + other_half),
                (to_core(far_two), None, (c ^ 3) * rows + other_half),
            ],
            features,
            packed[2],
        )
    else:
        normed = norm(tokens, norm_gain)
        response = respond(medium_filter, decay, tables[0], width)
        before_rows = spread_last(normed[length - edge :])
        full = lax.all_gather(weights, "context", axis=1, tiled=True)
        packed = {b: pack([(full, b, 0)], features) for b in range(branches)}

    gathered = lax.all_gather(normed, "tensor", axis=0, tiled=True)
    if paired:
        gate_taps = after(short_filter, response, packed[0])
    else:
        gate_taps = short_filter
    gated, head, edges = gate(gathered, packed[1], packed[2], gate_taps, medium_count, width)
    halo = to_next(edges)
    if paired:
        far_zero = after(far[0], gated)
        packed[0] = pack(
            [
                (far_zero, None, (c ^ 2) * rows + other_half),
                (to_core(far_zero), None, (c ^ 3) * rows + other_half),
            ],
            features,
            packed[0],
        )
    query_rows = query(gathered, before_rows, packed[0], short_filter, width)
    combined = mix(gated, halo, head, short_filter, response, query_rows, tables, width)
    if paired:
        mine = lax.dynamic_slice(w_out, (g * out_half, 0), (out_half, channels))
        chips = [[0, 2], [1, 3]]
        pair = lax.all_gather(
            after(mine, near[1]), "context", axis=0, tiled=True, axis_index_groups=chips
        )
        pair = after(pair, query_rows)
        near_out = lax.dynamic_slice(pair, ((1 - c // 2) * out_half, 0), (out_half, channels))
        far_out = to_group(near_out)
        out_peer = to_core(after(w_out, gated))
        near_core = to_core(near_out)

        def last_parts(earlier):
            late = after(far_out, earlier[1])
            return [late, to_core(late)]

        sets = [
            lambda _: [w_out],
            lambda _: [out_peer],
            lambda _: [near_out, near_core],
            last_parts,
        ]
    else:
        sets = [lambda _: [lax.all_gather(w_out, "context", axis=0, tiled=True)]]

    def plus(*terms):
        total = terms[0].astype(f32)
        for term in terms[1:]:
            total = total + term.astype(f32)
        return total.astype(bf16)

    results, partial, firsts, pending = [], [], [], []
    for make in sets:
        parts = make(firsts)
        partial = [
            lax.dot_general(
                combined, part, (((1,), (1,)), ((), ())), preferred_element_type=f32
            ).astype(bf16)
            for part in parts
        ]
        combined = after(combined, *partial)

        def block(index, blocks=1, partial=partial):
            index = jnp.clip(index, 0, count - blocks)
            return jnp.concatenate(
                [
                    lax.dynamic_slice(p, (index * length, 0), (blocks * length, p.shape[1]))
                    for p in partial
                ],
                1,
            )

        if count == 4:
            far_pair = block(jnp.where(z < 2, 2, 0), 2)
            firsts.append(send(far_pair, {0: 1, 3: 2}))
            pending.append((far_pair, block(z), block(z ^ 1), partial[0]))
        else:
            up = down = None
            for s in range(1, count):
                rising = block(count + z - s)
                falling = block(z - count + s)
                if up is not None:
                    rising, falling = plus(rising, up), plus(falling, down)
                up, down = to_up(rising), to_down(falling)
            results.append(plus(block(z), up, down))
    for n, (far_pair, own, other, _) in enumerate(pending):
        got = plus(far_pair, firsts[n])
        if n + 1 < len(pending) - 1:
            got = after(got, pending[n + 1][3])
        got = send(got, {1: 2, 2: 1})
        low, high = got[:length], got[length:]
        odd = z % 2 == 1
        got_own = jnp.where(odd, high, low)
        got_other = jnp.where(odd, low, high)
        last = send(plus(other, got_other), {0: 1, 1: 0, 2: 3, 3: 2})
        results.append(plus(own, got_own, last))
    if not paired:
        return results[0]
    swap = lambda test, a, b: (jnp.where(test, b, a), jnp.where(test, a, b))
    e0, e1, e2, e3 = results
    e2, e3 = (
        jnp.concatenate(swap(g == 1, e2[:, at], e3[:, at]), 1)
        for at in (slice(0, out_half), slice(out_half, None))
    )
    odd = c % 2 == 1
    low = jnp.concatenate(swap(odd, e0, e1), 1)
    high = jnp.concatenate(swap(odd, e2, e3), 1)
    return jnp.concatenate(swap(c >= 2, low, high), 1)


def solution(mesh):
    in_specs = (
        P(axes, None),
        P(),
        P("context", None, "tensor"),
        P(None, None, "tensor"),
        P(None, "tensor"),
        P("tensor"),
        P("context", "tensor"),
    )
    return jax.shard_map(
        local, mesh=mesh, in_specs=in_specs, out_specs=P(axes, None), check_vma=False
    )
```

time: 233 us -> 313 us (1.34)
  the two profiles are of different devices: /device:TPU:10 before, /device:TPU:0 now
where the time goes in v3:
time: 313 us; the launch traced here: 312 us
  waiting for transfers between devices  120 us (38%)
  starting transfers between devices  57 us (18%)
  local copies, waits for them, and re-layouts  56.5 us (18%)
  Pallas kernels  42.9 us (14%)
  between operations  14.1 us (5%)
  matrix products  13.2 us (4%)
  other arithmetic  8.35 us (3%)
    ppermute x33, waiting for transfers between devices, move(): return lax.ppermute(value, axes, pairs)  120 us
    ppermute x33, starting transfers between devices, move(): return lax.ppermute(value, axes, pairs)  57 us
    unnamed x64, local copies, waits for them, and re-layouts  43.3 us
    pallas_call x6, Pallas kernels, pack(): pl.pallas_call(functools.partial(pack_kernel, kinds), in_specs=specs, out...  16.7 us
    dot_general x6, matrix products, local(): lax.dot_general(combined, part, (((1,), (1,)), ((), ())), preferred_eleme...  13.2 us
    pallas_call x1, Pallas kernels, gate(): pl.pallas_call(functools.partial(gate_kernel, width), in_specs=[in_hbm, i...  11.4 us
    pallas_call x1, Pallas kernels, query(): pl.pallas_call(functools.partial(query_kernel, width), in_specs=[in_hbm,...  7.29 us
  transfers between devices with their start and end apart: 35, of which 10 were waited for; matrix products, arithmetic and copies ran while one was open for 11% of the time, Pallas kernels for 14%

profile of v3, /device:TPU:0, one launch (start us, length us, event | category | flops | bytes accessed | tf_op | source)
XLA Modules:
  0.0 311.8 jit_solution(9444798034642379166)
XLA Ops:
  7.0 1.3 dynamic-slice_bitcast_fusion.2
  8.3 2.0 norm.1
  10.4 2.7 collective-permute-start
  13.1 2.7 dynamic-slice_bitcast_fusion
  15.8 21.0 %collective-permute-done.rest_2_ = bf16[512,1024]{1,0:T(8,128)(2,1)S(1)} collective-permute-done((bf16[512,1024]{1,0:T(8,128)(2,1)S(1)}, bf16[512,1024]{1,0:T(8,128)(2,1)S(1)}, u32[]{:S(2)}, u32[]{:S(2)}) %collective-permute-start) | collective-permute-done | bytes 1048608 | tf_op jit(solution)/shard_map/ppermute | solution.py:310
  36.8 1.7 collective-permute-start.5
  38.5 1.5 collective-permute-start.1
  40.0 21.9 %collective-permute-done.5.rest_2_ = bf16[512,1024]{1,0:T(8,128)(2,1)} collective-permute-done((bf16[512,1024]{1,0:T(8,128)(2,1)S(1)}, bf16[512,1024]{1,0:T(8,128)(2,1)}, u32[]{:S(2)}, u32[]{:S(2)}) %collective-permute-start.5) | collective-permute-done | bytes 1048608 | tf_op jit(solution)/shard_map/ppermute | solution.py:310
  64.2 1.3 collective-permute-start.8
  65.6 1.1 respond.1.response_ref
  66.6 1.2 copy-done.10
  67.8 26.0 %collective-permute-done.8 = bf16[16,4096]{1,0:T(8,128)(2,1)S(1)} collective-permute-done((bf16[16,4096]{1,0:T(8,128)(2,1)S(1)}, bf16[16,4096]{1,0:T(8,128)(2,1)S(1)}, u32[]{:S(2)}, u32[]{:S(2)}) %collective-permute-start.8) | collective-permute-done | bytes 131104 | tf_op jit(solution)/shard_map/ppermute | solution.py:310
  94.5 1.2 collective-permute-start.12
  95.7 1.5 collective-permute-start.9
  97.8 22.2 %collective-permute-done.12.rest_2_ = bf16[512,1024]{1,0:T(8,128)(2,1)S(1)} collective-permute-done((bf16[512,1024]{1,0:T(8,128)(2,1)}, bf16[512,1024]{1,0:T(8,128)(2,1)S(1)}, u32[]{:S(2)}, u32[]{:S(2)}) %collective-permute-start.12) | collective-permute-done | bytes 1048608 | tf_op jit(solution)/shard_map/ppermute | solution.py:310
  120.0 3.4 %pack.8.rest_2_ = bf16[4096,1024]{1,0:T(8,128)(2,1)S(1)} custom-call(s32[4]{0:T(128)S(1)} %pad_add_fusion.1.at_ref, bf16[3,1024,1024]{2,1,0:T(8,128)(2,1)} %bitcast.29, bf16[3,1024,1024]{2,1,0:T(8,128)(2,1)} %collective-permute-done.3.rest_1_, bf16[512,1024]{1,0:T(8,128)(2,1)} %collective-permute-done.5.rest_2_, ...), custom_call_target="tpu_custom_call" | custom-call | tf_op jit(solution)/shard_map/pack/pallas_call | solution.py:101
  123.4 3.3 %copy-done.4 = bf16[4096,1024]{1,0:T(8,128)(2,1)} copy-done((bf16[4096,1024]{1,0:T(8,128)(2,1)}, bf16[4096,1024]{1,0:T(8,128)(2,1)S(1)}, u32[]{:S(2)}) %copy-start.4) | copy-done | bytes 8388632
  127.3 3.4 %pack.6.rest_2_ = bf16[4096,1024]{1,0:T(8,128)(2,1)S(1)} custom-call(s32[4]{0:T(128)S(1)} %pad_add_fusion.1.at_ref, bf16[3,1024,1024]{2,1,0:T(8,128)(2,1)} %bitcast.30, bf16[3,1024,1024]{2,1,0:T(8,128)(2,1)} %collective-permute-done.3.rest_1_, bf16[512,1024]{1,0:T(8,128)(2,1)} %copy-done.26, bf16[512,1024]{1,0:T(8,128)(2,1)} %collective-permute-done.4.rest_3_), custom_call_target="tpu_custom_call" | custom-call | tf_op jit(solution)/shard_map/pack/pallas_call | solution.py:101
  130.8 2.1 pack.7.one_ref
  132.9 3.3 %copy-done.8 = bf16[4096,1024]{1,0:T(8,128)(2,1)} copy-done((bf16[4096,1024]{1,0:T(8,128)(2,1)}, bf16[4096,1024]{1,0:T(8,128)(2,1)S(1)}, u32[]{:S(2)}) %copy-start.8) | copy-done | bytes 8388632
  136.2 1.5 collective-permute-start.15
  137.7 2.3 constant_dynamic-slice_fusion.15
  139.9 3.6 %pack.10.rest_2_ = bf16[4096,1024]{1,0:T(8,128)(2,1)S(1)} custom-call(s32[4]{0:T(128)S(1)} %pad_add_fusion.1.at_ref, bf16[3,1024,1024]{2,1,0:T(8,128)(2,1)} %bitcast.31, bf16[3,1024,1024]{2,1,0:T(8,128)(2,1)} %collective-permute-done.3.rest_1_, bf16[512,1024]{1,0:T(8,128)(2,1)} %copy-done.27, bf16[512,1024]{1,0:T(8,128)(2,1)} %collective-permute-done.13.rest_3_), custom_call_target="tpu_custom_call" | custom-call | tf_op jit(solution)/shard_map/pack/pallas_call | solution.py:101
  143.6 3.3 %copy-done = bf16[4096,1024]{1,0:T(8,128)(2,1)} copy-done((bf16[4096,1024]{1,0:T(8,128)(2,1)}, bf16[4096,1024]{1,0:T(8,128)(2,1)S(1)}, u32[]{:S(2)}) %copy-start) | copy-done | bytes 8388632
  146.9 3.4 %copy-done.5 = bf16[4096,1024]{1,0:T(8,128)(2,1)S(1)} copy-done((bf16[4096,1024]{1,0:T(8,128)(2,1)S(1)}, bf16[4096,1024]{1,0:T(8,128)(2,1)}, u32[]{:S(2)}) %copy-start.5) | copy-done | bytes 8388632
  150.3 2.1 pack.9.two_ref
  152.4 3.3 %copy-done.6 = bf16[4096,1024]{1,0:T(8,128)(2,1)} copy-done((bf16[4096,1024]{1,0:T(8,128)(2,1)}, bf16[4096,1024]{1,0:T(8,128)(2,1)S(1)}, u32[]{:S(2)}) %copy-start.6) | copy-done | bytes 8388632
  155.8 3.4 %copy-done.7 = bf16[4096,1024]{1,0:T(8,128)(2,1)S(1)} copy-done((bf16[4096,1024]{1,0:T(8,128)(2,1)S(1)}, bf16[4096,1024]{1,0:T(8,128)(2,1)}, u32[]{:S(2)}) %copy-start.7) | copy-done | bytes 8388632
  159.2 3.4 %copy-done.9 = bf16[4096,1024]{1,0:T(8,128)(2,1)S(1)} copy-done((bf16[4096,1024]{1,0:T(8,128)(2,1)S(1)}, bf16[4096,1024]{1,0:T(8,128)(2,1)}, u32[]{:S(2)}) %copy-start.9) | copy-done | bytes 8388632
  162.5 11.4 %gate.1 = (bf16[512,1024]{1,0:T(8,128)(2,1)S(1)}, bf16[2,16,1024]{2,1,0:T(8,128)(2,1)S(1)}, bf16[160,1024]{1,0:T(8,128)(2,1)S(1)}) custom-call(bf16[512,4096]{1,0:T(8,128)(2,1)} %all-gather.3.cloned.1.call-done.x_ref, bf16[4096,1024]{1,0:T(8,128)(2,1)S(1)} %copy-done.9, bf16[4096,1024]{1,0:T(8,128)(2,1)S(1)} %copy-done.7, f32[3,3,1024]{2,1,0:T(4,128)S(1)} %copy-done.17), custom_call_target="tpu_custom_call" | custom-call | tf_op jit(solution)/shard_map/gate/pallas_call | solution.py:139
  176.0 2.1 collective-permute-start.14
  178.2 3.3 %collective-permute-done.16.rest_1_ = bf16[512,1024]{1,0:T(8,128)(2,1)S(1)} collective-permute-done((bf16[512,1024]{1,0:T(8,128)(2,1)}, bf16[512,1024]{1,0:T(8,128)(2,1)S(1)}, u32[]{:S(2)}, u32[]{:S(2)}) %collective-permute-start.16) | collective-permute-done | bytes 1048608 | tf_op jit(solution)/shard_map/ppermute | solution.py:310
  181.5 1.0 copy-done.28
  182.5 3.4 %copy-done.1 = bf16[4096,1024]{1,0:T(8,128)(2,1)S(1)} copy-done((bf16[4096,1024]{1,0:T(8,128)(2,1)S(1)}, bf16[4096,1024]{1,0:T(8,128)(2,1)}, u32[]{:S(2)}) %copy-start.1) | copy-done | bytes 8388632
  185.8 2.1 pack.11.weight_ref
  188.0 3.3 %copy-done.2 = bf16[4096,1024]{1,0:T(8,128)(2,1)} copy-done((bf16[4096,1024]{1,0:T(8,128)(2,1)}, bf16[4096,1024]{1,0:T(8,128)(2,1)S(1)}, u32[]{:S(2)}) %copy-start.2) | copy-done | bytes 8388632
  191.3 3.4 %copy-done.3 = bf16[4096,1024]{1,0:T(8,128)(2,1)S(1)} copy-done((bf16[4096,1024]{1,0:T(8,128)(2,1)S(1)}, bf16[4096,1024]{1,0:T(8,128)(2,1)}, u32[]{:S(2)}) %copy-start.3) | copy-done | bytes 8388632
  194.7 7.3 %query.1.query_ref = f32[512,1024]{1,0:T(8,128)S(1)} custom-call(bf16[512,4096]{1,0:T(8,128)(2,1)} %all-gather.3.cloned.1.call-done.x_ref, bf16[16,4096]{1,0:T(8,128)(2,1)} %add.125.before_ref, bf16[4096,1024]{1,0:T(8,128)(2,1)S(1)} %copy-done.3, f32[3,3,1024]{2,1,0:T(4,128)S(1)} %copy-done.17), custom_call_target="tpu_custom_call" | custom-call | tf_op jit(solution)/shard_map/query/pallas_call | solution.py:178
  202.0 2.3 constant_dynamic-slice_fusion.14
  206.1 1.4 copy-done.11
  207.5 1.2 copy-done.13
  208.8 1.0 copy-done.19
  210.6 4.5 %mix.1 = bf16[512,1024]{1,0:T(8,128)(2,1)S(1)} custom-call(bf16[512,1024]{1,0:T(8,128)(2,1)S(1)} %copy-done.13, bf16[160,1024]{1,0:T(8,128)(2,1)S(1)} %copy-done.19, bf16[2,16,1024]{2,1,0:T(8,128)(2,1)S(1)} %copy-done.22, f32[3,3,1024]{2,1,0:T(4,128)S(1)} %copy-done.17, f32[3,128,1024]{2,1,0:T(8,128)S(1)} %copy-done.11, f32[512,1024]{1,0:T(8,128)S(1)} %query.1.query_ref, ...), custom_call_target="tpu_custom_call" | custom-call | tf_op jit(solution)/shard_map/mix/pallas_call | solution.py:270
  215.1 2.9 convolution_convert_fusion.1
  218.8 2.1 collective-permute-start.30
  220.9 2.9 convolution_convert_fusion
  224.6 2.1 collective-permute-start.20
  226.7 2.8 convolution_convert_fusion.4
  230.5 2.0 convolution_convert_fusion.5
  234.2 2.1 collective-permute-start.25
  236.3 1.3 add_convert_fusion
  238.3 5.6 %collective-permute-done.20 = bf16[256,1024]{1,0:T(8,128)(2,1)} collective-permute-done((bf16[256,1024]{1,0:T(8,128)(2,1)}, bf16[256,1024]{1,0:T(8,128)(2,1)}, u32[]{:S(2)}, u32[]{:S(2)}) %collective-permute-start.20) | collective-permute-done | bytes 524320 | tf_op jit(solution)/shard_map/ppermute | solution.py:310
  243.9 1.0 constant_dynamic-slice_fusion.5
  244.9 9.4 %collective-permute-done.25 = bf16[256,1024]{1,0:T(8,128)(2,1)} collective-permute-done((bf16[256,1024]{1,0:T(8,128)(2,1)}, bf16[256,1024]{1,0:T(8,128)(2,1)}, u32[]{:S(2)}, u32[]{:S(2)}) %collective-permute-start.25) | collective-permute-done | bytes 524320 | tf_op jit(solution)/shard_map/ppermute | solution.py:310
  254.3 1.2 add_convert_fusion.2
  256.3 1.2 add_convert_fusion.1
  258.2 2.0 convolution_convert_fusion.3
  261.1 8.9 %collective-permute-start.22 = (bf16[256,1024]{1,0:T(8,128)(2,1)S(1)}, bf16[256,1024]{1,0:T(8,128)(2,1)S(1)}, u32[]{:S(2)}, u32[]{:S(2)}) collective-permute-start(bf16[256,1024]{1,0:T(8,128)(2,1)S(1)} %pad_maximum_fusion.1), channel_id=1, source_target_pairs={{0,1},{3,2},{4,5},{7,6},{8,9},{11,10},{12,13},{15,14},{16,17},{19,... | collective-permute-start | bytes 1572872 | tf_op jit(solution)/shard_map/ppermute | solution.py:310
  270.3 14.1 %collective-permute-start.29 = (bf16[128,1024]{1,0:T(8,128)(2,1)S(1)}, bf16[128,1024]{1,0:T(8,128)(2,1)S(1)}, u32[]{:S(2)}, u32[]{:S(2)}) collective-permute-start(bf16[128,1024]{1,0:T(8,128)(2,1)S(1)} %add_convert_fusion.7), channel_id=1, source_target_pairs={{0,1},{1,0},{2,3},{3,2},{4,5},{5,4},{6,7},{7,6},{8,9},{9,8},{10,11... | collective-permute-start | bytes 786440 | tf_op jit(solution)/shard_map/ppermute | solution.py:310
  285.5 2.0 collective-permute-start.27
  287.9 5.6 %collective-permute-done.29 = bf16[128,1024]{1,0:T(8,128)(2,1)S(1)} collective-permute-done((bf16[128,1024]{1,0:T(8,128)(2,1)S(1)}, bf16[128,1024]{1,0:T(8,128)(2,1)S(1)}, u32[]{:S(2)}, u32[]{:S(2)}) %collective-permute-start.29) | collective-permute-done | bytes 262176 | tf_op jit(solution)/shard_map/ppermute | solution.py:310
  294.1 4.9 %collective-permute-start.24 = (bf16[128,1024]{1,0:T(8,128)(2,1)S(1)}, bf16[128,1024]{1,0:T(8,128)(2,1)S(1)}, u32[]{:S(2)}, u32[]{:S(2)}) collective-permute-start(bf16[128,1024]{1,0:T(8,128)(2,1)S(1)} %add_convert_fusion.11), channel_id=1, source_target_pairs={{0,1},{1,0},{2,3},{3,2},{4,5},{5,4},{6,7},{7,6},{8,9},{9,8},{10,11... | collective-permute-start | bytes 786440 | tf_op jit(solution)/shard_map/ppermute | solution.py:310
  299.2 4.1 %collective-permute-done.24 = bf16[128,1024]{1,0:T(8,128)(2,1)S(1)} collective-permute-done((bf16[128,1024]{1,0:T(8,128)(2,1)S(1)}, bf16[128,1024]{1,0:T(8,128)(2,1)S(1)}, u32[]{:S(2)}, u32[]{:S(2)}) %collective-permute-start.24) | collective-permute-done | bytes 262176 | tf_op jit(solution)/shard_map/ppermute | solution.py:310
  303.9 1.1 pad_maximum_fusion
  (127 shorter events, 19.8 us)
Async XLA Ops:
  6.5 1.8 copy-start.14
  6.5 1.8 copy-start.31
  6.5 149.2 %all-gather.3.cloned.1.call-start = ((), (), s32[]{:S(2)}) async-start(), calls=%async_computation | async-start | bytes 5242880 | tf_op jit(solution)/shard_map/all_gather | solution.py:400
  6.5 113.5 %collective-permute-start.3 = (bf16[3,1024,1024]{2,1,0:T(8,128)(2,1)}, bf16[3,1024,1024]{2,1,0:T(8,128)(2,1)}, u32[]{:S(2)}, u32[]{:S(2)}) collective-permute-start(bf16[3,1024,1024]{2,1,0:T(8,128)(2,1)} %bitcast.27), channel_id=1, source_target_pairs={{0,4},{1,5},{2,6},{3,7},{4,0},{5,1},{6,2},{7,3},{8,12},{9,13},{10,... | collective-permute-start | bytes 18874376 | tf_op jit(solution)/shard_map/ppermute | solution.py:310
  10.3 55.2 %copy-start.15 = (f32[128,1024]{1,0:T(8,128)S(1)}, f32[128,1024]{1,0:T(8,128)}, u32[]{:S(2)}) copy-start(f32[128,1024]{1,0:T(8,128)} %filter_ref.1) | copy-start | bytes 1572868
  10.3 55.2 %copy-start.16 = (bf16[256,256]{1,0:T(8,128)(2,1)S(1)}, bf16[256,256]{1,0:T(8,128)(2,1)}, u32[]{:S(2)}) copy-start(bf16[256,256]{1,0:T(8,128)(2,1)} %constant.61.clone.fwd_ref) | copy-start | bytes 393220
  10.3 55.2 %copy-start.23 = (f32[1024]{0:T(1024)S(1)}, f32[1024]{0:T(1024)}, u32[]{:S(2)}) copy-start(f32[1024]{0:T(1024)} %param.14) | copy-start | bytes 12292
  10.3 191.7 %all-gather.5.cloned.1.call-start = ((), (), s32[]{:S(2)}) async-start(), calls=%async_computation.1 | async-start | bytes 3145728 | tf_op jit(solution)/shard_map/all_gather | solution.py:422
  10.4 26.4 %collective-permute-start = (bf16[512,1024]{1,0:T(8,128)(2,1)S(1)}, bf16[512,1024]{1,0:T(8,128)(2,1)S(1)}, u32[]{:S(2)}, u32[]{:S(2)}) collective-permute-start(bf16[512,1024]{1,0:T(8,128)(2,1)S(1)} %dynamic-slice_bitcast_fusion.2), channel_id=1, source_target_pairs={{0,8},{1,9},{2,10},{3,11},{4,12},{5,13},{6,14},{7,15},{8,0},{9,1},... | collective-permute-start | bytes 3145736 | tf_op jit(solution)/shard_map/ppermute | solution.py:310
  36.8 86.6 %copy-start.26 = (bf16[512,1024]{1,0:T(8,128)(2,1)}, bf16[512,1024]{1,0:T(8,128)(2,1)S(1)}, u32[]{:S(2)}) copy-start(bf16[512,1024]{1,0:T(8,128)(2,1)S(1)} %collective-permute-done.rest_2_) | copy-start | bytes 3145732
  36.8 25.1 %collective-permute-start.5 = (bf16[512,1024]{1,0:T(8,128)(2,1)S(1)}, bf16[512,1024]{1,0:T(8,128)(2,1)}, u32[]{:S(2)}, u32[]{:S(2)}) collective-permute-start(bf16[512,1024]{1,0:T(8,128)(2,1)S(1)} %get-tuple-element.28), channel_id=1, source_target_pairs={{0,8},{1,9},{2,10},{3,11},{4,12},{5,13},{6,14},{7,15},{8,0},{9,1},... | collective-permute-start | bytes 3145736 | tf_op jit(solution)/shard_map/ppermute | solution.py:310
  38.5 57.2 %collective-permute-start.1 = (bf16[512,1024]{1,0:T(8,128)(2,1)S(1)}, bf16[512,1024]{1,0:T(8,128)(2,1)}, u32[]{:S(2)}, u32[]{:S(2)}) collective-permute-start(bf16[512,1024]{1,0:T(8,128)(2,1)S(1)} %collective-permute-done.rest_2_), channel_id=1, source_target_pairs={{0,16},{1,17},{2,18},{3,19},{4,20},{5,21},{6,22},{7,23},{8,24},{9,... | collective-permute-start | bytes 3145736 | tf_op jit(solution)/shard_map/ppermute | solution.py:310
  61.9 35.3 %collective-permute-start.10 = (bf16[512,1024]{1,0:T(8,128)(2,1)}, bf16[512,1024]{1,0:T(8,128)(2,1)}, u32[]{:S(2)}, u32[]{:S(2)}) collective-permute-start(bf16[512,1024]{1,0:T(8,128)(2,1)} %collective-permute-done.5.rest_2_), channel_id=1, source_target_pairs={{0,4},{1,5},{2,6},{3,7},{4,0},{5,1},{6,2},{7,3},{8,12},{9,13},{10,... | collective-permute-start | bytes 3145736 | tf_op jit(solution)/shard_map/ppermute | solution.py:310
  62.8 0.7 collective-permute-start.6
  63.5 0.7 collective-permute-start.7
  64.2 29.6 %collective-permute-start.8 = (bf16[16,4096]{1,0:T(8,128)(2,1)S(1)}, bf16[16,4096]{1,0:T(8,128)(2,1)S(1)}, u32[]{:S(2)}, u32[]{:S(2)}) collective-permute-start(bf16[16,4096]{1,0:T(8,128)(2,1)S(1)} %add.124), channel_id=1, source_target_pairs={{2,0},{3,1},{6,4},{7,5},{10,8},{11,9},{14,12},{15,13},{18,16},{19,... | collective-permute-start | bytes 393224 | tf_op jit(solution)/shard_map/ppermute | solution.py:310
  66.6 1.2 copy-start.10
  94.5 25.5 %collective-permute-start.12 = (bf16[512,1024]{1,0:T(8,128)(2,1)}, bf16[512,1024]{1,0:T(8,128)(2,1)S(1)}, u32[]{:S(2)}, u32[]{:S(2)}) collective-permute-start(bf16[512,1024]{1,0:T(8,128)(2,1)} %get-tuple-element.31), channel_id=1, source_target_pairs={{0,8},{1,9},{2,10},{3,11},{4,12},{5,13},{6,14},{7,15},{8,0},{9,1},... | collective-permute-start | bytes 3145736 | tf_op jit(solution)/shard_map/ppermute | solution.py:310
  95.7 31.1 %collective-permute-start.9 = (bf16[512,1024]{1,0:T(8,128)(2,1)}, bf16[512,1024]{1,0:T(8,128)(2,1)}, u32[]{:S(2)}, u32[]{:S(2)}) collective-permute-start(bf16[512,1024]{1,0:T(8,128)(2,1)} %collective-permute-done.5.rest_2_), channel_id=1, source_target_pairs={{0,16},{1,17},{2,18},{3,19},{4,20},{5,21},{6,22},{7,23},{8,24},{9,... | collective-permute-start | bytes 3145736 | tf_op jit(solution)/shard_map/ppermute | solution.py:310
  97.2 30.1 %collective-permute-start.4 = (bf16[512,1024]{1,0:T(8,128)(2,1)S(1)}, bf16[512,1024]{1,0:T(8,128)(2,1)}, u32[]{:S(2)}, u32[]{:S(2)}) collective-permute-start(bf16[512,1024]{1,0:T(8,128)(2,1)S(1)} %collective-permute-done.rest_2_), channel_id=1, source_target_pairs={{0,4},{1,5},{2,6},{3,7},{4,0},{5,1},{6,2},{7,3},{8,12},{9,13},{10,... | collective-permute-start | bytes 3145736 | tf_op jit(solution)/shard_map/ppermute | solution.py:310
  97.2 33.6 %collective-permute-start.2 = (bf16[512,1024]{1,0:T(8,128)(2,1)}, bf16[512,1024]{1,0:T(8,128)(2,1)}, u32[]{:S(2)}, u32[]{:S(2)}) collective-permute-start(bf16[512,1024]{1,0:T(8,128)(2,1)} %collective-permute-done.1.rest_0_), channel_id=1, source_target_pairs={{0,4},{1,5},{2,6},{3,7},{4,0},{5,1},{6,2},{7,3},{8,12},{9,13},{10,... | collective-permute-start | bytes 3145736 | tf_op jit(solution)/shard_map/ppermute | solution.py:310
  120.0 12.9 %copy-start.27 = (bf16[512,1024]{1,0:T(8,128)(2,1)}, bf16[512,1024]{1,0:T(8,128)(2,1)S(1)}, u32[]{:S(2)}) copy-start(bf16[512,1024]{1,0:T(8,128)(2,1)S(1)} %collective-permute-done.12.rest_2_) | copy-start | bytes 3145732
  120.0 19.9 %collective-permute-start.13 = (bf16[512,1024]{1,0:T(8,128)(2,1)S(1)}, bf16[512,1024]{1,0:T(8,128)(2,1)}, u32[]{:S(2)}, u32[]{:S(2)}) collective-permute-start(bf16[512,1024]{1,0:T(8,128)(2,1)S(1)} %collective-permute-done.12.rest_2_), channel_id=1, source_target_pairs={{0,4},{1,5},{2,6},{3,7},{4,0},{5,1},{6,2},{7,3},{8,12},{9,13},{10,... | collective-permute-start | bytes 3145736 | tf_op jit(solution)/shard_map/ppermute | solution.py:310
  123.4 3.3 %copy-start.4 = (bf16[4096,1024]{1,0:T(8,128)(2,1)}, bf16[4096,1024]{1,0:T(8,128)(2,1)S(1)}, u32[]{:S(2)}) copy-start(bf16[4096,1024]{1,0:T(8,128)(2,1)S(1)} %pack.8.rest_2_) | copy-start | bytes 25165828
  126.8 20.2 %collective-permute-start.11 = (bf16[512,1024]{1,0:T(8,128)(2,1)}, bf16[512,1024]{1,0:T(8,128)(2,1)}, u32[]{:S(2)}, u32[]{:S(2)}) collective-permute-start(bf16[512,1024]{1,0:T(8,128)(2,1)} %collective-permute-done.9.rest_0_), channel_id=1, source_target_pairs={{0,4},{1,5},{2,6},{3,7},{4,0},{5,1},{6,2},{7,3},{8,12},{9,13},{10,... | collective-permute-start | bytes 3145736 | tf_op jit(solution)/shard_map/ppermute | solution.py:310
  132.9 3.3 %copy-start.8 = (bf16[4096,1024]{1,0:T(8,128)(2,1)}, bf16[4096,1024]{1,0:T(8,128)(2,1)S(1)}, u32[]{:S(2)}) copy-start(bf16[4096,1024]{1,0:T(8,128)(2,1)S(1)} %pack.7.one_ref) | copy-start | bytes 25165828
  136.2 39.3 %collective-permute-start.15 = (bf16[512,1024]{1,0:T(8,128)(2,1)S(1)}, bf16[512,1024]{1,0:T(8,128)(2,1)}, u32[]{:S(2)}, u32[]{:S(2)}) collective-permute-start(bf16[512,1024]{1,0:T(8,128)(2,1)S(1)} %collective-permute-done.12.rest_2_), channel_id=1, source_target_pairs={{0,16},{1,17},{2,18},{3,19},{4,20},{5,21},{6,22},{7,23},{8,24},{9,... | collective-permute-start | bytes 3145736 | tf_op jit(solution)/shard_map/ppermute | solution.py:310
  143.6 3.3 %copy-start = (bf16[4096,1024]{1,0:T(8,128)(2,1)}, bf16[4096,1024]{1,0:T(8,128)(2,1)S(1)}, u32[]{:S(2)}) copy-start(bf16[4096,1024]{1,0:T(8,128)(2,1)S(1)} %pack.10.rest_2_) | copy-start | bytes 25165828
  146.9 3.4 %copy-start.5 = (bf16[4096,1024]{1,0:T(8,128)(2,1)S(1)}, bf16[4096,1024]{1,0:T(8,128)(2,1)}, u32[]{:S(2)}) copy-start(bf16[4096,1024]{1,0:T(8,128)(2,1)} %copy-done.4) | copy-start | bytes 25165828
  150.3 5.5 %copy-start.17 = (f32[3,3,1024]{2,1,0:T(4,128)S(1)}, f32[3,3,1024]{2,1,0:T(4,128)}, u32[]{:S(2)}) copy-start(f32[3,3,1024]{2,1,0:T(4,128)} %short_ref.1) | copy-start | bytes 110596
  152.4 3.3 %copy-start.6 = (bf16[4096,1024]{1,0:T(8,128)(2,1)}, bf16[4096,1024]{1,0:T(8,128)(2,1)S(1)}, u32[]{:S(2)}) copy-start(bf16[4096,1024]{1,0:T(8,128)(2,1)S(1)} %pack.9.two_ref) | copy-start | bytes 25165828
  155.8 3.4 %copy-start.7 = (bf16[4096,1024]{1,0:T(8,128)(2,1)S(1)}, bf16[4096,1024]{1,0:T(8,128)(2,1)}, u32[]{:S(2)}) copy-start(bf16[4096,1024]{1,0:T(8,128)(2,1)} %copy-done.6) | copy-start | bytes 25165828
  159.2 3.4 %copy-start.9 = (bf16[4096,1024]{1,0:T(8,128)(2,1)S(1)}, bf16[4096,1024]{1,0:T(8,128)(2,1)}, u32[]{:S(2)}) copy-start(bf16[4096,1024]{1,0:T(8,128)(2,1)} %copy-done.8) | copy-start | bytes 25165828
  173.9 1.0 copy-start.12
  175.5 45.4 %collective-permute-start.17 = (bf16[1024,1024]{1,0:T(8,128)(2,1)}, bf16[1024,1024]{1,0:T(8,128)(2,1)}, u32[]{:S(2)}, u32[]{:S(2)}) collective-permute-start(bf16[1024,1024]{1,0:T(8,128)(2,1)} %param.15), channel_id=1, source_target_pairs={{0,4},{1,5},{2,6},{3,7},{4,0},{5,1},{6,2},{7,3},{8,12},{9,13},{10,... | collective-permute-start | bytes 6291464 | tf_op jit(solution)/shard_map/ppermute | solution.py:310
  175.5 6.0 %collective-permute-start.16 = (bf16[512,1024]{1,0:T(8,128)(2,1)}, bf16[512,1024]{1,0:T(8,128)(2,1)S(1)}, u32[]{:S(2)}, u32[]{:S(2)}) collective-permute-start(bf16[512,1024]{1,0:T(8,128)(2,1)} %collective-permute-done.15.rest_0_), channel_id=1, source_target_pairs={{0,4},{1,5},{2,6},{3,7},{4,0},{5,1},{6,2},{7,3},{8,12},{9,13},{10,... | collective-permute-start | bytes 3145736 | tf_op jit(solution)/shard_map/ppermute | solution.py:310
  176.0 29.3 %collective-permute-start.14 = (bf16[160,1024]{1,0:T(8,128)(2,1)S(1)}, bf16[160,1024]{1,0:T(8,128)(2,1)S(1)}, u32[]{:S(2)}, u32[]{:S(2)}) collective-permute-start(bf16[160,1024]{1,0:T(8,128)(2,1)S(1)} %get-tuple-element.34), channel_id=1, source_target_pairs={{0,4},{1,5},{2,6},{3,7},{4,8},{5,9},{6,10},{7,11},{8,12},{9,13},{1... | collective-permute-start | bytes 983048 | tf_op jit(solution)/shard_map/ppermute | solution.py:310
  181.5 1.0 copy-start.28
  182.5 3.4 %copy-start.1 = (bf16[4096,1024]{1,0:T(8,128)(2,1)S(1)}, bf16[4096,1024]{1,0:T(8,128)(2,1)}, u32[]{:S(2)}) copy-start(bf16[4096,1024]{1,0:T(8,128)(2,1)} %copy-done) | copy-start | bytes 25165828
  187.9 3.3 %copy-start.2 = (bf16[4096,1024]{1,0:T(8,128)(2,1)}, bf16[4096,1024]{1,0:T(8,128)(2,1)S(1)}, u32[]{:S(2)}) copy-start(bf16[4096,1024]{1,0:T(8,128)(2,1)S(1)} %pack.11.weight_ref) | copy-start | bytes 25165828
  191.3 3.4 %copy-start.3 = (bf16[4096,1024]{1,0:T(8,128)(2,1)S(1)}, bf16[4096,1024]{1,0:T(8,128)(2,1)}, u32[]{:S(2)}) copy-start(bf16[4096,1024]{1,0:T(8,128)(2,1)} %copy-done.2) | copy-start | bytes 25165828
  202.0 4.2 %copy-start.20 = (bf16[128,768]{1,0:T(8,128)(2,1)S(1)}, bf16[128,768]{1,0:T(8,128)(2,1)}, u32[]{:S(2)}) copy-start(bf16[128,768]{1,0:T(8,128)(2,1)} %constant.62.clone.inv_ref) | copy-start | bytes 589828
  204.3 22.4 %collective-permute-start.18 = (bf16[512,1024]{1,0:T(8,128)(2,1)}, bf16[512,1024]{1,0:T(8,128)(2,1)}, u32[]{:S(2)}, u32[]{:S(2)}) collective-permute-start(bf16[512,1024]{1,0:T(8,128)(2,1)} %constant_dynamic-slice_fusion.14), channel_id=1, source_target_pairs={{0,4},{1,5},{2,6},{3,7},{4,0},{5,1},{6,2},{7,3},{8,12},{9,13},{10,... | collective-permute-start | bytes 3145736 | tf_op jit(solution)/shard_map/ppermute | solution.py:310
  204.7 33.6 %collective-permute-start.19 = (bf16[512,1024]{1,0:T(8,128)(2,1)}, bf16[512,1024]{1,0:T(8,128)(2,1)}, u32[]{:S(2)}, u32[]{:S(2)}) collective-permute-start(bf16[512,1024]{1,0:T(8,128)(2,1)} %constant_dynamic-slice_fusion.14), channel_id=1, source_target_pairs={{0,16},{1,17},{2,18},{3,19},{4,20},{5,21},{6,22},{7,23},{8,24},{9,... | collective-permute-start | bytes 3145736 | tf_op jit(solution)/shard_map/ppermute | solution.py:310
  206.1 1.4 copy-start.11
  207.5 1.2 copy-start.13
  208.8 1.0 copy-start.19
  209.7 0.8 copy-start.22
  218.8 17.5 %collective-permute-start.30 = (bf16[256,1024]{1,0:T(8,128)(2,1)}, bf16[256,1024]{1,0:T(8,128)(2,1)}, u32[]{:S(2)}, u32[]{:S(2)}) collective-permute-start(bf16[256,1024]{1,0:T(8,128)(2,1)} %constant_dynamic-slice_fusion), channel_id=1, source_target_pairs={{0,1},{3,2},{4,5},{7,6},{8,9},{11,10},{12,13},{15,14},{16,17},{19,... | collective-permute-start | bytes 1572872 | tf_op jit(solution)/shard_map/ppermute | solution.py:310
  224.6 19.3 %collective-permute-start.20 = (bf16[256,1024]{1,0:T(8,128)(2,1)}, bf16[256,1024]{1,0:T(8,128)(2,1)}, u32[]{:S(2)}, u32[]{:S(2)}) collective-permute-start(bf16[256,1024]{1,0:T(8,128)(2,1)} %constant_dynamic-slice_fusion.13), channel_id=1, source_target_pairs={{0,1},{3,2},{4,5},{7,6},{8,9},{11,10},{12,13},{15,14},{16,17},{19,... | collective-permute-start | bytes 1572872 | tf_op jit(solution)/shard_map/ppermute | solution.py:310
  232.5 1.7 copy-start.29
  234.2 20.2 %collective-permute-start.25 = (bf16[256,1024]{1,0:T(8,128)(2,1)}, bf16[256,1024]{1,0:T(8,128)(2,1)}, u32[]{:S(2)}, u32[]{:S(2)}) collective-permute-start(bf16[256,1024]{1,0:T(8,128)(2,1)} %pad_maximum_fusion.2), channel_id=1, source_target_pairs={{0,1},{3,2},{4,5},{7,6},{8,9},{11,10},{12,13},{15,14},{16,17},{19,... | collective-permute-start | bytes 1572872 | tf_op jit(solution)/shard_map/ppermute | solution.py:310
  236.3 8.6 %copy-start.30 = (bf16[512,512]{1,0:T(8,128)(2,1)S(1)}, bf16[512,512]{1,0:T(8,128)(2,1)}, u32[]{:S(2)}) copy-start(bf16[512,512]{1,0:T(8,128)(2,1)} %copy-done.29) | copy-start | bytes 1572868
  236.3 18.1 %copy-start.25 = (bf16[256,512]{1,0:T(8,128)(2,1)S(1)}, bf16[256,512]{1,0:T(8,128)(2,1)}, u32[]{:S(2)}) copy-start(bf16[256,512]{1,0:T(8,128)(2,1)} %copy-done.24) | copy-start | bytes 786436
  237.6 32.4 %collective-permute-start.31 = (bf16[256,1024]{1,0:T(8,128)(2,1)S(1)}, bf16[256,1024]{1,0:T(8,128)(2,1)S(1)}, u32[]{:S(2)}, u32[]{:S(2)}) collective-permute-start(bf16[256,1024]{1,0:T(8,128)(2,1)S(1)} %add_convert_fusion), channel_id=1, source_target_pairs={{1,2},{2,1},{5,6},{6,5},{9,10},{10,9},{13,14},{14,13},{17,18},{18,... | collective-permute-start | bytes 1572872 | tf_op jit(solution)/shard_map/ppermute | solution.py:310
  243.9 16.3 %collective-permute-start.21 = (bf16[512,1024]{1,0:T(8,128)(2,1)}, bf16[512,1024]{1,0:T(8,128)(2,1)S(1)}, u32[]{:S(2)}, u32[]{:S(2)}) collective-permute-start(bf16[512,1024]{1,0:T(8,128)(2,1)} %collective-permute-done.19), channel_id=1, source_target_pairs={{0,4},{1,5},{2,6},{3,7},{4,0},{5,1},{6,2},{7,3},{8,12},{9,13},{10,... | collective-permute-start | bytes 3145736 | tf_op jit(solution)/shard_map/ppermute | solution.py:310
  255.5 29.8 %collective-permute-start.26 = (bf16[256,1024]{1,0:T(8,128)(2,1)S(1)}, bf16[256,1024]{1,0:T(8,128)(2,1)S(1)}, u32[]{:S(2)}, u32[]{:S(2)}) collective-permute-start(bf16[256,1024]{1,0:T(8,128)(2,1)S(1)} %add_convert_fusion.2), channel_id=1, source_target_pairs={{1,2},{2,1},{5,6},{6,5},{9,10},{10,9},{13,14},{14,13},{17,18},{18,... | collective-permute-start | bytes 1572872 | tf_op jit(solution)/shard_map/ppermute | solution.py:310
  257.5 12.7 %collective-permute-start.28 = (bf16[256,1024]{1,0:T(8,128)(2,1)S(1)}, bf16[256,1024]{1,0:T(8,128)(2,1)S(1)}, u32[]{:S(2)}, u32[]{:S(2)}) collective-permute-start(bf16[256,1024]{1,0:T(8,128)(2,1)S(1)} %add_convert_fusion.1), channel_id=1, source_target_pairs={{1,2},{2,1},{5,6},{6,5},{9,10},{10,9},{13,14},{14,13},{17,18},{18,... | collective-permute-start | bytes 1572872 | tf_op jit(solution)/shard_map/ppermute | solution.py:310
  261.1 23.4 %collective-permute-start.22 = (bf16[256,1024]{1,0:T(8,128)(2,1)S(1)}, bf16[256,1024]{1,0:T(8,128)(2,1)S(1)}, u32[]{:S(2)}, u32[]{:S(2)}) collective-permute-start(bf16[256,1024]{1,0:T(8,128)(2,1)S(1)} %pad_maximum_fusion.1), channel_id=1, source_target_pairs={{0,1},{3,2},{4,5},{7,6},{8,9},{11,10},{12,13},{15,14},{16,17},{19,... | collective-permute-start | bytes 1572872 | tf_op jit(solution)/shard_map/ppermute | solution.py:310
  270.1 17.8 %collective-permute-start.32 = (bf16[128,1024]{1,0:T(8,128)(2,1)S(1)}, bf16[128,1024]{1,0:T(8,128)(2,1)S(1)}, u32[]{:S(2)}, u32[]{:S(2)}) collective-permute-start(bf16[128,1024]{1,0:T(8,128)(2,1)S(1)} %add_convert_fusion.5), channel_id=1, source_target_pairs={{0,1},{1,0},{2,3},{3,2},{4,5},{5,4},{6,7},{7,6},{8,9},{9,8},{10,11... | collective-permute-start | bytes 786440 | tf_op jit(solution)/shard_map/ppermute | solution.py:310
  270.3 23.2 %collective-permute-start.29 = (bf16[128,1024]{1,0:T(8,128)(2,1)S(1)}, bf16[128,1024]{1,0:T(8,128)(2,1)S(1)}, u32[]{:S(2)}, u32[]{:S(2)}) collective-permute-start(bf16[128,1024]{1,0:T(8,128)(2,1)S(1)} %add_convert_fusion.7), channel_id=1, source_target_pairs={{0,1},{1,0},{2,3},{3,2},{4,5},{5,4},{6,7},{7,6},{8,9},{9,8},{10,11... | collective-permute-start | bytes 786440 | tf_op jit(solution)/shard_map/ppermute | solution.py:310
  284.7 9.3 %collective-permute-start.23 = (bf16[256,1024]{1,0:T(8,128)(2,1)S(1)}, bf16[256,1024]{1,0:T(8,128)(2,1)S(1)}, u32[]{:S(2)}, u32[]{:S(2)}) collective-permute-start(bf16[256,1024]{1,0:T(8,128)(2,1)S(1)} %add_convert_fusion.3), channel_id=1, source_target_pairs={{1,2},{2,1},{5,6},{6,5},{9,10},{10,9},{13,14},{14,13},{17,18},{18,... | collective-permute-start | bytes 1572872 | tf_op jit(solution)/shard_map/ppermute | solution.py:310
  285.5 13.5 %collective-permute-start.27 = (bf16[128,1024]{1,0:T(8,128)(2,1)S(1)}, bf16[128,1024]{1,0:T(8,128)(2,1)S(1)}, u32[]{:S(2)}, u32[]{:S(2)}) collective-permute-start(bf16[128,1024]{1,0:T(8,128)(2,1)S(1)} %add_convert_fusion.9), channel_id=1, source_target_pairs={{0,1},{1,0},{2,3},{3,2},{4,5},{5,4},{6,7},{7,6},{8,9},{9,8},{10,11... | collective-permute-start | bytes 786440 | tf_op jit(solution)/shard_map/ppermute | solution.py:310
  294.1 9.2 %collective-permute-start.24 = (bf16[128,1024]{1,0:T(8,128)(2,1)S(1)}, bf16[128,1024]{1,0:T(8,128)(2,1)S(1)}, u32[]{:S(2)}, u32[]{:S(2)}) collective-permute-start(bf16[128,1024]{1,0:T(8,128)(2,1)S(1)} %add_convert_fusion.11), channel_id=1, source_target_pairs={{0,1},{1,0},{2,3},{3,2},{4,5},{5,4},{6,7},{7,6},{8,9},{9,8},{10,11... | collective-permute-start | bytes 786440 | tf_op jit(solution)/shard_map/ppermute | solution.py:310
  (3 other events, 2.1 us)
Sparse Core Ops, SparseCore 0:
  10.4 88.6 all-gather.2
  140.1 29.7 all-gather.4

commit v4 on v3

--- a/solution.py
+++ b/solution.py
@@ -78,57 +78,88 @@
     return pltpu.with_memory_space_constraint(array, pltpu.MemorySpace.HBM)
 
 
-def pack_kernel(kinds, at_ref, *rest):
-    arrays = rest[: len(kinds)]
-    out_ref, sems = rest[-2:]
+def kinds_of(pieces):
+    return tuple((branch, array.shape[-2]) for array, branch, _ in pieces)
+
+
+def offsets(pieces):
+    return jnp.stack([jnp.asarray(p[2], jnp.int32) for p in pieces])
+
+
+def spans(kinds):
+    start = 0
+    for _, depth in kinds:
+        yield start, start + depth
+        start += depth
+
+
+def token_copies(kinds, at_ref, x_ref, target, sems):
     copies = []
-    for n, ((branch, depth), array) in enumerate(zip(kinds, arrays)):
-        source = array if branch is None else array.at[branch]
-        rows = pl.ds(pl.multiple_of(at_ref[n], min(depth, 256)), depth)
-        copies.append(pltpu.make_async_copy(source, out_ref.at[rows], sems.at[n]))
-    for copy in copies:
-        copy.start()
-    for copy in copies:
-        copy.wait()
-
-
-def pack(pieces, features, base=None):
-    channels = pieces[0][0].shape[-1]
-    kinds = tuple((branch, array.shape[-2]) for array, branch, _ in pieces)
-    at = jnp.stack([jnp.asarray(p[2], jnp.int32) for p in pieces])
-    operands = [at] + [hold(p[0]) for p in pieces] + ([] if base is None else [base])
-    specs = [in_smem] + [in_hbm] * len(pieces) + ([] if base is None else [in_vmem])
-    return pl.pallas_call(
-        functools.partial(pack_kernel, kinds),
-        in_specs=specs,
-        out_specs=in_vmem,
-        out_shape=pltpu.VMEM((features, channels), bf16),
-        scratch_shapes=[pltpu.SemaphoreType.DMA((len(pieces),))],
-        input_output_aliases={} if base is None else {len(operands) - 1: 0},
-        compiler_params=pltpu.CompilerParams(vmem_limit_bytes=1 << 20),
-        name="pack",
-    )(*operands)
-
-
-def gate_kernel(width, x_ref, one_ref, two_ref, taps_ref, gated_ref, head_ref, halo_ref, full, s, sem):
+    for n, (low, high) in enumerate(spans(kinds)):
+        columns = pl.ds(pl.multiple_of(at_ref[n], min(high - low, 256)), high - low)
+        copies.append(
+            pltpu.make_async_copy(x_ref.at[:, columns], target.at[:, low:high], sems.at[n])
+        )
+    return copies
+
+
+def weight_copies(kinds, arrays, target, sems):
+    copies = []
+    for n, (low, high) in enumerate(spans(kinds)):
+        branch = kinds[n][0]
+        source = arrays[n] if branch is None else arrays[n].at[branch]
+        copies.append(pltpu.make_async_copy(source, target.at[low:high], sems.at[n]))
+    return copies
+
+
+def add_up(kinds, width, waits, full, weight, s, first):
+    channels = weight.shape[1]
+    for n, (low, high) in enumerate(spans(kinds)):
+        for copies in waits:
+            copies[n].wait()
+        for i in range(channels // width):
+            columns = slice(i * width, (i + 1) * width)
+            term = jnp.dot(
+                full[:, low:high], weight[low:high, columns], preferred_element_type=f32
+            )
+            if n > 0:
+                term = s[first:, columns] + term
+            if n == len(kinds) - 1:
+                term = term.astype(bf16).astype(f32)
+            s[first:, columns] = term
+
+
+def gate_kernel(one, two, width, at_ref, x_ref, taps_ref, *rest):
+    arrays = rest[: len(one) + len(two)]
+    gated_ref, head_ref, halo_ref, full, weights, s1, feat, s2, sems = rest[len(arrays) :]
     slab, channels = gated_ref.shape
     count = halo_ref.shape[0] - 2 * edge
-    load = pltpu.make_async_copy(x_ref, full, sem.at[0])
-    load.start()
-    load.wait()
+    x_copies = token_copies(one, at_ref, x_ref, full, sems.at[0])
+    copies = [
+        weight_copies(one, arrays[: len(one)], weights.at[0], sems.at[1]),
+        weight_copies(two, arrays[len(one) :], weights.at[1], sems.at[2]),
+    ]
+    for x_copy, copy in zip(x_copies, copies[0]):
+        x_copy.start()
+        copy.start()
+    for copy in copies[1]:
+        copy.start()
+    s1[0:edge] = jnp.zeros((edge, channels), f32)
+    add_up(one, width, (x_copies, copies[0]), full, weights.at[0], s1, edge)
+    head_ref[0] = s1[edge : 2 * edge].astype(bf16)
+    halo_ref[count : count + edge] = s1[slab : slab + edge].astype(bf16)
+    feat[...] = short_sum(s1, taps_ref, 1, slab)
+    for copy in copies[1]:
+        copy.wait()
+    s2[0:edge] = jnp.zeros((edge, width), f32)
     for i in range(channels // width):
         columns = slice(i * width, (i + 1) * width)
-        taps = taps_ref[:, :, columns]
-        feats = []
-        for k, weight in enumerate((one_ref, two_ref)):
-            s[k, 0:edge] = jnp.zeros((edge, width), f32)
-            term = jnp.dot(full[...], weight[:, columns], preferred_element_type=f32)
-            s[k, edge : edge + slab] = term.astype(bf16).astype(f32)
-            head_ref[k, :, columns] = s[k, edge : 2 * edge].astype(bf16)
-            rows = slice(count + k * edge, count + (k + 1) * edge)
-            halo_ref[rows, columns] = s[k, slab : slab + edge].astype(bf16)
-            feats.append(short_sum(s.at[k], taps, k + 1, slab))
-        gated = (feats[0] * feats[1]).astype(bf16)
+        term = jnp.dot(full[...], weights[1, :, columns], preferred_element_type=f32)
+        s2[edge : edge + slab] = term.astype(bf16).astype(f32)
+        head_ref[1, :, columns] = s2[edge : 2 * edge].astype(bf16)
+        halo_ref[count + edge :, columns] = s2[slab : slab + edge].astype(bf16)
+        gated = feat[:, columns] * short_sum(s2, taps_ref[:, :, columns], 2, slab)
+        gated = gated.astype(bf16)
         gated_ref[:, columns] = gated
         halo_ref[0:count, columns] = gated[slab - count :]
 
@@ -137,8 +168,8 @@
     slab, features = x.shape
     channels = short_filter.shape[-1]
     return pl.pallas_call(
-        functools.partial(gate_kernel, width),
-        in_specs=[in_hbm, in_vmem, in_vmem, in_vmem],
+        functools.partial(gate_kernel, kinds_of(one), kinds_of(two), width),
+        in_specs=[in_smem, in_hbm, in_vmem] + [in_hbm] * (len(one) + len(two)),
         out_specs=[in_vmem] * 3,
         out_shape=[
             jax.ShapeDtypeStruct((slab, channels), bf16),
@@ -147,47 +178,48 @@
         ],
         scratch_shapes=[
             pltpu.VMEM((slab, features), bf16),
-            pltpu.VMEM((2, slab + edge, width), f32),
-            pltpu.SemaphoreType.DMA((1,)),
+            pltpu.VMEM((2, features, channels), bf16),
+            pltpu.VMEM((slab + edge, channels), f32),
+            pltpu.VMEM((slab, channels), f32),
+            pltpu.VMEM((slab + edge, width), f32),
+            pltpu.SemaphoreType.DMA((3, len(one))),
         ],
-        compiler_params=pltpu.CompilerParams(vmem_limit_bytes=16 << 20),
+        compiler_params=pltpu.CompilerParams(vmem_limit_bytes=40 << 20),
         name="gate",
-    )(hold(x), one, two, short_filter)
-
-
-def query_kernel(width, x_ref, before_ref, weight_ref, taps_ref, out_ref, full, s, sem):
+    )(offsets(one), hold(x), short_filter, *[hold(p[0]) for p in one + two])
+
+
+def query_kernel(kinds, width, at_ref, x_ref, before_ref, taps_ref, *rest):
+    arrays = rest[: len(kinds)]
+    out_ref, full, weight, s, sems = rest[len(arrays) :]
     slab, channels = out_ref.shape
-    loads = [
-        pltpu.make_async_copy(before_ref, full.at[0:edge], sem.at[0]),
-        pltpu.make_async_copy(x_ref, full.at[edge : edge + slab], sem.at[1]),
-    ]
-    for load in loads:
-        load.start()
-    for load in loads:
-        load.wait()
-    for i in range(channels // width):
-        columns = slice(i * width, (i + 1) * width)
-        term = jnp.dot(full[...], weight_ref[:, columns], preferred_element_type=f32)
-        s[...] = term.astype(bf16).astype(f32)
-        out_ref[:, columns] = short_sum(s, taps_ref[:, :, columns], 0, slab)
-
-
-def query(x, before, weight, short_filter, width):
+    x_copies = token_copies(kinds, at_ref, x_ref, full.at[edge : edge + slab], sems.at[0])
+    e_copies = token_copies(kinds, at_ref, before_ref, full.at[0:edge], sems.at[1])
+    copies = weight_copies(kinds, arrays, weight, sems.at[2])
+    for group in zip(e_copies, x_copies, copies):
+        for copy in group:
+            copy.start()
+    add_up(kinds, width, (e_copies, x_copies, copies), full, weight, s, 0)
+    out_ref[...] = short_sum(s, taps_ref, 0, slab)
+
+
+def query(x, before, pieces, short_filter, width):
     slab, features = x.shape
     channels = short_filter.shape[-1]
     return pl.pallas_call(
-        functools.partial(query_kernel, width),
-        in_specs=[in_hbm, in_hbm, in_vmem, in_vmem],
+        functools.partial(query_kernel, kinds_of(pieces), width),
+        in_specs=[in_smem, in_hbm, in_hbm, in_vmem] + [in_hbm] * len(pieces),
         out_specs=in_vmem,
         out_shape=jax.ShapeDtypeStruct((slab, channels), f32),
         scratch_shapes=[
             pltpu.VMEM((slab + edge, features), bf16),
-            pltpu.VMEM((slab + edge, width), f32),
-            pltpu.SemaphoreType.DMA((2,)),
+            pltpu.VMEM((features, channels), bf16),
+            pltpu.VMEM((slab + edge, channels), f32),
+            pltpu.SemaphoreType.DMA((3, len(pieces))),
         ],
-        compiler_params=pltpu.CompilerParams(vmem_limit_bytes=16 << 20),
+        compiler_params=pltpu.CompilerParams(vmem_limit_bytes=32 << 20),
         name="query",
-    )(hold(x), hold(before), weight, short_filter)
+    )(offsets(pieces), hold(x), hold(before), short_filter, *[hold(p[0]) for p in pieces])
 
 
 def transform(fwd_ref, block):
@@ -320,20 +352,6 @@
     def after(value, *earlier):
         return lax.optimization_barrier((value, *earlier))[0]
 
-    def spread_last(value):
-        value = move(
-            value, lambda i, j, k: (i, j + 1, k) if k == count - 1 else (i, -1, k)
-        )
-        held = 1
-        while held < count:
-            first, last = max(0, count - 2 * held), count - held
-            value = value + move(
-                value,
-                lambda i, j, k: (i, j, k - held) if k - held >= first and k >= last else (i, j, -1),
-            )
-            held += last - first
-        return value
-
     medium_count = medium_filter.shape[0]
     tables = fourier_tables(medium_count)
     weights = jnp.transpose(w_in, (1, 0, 2))
@@ -343,7 +361,7 @@
     if paired:
         first_half, other_half = g * half, (1 - g) * half
         peer = to_core(weights)
-        near, far, packed = {}, {}, {}
+        near, far, pieces = {}, {}, {}
         order = (1, 2, 0)
         for n, b in enumerate(order):
             source = after(weights, normed) if n else weights
@@ -352,69 +370,40 @@
             if n == 0:
                 normed = norm(after(tokens, mine), norm_gain)
                 response = respond(medium_filter, decay, tables[0], width)
-                before_rows = spread_last(normed[length - edge :])
             else:
                 mine = after(mine, near[order[n - 1]])
             near[b] = to_chip(mine)
             if n == 0:
                 ready = near[b]
             elif n == 1:
-                ready = after(near[b], far[1], response, before_rows)
+                ready = after(near[b], far[1], response)
             else:
-                ready = after(near[b], far[2], packed[1])
+                ready = after(near[b], far[2])
             far[b] = to_group(ready)
-            packed[b] = pack(
-                [
-                    (weights, b, c * rows),
-                    (peer, b, (c ^ 1) * rows),
-                    (near[b], None, (c ^ 2) * rows + first_half),
-                    (to_core(near[b]), None, (c ^ 3) * rows + first_half),
-                ],
-                features,
-            )
-            if b == 1:
-                packed[b] = pack(
-                    [
-                        (far[b], None, (c ^ 2) * rows + other_half),
-                        (to_core(far[b]), None, (c ^ 3) * rows + other_half),
-                    ],
-                    features,
-                    packed[b],
-                )
-        far_two = after(far[2], packed[2])
-        packed[2] = pack(
-            [
-                (far_two, None, (c ^ 2) * rows + other_half),
-                (to_core(far_two), None, (c ^ 3) * rows + other_half),
-            ],
-            features,
-            packed[2],
-        )
+            pieces[b] = [
+                (weights, b, c * rows),
+                (peer, b, (c ^ 1) * rows),
+                (near[b], None, (c ^ 2) * rows + first_half),
+                (to_core(near[b]), None, (c ^ 3) * rows + first_half),
+                (far[b], None, (c ^ 2) * rows + other_half),
+            ]
+            if b != 0:
+                pieces[b].append((to_core(far[b]), None, (c ^ 3) * rows + other_half))
     else:
         normed = norm(tokens, norm_gain)
         response = respond(medium_filter, decay, tables[0], width)
-        before_rows = spread_last(normed[length - edge :])
         full = lax.all_gather(weights, "context", axis=1, tiled=True)
-        packed = {b: pack([(full, b, 0)], features) for b in range(branches)}
+        pieces = {b: [(full, b, 0)] for b in range(branches)}
 
     gathered = lax.all_gather(normed, "tensor", axis=0, tiled=True)
+    gate_taps = after(short_filter, response)
+    gated, head, edges = gate(gathered, pieces[1], pieces[2], gate_taps, medium_count, width)
+    before_rows = to_next(after(gathered[slab - edge :], gated))
+    halo = to_next(after(edges, before_rows))
     if paired:
-        gate_taps = after(short_filter, response, packed[0])
-    else:
-        gate_taps = short_filter
-    gated, head, edges = gate(gathered, packed[1], packed[2], gate_taps, medium_count, width)
-    halo = to_next(edges)
-    if paired:
-        far_zero = after(far[0], gated)
-        packed[0] = pack(
-            [
-                (far_zero, None, (c ^ 2) * rows + other_half),
-                (to_core(far_zero), None, (c ^ 3) * rows + other_half),
-            ],
-            features,
-            packed[0],
-        )
-    query_rows = query(gathered, before_rows, packed[0], short_filter, width)
+        far_core = to_core(after(far[0], gated))
+        pieces[0].append((far_core, None, (c ^ 3) * rows + other_half))
+    query_rows = query(gathered, before_rows, pieces[0], short_filter, width)
     combined = mix(gated, halo, head, short_filter, response, query_rows, tables, width)
     if paired:
         mine = lax.dynamic_slice(w_out, (g * out_half, 0), (out_half, channels))

time: 313 us -> 248 us (0.79)
  local copies, waits for them, and re-layouts: 56.5 us -> 21.9 us
  waiting for transfers between devices: 120 us -> 97.2 us
  Pallas kernels: 42.9 us -> 29.4 us
  starting transfers between devices: 57 us -> 63.7 us
    unnamed x64 -> x52, local copies, waits for them, and re-layouts: 43.3 us -> 9.24 us
    ppermute x33 -> x31, waiting for transfers between devices: 120 us -> 96.2 us  [move(): return lax.ppermute(value, axes, pairs)]
    pallas_call x8 -> x2, Pallas kernels: 35.4 us -> 22 us  [the longest x1 13.2 us: gate(): pl.pallas_call(functools.partial(gate_kernel, kinds_of(one), kinds_of(two...]
    ppermute x33 -> x31, starting transfers between devices: 57 us -> 63.6 us  [move(): return lax.ppermute(value, axes, pairs)]
  transfers between devices with their start and end apart: 35 -> 33, of which waited for: 10 -> 13; matrix products, arithmetic and copies ran while one was open for 11% -> 12% of each run, Pallas kernels for 14% -> 11%
where the time goes in v4:
time: 248 us; the launch traced here: 247 us
  waiting for transfers between devices  97.2 us (39%)
  starting transfers between devices  63.7 us (26%)
  Pallas kernels  29.4 us (12%)
  local copies, waits for them, and re-layouts  21.9 us (9%)
  between operations  14 us (6%)
  matrix products  13.3 us (5%)
  other arithmetic  7.48 us (3%)
    ppermute x31, waiting for transfers between devices, move(): return lax.ppermute(value, axes, pairs)  96.2 us
    ppermute x31, starting transfers between devices, move(): return lax.ppermute(value, axes, pairs)  63.6 us
    dot_general x6, matrix products, local(): lax.dot_general(combined, part, (((1,), (1,)), ((), ())), preferred_eleme...  13.3 us
    pallas_call x1, Pallas kernels, gate(): pl.pallas_call(functools.partial(gate_kernel, kinds_of(one), kinds_of(two...  13.2 us
    unnamed x52, local copies, waits for them, and re-layouts  9.24 us
    pallas_call x1, Pallas kernels, query(): pl.pallas_call(functools.partial(query_kernel, kinds_of(pieces), width),...  8.78 us
  transfers between devices with their start and end apart: 33, of which 13 were waited for; matrix products, arithmetic and copies ran while one was open for 12% of the time, Pallas kernels for 11%

profile of v4, /device:TPU:0, one launch (start us, length us, event | category | flops | bytes accessed | tf_op | source)
XLA Modules:
  0.0 246.9 jit_solution(3055546778030121803)
XLA Ops:
  6.5 1.4 dynamic-slice_bitcast_fusion.2
  8.1 1.9 norm.1
  10.6 2.6 %collective-permute-start.1 = (bf16[512,1024]{1,0:T(8,128)(2,1)S(1)}, bf16[512,1024]{1,0:T(8,128)(2,1)S(1)}, u32[]{:S(2)}, u32[]{:S(2)}) collective-permute-start(bf16[512,1024]{1,0:T(8,128)(2,1)S(1)} %dynamic-slice_bitcast_fusion.2), channel_id=1, source_target_pairs={{0,8},{1,9},{2,10},{3,11},{4,12},{5,13},{6,14},{7,15},{8,0},{9,1},... | collective-permute-start | bytes 3145736 | tf_op jit(solution)/shard_map/ppermute | solution.py:342
  13.2 1.7 dynamic-slice_bitcast_fusion
  14.9 22.0 %collective-permute-done.1.rest_2_ = bf16[512,1024]{1,0:T(8,128)(2,1)S(1)} collective-permute-done((bf16[512,1024]{1,0:T(8,128)(2,1)S(1)}, bf16[512,1024]{1,0:T(8,128)(2,1)S(1)}, u32[]{:S(2)}, u32[]{:S(2)}) %collective-permute-start.1) | collective-permute-done | bytes 1048608 | tf_op jit(solution)/shard_map/ppermute | solution.py:342
  37.0 1.8 collective-permute-start.5
  38.7 1.5 collective-permute-start.3
  40.3 1.0 respond.1.response_ref
  41.3 1.1 copy-done
  42.5 19.6 %collective-permute-done.5.rest_8_ = bf16[512,1024]{1,0:T(8,128)(2,1)} collective-permute-done((bf16[512,1024]{1,0:T(8,128)(2,1)S(1)}, bf16[512,1024]{1,0:T(8,128)(2,1)}, u32[]{:S(2)}, u32[]{:S(2)}) %collective-permute-start.5) | collective-permute-done | bytes 1048608 | tf_op jit(solution)/shard_map/ppermute | solution.py:342
  62.1 1.3 collective-permute-done.3.rest_4_
  63.4 1.5 collective-permute-start.7
  65.9 21.4 %collective-permute-done.7.rest_10_ = bf16[512,1024]{1,0:T(8,128)(2,1)} collective-permute-done((bf16[512,1024]{1,0:T(8,128)(2,1)}, bf16[512,1024]{1,0:T(8,128)(2,1)}, u32[]{:S(2)}, u32[]{:S(2)}) %collective-permute-start.7) | collective-permute-done | bytes 1048608 | tf_op jit(solution)/shard_map/ppermute | solution.py:342
  87.3 0.9 collective-permute-done.11.rest_2_
  88.3 1.0 copy-done.21
  89.3 1.1 collective-permute-start.13
  90.3 2.3 constant_dynamic-slice_fusion.15
  92.7 0.9 all-gather.3.cloned.1.call-done.x_ref
  93.7 13.2 %gate.1 = (bf16[512,1024]{1,0:T(8,128)(2,1)S(1)}, bf16[2,16,1024]{2,1,0:T(8,128)(2,1)S(1)}, bf16[160,1024]{1,0:T(8,128)(2,1)S(1)}) custom-call(s32[6]{0:T(128)S(1)} %stack.34.at_ref, bf16[512,4096]{1,0:T(8,128)(2,1)} %all-gather.3.cloned.1.call-done.x_ref, f32[3,3,1024]{2,1,0:T(4,128)S(1)} %copy-done.7, bf16[3,1024,1024]{2,1,0:T(8,128)(2,1)} %bitcast.29, ...), custom_call_target="tpu_custom_call" | custom-call | tf_op jit(solution)/shard_map/gate/pallas_call | solution.py:170
  106.9 1.0 copy-done.2
  108.4 6.4 %collective-permute-done.13.rest_4_ = bf16[512,1024]{1,0:T(8,128)(2,1)S(1)} collective-permute-done((bf16[512,1024]{1,0:T(8,128)(2,1)S(1)}, bf16[512,1024]{1,0:T(8,128)(2,1)S(1)}, u32[]{:S(2)}, u32[]{:S(2)}) %collective-permute-start.13) | collective-permute-done | bytes 1048608 | tf_op jit(solution)/shard_map/ppermute | solution.py:342
  114.8 1.0 slice.52
  115.8 2.3 collective-permute-start.9
  118.1 1.0 collective-permute-done.9.before_ref
  119.1 6.1 %collective-permute-start.10 = (bf16[160,1024]{1,0:T(8,128)(2,1)S(1)}, bf16[160,1024]{1,0:T(8,128)(2,1)S(1)}, u32[]{:S(2)}, u32[]{:S(2)}) collective-permute-start(bf16[160,1024]{1,0:T(8,128)(2,1)S(1)} %get-tuple-element.35), channel_id=1, source_target_pairs={{0,4},{1,5},{2,6},{3,7},{4,8},{5,9},{6,10},{7,11},{8,12},{9,13},{1... | collective-permute-start | bytes 983048 | tf_op jit(solution)/shard_map/ppermute | solution.py:342
  125.3 8.8 %query.1.query_ref = f32[512,1024]{1,0:T(8,128)S(1)} custom-call(s32[6]{0:T(128)S(1)} %stack.34.at_ref, bf16[512,4096]{1,0:T(8,128)(2,1)} %all-gather.3.cloned.1.call-done.x_ref, bf16[16,4096]{1,0:T(8,128)(2,1)} %copy-done.24, f32[3,3,1024]{2,1,0:T(4,128)S(1)} %copy-done.7, bf16[3,1024,1024]{2,1,0:T(8,128)(2,1)} %bitcast.31, ...), custom_call_target="tpu_custom_call" | custom-call | tf_op jit(solution)/shard_map/query/pallas_call | solution.py:209
  134.1 2.3 constant_dynamic-slice_fusion.14
  136.5 2.5 collective-permute-start.16
  138.9 0.8 collective-permute-start.17
  139.7 0.7 copy-done.8
  140.4 1.4 copy-done.1
  141.8 1.2 copy-done.3
  143.1 1.0 copy-done.9
  144.0 0.8 copy-done.12
  144.9 4.5 %mix.1 = bf16[512,1024]{1,0:T(8,128)(2,1)S(1)} custom-call(bf16[512,1024]{1,0:T(8,128)(2,1)S(1)} %copy-done.3, bf16[160,1024]{1,0:T(8,128)(2,1)S(1)} %copy-done.9, bf16[2,16,1024]{2,1,0:T(8,128)(2,1)S(1)} %copy-done.12, f32[3,3,1024]{2,1,0:T(4,128)S(1)} %copy-done.7, f32[3,128,1024]{2,1,0:T(8,128)S(1)} %copy-done.1, f32[512,1024]{1,0:T(8,128)S(1)} %query.1.query_ref, ...), custom_call_target="tpu_custom_call" | custom-call | tf_op jit(solution)/shard_map/mix/pallas_call | solution.py:302
  149.4 2.9 %convolution_convert_fusion.1 = bf16[512,1024]{1,0:T(8,128)(2,1)S(1)} fusion(bf16[512,1024]{1,0:T(8,128)(2,1)S(1)} %mix.1, bf16[1024,1024]{1,0:T(8,128)(2,1)} %param.15), kind=kOutput, calls=%fused_computation.1 | convolution fusion | flops 1074266112 | bytes 4194304 | tf_op jit(solution)/shard_map/dot_general | solution.py:443
  152.3 0.8 constant_dynamic-slice_fusion
  153.1 4.3 %collective-permute-start.28 = (bf16[256,1024]{1,0:T(8,128)(2,1)}, bf16[256,1024]{1,0:T(8,128)(2,1)}, u32[]{:S(2)}, u32[]{:S(2)}) collective-permute-start(bf16[256,1024]{1,0:T(8,128)(2,1)} %constant_dynamic-slice_fusion), channel_id=1, source_target_pairs={{0,1},{3,2},{4,5},{7,6},{8,9},{11,10},{12,13},{15,14},{16,17},{19,... | collective-permute-start | bytes 1572872 | tf_op jit(solution)/shard_map/ppermute | solution.py:342
  157.4 2.9 %convolution_convert_fusion = bf16[512,1024]{1,0:T(8,128)(2,1)S(1)} fusion(bf16[512,1024]{1,0:T(8,128)(2,1)S(1)} %mix.1, bf16[1024,1024]{1,0:T(8,128)(2,1)} %collective-permute-done.15), kind=kOutput, calls=%fused_computation | convolution fusion | flops 1074266112 | bytes 4194304 | tf_op jit(solution)/shard_map/dot_general | solution.py:443
  160.3 0.8 constant_dynamic-slice_fusion.13
  161.1 2.1 collective-permute-start.18
  163.2 2.8 %convolution_convert_fusion.4 = bf16[512,512]{1,0:T(8,128)(2,1)} fusion(bf16[512,1024]{1,0:T(8,128)(2,1)S(1)} %mix.1, bf16[512,1024]{1,0:T(8,128)(2,1)} %collective-permute-done.16), kind=kOutput, calls=%fused_computation.4 | convolution fusion | flops 537133056 | bytes 2621440 | tf_op jit(solution)/shard_map/dot_general | solution.py:443
  166.0 1.0 constant_dynamic-slice_fusion.3
  166.9 2.1 convolution_convert_fusion.5
  169.1 0.8 copy-done.16
  169.8 0.9 pad_maximum_fusion.2
  170.7 2.1 collective-permute-start.23
  172.8 1.3 add_convert_fusion
  174.2 0.7 collective-permute-start.29
  174.9 5.6 %collective-permute-done.18 = bf16[256,1024]{1,0:T(8,128)(2,1)} collective-permute-done((bf16[256,1024]{1,0:T(8,128)(2,1)}, bf16[256,1024]{1,0:T(8,128)(2,1)}, u32[]{:S(2)}, u32[]{:S(2)}) %collective-permute-start.18) | collective-permute-done | bytes 524320 | tf_op jit(solution)/shard_map/ppermute | solution.py:342
  180.4 1.0 constant_dynamic-slice_fusion.5
  181.5 8.9 %collective-permute-done.23 = bf16[256,1024]{1,0:T(8,128)(2,1)} collective-permute-done((bf16[256,1024]{1,0:T(8,128)(2,1)}, bf16[256,1024]{1,0:T(8,128)(2,1)}, u32[]{:S(2)}, u32[]{:S(2)}) %collective-permute-start.23) | collective-permute-done | bytes 524320 | tf_op jit(solution)/shard_map/ppermute | solution.py:342
  190.4 1.2 add_convert_fusion.2
  192.3 1.2 add_convert_fusion.1
  194.3 2.0 convolution_convert_fusion.3
  196.3 0.7 convolution_convert_fusion.2
  197.1 8.9 %collective-permute-start.20 = (bf16[256,1024]{1,0:T(8,128)(2,1)S(1)}, bf16[256,1024]{1,0:T(8,128)(2,1)S(1)}, u32[]{:S(2)}, u32[]{:S(2)}) collective-permute-start(bf16[256,1024]{1,0:T(8,128)(2,1)S(1)} %pad_maximum_fusion.1), channel_id=1, source_target_pairs={{0,1},{3,2},{4,5},{7,6},{8,9},{11,10},{12,13},{15,14},{16,17},{19,... | collective-permute-start | bytes 1572872 | tf_op jit(solution)/shard_map/ppermute | solution.py:342
  206.4 13.7 %collective-permute-start.27 = (bf16[128,1024]{1,0:T(8,128)(2,1)S(1)}, bf16[128,1024]{1,0:T(8,128)(2,1)S(1)}, u32[]{:S(2)}, u32[]{:S(2)}) collective-permute-start(bf16[128,1024]{1,0:T(8,128)(2,1)S(1)} %add_convert_fusion.7), channel_id=1, source_target_pairs={{0,1},{1,0},{2,3},{3,2},{4,5},{5,4},{6,7},{7,6},{8,9},{9,8},{10,11... | collective-permute-start | bytes 786440 | tf_op jit(solution)/shard_map/ppermute | solution.py:342
  220.3 0.7 collective-permute-start.21
  221.1 3.6 %collective-permute-start.25 = (bf16[128,1024]{1,0:T(8,128)(2,1)S(1)}, bf16[128,1024]{1,0:T(8,128)(2,1)S(1)}, u32[]{:S(2)}, u32[]{:S(2)}) collective-permute-start(bf16[128,1024]{1,0:T(8,128)(2,1)S(1)} %add_convert_fusion.9), channel_id=1, source_target_pairs={{0,1},{1,0},{2,3},{3,2},{4,5},{5,4},{6,7},{7,6},{8,9},{9,8},{10,11... | collective-permute-start | bytes 786440 | tf_op jit(solution)/shard_map/ppermute | solution.py:342
  224.7 4.9 %collective-permute-done.27 = bf16[128,1024]{1,0:T(8,128)(2,1)S(1)} collective-permute-done((bf16[128,1024]{1,0:T(8,128)(2,1)S(1)}, bf16[128,1024]{1,0:T(8,128)(2,1)S(1)}, u32[]{:S(2)}, u32[]{:S(2)}) %collective-permute-start.27) | collective-permute-done | bytes 262176 | tf_op jit(solution)/shard_map/ppermute | solution.py:342
  230.1 4.0 %collective-permute-start.22 = (bf16[128,1024]{1,0:T(8,128)(2,1)S(1)}, bf16[128,1024]{1,0:T(8,128)(2,1)S(1)}, u32[]{:S(2)}, u32[]{:S(2)}) collective-permute-start(bf16[128,1024]{1,0:T(8,128)(2,1)S(1)} %add_convert_fusion.11), channel_id=1, source_target_pairs={{0,1},{1,0},{2,3},{3,2},{4,5},{5,4},{6,7},{7,6},{8,9},{9,8},{10,11... | collective-permute-start | bytes 786440 | tf_op jit(solution)/shard_map/ppermute | solution.py:342
  234.5 4.0 %collective-permute-done.22 = bf16[128,1024]{1,0:T(8,128)(2,1)S(1)} collective-permute-done((bf16[128,1024]{1,0:T(8,128)(2,1)S(1)}, bf16[128,1024]{1,0:T(8,128)(2,1)S(1)}, u32[]{:S(2)}, u32[]{:S(2)}) %collective-permute-start.22) | collective-permute-done | bytes 262176 | tf_op jit(solution)/shard_map/ppermute | solution.py:342
  239.0 1.1 pad_maximum_fusion
  (102 shorter events, 6.1 us)
Async XLA Ops:
  6.5 1.6 copy-start.4
  6.5 1.4 copy-start.25
  6.5 87.1 %all-gather.3.cloned.1.call-start = ((), (), s32[]{:S(2)}) async-start(), calls=%async_computation | async-start | bytes 5242880 | tf_op jit(solution)/shard_map/all_gather | solution.py:398
  10.0 124.1 %all-gather.5.cloned.1.call-start = ((), (), s32[]{:S(2)}) async-start(), calls=%async_computation.1 | async-start | bytes 3145728 | tf_op jit(solution)/shard_map/all_gather | solution.py:411
  10.1 30.2 %copy-start.5 = (f32[128,1024]{1,0:T(8,128)S(1)}, f32[128,1024]{1,0:T(8,128)}, u32[]{:S(2)}) copy-start(f32[128,1024]{1,0:T(8,128)} %filter_ref.1) | copy-start | bytes 1572868
  10.1 30.1 %copy-start.6 = (bf16[256,256]{1,0:T(8,128)(2,1)S(1)}, bf16[256,256]{1,0:T(8,128)(2,1)}, u32[]{:S(2)}) copy-start(bf16[256,256]{1,0:T(8,128)(2,1)} %constant.61.clone.fwd_ref) | copy-start | bytes 393220
  10.1 30.1 %copy-start.13 = (f32[1024]{0:T(1024)S(1)}, f32[1024]{0:T(1024)}, u32[]{:S(2)}) copy-start(f32[1024]{0:T(1024)} %param.14) | copy-start | bytes 12292
  10.1 83.5 %collective-permute-start = (bf16[3,1024,1024]{2,1,0:T(8,128)(2,1)}, bf16[3,1024,1024]{2,1,0:T(8,128)(2,1)}, u32[]{:S(2)}, u32[]{:S(2)}) collective-permute-start(bf16[3,1024,1024]{2,1,0:T(8,128)(2,1)} %bitcast.27), channel_id=1, source_target_pairs={{0,4},{1,5},{2,6},{3,7},{4,0},{5,1},{6,2},{7,3},{8,12},{9,13},{10,... | collective-permute-start | bytes 18874376 | tf_op jit(solution)/shard_map/ppermute | solution.py:342
  10.6 26.3 %collective-permute-start.1 = (bf16[512,1024]{1,0:T(8,128)(2,1)S(1)}, bf16[512,1024]{1,0:T(8,128)(2,1)S(1)}, u32[]{:S(2)}, u32[]{:S(2)}) collective-permute-start(bf16[512,1024]{1,0:T(8,128)(2,1)S(1)} %dynamic-slice_bitcast_fusion.2), channel_id=1, source_target_pairs={{0,8},{1,9},{2,10},{3,11},{4,12},{5,13},{6,14},{7,15},{8,0},{9,1},... | collective-permute-start | bytes 3145736 | tf_op jit(solution)/shard_map/ppermute | solution.py:342
  37.0 51.3 %copy-start.20 = (bf16[512,1024]{1,0:T(8,128)(2,1)}, bf16[512,1024]{1,0:T(8,128)(2,1)S(1)}, u32[]{:S(2)}) copy-start(bf16[512,1024]{1,0:T(8,128)(2,1)S(1)} %collective-permute-done.1.rest_2_) | copy-start | bytes 3145732
  37.0 25.1 %collective-permute-start.5 = (bf16[512,1024]{1,0:T(8,128)(2,1)S(1)}, bf16[512,1024]{1,0:T(8,128)(2,1)}, u32[]{:S(2)}, u32[]{:S(2)}) collective-permute-start(bf16[512,1024]{1,0:T(8,128)(2,1)S(1)} %get-tuple-element.30), channel_id=1, source_target_pairs={{0,8},{1,9},{2,10},{3,11},{4,12},{5,13},{6,14},{7,15},{8,0},{9,1},... | collective-permute-start | bytes 3145736 | tf_op jit(solution)/shard_map/ppermute | solution.py:342
  38.7 24.6 %collective-permute-start.3 = (bf16[512,1024]{1,0:T(8,128)(2,1)S(1)}, bf16[512,1024]{1,0:T(8,128)(2,1)}, u32[]{:S(2)}, u32[]{:S(2)}) collective-permute-start(bf16[512,1024]{1,0:T(8,128)(2,1)S(1)} %collective-permute-done.1.rest_2_), channel_id=1, source_target_pairs={{0,16},{1,17},{2,18},{3,19},{4,20},{5,21},{6,22},{7,23},{8,24},{9,... | collective-permute-start | bytes 3145736 | tf_op jit(solution)/shard_map/ppermute | solution.py:342
  41.3 1.1 copy-start
  42.5 51.2 %copy-start.7 = (f32[3,3,1024]{2,1,0:T(4,128)S(1)}, f32[3,3,1024]{2,1,0:T(4,128)}, u32[]{:S(2)}) copy-start(f32[3,3,1024]{2,1,0:T(4,128)} %short_ref.1) | copy-start | bytes 110596
  63.4 23.9 %collective-permute-start.7 = (bf16[512,1024]{1,0:T(8,128)(2,1)}, bf16[512,1024]{1,0:T(8,128)(2,1)}, u32[]{:S(2)}, u32[]{:S(2)}) collective-permute-start(bf16[512,1024]{1,0:T(8,128)(2,1)} %collective-permute-done.5.rest_8_), channel_id=1, source_target_pairs={{0,16},{1,17},{2,18},{3,19},{4,20},{5,21},{6,22},{7,23},{8,24},{9,... | collective-permute-start | bytes 3145736 | tf_op jit(solution)/shard_map/ppermute | solution.py:342
  64.9 23.3 %collective-permute-start.11 = (bf16[512,1024]{1,0:T(8,128)(2,1)S(1)}, bf16[512,1024]{1,0:T(8,128)(2,1)S(1)}, u32[]{:S(2)}, u32[]{:S(2)}) collective-permute-start(bf16[512,1024]{1,0:T(8,128)(2,1)S(1)} %get-tuple-element.37), channel_id=1, source_target_pairs={{0,8},{1,9},{2,10},{3,11},{4,12},{5,13},{6,14},{7,15},{8,0},{9,1},... | collective-permute-start | bytes 3145736 | tf_op jit(solution)/shard_map/ppermute | solution.py:342
  65.4 22.8 %collective-permute-start.2 = (bf16[512,1024]{1,0:T(8,128)(2,1)S(1)}, bf16[512,1024]{1,0:T(8,128)(2,1)S(1)}, u32[]{:S(2)}, u32[]{:S(2)}) collective-permute-start(bf16[512,1024]{1,0:T(8,128)(2,1)S(1)} %collective-permute-done.1.rest_2_), channel_id=1, source_target_pairs={{0,4},{1,5},{2,6},{3,7},{4,0},{5,1},{6,2},{7,3},{8,12},{9,13},{10,... | collective-permute-start | bytes 3145736 | tf_op jit(solution)/shard_map/ppermute | solution.py:342
  65.4 27.3 %collective-permute-start.6 = (bf16[512,1024]{1,0:T(8,128)(2,1)}, bf16[512,1024]{1,0:T(8,128)(2,1)}, u32[]{:S(2)}, u32[]{:S(2)}) collective-permute-start(bf16[512,1024]{1,0:T(8,128)(2,1)} %collective-permute-done.5.rest_8_), channel_id=1, source_target_pairs={{0,4},{1,5},{2,6},{3,7},{4,0},{5,1},{6,2},{7,3},{8,12},{9,13},{10,... | collective-permute-start | bytes 3145736 | tf_op jit(solution)/shard_map/ppermute | solution.py:342
  87.3 5.4 %collective-permute-start.4 = (bf16[512,1024]{1,0:T(8,128)(2,1)}, bf16[512,1024]{1,0:T(8,128)(2,1)}, u32[]{:S(2)}, u32[]{:S(2)}) collective-permute-start(bf16[512,1024]{1,0:T(8,128)(2,1)} %collective-permute-done.3.rest_4_), channel_id=1, source_target_pairs={{0,4},{1,5},{2,6},{3,7},{4,0},{5,1},{6,2},{7,3},{8,12},{9,13},{10,... | collective-permute-start | bytes 3145736 | tf_op jit(solution)/shard_map/ppermute | solution.py:342
  88.2 19.6 %copy-start.18 = (bf16[512,1024]{1,0:T(8,128)(2,1)}, bf16[512,1024]{1,0:T(8,128)(2,1)S(1)}, u32[]{:S(2)}) copy-start(bf16[512,1024]{1,0:T(8,128)(2,1)S(1)} %collective-permute-done.11.rest_2_) | copy-start | bytes 3145732
  88.2 4.5 %collective-permute-start.8 = (bf16[512,1024]{1,0:T(8,128)(2,1)}, bf16[512,1024]{1,0:T(8,128)(2,1)}, u32[]{:S(2)}, u32[]{:S(2)}) collective-permute-start(bf16[512,1024]{1,0:T(8,128)(2,1)} %collective-permute-done.7.rest_10_), channel_id=1, source_target_pairs={{0,4},{1,5},{2,6},{3,7},{4,0},{5,1},{6,2},{7,3},{8,12},{9,13},{10,... | collective-permute-start | bytes 3145736 | tf_op jit(solution)/shard_map/ppermute | solution.py:342
  88.2 1.0 copy-start.21
  89.3 25.5 %collective-permute-start.13 = (bf16[512,1024]{1,0:T(8,128)(2,1)S(1)}, bf16[512,1024]{1,0:T(8,128)(2,1)S(1)}, u32[]{:S(2)}, u32[]{:S(2)}) collective-permute-start(bf16[512,1024]{1,0:T(8,128)(2,1)S(1)} %collective-permute-done.11.rest_2_), channel_id=1, source_target_pairs={{0,16},{1,17},{2,18},{3,19},{4,20},{5,21},{6,22},{7,23},{8,24},{9,... | collective-permute-start | bytes 3145736 | tf_op jit(solution)/shard_map/ppermute | solution.py:342
  106.9 1.0 copy-start.2
  107.9 11.3 %copy-start.11 = (bf16[2,16,1024]{2,1,0:T(8,128)(2,1)}, bf16[2,16,1024]{2,1,0:T(8,128)(2,1)S(1)}, u32[]{:S(2)}) copy-start(bf16[2,16,1024]{2,1,0:T(8,128)(2,1)S(1)} %get-tuple-element.36.head_ref) | copy-start | bytes 196612
  107.9 49.5 %collective-permute-start.15 = (bf16[1024,1024]{1,0:T(8,128)(2,1)}, bf16[1024,1024]{1,0:T(8,128)(2,1)}, u32[]{:S(2)}, u32[]{:S(2)}) collective-permute-start(bf16[1024,1024]{1,0:T(8,128)(2,1)} %param.15), channel_id=1, source_target_pairs={{0,4},{1,5},{2,6},{3,7},{4,0},{5,1},{6,2},{7,3},{8,12},{9,13},{10,... | collective-permute-start | bytes 6291464 | tf_op jit(solution)/shard_map/ppermute | solution.py:342
  107.9 17.4 %collective-permute-start.12 = (bf16[512,1024]{1,0:T(8,128)(2,1)S(1)}, bf16[512,1024]{1,0:T(8,128)(2,1)}, u32[]{:S(2)}, u32[]{:S(2)}) collective-permute-start(bf16[512,1024]{1,0:T(8,128)(2,1)S(1)} %collective-permute-done.11.rest_2_), channel_id=1, source_target_pairs={{0,4},{1,5},{2,6},{3,7},{4,0},{5,1},{6,2},{7,3},{8,12},{9,13},{10,... | collective-permute-start | bytes 3145736 | tf_op jit(solution)/shard_map/ppermute | solution.py:342
  114.8 10.5 %copy-start.19 = (bf16[512,1024]{1,0:T(8,128)(2,1)}, bf16[512,1024]{1,0:T(8,128)(2,1)S(1)}, u32[]{:S(2)}) copy-start(bf16[512,1024]{1,0:T(8,128)(2,1)S(1)} %collective-permute-done.13.rest_4_) | copy-start | bytes 3145732
  114.8 10.5 %collective-permute-start.14 = (bf16[512,1024]{1,0:T(8,128)(2,1)S(1)}, bf16[512,1024]{1,0:T(8,128)(2,1)}, u32[]{:S(2)}, u32[]{:S(2)}) collective-permute-start(bf16[512,1024]{1,0:T(8,128)(2,1)S(1)} %collective-permute-done.13.rest_4_), channel_id=1, source_target_pairs={{0,4},{1,5},{2,6},{3,7},{4,0},{5,1},{6,2},{7,3},{8,12},{9,13},{10,... | collective-permute-start | bytes 3145736 | tf_op jit(solution)/shard_map/ppermute | solution.py:342
  115.8 3.3 %collective-permute-start.9 = (bf16[16,4096]{1,0:T(8,128)(2,1)S(1)}, bf16[16,4096]{1,0:T(8,128)(2,1)S(1)}, u32[]{:S(2)}, u32[]{:S(2)}) collective-permute-start(bf16[16,4096]{1,0:T(8,128)(2,1)S(1)} %slice.52), channel_id=1, source_target_pairs={{0,4},{1,5},{2,6},{3,7},{4,8},{5,9},{6,10},{7,11},{8,12},{9,13},{1... | collective-permute-start | bytes 393224 | tf_op jit(solution)/shard_map/ppermute | solution.py:342
  119.1 6.2 %copy-start.24 = (bf16[16,4096]{1,0:T(8,128)(2,1)}, bf16[16,4096]{1,0:T(8,128)(2,1)S(1)}, u32[]{:S(2)}) copy-start(bf16[16,4096]{1,0:T(8,128)(2,1)S(1)} %collective-permute-done.9.before_ref) | copy-start | bytes 393220
  119.1 20.6 %collective-permute-start.10 = (bf16[160,1024]{1,0:T(8,128)(2,1)S(1)}, bf16[160,1024]{1,0:T(8,128)(2,1)S(1)}, u32[]{:S(2)}, u32[]{:S(2)}) collective-permute-start(bf16[160,1024]{1,0:T(8,128)(2,1)S(1)} %get-tuple-element.35), channel_id=1, source_target_pairs={{0,4},{1,5},{2,6},{3,7},{4,8},{5,9},{6,10},{7,11},{8,12},{9,13},{1... | collective-permute-start | bytes 983048 | tf_op jit(solution)/shard_map/ppermute | solution.py:342
  134.1 6.3 %copy-start.10 = (bf16[128,768]{1,0:T(8,128)(2,1)S(1)}, bf16[128,768]{1,0:T(8,128)(2,1)}, u32[]{:S(2)}) copy-start(bf16[128,768]{1,0:T(8,128)(2,1)} %constant.62.clone.inv_ref) | copy-start | bytes 589828
  136.5 26.8 %collective-permute-start.16 = (bf16[512,1024]{1,0:T(8,128)(2,1)}, bf16[512,1024]{1,0:T(8,128)(2,1)}, u32[]{:S(2)}, u32[]{:S(2)}) collective-permute-start(bf16[512,1024]{1,0:T(8,128)(2,1)} %constant_dynamic-slice_fusion.14), channel_id=1, source_target_pairs={{0,4},{1,5},{2,6},{3,7},{4,0},{5,1},{6,2},{7,3},{8,12},{9,13},{10,... | collective-permute-start | bytes 3145736 | tf_op jit(solution)/shard_map/ppermute | solution.py:342
  138.9 35.9 %collective-permute-start.17 = (bf16[512,1024]{1,0:T(8,128)(2,1)}, bf16[512,1024]{1,0:T(8,128)(2,1)}, u32[]{:S(2)}, u32[]{:S(2)}) collective-permute-start(bf16[512,1024]{1,0:T(8,128)(2,1)} %constant_dynamic-slice_fusion.14), channel_id=1, source_target_pairs={{0,16},{1,17},{2,18},{3,19},{4,20},{5,21},{6,22},{7,23},{8,24},{9,... | collective-permute-start | bytes 3145736 | tf_op jit(solution)/shard_map/ppermute | solution.py:342
  139.7 0.7 copy-start.8
  140.4 1.4 copy-start.1
  141.8 1.2 copy-start.3
  143.1 1.0 copy-start.9
  144.0 0.8 copy-start.12
  153.1 19.7 %collective-permute-start.28 = (bf16[256,1024]{1,0:T(8,128)(2,1)}, bf16[256,1024]{1,0:T(8,128)(2,1)}, u32[]{:S(2)}, u32[]{:S(2)}) collective-permute-start(bf16[256,1024]{1,0:T(8,128)(2,1)} %constant_dynamic-slice_fusion), channel_id=1, source_target_pairs={{0,1},{3,2},{4,5},{7,6},{8,9},{11,10},{12,13},{15,14},{16,17},{19,... | collective-permute-start | bytes 1572872 | tf_op jit(solution)/shard_map/ppermute | solution.py:342
  161.1 19.3 %collective-permute-start.18 = (bf16[256,1024]{1,0:T(8,128)(2,1)}, bf16[256,1024]{1,0:T(8,128)(2,1)}, u32[]{:S(2)}, u32[]{:S(2)}) collective-permute-start(bf16[256,1024]{1,0:T(8,128)(2,1)} %constant_dynamic-slice_fusion.13), channel_id=1, source_target_pairs={{0,1},{3,2},{4,5},{7,6},{8,9},{11,10},{12,13},{15,14},{16,17},{19,... | collective-permute-start | bytes 1572872 | tf_op jit(solution)/shard_map/ppermute | solution.py:342
  166.9 3.8 %copy-start.14 = (bf16[256,512]{1,0:T(8,128)(2,1)}, bf16[256,512]{1,0:T(8,128)(2,1)S(1)}, u32[]{:S(2)}) copy-start(bf16[256,512]{1,0:T(8,128)(2,1)S(1)} %constant_dynamic-slice_fusion.3) | copy-start | bytes 786436
  169.0 1.7 copy-start.22
  169.1 0.8 copy-start.16
  170.7 19.7 %collective-permute-start.23 = (bf16[256,1024]{1,0:T(8,128)(2,1)}, bf16[256,1024]{1,0:T(8,128)(2,1)}, u32[]{:S(2)}, u32[]{:S(2)}) collective-permute-start(bf16[256,1024]{1,0:T(8,128)(2,1)} %pad_maximum_fusion.2), channel_id=1, source_target_pairs={{0,1},{3,2},{4,5},{7,6},{8,9},{11,10},{12,13},{15,14},{16,17},{19,... | collective-permute-start | bytes 1572872 | tf_op jit(solution)/shard_map/ppermute | solution.py:342
  172.8 8.6 %copy-start.23 = (bf16[512,512]{1,0:T(8,128)(2,1)S(1)}, bf16[512,512]{1,0:T(8,128)(2,1)}, u32[]{:S(2)}) copy-start(bf16[512,512]{1,0:T(8,128)(2,1)} %copy-done.22) | copy-start | bytes 1572868
  172.8 17.6 %copy-start.15 = (bf16[256,512]{1,0:T(8,128)(2,1)S(1)}, bf16[256,512]{1,0:T(8,128)(2,1)}, u32[]{:S(2)}) copy-start(bf16[256,512]{1,0:T(8,128)(2,1)} %copy-done.14) | copy-start | bytes 786436
  172.8 17.6 %copy-start.17 = (bf16[256,512]{1,0:T(8,128)(2,1)S(1)}, bf16[256,512]{1,0:T(8,128)(2,1)}, u32[]{:S(2)}) copy-start(bf16[256,512]{1,0:T(8,128)(2,1)} %copy-done.16) | copy-start | bytes 786436
  174.2 31.9 %collective-permute-start.29 = (bf16[256,1024]{1,0:T(8,128)(2,1)S(1)}, bf16[256,1024]{1,0:T(8,128)(2,1)S(1)}, u32[]{:S(2)}, u32[]{:S(2)}) collective-permute-start(bf16[256,1024]{1,0:T(8,128)(2,1)S(1)} %add_convert_fusion), channel_id=1, source_target_pairs={{1,2},{2,1},{5,6},{6,5},{9,10},{10,9},{13,14},{14,13},{17,18},{18,... | collective-permute-start | bytes 1572872 | tf_op jit(solution)/shard_map/ppermute | solution.py:342
  180.4 15.8 %collective-permute-start.19 = (bf16[512,1024]{1,0:T(8,128)(2,1)}, bf16[512,1024]{1,0:T(8,128)(2,1)S(1)}, u32[]{:S(2)}, u32[]{:S(2)}) collective-permute-start(bf16[512,1024]{1,0:T(8,128)(2,1)} %collective-permute-done.17), channel_id=1, source_target_pairs={{0,4},{1,5},{2,6},{3,7},{4,0},{5,1},{6,2},{7,3},{8,12},{9,13},{10,... | collective-permute-start | bytes 3145736 | tf_op jit(solution)/shard_map/ppermute | solution.py:342
  191.6 29.3 %collective-permute-start.24 = (bf16[256,1024]{1,0:T(8,128)(2,1)S(1)}, bf16[256,1024]{1,0:T(8,128)(2,1)S(1)}, u32[]{:S(2)}, u32[]{:S(2)}) collective-permute-start(bf16[256,1024]{1,0:T(8,128)(2,1)S(1)} %add_convert_fusion.2), channel_id=1, source_target_pairs={{1,2},{2,1},{5,6},{6,5},{9,10},{10,9},{13,14},{14,13},{17,18},{18,... | collective-permute-start | bytes 1572872 | tf_op jit(solution)/shard_map/ppermute | solution.py:342
  193.6 12.7 %collective-permute-start.26 = (bf16[256,1024]{1,0:T(8,128)(2,1)S(1)}, bf16[256,1024]{1,0:T(8,128)(2,1)S(1)}, u32[]{:S(2)}, u32[]{:S(2)}) collective-permute-start(bf16[256,1024]{1,0:T(8,128)(2,1)S(1)} %add_convert_fusion.1), channel_id=1, source_target_pairs={{1,2},{2,1},{5,6},{6,5},{9,10},{10,9},{13,14},{14,13},{17,18},{18,... | collective-permute-start | bytes 1572872 | tf_op jit(solution)/shard_map/ppermute | solution.py:342
  197.1 23.0 %collective-permute-start.20 = (bf16[256,1024]{1,0:T(8,128)(2,1)S(1)}, bf16[256,1024]{1,0:T(8,128)(2,1)S(1)}, u32[]{:S(2)}, u32[]{:S(2)}) collective-permute-start(bf16[256,1024]{1,0:T(8,128)(2,1)S(1)} %pad_maximum_fusion.1), channel_id=1, source_target_pairs={{0,1},{3,2},{4,5},{7,6},{8,9},{11,10},{12,13},{15,14},{16,17},{19,... | collective-permute-start | bytes 1572872 | tf_op jit(solution)/shard_map/ppermute | solution.py:342
  206.2 18.5 %collective-permute-start.30 = (bf16[128,1024]{1,0:T(8,128)(2,1)S(1)}, bf16[128,1024]{1,0:T(8,128)(2,1)S(1)}, u32[]{:S(2)}, u32[]{:S(2)}) collective-permute-start(bf16[128,1024]{1,0:T(8,128)(2,1)S(1)} %add_convert_fusion.5), channel_id=1, source_target_pairs={{0,1},{1,0},{2,3},{3,2},{4,5},{5,4},{6,7},{7,6},{8,9},{9,8},{10,11... | collective-permute-start | bytes 786440 | tf_op jit(solution)/shard_map/ppermute | solution.py:342
  206.4 23.2 %collective-permute-start.27 = (bf16[128,1024]{1,0:T(8,128)(2,1)S(1)}, bf16[128,1024]{1,0:T(8,128)(2,1)S(1)}, u32[]{:S(2)}, u32[]{:S(2)}) collective-permute-start(bf16[128,1024]{1,0:T(8,128)(2,1)S(1)} %add_convert_fusion.7), channel_id=1, source_target_pairs={{0,1},{1,0},{2,3},{3,2},{4,5},{5,4},{6,7},{7,6},{8,9},{9,8},{10,11... | collective-permute-start | bytes 786440 | tf_op jit(solution)/shard_map/ppermute | solution.py:342
  220.3 9.7 %collective-permute-start.21 = (bf16[256,1024]{1,0:T(8,128)(2,1)S(1)}, bf16[256,1024]{1,0:T(8,128)(2,1)S(1)}, u32[]{:S(2)}, u32[]{:S(2)}) collective-permute-start(bf16[256,1024]{1,0:T(8,128)(2,1)S(1)} %add_convert_fusion.3), channel_id=1, source_target_pairs={{1,2},{2,1},{5,6},{6,5},{9,10},{10,9},{13,14},{14,13},{17,18},{18,... | collective-permute-start | bytes 1572872 | tf_op jit(solution)/shard_map/ppermute | solution.py:342
  221.1 13.2 %collective-permute-start.25 = (bf16[128,1024]{1,0:T(8,128)(2,1)S(1)}, bf16[128,1024]{1,0:T(8,128)(2,1)S(1)}, u32[]{:S(2)}, u32[]{:S(2)}) collective-permute-start(bf16[128,1024]{1,0:T(8,128)(2,1)S(1)} %add_convert_fusion.9), channel_id=1, source_target_pairs={{0,1},{1,0},{2,3},{3,2},{4,5},{5,4},{6,7},{7,6},{8,9},{9,8},{10,11... | collective-permute-start | bytes 786440 | tf_op jit(solution)/shard_map/ppermute | solution.py:342
  230.1 8.3 %collective-permute-start.22 = (bf16[128,1024]{1,0:T(8,128)(2,1)S(1)}, bf16[128,1024]{1,0:T(8,128)(2,1)S(1)}, u32[]{:S(2)}, u32[]{:S(2)}) collective-permute-start(bf16[128,1024]{1,0:T(8,128)(2,1)S(1)} %add_convert_fusion.11), channel_id=1, source_target_pairs={{0,1},{1,0},{2,3},{3,2},{4,5},{5,4},{6,7},{7,6},{8,9},{9,8},{10,11... | collective-permute-start | bytes 786440 | tf_op jit(solution)/shard_map/ppermute | solution.py:342
Sparse Core Ops, SparseCore 0:
  10.2 83.4 all-gather.2
  95.2 31.6 all-gather.4

commit v5 on v4

--- a/solution.py
+++ b/solution.py
@@ -172,9 +172,9 @@
         in_specs=[in_smem, in_hbm, in_vmem] + [in_hbm] * (len(one) + len(two)),
         out_specs=[in_vmem] * 3,
         out_shape=[
-            jax.ShapeDtypeStruct((slab, channels), bf16),
-            jax.ShapeDtypeStruct((2, edge, channels), bf16),
-            jax.ShapeDtypeStruct((taps + 2 * edge, channels), bf16),
+            pltpu.MemorySpace.HBM((slab, channels), bf16),
+            pltpu.MemorySpace.HBM((2, edge, channels), bf16),
+            pltpu.MemorySpace.HBM((taps + 2 * edge, channels), bf16),
         ],
         scratch_shapes=[
             pltpu.VMEM((slab, features), bf16),
@@ -248,7 +248,7 @@
             pl.BlockSpec(forward.shape, lambda i: (0, 0)),
         ],
         out_specs=pl.BlockSpec((3, taps, width), lambda i: (0, 0, i)),
-        out_shape=jax.ShapeDtypeStruct((3, taps, channels), f32),
+        out_shape=pltpu.MemorySpace.HBM((3, taps, channels), f32),
         compiler_params=pltpu.CompilerParams(vmem_limit_bytes=8 << 20),
         name="respond",
     )(medium_filter, decay.reshape(1, channels), forward)
@@ -317,7 +317,7 @@
         scratch_shapes=[pltpu.VMEM((2 * edge, width), f32)],
         compiler_params=pltpu.CompilerParams(vmem_limit_bytes=16 << 20),
         name="mix",
-    )(gated, halo, head, short_filter, response, query_rows, forward, inverse)
+    )(hold(gated), hold(halo), hold(head), short_filter, hold(response), query_rows, forward, inverse)
 
 
 def local(tokens, norm_gain, w_in, short_filter, medium_filter, decay, w_out):
@@ -357,29 +357,25 @@
     weights = jnp.transpose(w_in, (1, 0, 2))
     half = rows // 2
     out_rows = w_out.shape[0]
-    out_half = out_rows // 2
     if paired:
         first_half, other_half = g * half, (1 - g) * half
         peer = to_core(weights)
         near, far, pieces = {}, {}, {}
-        order = (1, 2, 0)
-        for n, b in enumerate(order):
-            source = after(weights, normed) if n else weights
-            mine = lax.dynamic_slice(source, (b, first_half, 0), (1, half, channels))
-            mine = mine.reshape(half, channels)
-            if n == 0:
-                normed = norm(after(tokens, mine), norm_gain)
-                response = respond(medium_filter, decay, tables[0], width)
-            else:
-                mine = after(mine, near[order[n - 1]])
-            near[b] = to_chip(mine)
-            if n == 0:
-                ready = near[b]
-            elif n == 1:
-                ready = after(near[b], far[1], response)
-            else:
-                ready = after(near[b], far[2])
-            far[b] = to_group(ready)
+        def cut(source, b, first, depth):
+            part = lax.dynamic_slice(source, (b, first, 0), (1, depth, channels))
+            return part.reshape(depth, channels)
+
+        mine = cut(weights, 1, first_half, half)
+        normed = norm(after(tokens, mine), norm_gain)
+        response = respond(medium_filter, decay, tables[0], width)
+        near[1] = to_chip(mine)
+        far[1] = to_group(near[1])
+        source = after(weights, normed)
+        near[2] = to_chip(after(cut(source, 2, first_half, half), near[1]))
+        far[2] = to_group(after(near[2], far[1], response, peer))
+        near[0] = to_chip(after(cut(source, 0, first_half, half), near[2]))
+        far[0] = to_group(after(near[0], far[2]))
+        for b in (1, 2, 0):
             pieces[b] = [
                 (weights, b, c * rows),
                 (peer, b, (c ^ 1) * rows),
@@ -388,7 +384,8 @@
                 (far[b], None, (c ^ 2) * rows + other_half),
             ]
             if b != 0:
-                pieces[b].append((to_core(far[b]), None, (c ^ 3) * rows + other_half))
+                late = after(far[2], near[0]) if b == 2 else far[1]
+                pieces[b].append((to_core(late), None, (c ^ 3) * rows + other_half))
     else:
         normed = norm(tokens, norm_gain)
         response = respond(medium_filter, decay, tables[0], width)
@@ -401,34 +398,17 @@
     before_rows = to_next(after(gathered[slab - edge :], gated))
     halo = to_next(after(edges, before_rows))
     if paired:
-        far_core = to_core(after(far[0], gated))
-        pieces[0].append((far_core, None, (c ^ 3) * rows + other_half))
+        last = to_core(after(far[0], before_rows))
+        pieces[0].append((last, None, (c ^ 3) * rows + other_half))
     query_rows = query(gathered, before_rows, pieces[0], short_filter, width)
     combined = mix(gated, halo, head, short_filter, response, query_rows, tables, width)
     if paired:
-        mine = lax.dynamic_slice(w_out, (g * out_half, 0), (out_half, channels))
-        chips = [[0, 2], [1, 3]]
-        pair = lax.all_gather(
-            after(mine, near[1]), "context", axis=0, tiled=True, axis_index_groups=chips
-        )
-        pair = after(pair, query_rows)
-        near_out = lax.dynamic_slice(pair, ((1 - c // 2) * out_half, 0), (out_half, channels))
-        far_out = to_group(near_out)
+        out_full = lax.all_gather(after(w_out, near[1]), "context", axis=0, tiled=True)
         out_peer = to_core(after(w_out, gated))
-        near_core = to_core(near_out)
-
-        def last_parts(earlier):
-            late = after(far_out, earlier[1])
-            return [late, to_core(late)]
-
-        sets = [
-            lambda _: [w_out],
-            lambda _: [out_peer],
-            lambda _: [near_out, near_core],
-            last_parts,
-        ]
+        part = lambda i: lax.dynamic_slice(out_full, ((c ^ i) * out_rows, 0), (out_rows, channels))
+        sets = [w_out, out_peer, part(2), part(3)]
     else:
-        sets = [lambda _: [lax.all_gather(w_out, "context", axis=0, tiled=True)]]
+        sets = [lax.all_gather(w_out, "context", axis=0, tiled=True)]
 
     def plus(*terms):
         total = terms[0].astype(f32)
@@ -436,31 +416,33 @@
             total = total + term.astype(f32)
         return total.astype(bf16)
 
-    results, partial, firsts, pending = [], [], [], []
-    for make in sets:
-        parts = make(firsts)
-        partial = [
-            lax.dot_general(
-                combined, part, (((1,), (1,)), ((), ())), preferred_element_type=f32
-            ).astype(bf16)
-            for part in parts
-        ]
-        combined = after(combined, *partial)
+    def product(rows_out):
+        return lax.dot_general(
+            combined, rows_out, (((1,), (1,)), ((), ())), preferred_element_type=f32
+        ).astype(bf16)
+
+    results, firsts = [], []
+    for rows_out in sets:
+        partial = product(rows_out)
+        combined = after(combined, partial)
 
         def block(index, blocks=1, partial=partial):
             index = jnp.clip(index, 0, count - blocks)
-            return jnp.concatenate(
-                [
-                    lax.dynamic_slice(p, (index * length, 0), (blocks * length, p.shape[1]))
-                    for p in partial
-                ],
-                1,
+            return lax.dynamic_slice(
+                partial, (index * length, 0), (blocks * length, partial.shape[1])
             )
 
         if count == 4:
             far_pair = block(jnp.where(z < 2, 2, 0), 2)
             firsts.append(send(far_pair, {0: 1, 3: 2}))
-            pending.append((far_pair, block(z), block(z ^ 1), partial[0]))
+            got = plus(far_pair, firsts[-1])
+            got = send(got, {1: 2, 2: 1})
+            low, high = got[:length], got[length:]
+            odd = z % 2 == 1
+            got_own = jnp.where(odd, high, low)
+            got_other = jnp.where(odd, low, high)
+            last = send(plus(block(z ^ 1), got_other), {0: 1, 1: 0, 2: 3, 3: 2})
+            results.append(plus(block(z), got_own, last))
         else:
             up = down = None
             for s in range(1, count):
@@ -470,25 +452,10 @@
                     rising, falling = plus(rising, up), plus(falling, down)
                 up, down = to_up(rising), to_down(falling)
             results.append(plus(block(z), up, down))
-    for n, (far_pair, own, other, _) in enumerate(pending):
-        got = plus(far_pair, firsts[n])
-        if n + 1 < len(pending) - 1:
-            got = after(got, pending[n + 1][3])
-        got = send(got, {1: 2, 2: 1})
-        low, high = got[:length], got[length:]
-        odd = z % 2 == 1
-        got_own = jnp.where(odd, high, low)
-        got_other = jnp.where(odd, low, high)
-        last = send(plus(other, got_other), {0: 1, 1: 0, 2: 3, 3: 2})
-        results.append(plus(own, got_own, last))
     if not paired:
         return results[0]
     swap = lambda test, a, b: (jnp.where(test, b, a), jnp.where(test, a, b))
     e0, e1, e2, e3 = results
-    e2, e3 = (
-        jnp.concatenate(swap(g == 1, e2[:, at], e3[:, at]), 1)
-        for at in (slice(0, out_half), slice(out_half, None))
-    )
     odd = c % 2 == 1
     low = jnp.concatenate(swap(odd, e0, e1), 1)
     high = jnp.concatenate(swap(odd, e2, e3), 1)

time: 248 us -> 231 us (0.931)
  local copies, waits for them, and re-layouts: 21.9 us -> 7.35 us
  starting transfers between devices: 63.7 us -> 59.5 us
  Pallas kernels: 29.4 us -> 32.8 us
    unnamed x52 -> x24, local copies, waits for them, and re-layouts: 9.24 us -> 1.03 us
    dynamic_slice x12 -> x4, local copies, waits for them, and re-layouts: 8.38 us -> 1.77 us  [block(): lax.dynamic_slice(partial, (index * length, 0), (blocks * length, partial...]
    ppermute x31 -> x28, waiting for transfers between devices: 96.2 us -> 90.3 us  [move(): return lax.ppermute(value, axes, pairs)]
    all_gather x1, waiting for transfers between devices: 0.02 us -> 5.29 us  [local(): lax.all_gather(after(w_out, near[1]), 'context', axis=0, tiled=True)]
    ppermute x31 -> x28, starting transfers between devices: 63.6 us -> 59.4 us  [move(): return lax.ppermute(value, axes, pairs)]
    dot_general x6 -> x4, matrix products: 13.3 us -> 11.5 us  [product(): lax.dot_general(combined, rows_out, (((1,), (1,)), ((), ())), preferred_e...]
  transfers between devices with their start and end apart: 33 -> 30, of which waited for: 13 -> 11; matrix products, arithmetic and copies ran while one was open for 12% -> 9% of each run, Pallas kernels for 11% -> 14%
where the time goes in v5:
time: 231 us; the launch traced here: 228 us
  waiting for transfers between devices  97.7 us (42%)
  starting transfers between devices  59.5 us (26%)
  Pallas kernels  32.8 us (14%)
  between operations  13.8 us (6%)
  matrix products  11.5 us (5%)
  local copies, waits for them, and re-layouts  7.35 us (3%)
  other arithmetic  5.47 us (2%)
    ppermute x28, waiting for transfers between devices, move(): return lax.ppermute(value, axes, pairs)  90.3 us
    ppermute x28, starting transfers between devices, move(): return lax.ppermute(value, axes, pairs)  59.4 us
    pallas_call x1, Pallas kernels, gate(): pl.pallas_call(functools.partial(gate_kernel, kinds_of(one), kinds_of(two...  14.5 us
    dot_general x4, matrix products, product(): lax.dot_general(combined, rows_out, (((1,), (1,)), ((), ())), preferred_e...  11.5 us
    pallas_call x1, Pallas kernels, query(): pl.pallas_call(functools.partial(query_kernel, kinds_of(pieces), width),...  8.77 us
    pallas_call x1, Pallas kernels, mix(): pl.pallas_call(mix_kernel, grid=(channels // width,), in_specs=[col(slab)...  5.36 us
    all_gather x1, waiting for transfers between devices, local(): lax.all_gather(after(w_out, near[1]), 'context', axis=0, tiled=True)  5.29 us
  transfers between devices with their start and end apart: 30, of which 11 were waited for; matrix products, arithmetic and copies ran while one was open for 9% of the time, Pallas kernels for 14%

profile of v5, /device:TPU:0, one launch (start us, length us, event | category | flops | bytes accessed | tf_op | source)
XLA Modules:
  0.0 228.1 jit_solution(9001070647246808060)
XLA Ops:
  6.5 1.4 dynamic-slice_bitcast_fusion.2
  8.0 0.1 copy-done
  8.1 1.9 norm.1
  10.1 3.0 %collective-permute-start.1 = (bf16[512,1024]{1,0:T(8,128)(2,1)S(1)}, bf16[512,1024]{1,0:T(8,128)(2,1)S(1)}, u32[]{:S(2)}, u32[]{:S(2)}) collective-permute-start(bf16[512,1024]{1,0:T(8,128)(2,1)S(1)} %dynamic-slice_bitcast_fusion.2), channel_id=1, source_target_pairs={{0,8},{1,9},{2,10},{3,11},{4,12},{5,13},{6,14},{7,15},{8,0},{9,1},... | collective-permute-start | bytes 3145736 | tf_op jit(solution)/shard_map/ppermute | solution.py:342
  13.1 23.2 %collective-permute-done.1.rest_2_ = bf16[512,1024]{1,0:T(8,128)(2,1)S(1)} collective-permute-done((bf16[512,1024]{1,0:T(8,128)(2,1)S(1)}, bf16[512,1024]{1,0:T(8,128)(2,1)S(1)}, u32[]{:S(2)}, u32[]{:S(2)}) %collective-permute-start.1) | collective-permute-done | bytes 1048608 | tf_op jit(solution)/shard_map/ppermute | solution.py:342
  36.4 2.1 dynamic-slice_bitcast_fusion
  38.6 1.8 collective-permute-start.5
  40.4 1.5 collective-permute-start.3
  41.9 2.3 %respond.1.response_ref = f32[3,128,1024]{2,1,0:T(8,128)} custom-call(f32[128,1024]{1,0:T(8,128)S(1)} %copy-done.1, f32[1,1024]{1,0:T(1,128)S(1)} %bitcast.20, bf16[256,256]{1,0:T(8,128)(2,1)S(1)} %copy-done.2), custom_call_target="tpu_custom_call" | custom-call | tf_op jit(solution)/shard_map/respond/pallas_call | solution.py:242
  44.2 19.7 %collective-permute-done.5.rest_8_ = bf16[512,1024]{1,0:T(8,128)(2,1)} collective-permute-done((bf16[512,1024]{1,0:T(8,128)(2,1)S(1)}, bf16[512,1024]{1,0:T(8,128)(2,1)}, u32[]{:S(2)}, u32[]{:S(2)}) %collective-permute-start.5) | collective-permute-done | bytes 1048608 | tf_op jit(solution)/shard_map/ppermute | solution.py:342
  63.9 1.7 collective-permute-start.8
  65.6 1.5 collective-permute-start.7
  67.1 0.5 collective-permute-start.6
  67.7 20.5 %collective-permute-done.8.rest_2_ = bf16[512,1024]{1,0:T(8,128)(2,1)S(1)} collective-permute-done((bf16[512,1024]{1,0:T(8,128)(2,1)S(1)}, bf16[512,1024]{1,0:T(8,128)(2,1)S(1)}, u32[]{:S(2)}, u32[]{:S(2)}) %collective-permute-start.8) | collective-permute-done | bytes 1048608 | tf_op jit(solution)/shard_map/ppermute | solution.py:342
  88.2 1.8 collective-permute-done.7.rest_10_
  90.0 1.5 collective-permute-start.13
  91.5 0.1 stack.34.at_ref
  91.6 2.1 all-gather.3.cloned.1.call-done.x_ref
  93.7 14.5 %gate.1 = (bf16[512,1024]{1,0:T(8,128)(2,1)}, bf16[2,16,1024]{2,1,0:T(8,128)(2,1)}, bf16[160,1024]{1,0:T(8,128)(2,1)}) custom-call(s32[6]{0:T(128)S(1)} %stack.34.at_ref, bf16[512,4096]{1,0:T(8,128)(2,1)} %all-gather.3.cloned.1.call-done.x_ref, f32[3,3,1024]{2,1,0:T(4,128)S(1)} %copy-done.3, bf16[3,1024,1024]{2,1,0:T(8,128)(2,1)} %bitcast.23, ...), custom_call_target="tpu_custom_call" | custom-call | tf_op jit(solution)/shard_map/gate/pallas_call | solution.py:170
  108.1 0.1 collective-permute-start.15
  108.2 0.9 slice.36
  109.1 2.4 %collective-permute-start.10 = (bf16[16,4096]{1,0:T(8,128)(2,1)S(1)}, bf16[16,4096]{1,0:T(8,128)(2,1)S(1)}, u32[]{:S(2)}, u32[]{:S(2)}) collective-permute-start(bf16[16,4096]{1,0:T(8,128)(2,1)S(1)} %slice.36), channel_id=1, source_target_pairs={{0,4},{1,5},{2,6},{3,7},{4,8},{5,9},{6,10},{7,11},{8,12},{9,13},{1... | collective-permute-start | bytes 393224 | tf_op jit(solution)/shard_map/ppermute | solution.py:342
  111.6 1.0 collective-permute-start.12
  112.6 2.9 %collective-permute-done.13.rest_4_ = bf16[512,1024]{1,0:T(8,128)(2,1)S(1)} collective-permute-done((bf16[512,1024]{1,0:T(8,128)(2,1)S(1)}, bf16[512,1024]{1,0:T(8,128)(2,1)S(1)}, u32[]{:S(2)}, u32[]{:S(2)}) %collective-permute-start.13) | collective-permute-done | bytes 1048608 | tf_op jit(solution)/shard_map/ppermute | solution.py:342
  115.5 1.6 collective-permute-start.14
  117.2 2.7 %collective-permute-start.11 = (bf16[160,1024]{1,0:T(8,128)(2,1)}, bf16[160,1024]{1,0:T(8,128)(2,1)}, u32[]{:S(2)}, u32[]{:S(2)}) collective-permute-start(bf16[160,1024]{1,0:T(8,128)(2,1)} %get-tuple-element.34), channel_id=1, source_target_pairs={{0,4},{1,5},{2,6},{3,7},{4,8},{5,9},{6,10},{7,11},{8,12},{9,13},{1... | collective-permute-start | bytes 983048 | tf_op jit(solution)/shard_map/ppermute | solution.py:342
  119.8 0.1 collective-permute-done.14.rest_5_
  120.0 0.9 copy-done.8
  120.8 8.8 %query.1.query_ref = f32[512,1024]{1,0:T(8,128)S(1)} custom-call(s32[6]{0:T(128)S(1)} %stack.34.at_ref, bf16[512,4096]{1,0:T(8,128)(2,1)} %all-gather.3.cloned.1.call-done.x_ref, bf16[16,4096]{1,0:T(8,128)(2,1)} %copy-done.10, f32[3,3,1024]{2,1,0:T(4,128)S(1)} %copy-done.3, bf16[3,1024,1024]{2,1,0:T(8,128)(2,1)} %bitcast.25, ...), custom_call_target="tpu_custom_call" | custom-call | tf_op jit(solution)/shard_map/query/pallas_call | solution.py:209
  129.6 5.4 %mix.1 = bf16[512,1024]{1,0:T(8,128)(2,1)S(1)} custom-call(bf16[512,1024]{1,0:T(8,128)(2,1)} %get-tuple-element.31.gated_ref, bf16[160,1024]{1,0:T(8,128)(2,1)} %collective-permute-done.11.halo_ref, bf16[2,16,1024]{2,1,0:T(8,128)(2,1)} %get-tuple-element.35.head_ref, f32[3,3,1024]{2,1,0:T(4,128)S(1)} %copy-done.3, f32[3,128,1024]{2,1,0:T(8,128)} %respond.1.response_ref, ...), custom_call_target="tpu_custom_call" | custom-call | tf_op jit(solution)/shard_map/mix/pallas_call | solution.py:302
  135.0 2.9 %convolution_convert_fusion.1 = bf16[512,1024]{1,0:T(8,128)(2,1)S(1)} fusion(bf16[512,1024]{1,0:T(8,128)(2,1)S(1)} %mix.1, bf16[1024,1024]{1,0:T(8,128)(2,1)} %param.15), kind=kOutput, calls=%fused_computation.7 | convolution fusion | flops 1074266112 | bytes 4194304 | tf_op jit(solution)/shard_map/dot_general | solution.py:420
  137.9 0.8 constant_dynamic-slice_fusion
  138.7 3.3 %collective-permute-start.25 = (bf16[256,1024]{1,0:T(8,128)(2,1)}, bf16[256,1024]{1,0:T(8,128)(2,1)}, u32[]{:S(2)}, u32[]{:S(2)}) collective-permute-start(bf16[256,1024]{1,0:T(8,128)(2,1)} %constant_dynamic-slice_fusion), channel_id=1, source_target_pairs={{0,1},{3,2},{4,5},{7,6},{8,9},{11,10},{12,13},{15,14},{16,17},{19,... | collective-permute-start | bytes 1572872 | tf_op jit(solution)/shard_map/ppermute | solution.py:342
  142.0 2.9 %convolution_convert_fusion = bf16[512,1024]{1,0:T(8,128)(2,1)S(1)} fusion(bf16[512,1024]{1,0:T(8,128)(2,1)S(1)} %mix.1, bf16[1024,1024]{1,0:T(8,128)(2,1)} %collective-permute-done.15), kind=kOutput, calls=%fused_computation.6 | convolution fusion | flops 1074266112 | bytes 4194304 | tf_op jit(solution)/shard_map/dot_general | solution.py:420
  144.9 0.8 constant_dynamic-slice_fusion.1
  145.8 2.1 collective-permute-start.22
  147.9 5.3 %all-gather.5.cloned.1.call-done = bf16[4096,1024]{1,0:T(8,128)(2,1)} async-done(((bf16[1024,1024]{1,0:T(8,128)(2,1)}), bf16[4096,1024]{1,0:T(8,128)(2,1)}) %all-gather.5.cloned.1.call-update) | async-done | bytes 8388624 | tf_op jit(solution)/shard_map/all_gather | solution.py:406
  153.2 2.9 %fusion.4 = bf16[512,1024]{1,0:T(8,128)(2,1)S(1)} fusion(bf16[512,1024]{1,0:T(8,128)(2,1)S(1)} %mix.1, bf16[4096,1024]{1,0:T(8,128)(2,1)} %all-gather.5.cloned.1.call-done, s32[]{:T(128)S(6)} %select_n.123), kind=kOutput, calls=%fused_computation.4 | convolution fusion | flops 1074266112 | bytes 4194308 | tf_op jit(solution)/shard_map/dot_general | solution.py:420
  156.1 3.7 %collective-permute-start.19 = (bf16[256,1024]{1,0:T(8,128)(2,1)S(1)}, bf16[256,1024]{1,0:T(8,128)(2,1)S(1)}, u32[]{:S(2)}, u32[]{:S(2)}) collective-permute-start(bf16[256,1024]{1,0:T(8,128)(2,1)S(1)} %constant_dynamic-slice_fusion.2), channel_id=1, source_target_pairs={{0,1},{3,2},{4,5},{7,6},{8,9},{11,10},{12,13},{15,14},{16,17},{19,... | collective-permute-start | bytes 1572872 | tf_op jit(solution)/shard_map/ppermute | solution.py:342
  159.8 2.9 %fusion.7 = bf16[512,1024]{1,0:T(8,128)(2,1)S(1)} fusion(bf16[512,1024]{1,0:T(8,128)(2,1)S(1)} %mix.1, bf16[4096,1024]{1,0:T(8,128)(2,1)} %all-gather.5.cloned.1.call-done, s32[]{:T(128)S(6)} %select_n.124), kind=kOutput, calls=%fused_computation.5 | convolution fusion | flops 1074266112 | bytes 4194308 | tf_op jit(solution)/shard_map/dot_general | solution.py:420
  162.7 1.3 collective-permute-start.16
  164.0 1.2 add_convert_fusion
  165.3 0.7 collective-permute-start.26
  166.0 1.2 add_convert_fusion.1
  167.2 0.7 collective-permute-start.23
  167.9 6.7 %collective-permute-done.19 = bf16[256,1024]{1,0:T(8,128)(2,1)S(1)} collective-permute-done((bf16[256,1024]{1,0:T(8,128)(2,1)S(1)}, bf16[256,1024]{1,0:T(8,128)(2,1)S(1)}, u32[]{:S(2)}, u32[]{:S(2)}) %collective-permute-start.19) | collective-permute-done | bytes 524320 | tf_op jit(solution)/shard_map/ppermute | solution.py:342
  174.7 0.2 add_convert_fusion.2
  174.9 0.7 collective-permute-start.20
  175.6 10.3 %collective-permute-done.16 = bf16[256,1024]{1,0:T(8,128)(2,1)S(1)} collective-permute-done((bf16[256,1024]{1,0:T(8,128)(2,1)S(1)}, bf16[256,1024]{1,0:T(8,128)(2,1)S(1)}, u32[]{:S(2)}, u32[]{:S(2)}) %collective-permute-start.16) | collective-permute-done | bytes 524320 | tf_op jit(solution)/shard_map/ppermute | solution.py:342
  185.9 0.2 add_convert_fusion.3
  186.1 0.7 collective-permute-start.17
  186.8 0.1 add_convert_fusion.5
  187.0 5.3 %collective-permute-start.27 = (bf16[128,1024]{1,0:T(8,128)(2,1)S(1)}, bf16[128,1024]{1,0:T(8,128)(2,1)S(1)}, u32[]{:S(2)}, u32[]{:S(2)}) collective-permute-start(bf16[128,1024]{1,0:T(8,128)(2,1)S(1)} %add_convert_fusion.5), channel_id=1, source_target_pairs={{0,1},{1,0},{2,3},{3,2},{4,5},{5,4},{6,7},{7,6},{8,9},{9,8},{10,11... | collective-permute-start | bytes 786440 | tf_op jit(solution)/shard_map/ppermute | solution.py:342
  192.2 0.1 add_convert_fusion.7
  192.4 0.4 collective-permute-start.24
  192.7 0.1 add_convert_fusion.9
  192.9 11.1 %collective-permute-start.21 = (bf16[128,1024]{1,0:T(8,128)(2,1)S(1)}, bf16[128,1024]{1,0:T(8,128)(2,1)S(1)}, u32[]{:S(2)}, u32[]{:S(2)}) collective-permute-start(bf16[128,1024]{1,0:T(8,128)(2,1)S(1)} %add_convert_fusion.9), channel_id=1, source_target_pairs={{0,1},{1,0},{2,3},{3,2},{4,5},{5,4},{6,7},{7,6},{8,9},{9,8},{10,11... | collective-permute-start | bytes 786440 | tf_op jit(solution)/shard_map/ppermute | solution.py:342
  204.0 0.1 add_convert_fusion.11
  204.1 10.0 %collective-permute-start.18 = (bf16[128,1024]{1,0:T(8,128)(2,1)S(1)}, bf16[128,1024]{1,0:T(8,128)(2,1)S(1)}, u32[]{:S(2)}, u32[]{:S(2)}) collective-permute-start(bf16[128,1024]{1,0:T(8,128)(2,1)S(1)} %add_convert_fusion.11), channel_id=1, source_target_pairs={{0,1},{1,0},{2,3},{3,2},{4,5},{5,4},{6,7},{7,6},{8,9},{9,8},{10,11... | collective-permute-start | bytes 786440 | tf_op jit(solution)/shard_map/ppermute | solution.py:342
  214.1 0.4 broadcast_select_fusion.3
  214.5 5.0 %collective-permute-done.18 = bf16[128,1024]{1,0:T(8,128)(2,1)S(1)} collective-permute-done((bf16[128,1024]{1,0:T(8,128)(2,1)S(1)}, bf16[128,1024]{1,0:T(8,128)(2,1)S(1)}, u32[]{:S(2)}, u32[]{:S(2)}) %collective-permute-start.18) | collective-permute-done | bytes 262176 | tf_op jit(solution)/shard_map/ppermute | solution.py:342
  219.5 0.4 broadcast_select_fusion.5
  220.0 0.2 broadcast_select_fusion.1
  220.2 1.0 pad_maximum_fusion
  (54 shorter events, 0.4 us)
Async XLA Ops:
  6.5 1.6 copy-start
  6.5 1.4 copy-start.11
  6.5 87.1 %all-gather.3.cloned.1.call-start = ((), (), s32[]{:S(2)}) async-start(), calls=%async_computation | async-start | bytes 5242880 | tf_op jit(solution)/shard_map/all_gather | solution.py:395
  10.0 143.1 %all-gather.5.cloned.1.call-start = ((), (), s32[]{:S(2)}) async-start(), calls=%async_computation.1 | async-start | bytes 10485760 | tf_op jit(solution)/shard_map/all_gather | solution.py:406
  10.1 26.2 %collective-permute-start.1 = (bf16[512,1024]{1,0:T(8,128)(2,1)S(1)}, bf16[512,1024]{1,0:T(8,128)(2,1)S(1)}, u32[]{:S(2)}, u32[]{:S(2)}) collective-permute-start(bf16[512,1024]{1,0:T(8,128)(2,1)S(1)} %dynamic-slice_bitcast_fusion.2), channel_id=1, source_target_pairs={{0,8},{1,9},{2,10},{3,11},{4,12},{5,13},{6,14},{7,15},{8,0},{9,1},... | collective-permute-start | bytes 3145736 | tf_op jit(solution)/shard_map/ppermute | solution.py:342
  36.3 30.9 %copy-start.9 = (bf16[512,1024]{1,0:T(8,128)(2,1)}, bf16[512,1024]{1,0:T(8,128)(2,1)S(1)}, u32[]{:S(2)}) copy-start(bf16[512,1024]{1,0:T(8,128)(2,1)S(1)} %collective-permute-done.1.rest_2_) | copy-start | bytes 3145732
  36.3 5.6 %copy-start.1 = (f32[128,1024]{1,0:T(8,128)S(1)}, f32[128,1024]{1,0:T(8,128)}, u32[]{:S(2)}) copy-start(f32[128,1024]{1,0:T(8,128)} %filter_ref.1) | copy-start | bytes 1572868
  36.3 5.6 %copy-start.2 = (bf16[256,256]{1,0:T(8,128)(2,1)S(1)}, bf16[256,256]{1,0:T(8,128)(2,1)}, u32[]{:S(2)}) copy-start(bf16[256,256]{1,0:T(8,128)(2,1)} %constant.52.clone.fwd_ref) | copy-start | bytes 393220
  36.3 5.6 %copy-start.5 = (f32[1024]{0:T(1024)S(1)}, f32[1024]{0:T(1024)}, u32[]{:S(2)}) copy-start(f32[1024]{0:T(1024)} %param.14) | copy-start | bytes 12292
  36.3 29.3 %collective-permute-start = (bf16[3,1024,1024]{2,1,0:T(8,128)(2,1)}, bf16[3,1024,1024]{2,1,0:T(8,128)(2,1)}, u32[]{:S(2)}, u32[]{:S(2)}) collective-permute-start(bf16[3,1024,1024]{2,1,0:T(8,128)(2,1)} %bitcast.21), channel_id=1, source_target_pairs={{0,4},{1,5},{2,6},{3,7},{4,0},{5,1},{6,2},{7,3},{8,12},{9,13},{10,... | collective-permute-start | bytes 18874376 | tf_op jit(solution)/shard_map/ppermute | solution.py:342
  38.6 55.1 %copy-start.3 = (f32[3,3,1024]{2,1,0:T(4,128)S(1)}, f32[3,3,1024]{2,1,0:T(4,128)}, u32[]{:S(2)}) copy-start(f32[3,3,1024]{2,1,0:T(4,128)} %short_ref.1) | copy-start | bytes 110596
  38.6 25.3 %collective-permute-start.5 = (bf16[512,1024]{1,0:T(8,128)(2,1)S(1)}, bf16[512,1024]{1,0:T(8,128)(2,1)}, u32[]{:S(2)}, u32[]{:S(2)}) collective-permute-start(bf16[512,1024]{1,0:T(8,128)(2,1)S(1)} %get-tuple-element.27), channel_id=1, source_target_pairs={{0,8},{1,9},{2,10},{3,11},{4,12},{5,13},{6,14},{7,15},{8,0},{9,1},... | collective-permute-start | bytes 3145736 | tf_op jit(solution)/shard_map/ppermute | solution.py:342
  40.4 25.2 %collective-permute-start.3 = (bf16[512,1024]{1,0:T(8,128)(2,1)S(1)}, bf16[512,1024]{1,0:T(8,128)(2,1)}, u32[]{:S(2)}, u32[]{:S(2)}) collective-permute-start(bf16[512,1024]{1,0:T(8,128)(2,1)S(1)} %collective-permute-done.1.rest_2_), channel_id=1, source_target_pairs={{0,16},{1,17},{2,18},{3,19},{4,20},{5,21},{6,22},{7,23},{8,24},{9,... | collective-permute-start | bytes 3145736 | tf_op jit(solution)/shard_map/ppermute | solution.py:342
  63.9 24.3 %collective-permute-start.8 = (bf16[512,1024]{1,0:T(8,128)(2,1)S(1)}, bf16[512,1024]{1,0:T(8,128)(2,1)S(1)}, u32[]{:S(2)}, u32[]{:S(2)}) collective-permute-start(bf16[512,1024]{1,0:T(8,128)(2,1)S(1)} %get-tuple-element.29), channel_id=1, source_target_pairs={{0,8},{1,9},{2,10},{3,11},{4,12},{5,13},{6,14},{7,15},{8,0},{9,1},... | collective-permute-start | bytes 3145736 | tf_op jit(solution)/shard_map/ppermute | solution.py:342
  65.6 24.3 %collective-permute-start.7 = (bf16[512,1024]{1,0:T(8,128)(2,1)}, bf16[512,1024]{1,0:T(8,128)(2,1)}, u32[]{:S(2)}, u32[]{:S(2)}) collective-permute-start(bf16[512,1024]{1,0:T(8,128)(2,1)} %collective-permute-done.5.rest_8_), channel_id=1, source_target_pairs={{0,16},{1,17},{2,18},{3,19},{4,20},{5,21},{6,22},{7,23},{8,24},{9,... | collective-permute-start | bytes 3145736 | tf_op jit(solution)/shard_map/ppermute | solution.py:342
  67.1 24.4 %collective-permute-start.2 = (bf16[512,1024]{1,0:T(8,128)(2,1)S(1)}, bf16[512,1024]{1,0:T(8,128)(2,1)}, u32[]{:S(2)}, u32[]{:S(2)}) collective-permute-start(bf16[512,1024]{1,0:T(8,128)(2,1)S(1)} %collective-permute-done.1.rest_2_), channel_id=1, source_target_pairs={{0,4},{1,5},{2,6},{3,7},{4,0},{5,1},{6,2},{7,3},{8,12},{9,13},{10,... | collective-permute-start | bytes 3145736 | tf_op jit(solution)/shard_map/ppermute | solution.py:342
  67.1 24.4 %collective-permute-start.6 = (bf16[512,1024]{1,0:T(8,128)(2,1)}, bf16[512,1024]{1,0:T(8,128)(2,1)}, u32[]{:S(2)}, u32[]{:S(2)}) collective-permute-start(bf16[512,1024]{1,0:T(8,128)(2,1)} %collective-permute-done.5.rest_8_), channel_id=1, source_target_pairs={{0,4},{1,5},{2,6},{3,7},{4,0},{5,1},{6,2},{7,3},{8,12},{9,13},{10,... | collective-permute-start | bytes 3145736 | tf_op jit(solution)/shard_map/ppermute | solution.py:342
  67.7 23.9 %collective-permute-start.4 = (bf16[512,1024]{1,0:T(8,128)(2,1)}, bf16[512,1024]{1,0:T(8,128)(2,1)}, u32[]{:S(2)}, u32[]{:S(2)}) collective-permute-start(bf16[512,1024]{1,0:T(8,128)(2,1)} %collective-permute-done.3.rest_4_), channel_id=1, source_target_pairs={{0,4},{1,5},{2,6},{3,7},{4,0},{5,1},{6,2},{7,3},{8,12},{9,13},{10,... | collective-permute-start | bytes 3145736 | tf_op jit(solution)/shard_map/ppermute | solution.py:342
  88.2 23.4 %copy-start.6 = (bf16[512,1024]{1,0:T(8,128)(2,1)}, bf16[512,1024]{1,0:T(8,128)(2,1)S(1)}, u32[]{:S(2)}) copy-start(bf16[512,1024]{1,0:T(8,128)(2,1)S(1)} %collective-permute-done.8.rest_2_) | copy-start | bytes 3145732
  90.0 3.7 %collective-permute-start.9 = (bf16[512,1024]{1,0:T(8,128)(2,1)}, bf16[512,1024]{1,0:T(8,128)(2,1)}, u32[]{:S(2)}, u32[]{:S(2)}) collective-permute-start(bf16[512,1024]{1,0:T(8,128)(2,1)} %collective-permute-done.7.rest_10_), channel_id=1, source_target_pairs={{0,4},{1,5},{2,6},{3,7},{4,0},{5,1},{6,2},{7,3},{8,12},{9,13},{10,... | collective-permute-start | bytes 3145736 | tf_op jit(solution)/shard_map/ppermute | solution.py:342
  90.0 25.6 %collective-permute-start.13 = (bf16[512,1024]{1,0:T(8,128)(2,1)S(1)}, bf16[512,1024]{1,0:T(8,128)(2,1)S(1)}, u32[]{:S(2)}, u32[]{:S(2)}) collective-permute-start(bf16[512,1024]{1,0:T(8,128)(2,1)S(1)} %collective-permute-done.8.rest_2_), channel_id=1, source_target_pairs={{0,16},{1,17},{2,18},{3,19},{4,20},{5,21},{6,22},{7,23},{8,24},{9,... | collective-permute-start | bytes 3145736 | tf_op jit(solution)/shard_map/ppermute | solution.py:342
  108.1 33.9 %collective-permute-start.15 = (bf16[1024,1024]{1,0:T(8,128)(2,1)}, bf16[1024,1024]{1,0:T(8,128)(2,1)}, u32[]{:S(2)}, u32[]{:S(2)}) collective-permute-start(bf16[1024,1024]{1,0:T(8,128)(2,1)} %param.15), channel_id=1, source_target_pairs={{0,4},{1,5},{2,6},{3,7},{4,0},{5,1},{6,2},{7,3},{8,12},{9,13},{10,... | collective-permute-start | bytes 6291464 | tf_op jit(solution)/shard_map/ppermute | solution.py:342
  109.1 6.4 %collective-permute-start.10 = (bf16[16,4096]{1,0:T(8,128)(2,1)S(1)}, bf16[16,4096]{1,0:T(8,128)(2,1)S(1)}, u32[]{:S(2)}, u32[]{:S(2)}) collective-permute-start(bf16[16,4096]{1,0:T(8,128)(2,1)S(1)} %slice.36), channel_id=1, source_target_pairs={{0,4},{1,5},{2,6},{3,7},{4,8},{5,9},{6,10},{7,11},{8,12},{9,13},{1... | collective-permute-start | bytes 393224 | tf_op jit(solution)/shard_map/ppermute | solution.py:342
  111.6 8.3 %collective-permute-start.12 = (bf16[512,1024]{1,0:T(8,128)(2,1)S(1)}, bf16[512,1024]{1,0:T(8,128)(2,1)S(1)}, u32[]{:S(2)}, u32[]{:S(2)}) collective-permute-start(bf16[512,1024]{1,0:T(8,128)(2,1)S(1)} %collective-permute-done.8.rest_2_), channel_id=1, source_target_pairs={{0,4},{1,5},{2,6},{3,7},{4,0},{5,1},{6,2},{7,3},{8,12},{9,13},{10,... | collective-permute-start | bytes 3145736 | tf_op jit(solution)/shard_map/ppermute | solution.py:342
  115.5 4.4 %copy-start.7 = (bf16[512,1024]{1,0:T(8,128)(2,1)}, bf16[512,1024]{1,0:T(8,128)(2,1)S(1)}, u32[]{:S(2)}) copy-start(bf16[512,1024]{1,0:T(8,128)(2,1)S(1)} %collective-permute-done.13.rest_4_) | copy-start | bytes 3145732
  115.5 4.4 %copy-start.10 = (bf16[16,4096]{1,0:T(8,128)(2,1)}, bf16[16,4096]{1,0:T(8,128)(2,1)S(1)}, u32[]{:S(2)}) copy-start(bf16[16,4096]{1,0:T(8,128)(2,1)S(1)} %collective-permute-done.10.before_ref) | copy-start | bytes 393220
  115.5 4.4 %collective-permute-start.14 = (bf16[512,1024]{1,0:T(8,128)(2,1)S(1)}, bf16[512,1024]{1,0:T(8,128)(2,1)}, u32[]{:S(2)}, u32[]{:S(2)}) collective-permute-start(bf16[512,1024]{1,0:T(8,128)(2,1)S(1)} %collective-permute-done.13.rest_4_), channel_id=1, source_target_pairs={{0,4},{1,5},{2,6},{3,7},{4,0},{5,1},{6,2},{7,3},{8,12},{9,13},{10,... | collective-permute-start | bytes 3145736 | tf_op jit(solution)/shard_map/ppermute | solution.py:342
  117.2 12.4 %collective-permute-start.11 = (bf16[160,1024]{1,0:T(8,128)(2,1)}, bf16[160,1024]{1,0:T(8,128)(2,1)}, u32[]{:S(2)}, u32[]{:S(2)}) collective-permute-start(bf16[160,1024]{1,0:T(8,128)(2,1)} %get-tuple-element.34), channel_id=1, source_target_pairs={{0,4},{1,5},{2,6},{3,7},{4,8},{5,9},{6,10},{7,11},{8,12},{9,13},{1... | collective-permute-start | bytes 983048 | tf_op jit(solution)/shard_map/ppermute | solution.py:342
  119.8 9.8 %copy-start.4 = (bf16[128,768]{1,0:T(8,128)(2,1)S(1)}, bf16[128,768]{1,0:T(8,128)(2,1)}, u32[]{:S(2)}) copy-start(bf16[128,768]{1,0:T(8,128)(2,1)} %constant.53.clone.inv_ref) | copy-start | bytes 589828
  119.8 1.0 copy-start.8
  138.7 25.3 %collective-permute-start.25 = (bf16[256,1024]{1,0:T(8,128)(2,1)}, bf16[256,1024]{1,0:T(8,128)(2,1)}, u32[]{:S(2)}, u32[]{:S(2)}) collective-permute-start(bf16[256,1024]{1,0:T(8,128)(2,1)} %constant_dynamic-slice_fusion), channel_id=1, source_target_pairs={{0,1},{3,2},{4,5},{7,6},{8,9},{11,10},{12,13},{15,14},{16,17},{19,... | collective-permute-start | bytes 1572872 | tf_op jit(solution)/shard_map/ppermute | solution.py:342
  145.8 20.2 %collective-permute-start.22 = (bf16[256,1024]{1,0:T(8,128)(2,1)}, bf16[256,1024]{1,0:T(8,128)(2,1)}, u32[]{:S(2)}, u32[]{:S(2)}) collective-permute-start(bf16[256,1024]{1,0:T(8,128)(2,1)} %constant_dynamic-slice_fusion.1), channel_id=1, source_target_pairs={{0,1},{3,2},{4,5},{7,6},{8,9},{11,10},{12,13},{15,14},{16,17},{19,... | collective-permute-start | bytes 1572872 | tf_op jit(solution)/shard_map/ppermute | solution.py:342
  156.1 18.6 %collective-permute-start.19 = (bf16[256,1024]{1,0:T(8,128)(2,1)S(1)}, bf16[256,1024]{1,0:T(8,128)(2,1)S(1)}, u32[]{:S(2)}, u32[]{:S(2)}) collective-permute-start(bf16[256,1024]{1,0:T(8,128)(2,1)S(1)} %constant_dynamic-slice_fusion.2), channel_id=1, source_target_pairs={{0,1},{3,2},{4,5},{7,6},{8,9},{11,10},{12,13},{15,14},{16,17},{19,... | collective-permute-start | bytes 1572872 | tf_op jit(solution)/shard_map/ppermute | solution.py:342
  162.7 23.2 %collective-permute-start.16 = (bf16[256,1024]{1,0:T(8,128)(2,1)S(1)}, bf16[256,1024]{1,0:T(8,128)(2,1)S(1)}, u32[]{:S(2)}, u32[]{:S(2)}) collective-permute-start(bf16[256,1024]{1,0:T(8,128)(2,1)S(1)} %constant_dynamic-slice_fusion.3), channel_id=1, source_target_pairs={{0,1},{3,2},{4,5},{7,6},{8,9},{11,10},{12,13},{15,14},{16,17},{19,... | collective-permute-start | bytes 1572872 | tf_op jit(solution)/shard_map/ppermute | solution.py:342
  165.3 21.5 %collective-permute-start.26 = (bf16[256,1024]{1,0:T(8,128)(2,1)S(1)}, bf16[256,1024]{1,0:T(8,128)(2,1)S(1)}, u32[]{:S(2)}, u32[]{:S(2)}) collective-permute-start(bf16[256,1024]{1,0:T(8,128)(2,1)S(1)} %add_convert_fusion), channel_id=1, source_target_pairs={{1,2},{2,1},{5,6},{6,5},{9,10},{10,9},{13,14},{14,13},{17,18},{18,... | collective-permute-start | bytes 1572872 | tf_op jit(solution)/shard_map/ppermute | solution.py:342
  167.2 25.0 %collective-permute-start.23 = (bf16[256,1024]{1,0:T(8,128)(2,1)S(1)}, bf16[256,1024]{1,0:T(8,128)(2,1)S(1)}, u32[]{:S(2)}, u32[]{:S(2)}) collective-permute-start(bf16[256,1024]{1,0:T(8,128)(2,1)S(1)} %add_convert_fusion.1), channel_id=1, source_target_pairs={{1,2},{2,1},{5,6},{6,5},{9,10},{10,9},{13,14},{14,13},{17,18},{18,... | collective-permute-start | bytes 1572872 | tf_op jit(solution)/shard_map/ppermute | solution.py:342
  174.9 17.9 %collective-permute-start.20 = (bf16[256,1024]{1,0:T(8,128)(2,1)S(1)}, bf16[256,1024]{1,0:T(8,128)(2,1)S(1)}, u32[]{:S(2)}, u32[]{:S(2)}) collective-permute-start(bf16[256,1024]{1,0:T(8,128)(2,1)S(1)} %add_convert_fusion.2), channel_id=1, source_target_pairs={{1,2},{2,1},{5,6},{6,5},{9,10},{10,9},{13,14},{14,13},{17,18},{18,... | collective-permute-start | bytes 1572872 | tf_op jit(solution)/shard_map/ppermute | solution.py:342
  186.1 17.9 %collective-permute-start.17 = (bf16[256,1024]{1,0:T(8,128)(2,1)S(1)}, bf16[256,1024]{1,0:T(8,128)(2,1)S(1)}, u32[]{:S(2)}, u32[]{:S(2)}) collective-permute-start(bf16[256,1024]{1,0:T(8,128)(2,1)S(1)} %add_convert_fusion.3), channel_id=1, source_target_pairs={{1,2},{2,1},{5,6},{6,5},{9,10},{10,9},{13,14},{14,13},{17,18},{18,... | collective-permute-start | bytes 1572872 | tf_op jit(solution)/shard_map/ppermute | solution.py:342
  187.0 27.1 %collective-permute-start.27 = (bf16[128,1024]{1,0:T(8,128)(2,1)S(1)}, bf16[128,1024]{1,0:T(8,128)(2,1)S(1)}, u32[]{:S(2)}, u32[]{:S(2)}) collective-permute-start(bf16[128,1024]{1,0:T(8,128)(2,1)S(1)} %add_convert_fusion.5), channel_id=1, source_target_pairs={{0,1},{1,0},{2,3},{3,2},{4,5},{5,4},{6,7},{7,6},{8,9},{9,8},{10,11... | collective-permute-start | bytes 786440 | tf_op jit(solution)/shard_map/ppermute | solution.py:342
  192.4 21.7 %collective-permute-start.24 = (bf16[128,1024]{1,0:T(8,128)(2,1)S(1)}, bf16[128,1024]{1,0:T(8,128)(2,1)S(1)}, u32[]{:S(2)}, u32[]{:S(2)}) collective-permute-start(bf16[128,1024]{1,0:T(8,128)(2,1)S(1)} %add_convert_fusion.7), channel_id=1, source_target_pairs={{0,1},{1,0},{2,3},{3,2},{4,5},{5,4},{6,7},{7,6},{8,9},{9,8},{10,11... | collective-permute-start | bytes 786440 | tf_op jit(solution)/shard_map/ppermute | solution.py:342
  192.9 21.7 %collective-permute-start.21 = (bf16[128,1024]{1,0:T(8,128)(2,1)S(1)}, bf16[128,1024]{1,0:T(8,128)(2,1)S(1)}, u32[]{:S(2)}, u32[]{:S(2)}) collective-permute-start(bf16[128,1024]{1,0:T(8,128)(2,1)S(1)} %add_convert_fusion.9), channel_id=1, source_target_pairs={{0,1},{1,0},{2,3},{3,2},{4,5},{5,4},{6,7},{7,6},{8,9},{9,8},{10,11... | collective-permute-start | bytes 786440 | tf_op jit(solution)/shard_map/ppermute | solution.py:342
  204.1 15.4 %collective-permute-start.18 = (bf16[128,1024]{1,0:T(8,128)(2,1)S(1)}, bf16[128,1024]{1,0:T(8,128)(2,1)S(1)}, u32[]{:S(2)}, u32[]{:S(2)}) collective-permute-start(bf16[128,1024]{1,0:T(8,128)(2,1)S(1)} %add_convert_fusion.11), channel_id=1, source_target_pairs={{0,1},{1,0},{2,3},{3,2},{4,5},{5,4},{6,7},{7,6},{8,9},{9,8},{10,11... | collective-permute-start | bytes 786440 | tf_op jit(solution)/shard_map/ppermute | solution.py:342
Sparse Core Ops, SparseCore 0:
  10.2 83.4 all-gather.2
  95.2 57.8 all-gather.4

commit v6 on v5

--- a/solution.py
+++ b/solution.py
@@ -113,6 +113,7 @@
 
 
 def add_up(kinds, width, waits, full, weight, s, first):
+    rows = slice(first, None)
     channels = weight.shape[1]
     for n, (low, high) in enumerate(spans(kinds)):
         for copies in waits:
@@ -123,10 +124,10 @@
                 full[:, low:high], weight[low:high, columns], preferred_element_type=f32
             )
             if n > 0:
-                term = s[first:, columns] + term
-            if n == len(kinds) - 1:
+                term = s[rows, columns] + term
+            if n == len(kinds) - 1 and first is not None:
                 term = term.astype(bf16).astype(f32)
-            s[first:, columns] = term
+            s[rows, columns] = term
 
 
 def gate_kernel(one, two, width, at_ref, x_ref, taps_ref, *rest):
@@ -185,11 +186,29 @@
             pltpu.SemaphoreType.DMA((3, len(one))),
         ],
         compiler_params=pltpu.CompilerParams(vmem_limit_bytes=40 << 20),
+        cost_estimate=pl.CostEstimate(
+            flops=4 * slab * features * channels,
+            transcendentals=0,
+            bytes_accessed=2 * features * (slab + 2 * channels),
+        ),
         name="gate",
     )(offsets(one), hold(x), short_filter, *[hold(p[0]) for p in one + two])
 
 
-def query_kernel(kinds, width, at_ref, x_ref, before_ref, taps_ref, *rest):
+def query_start_kernel(kinds, width, at_ref, x_ref, before_ref, *rest):
+    arrays = rest[: len(kinds)]
+    sum_ref, full, weight, sems = rest[len(arrays) :]
+    slab = x_ref.shape[0]
+    x_copies = token_copies(kinds, at_ref, x_ref, full.at[edge : edge + slab], sems.at[0])
+    e_copies = token_copies(kinds, at_ref, before_ref, full.at[0:edge], sems.at[1])
+    copies = weight_copies(kinds, arrays, weight, sems.at[2])
+    for group in zip(e_copies, x_copies, copies):
+        for copy in group:
+            copy.start()
+    add_up(kinds, width, (e_copies, x_copies, copies), full, weight, sum_ref, None)
+
+
+def query_end_kernel(kinds, width, at_ref, x_ref, before_ref, sum_ref, taps_ref, *rest):
     arrays = rest[: len(kinds)]
     out_ref, full, weight, s, sems = rest[len(arrays) :]
     slab, channels = out_ref.shape
@@ -199,27 +218,65 @@
     for group in zip(e_copies, x_copies, copies):
         for copy in group:
             copy.start()
-    add_up(kinds, width, (e_copies, x_copies, copies), full, weight, s, 0)
-    out_ref[...] = short_sum(s, taps_ref, 0, slab)
-
-
-def query(x, before, pieces, short_filter, width):
+    for group in zip(e_copies, x_copies, copies):
+        for copy in group:
+            copy.wait()
+    for i in range(channels // width):
+        columns = slice(i * width, (i + 1) * width)
+        term = jnp.dot(full[...], weight[:, columns], preferred_element_type=f32)
+        s[...] = (sum_ref[:, columns] + term).astype(bf16).astype(f32)
+        out_ref[:, columns] = short_sum(s, taps_ref[:, :, columns], 0, slab)
+
+
+def query_start(x, before, pieces, width):
+    slab, features = x.shape
+    channels = pieces[0][0].shape[-1]
+    kinds = kinds_of(pieces)
+    depth = sum(k[1] for k in kinds)
+    return pl.pallas_call(
+        functools.partial(query_start_kernel, kinds, width),
+        in_specs=[in_smem, in_hbm, in_hbm] + [in_hbm] * len(pieces),
+        out_specs=in_vmem,
+        out_shape=jax.ShapeDtypeStruct((slab + edge, channels), f32),
+        scratch_shapes=[
+            pltpu.VMEM((slab + edge, depth), bf16),
+            pltpu.VMEM((depth, channels), bf16),
+            pltpu.SemaphoreType.DMA((3, len(pieces))),
+        ],
+        compiler_params=pltpu.CompilerParams(vmem_limit_bytes=24 << 20),
+        cost_estimate=pl.CostEstimate(
+            flops=2 * slab * depth * channels,
+            transcendentals=0,
+            bytes_accessed=2 * depth * (slab + channels),
+        ),
+        name="query_start",
+    )(offsets(pieces), hold(x), hold(before), *[hold(p[0]) for p in pieces])
+
+
+def query_end(x, before, pieces, total, short_filter, width):
     slab, features = x.shape
     channels = short_filter.shape[-1]
+    kinds = kinds_of(pieces)
+    depth = sum(k[1] for k in kinds)
     return pl.pallas_call(
-        functools.partial(query_kernel, kinds_of(pieces), width),
-        in_specs=[in_smem, in_hbm, in_hbm, in_vmem] + [in_hbm] * len(pieces),
+        functools.partial(query_end_kernel, kinds, width),
+        in_specs=[in_smem, in_hbm, in_hbm, in_vmem, in_vmem] + [in_hbm] * len(pieces),
         out_specs=in_vmem,
         out_shape=jax.ShapeDtypeStruct((slab, channels), f32),
         scratch_shapes=[
-            pltpu.VMEM((slab + edge, features), bf16),
-            pltpu.VMEM((features, channels), bf16),
-            pltpu.VMEM((slab + edge, channels), f32),
+            pltpu.VMEM((slab + edge, depth), bf16),
+            pltpu.VMEM((depth, channels), bf16),
+            pltpu.VMEM((slab + edge, width), f32),
             pltpu.SemaphoreType.DMA((3, len(pieces))),
         ],
-        compiler_params=pltpu.CompilerParams(vmem_limit_bytes=32 << 20),
-        name="query",
-    )(offsets(pieces), hold(x), hold(before), short_filter, *[hold(p[0]) for p in pieces])
+        compiler_params=pltpu.CompilerParams(vmem_limit_bytes=24 << 20),
+        cost_estimate=pl.CostEstimate(
+            flops=2 * slab * depth * channels,
+            transcendentals=0,
+            bytes_accessed=2 * depth * (slab + channels),
+        ),
+        name="query_end",
+    )(offsets(pieces), hold(x), hold(before), total, short_filter, *[hold(p[0]) for p in pieces])
 
 
 def transform(fwd_ref, block):
@@ -352,6 +409,16 @@
     def after(value, *earlier):
         return lax.optimization_barrier((value, *earlier))[0]
 
+    def hop(value, held):
+        first, last = max(0, count - 2 * held), count - held
+        return value + move(
+            value,
+            lambda i, j, k: (i, j, k - held) if k - held >= first and k >= last else (i, j, -1),
+        )
+
+    def from_last_slab(value):
+        return move(value, lambda i, j, k: (i, j + 1, k) if k == count - 1 else (i, -1, k))
+
     medium_count = medium_filter.shape[0]
     tables = fourier_tables(medium_count)
     weights = jnp.transpose(w_in, (1, 0, 2))
@@ -372,7 +439,9 @@
         far[1] = to_group(near[1])
         source = after(weights, normed)
         near[2] = to_chip(after(cut(source, 2, first_half, half), near[1]))
-        far[2] = to_group(after(near[2], far[1], response, peer))
+        before_rows = hop(after(from_last_slab(normed[length - edge :]), near[1]), 1)
+        far[2] = to_group(after(near[2], far[1], response, peer, before_rows))
+        before_rows = hop(after(before_rows, near[2]), 2)
         near[0] = to_chip(after(cut(source, 0, first_half, half), near[2]))
         far[0] = to_group(after(near[0], far[2]))
         for b in (1, 2, 0):
@@ -384,27 +453,36 @@
                 (far[b], None, (c ^ 2) * rows + other_half),
             ]
             if b != 0:
-                late = after(far[2], near[0]) if b == 2 else far[1]
+                late = after(far[2], near[0], before_rows) if b == 2 else far[1]
                 pieces[b].append((to_core(late), None, (c ^ 3) * rows + other_half))
     else:
         normed = norm(tokens, norm_gain)
         response = respond(medium_filter, decay, tables[0], width)
         full = lax.all_gather(weights, "context", axis=1, tiled=True)
-        pieces = {b: [(full, b, 0)] for b in range(branches)}
+        pieces = {b: [(full, b, 0)] for b in (1, 2)}
+        middle = features // 2
+        pieces[0] = [(full[0, :middle], None, 0), (full[0, middle:], None, middle)]
+        before_rows = from_last_slab(normed[length - edge :])
+        held = 1
+        while held < count:
+            before_rows = hop(before_rows, held)
+            held *= 2
 
     gathered = lax.all_gather(normed, "tensor", axis=0, tiled=True)
     gate_taps = after(short_filter, response)
     gated, head, edges = gate(gathered, pieces[1], pieces[2], gate_taps, medium_count, width)
-    before_rows = to_next(after(gathered[slab - edge :], gated))
-    halo = to_next(after(edges, before_rows))
+    halo = to_next(edges)
+    early = len(pieces[0]) - 1
+    before_rows = after(before_rows, gated)
+    total = query_start(gathered, before_rows, pieces[0][:early], width)
     if paired:
-        last = to_core(after(far[0], before_rows))
+        last = to_core(after(far[0], gated))
         pieces[0].append((last, None, (c ^ 3) * rows + other_half))
-    query_rows = query(gathered, before_rows, pieces[0], short_filter, width)
+    query_rows = query_end(gathered, before_rows, pieces[0][early:], total, short_filter, width)
     combined = mix(gated, halo, head, short_filter, response, query_rows, tables, width)
     if paired:
         out_full = lax.all_gather(after(w_out, near[1]), "context", axis=0, tiled=True)
-        out_peer = to_core(after(w_out, gated))
+        out_peer = to_core(after(w_out, total))
         part = lambda i: lax.dynamic_slice(out_full, ((c ^ i) * out_rows, 0), (out_rows, channels))
         sets = [w_out, out_peer, part(2), part(3)]
     else:
@@ -421,8 +499,12 @@
             combined, rows_out, (((1,), (1,)), ((), ())), preferred_element_type=f32
         ).astype(bf16)
 
-    results, firsts = [], []
-    for rows_out in sets:
+    results, firsts, seconds = [], [], []
+    for n, rows_out in enumerate(sets):
+        if paired and n == 2:
+            combined = after(combined, firsts[1])
+        if paired and n == 3:
+            combined = after(combined, seconds[0])
         partial = product(rows_out)
         combined = after(combined, partial)
 
@@ -437,6 +519,7 @@
             firsts.append(send(far_pair, {0: 1, 3: 2}))
             got = plus(far_pair, firsts[-1])
             got = send(got, {1: 2, 2: 1})
+            seconds.append(got)
             low, high = got[:length], got[length:]
             odd = z % 2 == 1
             got_own = jnp.where(odd, high, low)

time: 231 us -> 235 us (1.017)
  starting transfers between devices: 59.5 us -> 49.8 us
  other arithmetic: 5.47 us -> 10.3 us
  waiting for transfers between devices: 97.7 us -> 102 us
    ppermute x28 -> x30, starting transfers between devices: 59.4 us -> 49.8 us  [move(): return lax.ppermute(value, axes, pairs)]
    ppermute x28 -> x30, waiting for transfers between devices: 90.3 us -> 97.8 us  [move(): return lax.ppermute(value, axes, pairs)]
    all_gather x1, waiting for transfers between devices: 5.29 us -> 0.01 us  [local(): lax.all_gather(after(w_out, near[1]), 'context', axis=0, tiled=True)]
    convert_element_type x8, other arithmetic: 3.36 us -> 6.36 us  [plus(): return total.astype(bf16)]
    pallas_call x1 -> x2, Pallas kernels: 8.77 us -> 11 us  [the longest x1 6.63 us: query_start(): pl.pallas_call(functools.partial(query_start_kernel, kinds, width), in_sp...]
  transfers between devices with their start and end apart: 30 -> 32, of which waited for: 11 -> 12; matrix products, arithmetic and copies ran while one was open for 9% -> 10% of each run, Pallas kernels for 14% -> 14%
where the time goes in v6:
time: 235 us; the launch traced here: 231 us
  waiting for transfers between devices  102 us (43%)
  starting transfers between devices  49.8 us (21%)
  Pallas kernels  35 us (15%)
  between operations  13.8 us (6%)
  matrix products  11.9 us (5%)
  other arithmetic  10.3 us (4%)
  local copies, waits for them, and re-layouts  8.28 us (4%)
    ppermute x30, waiting for transfers between devices, move(): return lax.ppermute(value, axes, pairs)  97.8 us
    ppermute x30, starting transfers between devices, move(): return lax.ppermute(value, axes, pairs)  49.8 us
    pallas_call x1, Pallas kernels, gate(): pl.pallas_call(functools.partial(gate_kernel, kinds_of(one), kinds_of(two...  14.5 us
    dot_general x4, matrix products, product(): lax.dot_general(combined, rows_out, (((1,), (1,)), ((), ())), preferred_e...  11.9 us
    pallas_call x1, Pallas kernels, query_start(): pl.pallas_call(functools.partial(query_start_kernel, kinds, width), in_sp...  6.63 us
    convert_element_type x8, other arithmetic, plus(): return total.astype(bf16)  6.36 us
    pallas_call x1, Pallas kernels, mix(): pl.pallas_call(mix_kernel, grid=(channels // width,), in_specs=[col(slab)...  5.37 us
  transfers between devices with their start and end apart: 32, of which 12 were waited for; matrix products, arithmetic and copies ran while one was open for 10% of the time, Pallas kernels for 14%

profile of v6, /device:TPU:0, one launch (start us, length us, event | category | flops | bytes accessed | tf_op | source)
XLA Modules:
  0.0 230.8 jit_solution(9944568356811919963)
XLA Ops:
  6.5 1.4 dynamic-slice_bitcast_fusion.2
  8.1 1.9 norm.1
  10.1 3.0 %collective-permute-start.1 = (bf16[512,1024]{1,0:T(8,128)(2,1)S(1)}, bf16[512,1024]{1,0:T(8,128)(2,1)S(1)}, u32[]{:S(2)}, u32[]{:S(2)}) collective-permute-start(bf16[512,1024]{1,0:T(8,128)(2,1)S(1)} %dynamic-slice_bitcast_fusion.2), channel_id=1, source_target_pairs={{0,8},{1,9},{2,10},{3,11},{4,12},{5,13},{6,14},{7,15},{8,0},{9,1},... | collective-permute-start | bytes 3145736 | tf_op jit(solution)/shard_map/ppermute | solution.py:399
  13.1 23.2 %collective-permute-done.1.rest_2_ = bf16[512,1024]{1,0:T(8,128)(2,1)S(1)} collective-permute-done((bf16[512,1024]{1,0:T(8,128)(2,1)S(1)}, bf16[512,1024]{1,0:T(8,128)(2,1)S(1)}, u32[]{:S(2)}, u32[]{:S(2)}) %collective-permute-start.1) | collective-permute-done | bytes 1048608 | tf_op jit(solution)/shard_map/ppermute | solution.py:399
  36.3 2.1 dynamic-slice_bitcast_fusion
  38.4 1.8 collective-permute-start.5
  40.3 1.5 collective-permute-start.3
  41.8 0.9 slice.36
  42.7 0.7 collective-permute-start.7
  43.4 0.7 collective-permute-start.8
  44.1 2.3 respond.1.response_ref
  46.4 16.6 %collective-permute-done.5.rest_8_ = bf16[512,1024]{1,0:T(8,128)(2,1)S(1)} collective-permute-done((bf16[512,1024]{1,0:T(8,128)(2,1)S(1)}, bf16[512,1024]{1,0:T(8,128)(2,1)S(1)}, u32[]{:S(2)}, u32[]{:S(2)}) %collective-permute-start.5) | collective-permute-done | bytes 1048608 | tf_op jit(solution)/shard_map/ppermute | solution.py:399
  63.0 1.4 collective-permute-start.10
  64.4 1.6 collective-permute-start.9
  66.0 1.3 collective-permute-start.11
  67.4 0.5 collective-permute-start.4
  67.9 24.6 %collective-permute-done.11 = bf16[16,4096]{1,0:T(8,128)(2,1)S(1)} collective-permute-done((bf16[16,4096]{1,0:T(8,128)(2,1)S(1)}, bf16[16,4096]{1,0:T(8,128)(2,1)S(1)}, u32[]{:S(2)}, u32[]{:S(2)}) %collective-permute-start.11) | collective-permute-done | bytes 131104 | tf_op jit(solution)/shard_map/ppermute | solution.py:399
  92.5 0.7 add.116.before_ref
  93.1 0.5 collective-permute-start.12
  93.9 0.8 collective-permute-start.15
  94.7 0.6 collective-permute-done.6.rest_9_
  95.2 3.9 %all-gather.3.cloned.1.call-done.x_ref = bf16[512,4096]{1,0:T(8,128)(2,1)} async-done(((bf16[128,4096]{1,0:T(8,128)(2,1)}), bf16[512,4096]{1,0:T(8,128)(2,1)}) %all-gather.3.cloned.1.call-update) | async-done | bytes 4194320 | tf_op jit(solution)/shard_map/all_gather | solution.py:471
  99.1 14.5 %gate.1 = (bf16[512,1024]{1,0:T(8,128)(2,1)}, bf16[2,16,1024]{2,1,0:T(8,128)(2,1)}, bf16[160,1024]{1,0:T(8,128)(2,1)}) custom-call(s32[6]{0:T(128)S(1)} %stack.39.at_ref, bf16[512,4096]{1,0:T(8,128)(2,1)} %all-gather.3.cloned.1.call-done.x_ref, f32[3,3,1024]{2,1,0:T(4,128)S(1)} %copy-done.3, bf16[3,1024,1024]{2,1,0:T(8,128)(2,1)} %bitcast.23, ...), custom_call_target="tpu_custom_call" | custom-call | flops 8589934592 | bytes 20971520 | tf_op jit(solution)/shard_map/gate/pallas_call | solution.py:171
  113.6 6.6 %query_start.1.sum_ref = f32[528,1024]{1,0:T(8,128)S(1)} custom-call(s32[4]{0:T(128)S(1)} %pad_add_fusion.1.at_ref, bf16[512,4096]{1,0:T(8,128)(2,1)} %all-gather.3.cloned.1.call-done.x_ref, bf16[16,4096]{1,0:T(8,128)(2,1)} %add.116.before_ref, bf16[3,1024,1024]{2,1,0:T(8,128)(2,1)} %bitcast.25, bf16[3,1024,1024]{2,1,0:T(8,128)(2,1)} %collective-permute-done.rest_1_.rest_7_, ...), custom_call_target="tpu_custom_call" | custom-call | flops 3221225472 | bytes 9437184 | tf_op jit(solution)/shard_map/query_start/pallas_call | solution.py:236
  120.3 0.5 collective-permute-start.16
  120.8 2.7 %collective-permute-start.13 = (bf16[160,1024]{1,0:T(8,128)(2,1)}, bf16[160,1024]{1,0:T(8,128)(2,1)}, u32[]{:S(2)}, u32[]{:S(2)}) collective-permute-start(bf16[160,1024]{1,0:T(8,128)(2,1)} %get-tuple-element.37), channel_id=1, source_target_pairs={{0,4},{1,5},{2,6},{3,7},{4,8},{5,9},{6,10},{7,11},{8,12},{9,13},{1... | collective-permute-start | bytes 983048 | tf_op jit(solution)/shard_map/ppermute | solution.py:399
  123.6 3.0 %collective-permute-done.16.rest_1_ = bf16[512,1024]{1,0:T(8,128)(2,1)S(1)} collective-permute-done((bf16[512,1024]{1,0:T(8,128)(2,1)}, bf16[512,1024]{1,0:T(8,128)(2,1)S(1)}, u32[]{:S(2)}, u32[]{:S(2)}) %collective-permute-start.16) | collective-permute-done | bytes 1048608 | tf_op jit(solution)/shard_map/ppermute | solution.py:399
  126.6 1.0 copy-done.13
  127.6 4.3 %query_end.1.query_ref = f32[512,1024]{1,0:T(8,128)S(1)} custom-call(s32[2]{0:T(128)S(1)} %pad_add_fusion.at_ref, bf16[512,4096]{1,0:T(8,128)(2,1)} %all-gather.3.cloned.1.call-done.x_ref, bf16[16,4096]{1,0:T(8,128)(2,1)} %add.116.before_ref, f32[528,1024]{1,0:T(8,128)S(1)} %query_start.1.sum_ref, f32[3,3,1024]{2,1,0:T(4,128)S(1)} %copy-done.3, ...), custom_call_target="tpu_custom_call" | custom-call | flops 1073741824 | bytes 3145728 | tf_op jit(solution)/shard_map/query_end/pallas_call | solution.py:261
  132.0 5.4 %mix.1 = bf16[512,1024]{1,0:T(8,128)(2,1)S(1)} custom-call(bf16[512,1024]{1,0:T(8,128)(2,1)} %get-tuple-element.36.gated_ref, bf16[160,1024]{1,0:T(8,128)(2,1)} %collective-permute-done.13.halo_ref, bf16[2,16,1024]{2,1,0:T(8,128)(2,1)} %get-tuple-element.38.head_ref, f32[3,3,1024]{2,1,0:T(4,128)S(1)} %copy-done.3, f32[3,128,1024]{2,1,0:T(8,128)} %respond.1.response_ref, ...), custom_call_target="tpu_custom_call" | custom-call | tf_op jit(solution)/shard_map/mix/pallas_call | solution.py:359
  137.3 2.9 %convolution_convert_fusion.1 = bf16[512,1024]{1,0:T(8,128)(2,1)S(1)} fusion(bf16[512,1024]{1,0:T(8,128)(2,1)S(1)} %mix.1, bf16[1024,1024]{1,0:T(8,128)(2,1)} %param.15), kind=kOutput, calls=%fused_computation.7 | convolution fusion | flops 1074266112 | bytes 4194304 | tf_op jit(solution)/shard_map/dot_general | solution.py:498
  140.3 1.3 collective-permute-start.19
  141.6 2.9 %convolution_convert_fusion = bf16[512,1024]{1,0:T(8,128)(2,1)S(1)} fusion(bf16[512,1024]{1,0:T(8,128)(2,1)S(1)} %mix.1, bf16[1024,1024]{1,0:T(8,128)(2,1)} %collective-permute-done.17), kind=kOutput, calls=%fused_computation.6 | convolution fusion | flops 1074266112 | bytes 4194304 | tf_op jit(solution)/shard_map/dot_general | solution.py:498
  144.5 0.8 constant_dynamic-slice_fusion.3
  145.3 2.1 collective-permute-start.18
  147.4 3.6 %collective-permute-done.19 = bf16[256,1024]{1,0:T(8,128)(2,1)S(1)} collective-permute-done((bf16[256,1024]{1,0:T(8,128)(2,1)S(1)}, bf16[256,1024]{1,0:T(8,128)(2,1)S(1)}, u32[]{:S(2)}, u32[]{:S(2)}) %collective-permute-start.19) | collective-permute-done | bytes 524320 | tf_op jit(solution)/shard_map/ppermute | solution.py:399
  151.0 1.0 add_convert_fusion.3
  152.0 1.5 collective-permute-start.20
  153.5 8.9 %collective-permute-done.18 = bf16[256,1024]{1,0:T(8,128)(2,1)} collective-permute-done((bf16[256,1024]{1,0:T(8,128)(2,1)}, bf16[256,1024]{1,0:T(8,128)(2,1)}, u32[]{:S(2)}, u32[]{:S(2)}) %collective-permute-start.18) | collective-permute-done | bytes 524320 | tf_op jit(solution)/shard_map/ppermute | solution.py:399
  162.3 2.9 %fusion.4 = bf16[512,1024]{1,0:T(8,128)(2,1)S(1)} fusion(bf16[512,1024]{1,0:T(8,128)(2,1)S(1)} %mix.1, bf16[4096,1024]{1,0:T(8,128)(2,1)} %all-gather.5.cloned.1.call-done, s32[]{:T(128)S(6)} %select_n.125), kind=kOutput, calls=%fused_computation.4 | convolution fusion | flops 1074266112 | bytes 4194308 | tf_op jit(solution)/shard_map/dot_general | solution.py:498
  165.2 3.3 %fusion.7 = bf16[512,1024]{1,0:T(8,128)(2,1)S(1)} fusion(bf16[512,1024]{1,0:T(8,128)(2,1)S(1)} %mix.1, bf16[4096,1024]{1,0:T(8,128)(2,1)} %all-gather.5.cloned.1.call-done, s32[]{:T(128)S(6)} %select_n.126), kind=kOutput, calls=%fused_computation.5 | convolution fusion | flops 1074266112 | bytes 4194308 | tf_op jit(solution)/shard_map/dot_general | solution.py:498
  168.5 0.9 constant_dynamic-slice_fusion.1
  169.4 5.2 %collective-permute-start.21 = (bf16[256,1024]{1,0:T(8,128)(2,1)}, bf16[256,1024]{1,0:T(8,128)(2,1)}, u32[]{:S(2)}, u32[]{:S(2)}) collective-permute-start(bf16[256,1024]{1,0:T(8,128)(2,1)} %constant_dynamic-slice_fusion.1), channel_id=1, source_target_pairs={{0,1},{3,2},{4,5},{7,6},{8,9},{11,10},{12,13},{15,14},{16,17},{19,... | collective-permute-start | bytes 1572872 | tf_op jit(solution)/shard_map/ppermute | solution.py:399
  174.6 0.8 constant_dynamic-slice_fusion
  175.4 2.2 collective-permute-start.24
  177.7 1.2 add_convert_fusion
  178.9 0.7 collective-permute-start.27
  179.6 1.4 collective-permute-done.21
  181.0 1.4 add_convert_fusion.2
  182.4 0.8 collective-permute-start.22
  183.2 9.0 %collective-permute-done.24 = bf16[256,1024]{1,0:T(8,128)(2,1)} collective-permute-done((bf16[256,1024]{1,0:T(8,128)(2,1)}, bf16[256,1024]{1,0:T(8,128)(2,1)}, u32[]{:S(2)}, u32[]{:S(2)}) %collective-permute-start.24) | collective-permute-done | bytes 524320 | tf_op jit(solution)/shard_map/ppermute | solution.py:399
  192.2 1.2 add_convert_fusion.1
  193.5 0.7 collective-permute-start.25
  194.2 1.2 add_convert_fusion.5
  195.3 6.7 %collective-permute-start.29 = (bf16[128,1024]{1,0:T(8,128)(2,1)S(1)}, bf16[128,1024]{1,0:T(8,128)(2,1)S(1)}, u32[]{:S(2)}, u32[]{:S(2)}) collective-permute-start(bf16[128,1024]{1,0:T(8,128)(2,1)S(1)} %add_convert_fusion.5), channel_id=1, source_target_pairs={{0,1},{1,0},{2,3},{3,2},{4,5},{5,4},{6,7},{7,6},{8,9},{9,8},{10,11... | collective-permute-start | bytes 786440 | tf_op jit(solution)/shard_map/ppermute | solution.py:399
  202.2 0.1 add_convert_fusion.11
  202.4 2.1 collective-permute-start.23
  204.6 9.2 %collective-permute-start.26 = (bf16[128,1024]{1,0:T(8,128)(2,1)S(1)}, bf16[128,1024]{1,0:T(8,128)(2,1)S(1)}, u32[]{:S(2)}, u32[]{:S(2)}) collective-permute-start(bf16[128,1024]{1,0:T(8,128)(2,1)S(1)} %add_convert_fusion.9), channel_id=1, source_target_pairs={{0,1},{1,0},{2,3},{3,2},{4,5},{5,4},{6,7},{7,6},{8,9},{9,8},{10,11... | collective-permute-start | bytes 786440 | tf_op jit(solution)/shard_map/ppermute | solution.py:399
  213.8 1.4 broadcast_select_fusion.3
  215.3 1.4 collective-permute-done.23
  216.6 5.6 %collective-permute-done.26 = bf16[128,1024]{1,0:T(8,128)(2,1)S(1)} collective-permute-done((bf16[128,1024]{1,0:T(8,128)(2,1)S(1)}, bf16[128,1024]{1,0:T(8,128)(2,1)S(1)}, u32[]{:S(2)}, u32[]{:S(2)}) %collective-permute-start.26) | collective-permute-done | bytes 262176 | tf_op jit(solution)/shard_map/ppermute | solution.py:399
  222.3 0.4 broadcast_select_fusion.5
  222.7 0.2 broadcast_select_fusion.1
  222.9 1.1 pad_maximum_fusion
  (69 shorter events, 1.3 us)
Async XLA Ops:
  6.5 1.6 copy-start
  6.5 1.4 copy-start.14
  6.5 92.6 %all-gather.3.cloned.1.call-start = ((), (), s32[]{:S(2)}) async-start(), calls=%async_computation | async-start | bytes 5242880 | tf_op jit(solution)/shard_map/all_gather | solution.py:471
  10.0 152.3 %all-gather.5.cloned.1.call-start = ((), (), s32[]{:S(2)}) async-start(), calls=%async_computation.1 | async-start | bytes 10485760 | tf_op jit(solution)/shard_map/all_gather | solution.py:484
  10.1 26.2 %collective-permute-start.1 = (bf16[512,1024]{1,0:T(8,128)(2,1)S(1)}, bf16[512,1024]{1,0:T(8,128)(2,1)S(1)}, u32[]{:S(2)}, u32[]{:S(2)}) collective-permute-start(bf16[512,1024]{1,0:T(8,128)(2,1)S(1)} %dynamic-slice_bitcast_fusion.2), channel_id=1, source_target_pairs={{0,8},{1,9},{2,10},{3,11},{4,12},{5,13},{6,14},{7,15},{8,0},{9,1},... | collective-permute-start | bytes 3145736 | tf_op jit(solution)/shard_map/ppermute | solution.py:399
  13.1 51.3 %collective-permute-start = (bf16[3,1024,1024]{2,1,0:T(8,128)(2,1)}, bf16[3,1024,1024]{2,1,0:T(8,128)(2,1)}, u32[]{:S(2)}, u32[]{:S(2)}) collective-permute-start(bf16[3,1024,1024]{2,1,0:T(8,128)(2,1)} %bitcast.21), channel_id=1, source_target_pairs={{0,4},{1,5},{2,6},{3,7},{4,0},{5,1},{6,2},{7,3},{8,12},{9,13},{10,... | collective-permute-start | bytes 18874376 | tf_op jit(solution)/shard_map/ppermute | solution.py:399
  36.3 31.0 %copy-start.10 = (bf16[512,1024]{1,0:T(8,128)(2,1)}, bf16[512,1024]{1,0:T(8,128)(2,1)S(1)}, u32[]{:S(2)}) copy-start(bf16[512,1024]{1,0:T(8,128)(2,1)S(1)} %collective-permute-done.1.rest_2_) | copy-start | bytes 3145732
  36.3 7.8 %copy-start.1 = (f32[128,1024]{1,0:T(8,128)S(1)}, f32[128,1024]{1,0:T(8,128)}, u32[]{:S(2)}) copy-start(f32[128,1024]{1,0:T(8,128)} %filter_ref.1) | copy-start | bytes 1572868
  36.3 7.8 %copy-start.2 = (bf16[256,256]{1,0:T(8,128)(2,1)S(1)}, bf16[256,256]{1,0:T(8,128)(2,1)}, u32[]{:S(2)}) copy-start(bf16[256,256]{1,0:T(8,128)(2,1)} %constant.52.clone.fwd_ref) | copy-start | bytes 393220
  36.3 7.8 %copy-start.5 = (f32[1024]{0:T(1024)S(1)}, f32[1024]{0:T(1024)}, u32[]{:S(2)}) copy-start(f32[1024]{0:T(1024)} %param.14) | copy-start | bytes 12292
  38.4 60.7 %copy-start.3 = (f32[3,3,1024]{2,1,0:T(4,128)S(1)}, f32[3,3,1024]{2,1,0:T(4,128)}, u32[]{:S(2)}) copy-start(f32[3,3,1024]{2,1,0:T(4,128)} %short_ref.1) | copy-start | bytes 110596
  38.4 24.5 %collective-permute-start.5 = (bf16[512,1024]{1,0:T(8,128)(2,1)S(1)}, bf16[512,1024]{1,0:T(8,128)(2,1)S(1)}, u32[]{:S(2)}, u32[]{:S(2)}) collective-permute-start(bf16[512,1024]{1,0:T(8,128)(2,1)S(1)} %get-tuple-element.30), channel_id=1, source_target_pairs={{0,8},{1,9},{2,10},{3,11},{4,12},{5,13},{6,14},{7,15},{8,0},{9,1},... | collective-permute-start | bytes 3145736 | tf_op jit(solution)/shard_map/ppermute | solution.py:399
  40.3 24.1 %collective-permute-start.3 = (bf16[512,1024]{1,0:T(8,128)(2,1)S(1)}, bf16[512,1024]{1,0:T(8,128)(2,1)S(1)}, u32[]{:S(2)}, u32[]{:S(2)}) collective-permute-start(bf16[512,1024]{1,0:T(8,128)(2,1)S(1)} %collective-permute-done.1.rest_2_), channel_id=1, source_target_pairs={{0,16},{1,17},{2,18},{3,19},{4,20},{5,21},{6,22},{7,23},{8,24},{9,... | collective-permute-start | bytes 3145736 | tf_op jit(solution)/shard_map/ppermute | solution.py:399
  42.7 0.7 collective-permute-start.7
  43.4 3.0 %collective-permute-start.8 = (bf16[16,4096]{1,0:T(8,128)(2,1)S(1)}, bf16[16,4096]{1,0:T(8,128)(2,1)S(1)}, u32[]{:S(2)}, u32[]{:S(2)}) collective-permute-start(bf16[16,4096]{1,0:T(8,128)(2,1)S(1)} %collective-permute-done.7), channel_id=1, source_target_pairs={{3,2},{7,6},{11,10},{15,14},{19,18},{23,22},{27,26},{31,30}} | collective-permute-start | bytes 393224 | tf_op jit(solution)/shard_map/ppermute | solution.py:399
  63.0 36.1 %copy-start.11 = (bf16[512,1024]{1,0:T(8,128)(2,1)}, bf16[512,1024]{1,0:T(8,128)(2,1)S(1)}, u32[]{:S(2)}) copy-start(bf16[512,1024]{1,0:T(8,128)(2,1)S(1)} %collective-permute-done.5.rest_8_) | copy-start | bytes 3145732
  63.0 30.2 %collective-permute-start.10 = (bf16[512,1024]{1,0:T(8,128)(2,1)S(1)}, bf16[512,1024]{1,0:T(8,128)(2,1)}, u32[]{:S(2)}, u32[]{:S(2)}) collective-permute-start(bf16[512,1024]{1,0:T(8,128)(2,1)S(1)} %get-tuple-element.33), channel_id=1, source_target_pairs={{0,8},{1,9},{2,10},{3,11},{4,12},{5,13},{6,14},{7,15},{8,0},{9,1},... | collective-permute-start | bytes 3145736 | tf_op jit(solution)/shard_map/ppermute | solution.py:399
  64.4 34.7 %copy-start.12 = (bf16[512,1024]{1,0:T(8,128)(2,1)}, bf16[512,1024]{1,0:T(8,128)(2,1)S(1)}, u32[]{:S(2)}) copy-start(bf16[512,1024]{1,0:T(8,128)(2,1)S(1)} %collective-permute-done.3.rest_4_) | copy-start | bytes 3145732
  64.4 28.7 %collective-permute-start.9 = (bf16[512,1024]{1,0:T(8,128)(2,1)S(1)}, bf16[512,1024]{1,0:T(8,128)(2,1)}, u32[]{:S(2)}, u32[]{:S(2)}) collective-permute-start(bf16[512,1024]{1,0:T(8,128)(2,1)S(1)} %collective-permute-done.5.rest_8_), channel_id=1, source_target_pairs={{0,16},{1,17},{2,18},{3,19},{4,20},{5,21},{6,22},{7,23},{8,24},{9,... | collective-permute-start | bytes 3145736 | tf_op jit(solution)/shard_map/ppermute | solution.py:399
  66.0 26.5 %collective-permute-start.11 = (bf16[16,4096]{1,0:T(8,128)(2,1)S(1)}, bf16[16,4096]{1,0:T(8,128)(2,1)S(1)}, u32[]{:S(2)}, u32[]{:S(2)}) collective-permute-start(bf16[16,4096]{1,0:T(8,128)(2,1)S(1)} %add.115), channel_id=1, source_target_pairs={{2,0},{3,1},{6,4},{7,5},{10,8},{11,9},{14,12},{15,13},{18,16},{19,... | collective-permute-start | bytes 393224 | tf_op jit(solution)/shard_map/ppermute | solution.py:399
  67.3 26.6 %collective-permute-start.2 = (bf16[512,1024]{1,0:T(8,128)(2,1)S(1)}, bf16[512,1024]{1,0:T(8,128)(2,1)}, u32[]{:S(2)}, u32[]{:S(2)}) collective-permute-start(bf16[512,1024]{1,0:T(8,128)(2,1)S(1)} %collective-permute-done.1.rest_2_), channel_id=1, source_target_pairs={{0,4},{1,5},{2,6},{3,7},{4,0},{5,1},{6,2},{7,3},{8,12},{9,13},{10,... | collective-permute-start | bytes 3145736 | tf_op jit(solution)/shard_map/ppermute | solution.py:399
  67.4 27.3 %collective-permute-start.4 = (bf16[512,1024]{1,0:T(8,128)(2,1)S(1)}, bf16[512,1024]{1,0:T(8,128)(2,1)}, u32[]{:S(2)}, u32[]{:S(2)}) collective-permute-start(bf16[512,1024]{1,0:T(8,128)(2,1)S(1)} %collective-permute-done.3.rest_4_), channel_id=1, source_target_pairs={{0,4},{1,5},{2,6},{3,7},{4,0},{5,1},{6,2},{7,3},{8,12},{9,13},{10,... | collective-permute-start | bytes 3145736 | tf_op jit(solution)/shard_map/ppermute | solution.py:399
  92.4 2.8 %collective-permute-start.6 = (bf16[512,1024]{1,0:T(8,128)(2,1)S(1)}, bf16[512,1024]{1,0:T(8,128)(2,1)}, u32[]{:S(2)}, u32[]{:S(2)}) collective-permute-start(bf16[512,1024]{1,0:T(8,128)(2,1)S(1)} %collective-permute-done.5.rest_8_), channel_id=1, source_target_pairs={{0,4},{1,5},{2,6},{3,7},{4,0},{5,1},{6,2},{7,3},{8,12},{9,13},{10,... | collective-permute-start | bytes 3145736 | tf_op jit(solution)/shard_map/ppermute | solution.py:399
  93.1 6.0 %collective-permute-start.12 = (bf16[512,1024]{1,0:T(8,128)(2,1)}, bf16[512,1024]{1,0:T(8,128)(2,1)}, u32[]{:S(2)}, u32[]{:S(2)}) collective-permute-start(bf16[512,1024]{1,0:T(8,128)(2,1)} %collective-permute-done.9.rest_10_), channel_id=1, source_target_pairs={{0,4},{1,5},{2,6},{3,7},{4,0},{5,1},{6,2},{7,3},{8,12},{9,13},{10,... | collective-permute-start | bytes 3145736 | tf_op jit(solution)/shard_map/ppermute | solution.py:399
  93.6 19.9 %collective-permute-start.14 = (bf16[512,1024]{1,0:T(8,128)(2,1)}, bf16[512,1024]{1,0:T(8,128)(2,1)}, u32[]{:S(2)}, u32[]{:S(2)}) collective-permute-start(bf16[512,1024]{1,0:T(8,128)(2,1)} %collective-permute-done.10.rest_2_), channel_id=1, source_target_pairs={{0,4},{1,5},{2,6},{3,7},{4,0},{5,1},{6,2},{7,3},{8,12},{9,13},{10,... | collective-permute-start | bytes 3145736 | tf_op jit(solution)/shard_map/ppermute | solution.py:399
  93.9 26.4 %collective-permute-start.15 = (bf16[512,1024]{1,0:T(8,128)(2,1)}, bf16[512,1024]{1,0:T(8,128)(2,1)}, u32[]{:S(2)}, u32[]{:S(2)}) collective-permute-start(bf16[512,1024]{1,0:T(8,128)(2,1)} %collective-permute-done.10.rest_2_), channel_id=1, source_target_pairs={{0,16},{1,17},{2,18},{3,19},{4,20},{5,21},{6,22},{7,23},{8,24},{9,... | collective-permute-start | bytes 3145736 | tf_op jit(solution)/shard_map/ppermute | solution.py:399
  120.2 21.4 %collective-permute-start.17 = (bf16[1024,1024]{1,0:T(8,128)(2,1)}, bf16[1024,1024]{1,0:T(8,128)(2,1)}, u32[]{:S(2)}, u32[]{:S(2)}) collective-permute-start(bf16[1024,1024]{1,0:T(8,128)(2,1)} %param.15), channel_id=1, source_target_pairs={{0,4},{1,5},{2,6},{3,7},{4,0},{5,1},{6,2},{7,3},{8,12},{9,13},{10,... | collective-permute-start | bytes 6291464 | tf_op jit(solution)/shard_map/ppermute | solution.py:399
  120.3 6.3 %collective-permute-start.16 = (bf16[512,1024]{1,0:T(8,128)(2,1)}, bf16[512,1024]{1,0:T(8,128)(2,1)S(1)}, u32[]{:S(2)}, u32[]{:S(2)}) collective-permute-start(bf16[512,1024]{1,0:T(8,128)(2,1)} %collective-permute-done.15.rest_0_), channel_id=1, source_target_pairs={{0,4},{1,5},{2,6},{3,7},{4,0},{5,1},{6,2},{7,3},{8,12},{9,13},{10,... | collective-permute-start | bytes 3145736 | tf_op jit(solution)/shard_map/ppermute | solution.py:399
  120.8 11.1 %collective-permute-start.13 = (bf16[160,1024]{1,0:T(8,128)(2,1)}, bf16[160,1024]{1,0:T(8,128)(2,1)}, u32[]{:S(2)}, u32[]{:S(2)}) collective-permute-start(bf16[160,1024]{1,0:T(8,128)(2,1)} %get-tuple-element.37), channel_id=1, source_target_pairs={{0,4},{1,5},{2,6},{3,7},{4,8},{5,9},{6,10},{7,11},{8,12},{9,13},{1... | collective-permute-start | bytes 983048 | tf_op jit(solution)/shard_map/ppermute | solution.py:399
  123.6 8.4 %copy-start.4 = (bf16[128,768]{1,0:T(8,128)(2,1)S(1)}, bf16[128,768]{1,0:T(8,128)(2,1)}, u32[]{:S(2)}) copy-start(bf16[128,768]{1,0:T(8,128)(2,1)} %constant.53.clone.inv_ref) | copy-start | bytes 589828
  126.6 1.0 copy-start.13
  140.3 10.7 %collective-permute-start.19 = (bf16[256,1024]{1,0:T(8,128)(2,1)S(1)}, bf16[256,1024]{1,0:T(8,128)(2,1)S(1)}, u32[]{:S(2)}, u32[]{:S(2)}) collective-permute-start(bf16[256,1024]{1,0:T(8,128)(2,1)S(1)} %constant_dynamic-slice_fusion.2), channel_id=1, source_target_pairs={{0,1},{3,2},{4,5},{7,6},{8,9},{11,10},{12,13},{15,14},{16,17},{19,... | collective-permute-start | bytes 1572872 | tf_op jit(solution)/shard_map/ppermute | solution.py:399
  145.3 17.0 %collective-permute-start.18 = (bf16[256,1024]{1,0:T(8,128)(2,1)}, bf16[256,1024]{1,0:T(8,128)(2,1)}, u32[]{:S(2)}, u32[]{:S(2)}) collective-permute-start(bf16[256,1024]{1,0:T(8,128)(2,1)} %constant_dynamic-slice_fusion.3), channel_id=1, source_target_pairs={{0,1},{3,2},{4,5},{7,6},{8,9},{11,10},{12,13},{15,14},{16,17},{19,... | collective-permute-start | bytes 1572872 | tf_op jit(solution)/shard_map/ppermute | solution.py:399
  152.0 13.2 %collective-permute-start.20 = (bf16[256,1024]{1,0:T(8,128)(2,1)}, bf16[256,1024]{1,0:T(8,128)(2,1)}, u32[]{:S(2)}, u32[]{:S(2)}) collective-permute-start(bf16[256,1024]{1,0:T(8,128)(2,1)} %add_convert_fusion.3), channel_id=1, source_target_pairs={{1,2},{2,1},{5,6},{6,5},{9,10},{10,9},{13,14},{14,13},{17,18},{18,... | collective-permute-start | bytes 1572872 | tf_op jit(solution)/shard_map/ppermute | solution.py:399
  165.2 9.4 %copy-start.6 = (bf16[512,1024]{1,0:T(8,128)(2,1)}, bf16[512,1024]{1,0:T(8,128)(2,1)S(1)}, u32[]{:S(2)}) copy-start(bf16[512,1024]{1,0:T(8,128)(2,1)S(1)} %fusion.4) | copy-start | bytes 3145732
  168.5 7.0 %copy-start.8 = (bf16[512,1024]{1,0:T(8,128)(2,1)}, bf16[512,1024]{1,0:T(8,128)(2,1)S(1)}, u32[]{:S(2)}) copy-start(bf16[512,1024]{1,0:T(8,128)(2,1)S(1)} %fusion.7) | copy-start | bytes 3145732
  169.4 11.6 %collective-permute-start.21 = (bf16[256,1024]{1,0:T(8,128)(2,1)}, bf16[256,1024]{1,0:T(8,128)(2,1)}, u32[]{:S(2)}, u32[]{:S(2)}) collective-permute-start(bf16[256,1024]{1,0:T(8,128)(2,1)} %constant_dynamic-slice_fusion.1), channel_id=1, source_target_pairs={{0,1},{3,2},{4,5},{7,6},{8,9},{11,10},{12,13},{15,14},{16,17},{19,... | collective-permute-start | bytes 1572872 | tf_op jit(solution)/shard_map/ppermute | solution.py:399
  175.4 16.8 %copy-start.7 = (bf16[512,1024]{1,0:T(8,128)(2,1)S(1)}, bf16[512,1024]{1,0:T(8,128)(2,1)}, u32[]{:S(2)}) copy-start(bf16[512,1024]{1,0:T(8,128)(2,1)} %copy-done.6) | copy-start | bytes 3145732
  175.4 16.8 %collective-permute-start.24 = (bf16[256,1024]{1,0:T(8,128)(2,1)}, bf16[256,1024]{1,0:T(8,128)(2,1)}, u32[]{:S(2)}, u32[]{:S(2)}) collective-permute-start(bf16[256,1024]{1,0:T(8,128)(2,1)} %constant_dynamic-slice_fusion), channel_id=1, source_target_pairs={{0,1},{3,2},{4,5},{7,6},{8,9},{11,10},{12,13},{15,14},{16,17},{19,... | collective-permute-start | bytes 1572872 | tf_op jit(solution)/shard_map/ppermute | solution.py:399
  178.9 23.1 %collective-permute-start.27 = (bf16[256,1024]{1,0:T(8,128)(2,1)S(1)}, bf16[256,1024]{1,0:T(8,128)(2,1)S(1)}, u32[]{:S(2)}, u32[]{:S(2)}) collective-permute-start(bf16[256,1024]{1,0:T(8,128)(2,1)S(1)} %add_convert_fusion), channel_id=1, source_target_pairs={{1,2},{2,1},{5,6},{6,5},{9,10},{10,9},{13,14},{14,13},{17,18},{18,... | collective-permute-start | bytes 1572872 | tf_op jit(solution)/shard_map/ppermute | solution.py:399
  182.4 19.8 %copy-start.9 = (bf16[512,1024]{1,0:T(8,128)(2,1)S(1)}, bf16[512,1024]{1,0:T(8,128)(2,1)}, u32[]{:S(2)}) copy-start(bf16[512,1024]{1,0:T(8,128)(2,1)} %copy-done.8) | copy-start | bytes 3145732
  182.4 19.8 %collective-permute-start.22 = (bf16[256,1024]{1,0:T(8,128)(2,1)S(1)}, bf16[256,1024]{1,0:T(8,128)(2,1)S(1)}, u32[]{:S(2)}, u32[]{:S(2)}) collective-permute-start(bf16[256,1024]{1,0:T(8,128)(2,1)S(1)} %add_convert_fusion.2), channel_id=1, source_target_pairs={{1,2},{2,1},{5,6},{6,5},{9,10},{10,9},{13,14},{14,13},{17,18},{18,... | collective-permute-start | bytes 1572872 | tf_op jit(solution)/shard_map/ppermute | solution.py:399
  193.5 11.0 %collective-permute-start.25 = (bf16[256,1024]{1,0:T(8,128)(2,1)S(1)}, bf16[256,1024]{1,0:T(8,128)(2,1)S(1)}, u32[]{:S(2)}, u32[]{:S(2)}) collective-permute-start(bf16[256,1024]{1,0:T(8,128)(2,1)S(1)} %add_convert_fusion.1), channel_id=1, source_target_pairs={{1,2},{2,1},{5,6},{6,5},{9,10},{10,9},{13,14},{14,13},{17,18},{18,... | collective-permute-start | bytes 1572872 | tf_op jit(solution)/shard_map/ppermute | solution.py:399
  195.3 18.5 %collective-permute-start.29 = (bf16[128,1024]{1,0:T(8,128)(2,1)S(1)}, bf16[128,1024]{1,0:T(8,128)(2,1)S(1)}, u32[]{:S(2)}, u32[]{:S(2)}) collective-permute-start(bf16[128,1024]{1,0:T(8,128)(2,1)S(1)} %add_convert_fusion.5), channel_id=1, source_target_pairs={{0,1},{1,0},{2,3},{3,2},{4,5},{5,4},{6,7},{7,6},{8,9},{9,8},{10,11... | collective-permute-start | bytes 786440 | tf_op jit(solution)/shard_map/ppermute | solution.py:399
  202.1 11.7 %collective-permute-start.28 = (bf16[128,1024]{1,0:T(8,128)(2,1)S(1)}, bf16[128,1024]{1,0:T(8,128)(2,1)S(1)}, u32[]{:S(2)}, u32[]{:S(2)}) collective-permute-start(bf16[128,1024]{1,0:T(8,128)(2,1)S(1)} %add_convert_fusion.7), channel_id=1, source_target_pairs={{0,1},{1,0},{2,3},{3,2},{4,5},{5,4},{6,7},{7,6},{8,9},{9,8},{10,11... | collective-permute-start | bytes 786440 | tf_op jit(solution)/shard_map/ppermute | solution.py:399
  202.4 14.3 %collective-permute-start.23 = (bf16[128,1024]{1,0:T(8,128)(2,1)S(1)}, bf16[128,1024]{1,0:T(8,128)(2,1)S(1)}, u32[]{:S(2)}, u32[]{:S(2)}) collective-permute-start(bf16[128,1024]{1,0:T(8,128)(2,1)S(1)} %add_convert_fusion.11), channel_id=1, source_target_pairs={{0,1},{1,0},{2,3},{3,2},{4,5},{5,4},{6,7},{7,6},{8,9},{9,8},{10,11... | collective-permute-start | bytes 786440 | tf_op jit(solution)/shard_map/ppermute | solution.py:399
  204.6 17.7 %collective-permute-start.26 = (bf16[128,1024]{1,0:T(8,128)(2,1)S(1)}, bf16[128,1024]{1,0:T(8,128)(2,1)S(1)}, u32[]{:S(2)}, u32[]{:S(2)}) collective-permute-start(bf16[128,1024]{1,0:T(8,128)(2,1)S(1)} %add_convert_fusion.9), channel_id=1, source_target_pairs={{0,1},{1,0},{2,3},{3,2},{4,5},{5,4},{6,7},{7,6},{8,9},{9,8},{10,11... | collective-permute-start | bytes 786440 | tf_op jit(solution)/shard_map/ppermute | solution.py:399
Sparse Core Ops, SparseCore 0:
  10.2 88.8 all-gather.2
  100.7 56.9 all-gather.4

commit v7 on v5

--- a/solution.py
+++ b/solution.py
@@ -113,6 +113,7 @@
 
 
 def add_up(kinds, width, waits, full, weight, s, first):
+    rows = slice(first, None)
     channels = weight.shape[1]
     for n, (low, high) in enumerate(spans(kinds)):
         for copies in waits:
@@ -123,26 +124,27 @@
                 full[:, low:high], weight[low:high, columns], preferred_element_type=f32
             )
             if n > 0:
-                term = s[first:, columns] + term
-            if n == len(kinds) - 1:
+                term = s[rows, columns] + term
+            if n == len(kinds) - 1 and first is not None:
                 term = term.astype(bf16).astype(f32)
-            s[first:, columns] = term
-
-
-def gate_kernel(one, two, width, at_ref, x_ref, taps_ref, *rest):
-    arrays = rest[: len(one) + len(two)]
-    gated_ref, head_ref, halo_ref, full, weights, s1, feat, s2, sems = rest[len(arrays) :]
+            s[rows, columns] = term
+
+
+def gate_kernel(one, two, three, width, at_ref, x_ref, taps_ref, *rest):
+    arrays = rest[: len(one) + len(two) + len(three)]
+    gated_ref, head_ref, halo_ref, sum_ref, full, weights, s1, feat, s2, sems = rest[len(arrays) :]
     slab, channels = gated_ref.shape
     count = halo_ref.shape[0] - 2 * edge
     x_copies = token_copies(one, at_ref, x_ref, full, sems.at[0])
     copies = [
         weight_copies(one, arrays[: len(one)], weights.at[0], sems.at[1]),
-        weight_copies(two, arrays[len(one) :], weights.at[1], sems.at[2]),
+        weight_copies(two, arrays[len(one) : -len(three)], weights.at[1], sems.at[2]),
+        weight_copies(three, arrays[-len(three) :], weights.at[2], sems.at[3]),
     ]
     for x_copy, copy in zip(x_copies, copies[0]):
         x_copy.start()
         copy.start()
-    for copy in copies[1]:
+    for copy in copies[1] + copies[2]:
         copy.start()
     s1[0:edge] = jnp.zeros((edge, channels), f32)
     add_up(one, width, (x_copies, copies[0]), full, weights.at[0], s1, edge)
@@ -162,64 +164,106 @@
         gated = gated.astype(bf16)
         gated_ref[:, columns] = gated
         halo_ref[0:count, columns] = gated[slab - count :]
-
-
-def gate(x, one, two, short_filter, taps, width):
+    for copy in copies[2]:
+        copy.wait()
+    depth = list(spans(three))[-1][1]
+    for i in range(channels // width):
+        columns = slice(i * width, (i + 1) * width)
+        sum_ref[:, columns] = jnp.dot(
+            full[:, 0:depth], weights[2, 0:depth, columns], preferred_element_type=f32
+        )
+
+
+def gate(x, one, two, three, short_filter, taps, width):
     slab, features = x.shape
     channels = short_filter.shape[-1]
     return pl.pallas_call(
-        functools.partial(gate_kernel, kinds_of(one), kinds_of(two), width),
-        in_specs=[in_smem, in_hbm, in_vmem] + [in_hbm] * (len(one) + len(two)),
-        out_specs=[in_vmem] * 3,
+        functools.partial(gate_kernel, kinds_of(one), kinds_of(two), kinds_of(three), width),
+        in_specs=[in_smem, in_hbm, in_vmem] + [in_hbm] * (len(one) + len(two) + len(three)),
+        out_specs=[in_vmem] * 4,
         out_shape=[
             pltpu.MemorySpace.HBM((slab, channels), bf16),
             pltpu.MemorySpace.HBM((2, edge, channels), bf16),
             pltpu.MemorySpace.HBM((taps + 2 * edge, channels), bf16),
+            jax.ShapeDtypeStruct((slab, channels), f32),
         ],
         scratch_shapes=[
             pltpu.VMEM((slab, features), bf16),
-            pltpu.VMEM((2, features, channels), bf16),
+            pltpu.VMEM((3, features, channels), bf16),
             pltpu.VMEM((slab + edge, channels), f32),
             pltpu.VMEM((slab, channels), f32),
             pltpu.VMEM((slab + edge, width), f32),
-            pltpu.SemaphoreType.DMA((3, len(one))),
-        ],
-        compiler_params=pltpu.CompilerParams(vmem_limit_bytes=40 << 20),
+            pltpu.SemaphoreType.DMA((4, len(one))),
+        ],
+        compiler_params=pltpu.CompilerParams(vmem_limit_bytes=48 << 20),
         name="gate",
-    )(offsets(one), hold(x), short_filter, *[hold(p[0]) for p in one + two])
-
-
-def query_kernel(kinds, width, at_ref, x_ref, before_ref, taps_ref, *rest):
+    )(offsets(one), hold(x), short_filter, *[hold(p[0]) for p in one + two + three])
+
+
+def query_kernel(kinds, width, at_ref, x_ref, sum_ref, *rest):
     arrays = rest[: len(kinds)]
-    out_ref, full, weight, s, sems = rest[len(arrays) :]
+    out_ref, tail_ref, full, weight, sems = rest[len(arrays) :]
     slab, channels = out_ref.shape
-    x_copies = token_copies(kinds, at_ref, x_ref, full.at[edge : edge + slab], sems.at[0])
-    e_copies = token_copies(kinds, at_ref, before_ref, full.at[0:edge], sems.at[1])
-    copies = weight_copies(kinds, arrays, weight, sems.at[2])
-    for group in zip(e_copies, x_copies, copies):
-        for copy in group:
-            copy.start()
-    add_up(kinds, width, (e_copies, x_copies, copies), full, weight, s, 0)
-    out_ref[...] = short_sum(s, taps_ref, 0, slab)
-
-
-def query(x, before, pieces, short_filter, width):
-    slab, features = x.shape
-    channels = short_filter.shape[-1]
+    x_copies = token_copies(kinds, at_ref, x_ref, full, sems.at[0])
+    copies = weight_copies(kinds, arrays, weight, sems.at[1])
+    for copy in x_copies + copies:
+        copy.start()
+    for copy in x_copies + copies:
+        copy.wait()
+    for i in range(channels // width):
+        columns = slice(i * width, (i + 1) * width)
+        term = jnp.dot(full[...], weight[:, columns], preferred_element_type=f32)
+        out_ref[:, columns] = (sum_ref[:, columns] + term).astype(bf16)
+    tail_ref[...] = out_ref[slab - edge :]
+
+
+def query(x, pieces, total, width):
+    slab, channels = total.shape
+    kinds = kinds_of(pieces)
+    depth = sum(k[1] for k in kinds)
     return pl.pallas_call(
-        functools.partial(query_kernel, kinds_of(pieces), width),
-        in_specs=[in_smem, in_hbm, in_hbm, in_vmem] + [in_hbm] * len(pieces),
-        out_specs=in_vmem,
-        out_shape=jax.ShapeDtypeStruct((slab, channels), f32),
+        functools.partial(query_kernel, kinds, width),
+        in_specs=[in_smem, in_hbm, in_vmem] + [in_hbm] * len(pieces),
+        out_specs=[in_vmem] * 2,
+        out_shape=[
+            jax.ShapeDtypeStruct((slab, channels), bf16),
+            pltpu.MemorySpace.HBM((edge, channels), bf16),
+        ],
         scratch_shapes=[
-            pltpu.VMEM((slab + edge, features), bf16),
-            pltpu.VMEM((features, channels), bf16),
-            pltpu.VMEM((slab + edge, channels), f32),
-            pltpu.SemaphoreType.DMA((3, len(pieces))),
-        ],
-        compiler_params=pltpu.CompilerParams(vmem_limit_bytes=32 << 20),
+            pltpu.VMEM((slab, depth), bf16),
+            pltpu.VMEM((depth, channels), bf16),
+            pltpu.SemaphoreType.DMA((2, len(pieces))),
+        ],
+        compiler_params=pltpu.CompilerParams(vmem_limit_bytes=16 << 20),
         name="query",
-    )(offsets(pieces), hold(x), hold(before), short_filter, *[hold(p[0]) for p in pieces])
+    )(offsets(pieces), hold(x), total, *[hold(p[0]) for p in pieces])
+
+
+def combine_kernel(projected_ref, before_ref, taps_ref, mixed_ref, out_ref, s):
+    slab = out_ref.shape[0]
+    s[0:edge] = before_ref[...].astype(f32)
+    s[edge : edge + slab] = projected_ref[...].astype(f32)
+    out_ref[...] = (short_sum(s, taps_ref, 0, slab) * mixed_ref[...]).astype(bf16)
+
+
+def combine(projected, before, short_filter, mixed, width):
+    slab, channels = mixed.shape
+    col = lambda rows: pl.BlockSpec((rows, width), lambda i: (0, i))
+    return pl.pallas_call(
+        combine_kernel,
+        grid=(channels // width,),
+        in_specs=[
+            col(slab),
+            col(edge),
+            pl.BlockSpec(short_filter.shape[:2] + (width,), lambda i: (0, 0, i)),
+            col(slab),
+        ],
+        out_specs=col(slab),
+        out_shape=jax.ShapeDtypeStruct((slab, channels), bf16),
+        scratch_shapes=[pltpu.VMEM((slab + edge, width), f32)],
+        compiler_params=pltpu.CompilerParams(vmem_limit_bytes=16 << 20),
+        name="combine",
+    )(projected, before, short_filter, mixed)
 
 
 def transform(fwd_ref, block):
@@ -255,7 +299,7 @@
 
 
 def mix_kernel(
-    gated_ref, halo_ref, head_ref, short_ref, response_ref, query_ref, fwd_ref, inv_ref, out_ref, s
+    gated_ref, halo_ref, head_ref, short_ref, response_ref, fwd_ref, inv_ref, out_ref, s
 ):
     taps = response_ref.shape[1]
     blocks = gated_ref.shape[0] // taps
@@ -286,14 +330,12 @@
         y = jnp.concatenate([x_cos * h_cos - x_sin * h_sin, x_sin * h_low + x_cos * h_sin], axis=0)
         high = y.astype(bf16)
         low = (y - high.astype(f32)).astype(bf16)
-        mixed = jnp.dot(
+        out_ref[b * taps : (b + 1) * taps] = jnp.dot(
             inv_ref[...], jnp.concatenate([high, low, high], axis=0), preferred_element_type=f32
         )
-        at = slice(b * taps, (b + 1) * taps)
-        out_ref[at] = (query_ref[at] * mixed).astype(bf16)
-
-
-def mix(gated, halo, head, short_filter, response, query_rows, tables, width):
+
+
+def mix(gated, halo, head, short_filter, response, tables, width):
     slab, channels = gated.shape
     count = response.shape[1]
     forward, inverse = tables
@@ -308,16 +350,15 @@
             cube(2, edge),
             cube(*short_filter.shape[:2]),
             cube(3, count),
-            col(slab),
             pl.BlockSpec(forward.shape, lambda i: (0, 0)),
             pl.BlockSpec(inverse.shape, lambda i: (0, 0)),
         ],
         out_specs=col(slab),
-        out_shape=jax.ShapeDtypeStruct((slab, channels), bf16),
+        out_shape=jax.ShapeDtypeStruct((slab, channels), f32),
         scratch_shapes=[pltpu.VMEM((2 * edge, width), f32)],
         compiler_params=pltpu.CompilerParams(vmem_limit_bytes=16 << 20),
         name="mix",
-    )(hold(gated), hold(halo), hold(head), short_filter, hold(response), query_rows, forward, inverse)
+    )(hold(gated), hold(halo), hold(head), short_filter, hold(response), forward, inverse)
 
 
 def local(tokens, norm_gain, w_in, short_filter, medium_filter, decay, w_out):
@@ -390,21 +431,26 @@
         normed = norm(tokens, norm_gain)
         response = respond(medium_filter, decay, tables[0], width)
         full = lax.all_gather(weights, "context", axis=1, tiled=True)
-        pieces = {b: [(full, b, 0)] for b in range(branches)}
+        pieces = {b: [(full, b, 0)] for b in (1, 2)}
+        middle = features // 2
+        pieces[0] = [(full[0, :middle], None, 0), (full[0, middle:], None, middle)]
 
     gathered = lax.all_gather(normed, "tensor", axis=0, tiled=True)
     gate_taps = after(short_filter, response)
-    gated, head, edges = gate(gathered, pieces[1], pieces[2], gate_taps, medium_count, width)
-    before_rows = to_next(after(gathered[slab - edge :], gated))
-    halo = to_next(after(edges, before_rows))
+    gated, head, edges, total = gate(
+        gathered, pieces[1], pieces[2], pieces[0][:-1], gate_taps, medium_count, width
+    )
+    halo = to_next(edges)
+    late = pieces[0][-1:]
     if paired:
-        last = to_core(after(far[0], before_rows))
-        pieces[0].append((last, None, (c ^ 3) * rows + other_half))
-    query_rows = query(gathered, before_rows, pieces[0], short_filter, width)
-    combined = mix(gated, halo, head, short_filter, response, query_rows, tables, width)
+        late.append((to_core(after(far[0], gated)), None, (c ^ 3) * rows + other_half))
+    projected, tail = query(gathered, late, after(total, halo), width)
+    before = to_next(tail)
+    mixed = mix(gated, halo, head, short_filter, response, tables, width)
+    combined = combine(projected, before, short_filter, mixed, width)
     if paired:
         out_full = lax.all_gather(after(w_out, near[1]), "context", axis=0, tiled=True)
-        out_peer = to_core(after(w_out, gated))
+        out_peer = to_core(after(w_out, tail))
         part = lambda i: lax.dynamic_slice(out_full, ((c ^ i) * out_rows, 0), (out_rows, channels))
         sets = [w_out, out_peer, part(2), part(3)]
     else:
@@ -421,8 +467,10 @@
             combined, rows_out, (((1,), (1,)), ((), ())), preferred_element_type=f32
         ).astype(bf16)
 
-    results, firsts = [], []
-    for rows_out in sets:
+    results, firsts, seconds = [], [], []
+    for n, rows_out in enumerate(sets):
+        if paired and n == 2:
+            combined = after(combined, firsts[1])
         partial = product(rows_out)
         combined = after(combined, partial)
 
@@ -436,7 +484,10 @@
             far_pair = block(jnp.where(z < 2, 2, 0), 2)
             firsts.append(send(far_pair, {0: 1, 3: 2}))
             got = plus(far_pair, firsts[-1])
+            if n >= 2:
+                got = after(got, seconds[n - 2])
             got = send(got, {1: 2, 2: 1})
+            seconds.append(got)
             low, high = got[:length], got[length:]
             odd = z % 2 == 1
             got_own = jnp.where(odd, high, low)

time: 231 us -> 248 us (1.074)
  waiting for transfers between devices: 97.7 us -> 105 us
  other arithmetic: 5.47 us -> 12.7 us
  starting transfers between devices: 59.5 us -> 62.3 us
    ppermute x28, waiting for transfers between devices: 90.3 us -> 103 us  [move(): return lax.ppermute(value, axes, pairs)]
    convert_element_type x8, other arithmetic: 3.36 us -> 9.33 us  [plus(): return total.astype(bf16)]
    all_gather x1, waiting for transfers between devices: 5.29 us -> 0.01 us  [local(): lax.all_gather(after(w_out, near[1]), 'context', axis=0, tiled=True)]
    ppermute x28, starting transfers between devices: 59.4 us -> 62.2 us  [move(): return lax.ppermute(value, axes, pairs)]
    pallas_call x1 -> x2, Pallas kernels: 8.77 us -> 6.34 us  [the longest x1 4.39 us: query(): pl.pallas_call(functools.partial(query_kernel, kinds, width), in_specs=[i...]
  transfers between devices with their start and end apart: 30 -> 30, of which waited for: 11 -> 13; matrix products, arithmetic and copies ran while one was open for 9% -> 11% of each run, Pallas kernels for 14% -> 12%
where the time goes in v7:
time: 248 us; the launch traced here: 247 us
  waiting for transfers between devices  105 us (42%)
  starting transfers between devices  62.3 us (25%)
  Pallas kernels  32.7 us (13%)
  between operations  13.8 us (6%)
  other arithmetic  12.7 us (5%)
  matrix products  11.6 us (5%)
  local copies, waits for them, and re-layouts  9.63 us (4%)
    ppermute x28, waiting for transfers between devices, move(): return lax.ppermute(value, axes, pairs)  103 us
    ppermute x28, starting transfers between devices, move(): return lax.ppermute(value, axes, pairs)  62.2 us
    pallas_call x1, Pallas kernels, gate(): pl.pallas_call(functools.partial(gate_kernel, kinds_of(one), kinds_of(two...  16.9 us
    dot_general x4, matrix products, product(): lax.dot_general(combined, rows_out, (((1,), (1,)), ((), ())), preferred_e...  11.6 us
    convert_element_type x8, other arithmetic, plus(): return total.astype(bf16)  9.33 us
    pallas_call x1, Pallas kernels, mix(): pl.pallas_call(mix_kernel, grid=(channels // width,), in_specs=[col(slab)...  5.37 us
  transfers between devices with their start and end apart: 30, of which 13 were waited for; matrix products, arithmetic and copies ran while one was open for 11% of the time, Pallas kernels for 12%

profile of v7, /device:TPU:0, one launch (start us, length us, event | category | flops | bytes accessed | tf_op | source)
XLA Modules:
  0.0 247.2 jit_solution(4298086969356247668)
XLA Ops:
  6.5 1.4 dynamic-slice_bitcast_fusion.2
  8.1 1.9 norm.1
  10.1 3.0 %collective-permute-start.1 = (bf16[512,1024]{1,0:T(8,128)(2,1)S(1)}, bf16[512,1024]{1,0:T(8,128)(2,1)S(1)}, u32[]{:S(2)}, u32[]{:S(2)}) collective-permute-start(bf16[512,1024]{1,0:T(8,128)(2,1)S(1)} %dynamic-slice_bitcast_fusion.2), channel_id=1, source_target_pairs={{0,8},{1,9},{2,10},{3,11},{4,12},{5,13},{6,14},{7,15},{8,0},{9,1},... | collective-permute-start | bytes 3145736 | tf_op jit(solution)/shard_map/ppermute | solution.py:383
  13.1 23.2 %collective-permute-done.1.rest_2_ = bf16[512,1024]{1,0:T(8,128)(2,1)S(1)} collective-permute-done((bf16[512,1024]{1,0:T(8,128)(2,1)S(1)}, bf16[512,1024]{1,0:T(8,128)(2,1)S(1)}, u32[]{:S(2)}, u32[]{:S(2)}) %collective-permute-start.1) | collective-permute-done | bytes 1048608 | tf_op jit(solution)/shard_map/ppermute | solution.py:383
  36.4 2.1 dynamic-slice_bitcast_fusion
  38.6 1.8 collective-permute-start.5
  40.4 1.5 collective-permute-start.3
  41.9 2.2 respond.1.response_ref
  44.1 19.6 %collective-permute-done.5.rest_8_ = bf16[512,1024]{1,0:T(8,128)(2,1)S(1)} collective-permute-done((bf16[512,1024]{1,0:T(8,128)(2,1)S(1)}, bf16[512,1024]{1,0:T(8,128)(2,1)S(1)}, u32[]{:S(2)}, u32[]{:S(2)}) %collective-permute-start.5) | collective-permute-done | bytes 1048608 | tf_op jit(solution)/shard_map/ppermute | solution.py:383
  63.8 1.7 collective-permute-start.8
  65.5 1.6 collective-permute-start.7
  67.1 0.5 collective-permute-start.6
  67.6 20.7 %collective-permute-done.8.rest_14_ = bf16[512,1024]{1,0:T(8,128)(2,1)} collective-permute-done((bf16[512,1024]{1,0:T(8,128)(2,1)S(1)}, bf16[512,1024]{1,0:T(8,128)(2,1)}, u32[]{:S(2)}, u32[]{:S(2)}) %collective-permute-start.8) | collective-permute-done | bytes 1048608 | tf_op jit(solution)/shard_map/ppermute | solution.py:383
  88.3 1.5 collective-permute-done.7.rest_10_
  89.8 1.1 copy-done.13
  90.9 1.5 collective-permute-start.12
  92.5 1.2 all-gather.3.cloned.1.call-done.x_ref
  93.7 16.9 %gate.1 = (bf16[512,1024]{1,0:T(8,128)(2,1)}, bf16[2,16,1024]{2,1,0:T(8,128)(2,1)}, bf16[160,1024]{1,0:T(8,128)(2,1)}, f32[512,1024]{1,0:T(8,128)S(1)}) custom-call(s32[6]{0:T(128)S(1)} %stack.33.at_ref, bf16[512,4096]{1,0:T(8,128)(2,1)} %all-gather.3.cloned.1.call-done.x_ref, f32[3,3,1024]{2,1,0:T(4,128)S(1)} %copy-done.3, bf16[3,1024,1024]{2,1,0:T(8,128)(2,1)} %bitcast.23, ...), custom_call_target="tpu_custom_call" | custom-call | tf_op jit(solution)/shard_map/gate/pallas_call | solution.py:180
  110.6 6.2 %collective-permute-done.12.rest_0_ = bf16[512,1024]{1,0:T(8,128)(2,1)} collective-permute-done((bf16[512,1024]{1,0:T(8,128)(2,1)}, bf16[512,1024]{1,0:T(8,128)(2,1)}, u32[]{:S(2)}, u32[]{:S(2)}) %collective-permute-start.12) | collective-permute-done | bytes 1048608 | tf_op jit(solution)/shard_map/ppermute | solution.py:383
  116.8 2.4 collective-permute-start.11
  119.3 1.4 collective-permute-done.11.halo_ref
  120.6 1.0 copy-done.14
  121.6 4.4 %query.1 = (bf16[512,1024]{1,0:T(8,128)(2,1)S(1)}, bf16[16,1024]{1,0:T(8,128)(2,1)}) custom-call(s32[2]{0:T(128)S(1)} %pad_add_fusion.at_ref, bf16[512,4096]{1,0:T(8,128)(2,1)} %all-gather.3.cloned.1.call-done.x_ref, f32[512,1024]{1,0:T(8,128)S(1)} %get-tuple-element.38.sum_ref, bf16[512,1024]{1,0:T(8,128)(2,1)} %collective-permute-done.12.rest_0_, ...), custom_call_target="tpu_custom_call" | custom-call | tf_op jit(solution)/shard_map/query/pallas_call | solution.py:224
  126.0 9.8 %collective-permute-start.15 = (bf16[1024,1024]{1,0:T(8,128)(2,1)}, bf16[1024,1024]{1,0:T(8,128)(2,1)}, u32[]{:S(2)}, u32[]{:S(2)}) collective-permute-start(bf16[1024,1024]{1,0:T(8,128)(2,1)} %param.15), channel_id=1, source_target_pairs={{0,4},{1,5},{2,6},{3,7},{4,0},{5,1},{6,2},{7,3},{8,12},{9,13},{10,... | collective-permute-start | bytes 6291464 | tf_op jit(solution)/shard_map/ppermute | solution.py:383
  135.9 2.1 collective-permute-start.14
  138.0 5.4 %mix.1.mixed_ref = f32[512,1024]{1,0:T(8,128)S(1)} custom-call(bf16[512,1024]{1,0:T(8,128)(2,1)} %get-tuple-element.40.gated_ref, bf16[160,1024]{1,0:T(8,128)(2,1)} %copy-done.15, bf16[2,16,1024]{2,1,0:T(8,128)(2,1)} %get-tuple-element.44.head_ref, f32[3,3,1024]{2,1,0:T(4,128)S(1)} %copy-done.3, f32[3,128,1024]{2,1,0:T(8,128)} %respond.1.response_ref, ...), custom_call_target="tpu_custom_call" | custom-call | tf_op jit(solution)/shard_map/mix/pallas_call | solution.py:344
  143.4 1.9 combine.1
  145.4 2.9 %convolution_convert_fusion.1 = bf16[512,1024]{1,0:T(8,128)(2,1)S(1)} fusion(bf16[512,1024]{1,0:T(8,128)(2,1)S(1)} %combine.1, bf16[1024,1024]{1,0:T(8,128)(2,1)} %param.15), kind=kOutput, calls=%fused_computation.7 | convolution fusion | flops 1074266112 | bytes 4194304 | tf_op jit(solution)/shard_map/dot_general | solution.py:466
  148.3 0.9 constant_dynamic-slice_fusion
  149.2 4.3 %collective-permute-start.22 = (bf16[256,1024]{1,0:T(8,128)(2,1)}, bf16[256,1024]{1,0:T(8,128)(2,1)}, u32[]{:S(2)}, u32[]{:S(2)}) collective-permute-start(bf16[256,1024]{1,0:T(8,128)(2,1)} %constant_dynamic-slice_fusion), channel_id=1, source_target_pairs={{0,1},{3,2},{4,5},{7,6},{8,9},{11,10},{12,13},{15,14},{16,17},{19,... | collective-permute-start | bytes 1572872 | tf_op jit(solution)/shard_map/ppermute | solution.py:383
  153.4 2.9 %convolution_convert_fusion = bf16[512,1024]{1,0:T(8,128)(2,1)S(1)} fusion(bf16[512,1024]{1,0:T(8,128)(2,1)S(1)} %combine.1, bf16[1024,1024]{1,0:T(8,128)(2,1)} %collective-permute-done.15), kind=kOutput, calls=%fused_computation.6 | convolution fusion | flops 1074266112 | bytes 4194304 | tf_op jit(solution)/shard_map/dot_general | solution.py:466
  156.3 0.8 constant_dynamic-slice_fusion.3
  157.1 2.1 collective-permute-start.16
  159.2 4.6 %collective-permute-done.22 = bf16[256,1024]{1,0:T(8,128)(2,1)} collective-permute-done((bf16[256,1024]{1,0:T(8,128)(2,1)}, bf16[256,1024]{1,0:T(8,128)(2,1)}, u32[]{:S(2)}, u32[]{:S(2)}) %collective-permute-start.22) | collective-permute-done | bytes 524320 | tf_op jit(solution)/shard_map/ppermute | solution.py:383
  163.8 2.0 add_convert_fusion
  165.9 1.5 collective-permute-start.23
  167.3 7.7 %collective-permute-done.16 = bf16[256,1024]{1,0:T(8,128)(2,1)} collective-permute-done((bf16[256,1024]{1,0:T(8,128)(2,1)}, bf16[256,1024]{1,0:T(8,128)(2,1)}, u32[]{:S(2)}, u32[]{:S(2)}) %collective-permute-start.16) | collective-permute-done | bytes 524320 | tf_op jit(solution)/shard_map/ppermute | solution.py:383
  175.1 2.9 %fusion.4 = bf16[512,1024]{1,0:T(8,128)(2,1)S(1)} fusion(bf16[512,1024]{1,0:T(8,128)(2,1)S(1)} %combine.1, bf16[4096,1024]{1,0:T(8,128)(2,1)} %all-gather.5.cloned.1.call-done, s32[]{:T(128)S(6)} %select_n.125), kind=kOutput, calls=%fused_computation.4 | convolution fusion | flops 1074266112 | bytes 4194308 | tf_op jit(solution)/shard_map/dot_general | solution.py:466
  178.0 0.9 constant_dynamic-slice_fusion.1
  178.9 5.2 %collective-permute-start.21 = (bf16[256,1024]{1,0:T(8,128)(2,1)}, bf16[256,1024]{1,0:T(8,128)(2,1)}, u32[]{:S(2)}, u32[]{:S(2)}) collective-permute-start(bf16[256,1024]{1,0:T(8,128)(2,1)} %constant_dynamic-slice_fusion.1), channel_id=1, source_target_pairs={{0,1},{3,2},{4,5},{7,6},{8,9},{11,10},{12,13},{15,14},{16,17},{19,... | collective-permute-start | bytes 1572872 | tf_op jit(solution)/shard_map/ppermute | solution.py:383
  184.1 2.9 %fusion.7 = bf16[512,1024]{1,0:T(8,128)(2,1)S(1)} fusion(bf16[512,1024]{1,0:T(8,128)(2,1)S(1)} %combine.1, bf16[4096,1024]{1,0:T(8,128)(2,1)} %all-gather.5.cloned.1.call-done, s32[]{:T(128)S(6)} %select_n.126), kind=kOutput, calls=%fused_computation.5 | convolution fusion | flops 1074266112 | bytes 4194308 | tf_op jit(solution)/shard_map/dot_general | solution.py:466
  187.0 0.9 constant_dynamic-slice_fusion.2
  187.9 0.2 copy-done.8
  188.1 2.1 collective-permute-start.17
  190.2 2.1 add_convert_fusion.2
  192.3 1.5 collective-permute-start.18
  193.8 1.6 collective-permute-done.21
  195.4 1.4 add_convert_fusion.1
  196.8 0.8 collective-permute-start.24
  197.6 9.0 %collective-permute-done.17 = bf16[256,1024]{1,0:T(8,128)(2,1)} collective-permute-done((bf16[256,1024]{1,0:T(8,128)(2,1)}, bf16[256,1024]{1,0:T(8,128)(2,1)}, u32[]{:S(2)}, u32[]{:S(2)}) %collective-permute-start.17) | collective-permute-done | bytes 524320 | tf_op jit(solution)/shard_map/ppermute | solution.py:383
  206.6 1.2 add_convert_fusion.3
  207.8 0.7 collective-permute-start.19
  208.6 1.2 add_convert_fusion.5
  209.7 5.3 %collective-permute-start.27 = (bf16[128,1024]{1,0:T(8,128)(2,1)S(1)}, bf16[128,1024]{1,0:T(8,128)(2,1)S(1)}, u32[]{:S(2)}, u32[]{:S(2)}) collective-permute-start(bf16[128,1024]{1,0:T(8,128)(2,1)S(1)} %add_convert_fusion.5), channel_id=1, source_target_pairs={{0,1},{1,0},{2,3},{3,2},{4,5},{5,4},{6,7},{7,6},{8,9},{9,8},{10,11... | collective-permute-start | bytes 786440 | tf_op jit(solution)/shard_map/ppermute | solution.py:383
  215.0 1.2 add_convert_fusion.7
  216.3 0.1 add_convert_fusion.9
  216.4 2.1 collective-permute-start.25
  218.6 10.5 %collective-permute-start.20 = (bf16[128,1024]{1,0:T(8,128)(2,1)S(1)}, bf16[128,1024]{1,0:T(8,128)(2,1)S(1)}, u32[]{:S(2)}, u32[]{:S(2)}) collective-permute-start(bf16[128,1024]{1,0:T(8,128)(2,1)S(1)} %add_convert_fusion.11), channel_id=1, source_target_pairs={{0,1},{1,0},{2,3},{3,2},{4,5},{5,4},{6,7},{7,6},{8,9},{9,8},{10,11... | collective-permute-start | bytes 786440 | tf_op jit(solution)/shard_map/ppermute | solution.py:383
  229.2 1.6 broadcast_select_fusion.3
  230.8 2.6 %collective-permute-done.25 = bf16[128,1024]{1,0:T(8,128)(2,1)S(1)} collective-permute-done((bf16[128,1024]{1,0:T(8,128)(2,1)S(1)}, bf16[128,1024]{1,0:T(8,128)(2,1)S(1)}, u32[]{:S(2)}, u32[]{:S(2)}) %collective-permute-start.25) | collective-permute-done | bytes 262176 | tf_op jit(solution)/shard_map/ppermute | solution.py:383
  233.4 5.3 %collective-permute-done.20 = bf16[128,1024]{1,0:T(8,128)(2,1)S(1)} collective-permute-done((bf16[128,1024]{1,0:T(8,128)(2,1)S(1)}, bf16[128,1024]{1,0:T(8,128)(2,1)S(1)}, u32[]{:S(2)}, u32[]{:S(2)}) %collective-permute-start.20) | collective-permute-done | bytes 262176 | tf_op jit(solution)/shard_map/ppermute | solution.py:383
  238.6 0.4 broadcast_select_fusion.5
  239.1 0.2 broadcast_select_fusion.1
  239.3 1.0 pad_maximum_fusion
  (65 shorter events, 0.8 us)
Async XLA Ops:
  6.5 1.6 copy-start
  6.5 1.4 copy-start.16
  6.5 87.1 %all-gather.3.cloned.1.call-start = ((), (), s32[]{:S(2)}) async-start(), calls=%async_computation | async-start | bytes 5242880 | tf_op jit(solution)/shard_map/all_gather | solution.py:438
  10.0 165.0 %all-gather.5.cloned.1.call-start = ((), (), s32[]{:S(2)}) async-start(), calls=%async_computation.1 | async-start | bytes 10485760 | tf_op jit(solution)/shard_map/all_gather | solution.py:452
  10.1 26.2 %collective-permute-start.1 = (bf16[512,1024]{1,0:T(8,128)(2,1)S(1)}, bf16[512,1024]{1,0:T(8,128)(2,1)S(1)}, u32[]{:S(2)}, u32[]{:S(2)}) collective-permute-start(bf16[512,1024]{1,0:T(8,128)(2,1)S(1)} %dynamic-slice_bitcast_fusion.2), channel_id=1, source_target_pairs={{0,8},{1,9},{2,10},{3,11},{4,12},{5,13},{6,14},{7,15},{8,0},{9,1},... | collective-permute-start | bytes 3145736 | tf_op jit(solution)/shard_map/ppermute | solution.py:383
  36.3 30.9 %copy-start.10 = (bf16[512,1024]{1,0:T(8,128)(2,1)}, bf16[512,1024]{1,0:T(8,128)(2,1)S(1)}, u32[]{:S(2)}) copy-start(bf16[512,1024]{1,0:T(8,128)(2,1)S(1)} %collective-permute-done.1.rest_2_) | copy-start | bytes 3145732
  36.3 5.6 %copy-start.1 = (f32[128,1024]{1,0:T(8,128)S(1)}, f32[128,1024]{1,0:T(8,128)}, u32[]{:S(2)}) copy-start(f32[128,1024]{1,0:T(8,128)} %filter_ref.1) | copy-start | bytes 1572868
  36.3 5.6 %copy-start.2 = (bf16[256,256]{1,0:T(8,128)(2,1)S(1)}, bf16[256,256]{1,0:T(8,128)(2,1)}, u32[]{:S(2)}) copy-start(bf16[256,256]{1,0:T(8,128)(2,1)} %constant.52.clone.fwd_ref) | copy-start | bytes 393220
  36.3 5.6 %copy-start.5 = (f32[1024]{0:T(1024)S(1)}, f32[1024]{0:T(1024)}, u32[]{:S(2)}) copy-start(f32[1024]{0:T(1024)} %param.14) | copy-start | bytes 12292
  36.3 29.2 %collective-permute-start = (bf16[3,1024,1024]{2,1,0:T(8,128)(2,1)}, bf16[3,1024,1024]{2,1,0:T(8,128)(2,1)}, u32[]{:S(2)}, u32[]{:S(2)}) collective-permute-start(bf16[3,1024,1024]{2,1,0:T(8,128)(2,1)} %bitcast.21), channel_id=1, source_target_pairs={{0,4},{1,5},{2,6},{3,7},{4,0},{5,1},{6,2},{7,3},{8,12},{9,13},{10,... | collective-permute-start | bytes 18874376 | tf_op jit(solution)/shard_map/ppermute | solution.py:383
  38.6 55.1 %copy-start.3 = (f32[3,3,1024]{2,1,0:T(4,128)S(1)}, f32[3,3,1024]{2,1,0:T(4,128)}, u32[]{:S(2)}) copy-start(f32[3,3,1024]{2,1,0:T(4,128)} %taps_ref.2) | copy-start | bytes 110596
  38.6 25.2 %collective-permute-start.5 = (bf16[512,1024]{1,0:T(8,128)(2,1)S(1)}, bf16[512,1024]{1,0:T(8,128)(2,1)S(1)}, u32[]{:S(2)}, u32[]{:S(2)}) collective-permute-start(bf16[512,1024]{1,0:T(8,128)(2,1)S(1)} %get-tuple-element.32), channel_id=1, source_target_pairs={{0,8},{1,9},{2,10},{3,11},{4,12},{5,13},{6,14},{7,15},{8,0},{9,1},... | collective-permute-start | bytes 3145736 | tf_op jit(solution)/shard_map/ppermute | solution.py:383
  40.4 25.1 %collective-permute-start.3 = (bf16[512,1024]{1,0:T(8,128)(2,1)S(1)}, bf16[512,1024]{1,0:T(8,128)(2,1)S(1)}, u32[]{:S(2)}, u32[]{:S(2)}) collective-permute-start(bf16[512,1024]{1,0:T(8,128)(2,1)S(1)} %collective-permute-done.1.rest_2_), channel_id=1, source_target_pairs={{0,16},{1,17},{2,18},{3,19},{4,20},{5,21},{6,22},{7,23},{8,24},{9,... | collective-permute-start | bytes 3145736 | tf_op jit(solution)/shard_map/ppermute | solution.py:383
  63.8 29.9 %copy-start.11 = (bf16[512,1024]{1,0:T(8,128)(2,1)}, bf16[512,1024]{1,0:T(8,128)(2,1)S(1)}, u32[]{:S(2)}) copy-start(bf16[512,1024]{1,0:T(8,128)(2,1)S(1)} %collective-permute-done.5.rest_8_) | copy-start | bytes 3145732
  63.8 24.5 %collective-permute-start.8 = (bf16[512,1024]{1,0:T(8,128)(2,1)S(1)}, bf16[512,1024]{1,0:T(8,128)(2,1)}, u32[]{:S(2)}, u32[]{:S(2)}) collective-permute-start(bf16[512,1024]{1,0:T(8,128)(2,1)S(1)} %get-tuple-element.34), channel_id=1, source_target_pairs={{0,8},{1,9},{2,10},{3,11},{4,12},{5,13},{6,14},{7,15},{8,0},{9,1},... | collective-permute-start | bytes 3145736 | tf_op jit(solution)/shard_map/ppermute | solution.py:383
  65.5 28.2 %copy-start.12 = (bf16[512,1024]{1,0:T(8,128)(2,1)}, bf16[512,1024]{1,0:T(8,128)(2,1)S(1)}, u32[]{:S(2)}) copy-start(bf16[512,1024]{1,0:T(8,128)(2,1)S(1)} %collective-permute-done.3.rest_4_) | copy-start | bytes 3145732
  65.5 24.3 %collective-permute-start.7 = (bf16[512,1024]{1,0:T(8,128)(2,1)S(1)}, bf16[512,1024]{1,0:T(8,128)(2,1)}, u32[]{:S(2)}, u32[]{:S(2)}) collective-permute-start(bf16[512,1024]{1,0:T(8,128)(2,1)S(1)} %collective-permute-done.5.rest_8_), channel_id=1, source_target_pairs={{0,16},{1,17},{2,18},{3,19},{4,20},{5,21},{6,22},{7,23},{8,24},{9,... | collective-permute-start | bytes 3145736 | tf_op jit(solution)/shard_map/ppermute | solution.py:383
  67.1 22.7 %collective-permute-start.2 = (bf16[512,1024]{1,0:T(8,128)(2,1)S(1)}, bf16[512,1024]{1,0:T(8,128)(2,1)S(1)}, u32[]{:S(2)}, u32[]{:S(2)}) collective-permute-start(bf16[512,1024]{1,0:T(8,128)(2,1)S(1)} %collective-permute-done.1.rest_2_), channel_id=1, source_target_pairs={{0,4},{1,5},{2,6},{3,7},{4,0},{5,1},{6,2},{7,3},{8,12},{9,13},{10,... | collective-permute-start | bytes 3145736 | tf_op jit(solution)/shard_map/ppermute | solution.py:383
  67.1 25.4 %collective-permute-start.6 = (bf16[512,1024]{1,0:T(8,128)(2,1)S(1)}, bf16[512,1024]{1,0:T(8,128)(2,1)}, u32[]{:S(2)}, u32[]{:S(2)}) collective-permute-start(bf16[512,1024]{1,0:T(8,128)(2,1)S(1)} %collective-permute-done.5.rest_8_), channel_id=1, source_target_pairs={{0,4},{1,5},{2,6},{3,7},{4,0},{5,1},{6,2},{7,3},{8,12},{9,13},{10,... | collective-permute-start | bytes 3145736 | tf_op jit(solution)/shard_map/ppermute | solution.py:383
  67.6 24.9 %collective-permute-start.4 = (bf16[512,1024]{1,0:T(8,128)(2,1)S(1)}, bf16[512,1024]{1,0:T(8,128)(2,1)}, u32[]{:S(2)}, u32[]{:S(2)}) collective-permute-start(bf16[512,1024]{1,0:T(8,128)(2,1)S(1)} %collective-permute-done.3.rest_4_), channel_id=1, source_target_pairs={{0,4},{1,5},{2,6},{3,7},{4,0},{5,1},{6,2},{7,3},{8,12},{9,13},{10,... | collective-permute-start | bytes 3145736 | tf_op jit(solution)/shard_map/ppermute | solution.py:383
  88.3 4.2 %collective-permute-start.10 = (bf16[512,1024]{1,0:T(8,128)(2,1)}, bf16[512,1024]{1,0:T(8,128)(2,1)}, u32[]{:S(2)}, u32[]{:S(2)}) collective-permute-start(bf16[512,1024]{1,0:T(8,128)(2,1)} %collective-permute-done.8.rest_14_), channel_id=1, source_target_pairs={{0,4},{1,5},{2,6},{3,7},{4,0},{5,1},{6,2},{7,3},{8,12},{9,13},{10,... | collective-permute-start | bytes 3145736 | tf_op jit(solution)/shard_map/ppermute | solution.py:383
  89.8 3.9 %collective-permute-start.9 = (bf16[512,1024]{1,0:T(8,128)(2,1)}, bf16[512,1024]{1,0:T(8,128)(2,1)}, u32[]{:S(2)}, u32[]{:S(2)}) collective-permute-start(bf16[512,1024]{1,0:T(8,128)(2,1)} %collective-permute-done.7.rest_10_), channel_id=1, source_target_pairs={{0,4},{1,5},{2,6},{3,7},{4,0},{5,1},{6,2},{7,3},{8,12},{9,13},{10,... | collective-permute-start | bytes 3145736 | tf_op jit(solution)/shard_map/ppermute | solution.py:383
  89.8 1.1 copy-start.13
  90.9 25.9 %collective-permute-start.12 = (bf16[512,1024]{1,0:T(8,128)(2,1)}, bf16[512,1024]{1,0:T(8,128)(2,1)}, u32[]{:S(2)}, u32[]{:S(2)}) collective-permute-start(bf16[512,1024]{1,0:T(8,128)(2,1)} %collective-permute-done.8.rest_14_), channel_id=1, source_target_pairs={{0,16},{1,17},{2,18},{3,19},{4,20},{5,21},{6,22},{7,23},{8,24},{9,... | collective-permute-start | bytes 3145736 | tf_op jit(solution)/shard_map/ppermute | solution.py:383
  116.8 3.9 %collective-permute-start.13 = (bf16[512,1024]{1,0:T(8,128)(2,1)}, bf16[512,1024]{1,0:T(8,128)(2,1)S(1)}, u32[]{:S(2)}, u32[]{:S(2)}) collective-permute-start(bf16[512,1024]{1,0:T(8,128)(2,1)} %collective-permute-done.12.rest_0_), channel_id=1, source_target_pairs={{0,4},{1,5},{2,6},{3,7},{4,0},{5,1},{6,2},{7,3},{8,12},{9,13},{10,... | collective-permute-start | bytes 3145736 | tf_op jit(solution)/shard_map/ppermute | solution.py:383
  116.8 3.9 %collective-permute-start.11 = (bf16[160,1024]{1,0:T(8,128)(2,1)}, bf16[160,1024]{1,0:T(8,128)(2,1)S(1)}, u32[]{:S(2)}, u32[]{:S(2)}) collective-permute-start(bf16[160,1024]{1,0:T(8,128)(2,1)} %get-tuple-element.37), channel_id=1, source_target_pairs={{0,4},{1,5},{2,6},{3,7},{4,8},{5,9},{6,10},{7,11},{8,12},{9,13},{1... | collective-permute-start | bytes 983048 | tf_op jit(solution)/shard_map/ppermute | solution.py:383
  120.6 17.4 %copy-start.15 = (bf16[160,1024]{1,0:T(8,128)(2,1)}, bf16[160,1024]{1,0:T(8,128)(2,1)S(1)}, u32[]{:S(2)}) copy-start(bf16[160,1024]{1,0:T(8,128)(2,1)S(1)} %collective-permute-done.11.halo_ref) | copy-start | bytes 983044
  120.6 17.4 %copy-start.4 = (bf16[128,768]{1,0:T(8,128)(2,1)S(1)}, bf16[128,768]{1,0:T(8,128)(2,1)}, u32[]{:S(2)}) copy-start(bf16[128,768]{1,0:T(8,128)(2,1)} %constant.53.clone.inv_ref) | copy-start | bytes 589828
  120.6 1.0 copy-start.14
  126.0 27.4 %collective-permute-start.15 = (bf16[1024,1024]{1,0:T(8,128)(2,1)}, bf16[1024,1024]{1,0:T(8,128)(2,1)}, u32[]{:S(2)}, u32[]{:S(2)}) collective-permute-start(bf16[1024,1024]{1,0:T(8,128)(2,1)} %param.15), channel_id=1, source_target_pairs={{0,4},{1,5},{2,6},{3,7},{4,0},{5,1},{6,2},{7,3},{8,12},{9,13},{10,... | collective-permute-start | bytes 6291464 | tf_op jit(solution)/shard_map/ppermute | solution.py:383
  135.9 7.5 %collective-permute-start.14 = (bf16[16,1024]{1,0:T(8,128)(2,1)}, bf16[16,1024]{1,0:T(8,128)(2,1)S(1)}, u32[]{:S(2)}, u32[]{:S(2)}) collective-permute-start(bf16[16,1024]{1,0:T(8,128)(2,1)} %get-tuple-element.43), channel_id=1, source_target_pairs={{0,4},{1,5},{2,6},{3,7},{4,8},{5,9},{6,10},{7,11},{8,12},{9,13},{1... | collective-permute-start | bytes 98312 | tf_op jit(solution)/shard_map/ppermute | solution.py:383
  149.2 14.7 %collective-permute-start.22 = (bf16[256,1024]{1,0:T(8,128)(2,1)}, bf16[256,1024]{1,0:T(8,128)(2,1)}, u32[]{:S(2)}, u32[]{:S(2)}) collective-permute-start(bf16[256,1024]{1,0:T(8,128)(2,1)} %constant_dynamic-slice_fusion), channel_id=1, source_target_pairs={{0,1},{3,2},{4,5},{7,6},{8,9},{11,10},{12,13},{15,14},{16,17},{19,... | collective-permute-start | bytes 1572872 | tf_op jit(solution)/shard_map/ppermute | solution.py:383
  157.1 17.9 %collective-permute-start.16 = (bf16[256,1024]{1,0:T(8,128)(2,1)}, bf16[256,1024]{1,0:T(8,128)(2,1)}, u32[]{:S(2)}, u32[]{:S(2)}) collective-permute-start(bf16[256,1024]{1,0:T(8,128)(2,1)} %constant_dynamic-slice_fusion.3), channel_id=1, source_target_pairs={{0,1},{3,2},{4,5},{7,6},{8,9},{11,10},{12,13},{15,14},{16,17},{19,... | collective-permute-start | bytes 1572872 | tf_op jit(solution)/shard_map/ppermute | solution.py:383
  165.9 30.9 %collective-permute-start.23 = (bf16[256,1024]{1,0:T(8,128)(2,1)}, bf16[256,1024]{1,0:T(8,128)(2,1)}, u32[]{:S(2)}, u32[]{:S(2)}) collective-permute-start(bf16[256,1024]{1,0:T(8,128)(2,1)} %add_convert_fusion), channel_id=1, source_target_pairs={{1,2},{2,1},{5,6},{6,5},{9,10},{10,9},{13,14},{14,13},{17,18},{18,... | collective-permute-start | bytes 1572872 | tf_op jit(solution)/shard_map/ppermute | solution.py:383
  177.9 9.0 %copy-start.6 = (bf16[512,1024]{1,0:T(8,128)(2,1)}, bf16[512,1024]{1,0:T(8,128)(2,1)S(1)}, u32[]{:S(2)}) copy-start(bf16[512,1024]{1,0:T(8,128)(2,1)S(1)} %fusion.4) | copy-start | bytes 3145732
  178.9 16.5 %collective-permute-start.21 = (bf16[256,1024]{1,0:T(8,128)(2,1)}, bf16[256,1024]{1,0:T(8,128)(2,1)}, u32[]{:S(2)}, u32[]{:S(2)}) collective-permute-start(bf16[256,1024]{1,0:T(8,128)(2,1)} %constant_dynamic-slice_fusion.1), channel_id=1, source_target_pairs={{0,1},{3,2},{4,5},{7,6},{8,9},{11,10},{12,13},{15,14},{16,17},{19,... | collective-permute-start | bytes 1572872 | tf_op jit(solution)/shard_map/ppermute | solution.py:383
  187.0 1.1 copy-start.8
  188.1 18.5 %collective-permute-start.17 = (bf16[256,1024]{1,0:T(8,128)(2,1)}, bf16[256,1024]{1,0:T(8,128)(2,1)}, u32[]{:S(2)}, u32[]{:S(2)}) collective-permute-start(bf16[256,1024]{1,0:T(8,128)(2,1)} %constant_dynamic-slice_fusion.2), channel_id=1, source_target_pairs={{0,1},{3,2},{4,5},{7,6},{8,9},{11,10},{12,13},{15,14},{16,17},{19,... | collective-permute-start | bytes 1572872 | tf_op jit(solution)/shard_map/ppermute | solution.py:383
  190.2 16.4 %copy-start.9 = (bf16[512,1024]{1,0:T(8,128)(2,1)S(1)}, bf16[512,1024]{1,0:T(8,128)(2,1)}, u32[]{:S(2)}) copy-start(bf16[512,1024]{1,0:T(8,128)(2,1)} %copy-done.8) | copy-start | bytes 3145732
  192.3 15.5 %collective-permute-start.18 = (bf16[256,1024]{1,0:T(8,128)(2,1)}, bf16[256,1024]{1,0:T(8,128)(2,1)}, u32[]{:S(2)}, u32[]{:S(2)}) collective-permute-start(bf16[256,1024]{1,0:T(8,128)(2,1)} %add_convert_fusion.2), channel_id=1, source_target_pairs={{1,2},{2,1},{5,6},{6,5},{9,10},{10,9},{13,14},{14,13},{17,18},{18,... | collective-permute-start | bytes 1572872 | tf_op jit(solution)/shard_map/ppermute | solution.py:383
  196.8 19.5 %copy-start.7 = (bf16[512,1024]{1,0:T(8,128)(2,1)S(1)}, bf16[512,1024]{1,0:T(8,128)(2,1)}, u32[]{:S(2)}) copy-start(bf16[512,1024]{1,0:T(8,128)(2,1)} %copy-done.6) | copy-start | bytes 3145732
  196.8 19.5 %collective-permute-start.24 = (bf16[256,1024]{1,0:T(8,128)(2,1)S(1)}, bf16[256,1024]{1,0:T(8,128)(2,1)S(1)}, u32[]{:S(2)}, u32[]{:S(2)}) collective-permute-start(bf16[256,1024]{1,0:T(8,128)(2,1)S(1)} %add_convert_fusion.1), channel_id=1, source_target_pairs={{1,2},{2,1},{5,6},{6,5},{9,10},{10,9},{13,14},{14,13},{17,18},{18,... | collective-permute-start | bytes 1572872 | tf_op jit(solution)/shard_map/ppermute | solution.py:383
  207.8 10.6 %collective-permute-start.19 = (bf16[256,1024]{1,0:T(8,128)(2,1)S(1)}, bf16[256,1024]{1,0:T(8,128)(2,1)S(1)}, u32[]{:S(2)}, u32[]{:S(2)}) collective-permute-start(bf16[256,1024]{1,0:T(8,128)(2,1)S(1)} %add_convert_fusion.3), channel_id=1, source_target_pairs={{1,2},{2,1},{5,6},{6,5},{9,10},{10,9},{13,14},{14,13},{17,18},{18,... | collective-permute-start | bytes 1572872 | tf_op jit(solution)/shard_map/ppermute | solution.py:383
  209.7 19.5 %collective-permute-start.27 = (bf16[128,1024]{1,0:T(8,128)(2,1)S(1)}, bf16[128,1024]{1,0:T(8,128)(2,1)S(1)}, u32[]{:S(2)}, u32[]{:S(2)}) collective-permute-start(bf16[128,1024]{1,0:T(8,128)(2,1)S(1)} %add_convert_fusion.5), channel_id=1, source_target_pairs={{0,1},{1,0},{2,3},{3,2},{4,5},{5,4},{6,7},{7,6},{8,9},{9,8},{10,11... | collective-permute-start | bytes 786440 | tf_op jit(solution)/shard_map/ppermute | solution.py:383
  216.2 13.0 %collective-permute-start.26 = (bf16[128,1024]{1,0:T(8,128)(2,1)S(1)}, bf16[128,1024]{1,0:T(8,128)(2,1)S(1)}, u32[]{:S(2)}, u32[]{:S(2)}) collective-permute-start(bf16[128,1024]{1,0:T(8,128)(2,1)S(1)} %add_convert_fusion.7), channel_id=1, source_target_pairs={{0,1},{1,0},{2,3},{3,2},{4,5},{5,4},{6,7},{7,6},{8,9},{9,8},{10,11... | collective-permute-start | bytes 786440 | tf_op jit(solution)/shard_map/ppermute | solution.py:383
  216.4 16.9 %collective-permute-start.25 = (bf16[128,1024]{1,0:T(8,128)(2,1)S(1)}, bf16[128,1024]{1,0:T(8,128)(2,1)S(1)}, u32[]{:S(2)}, u32[]{:S(2)}) collective-permute-start(bf16[128,1024]{1,0:T(8,128)(2,1)S(1)} %add_convert_fusion.9), channel_id=1, source_target_pairs={{0,1},{1,0},{2,3},{3,2},{4,5},{5,4},{6,7},{7,6},{8,9},{9,8},{10,11... | collective-permute-start | bytes 786440 | tf_op jit(solution)/shard_map/ppermute | solution.py:383
  218.6 20.0 %collective-permute-start.20 = (bf16[128,1024]{1,0:T(8,128)(2,1)S(1)}, bf16[128,1024]{1,0:T(8,128)(2,1)S(1)}, u32[]{:S(2)}, u32[]{:S(2)}) collective-permute-start(bf16[128,1024]{1,0:T(8,128)(2,1)S(1)} %add_convert_fusion.11), channel_id=1, source_target_pairs={{0,1},{1,0},{2,3},{3,2},{4,5},{5,4},{6,7},{7,6},{8,9},{9,8},{10,11... | collective-permute-start | bytes 786440 | tf_op jit(solution)/shard_map/ppermute | solution.py:383
Sparse Core Ops, SparseCore 0:
  10.2 83.4 all-gather.2
  95.2 56.8 all-gather.4

commit v8 on v7

--- a/solution.py
+++ b/solution.py
@@ -416,6 +416,9 @@
         far[2] = to_group(after(near[2], far[1], response, peer))
         near[0] = to_chip(after(cut(source, 0, first_half, half), near[2]))
         far[0] = to_group(after(near[0], far[2]))
+        out_half = out_rows // 2
+        mine = lax.dynamic_slice(w_out, (g * out_half, 0), (out_half, channels))
+        near_out = to_chip(after(mine, near[0]))
         for b in (1, 2, 0):
             pieces[b] = [
                 (weights, b, c * rows),
@@ -443,16 +446,15 @@
     halo = to_next(edges)
     late = pieces[0][-1:]
     if paired:
-        late.append((to_core(after(far[0], gated)), None, (c ^ 3) * rows + other_half))
-    projected, tail = query(gathered, late, after(total, halo), width)
+        late.append((to_core(after(far[0], near_out, halo)), None, (c ^ 3) * rows + other_half))
+    projected, tail = query(gathered, late, total, width)
     before = to_next(tail)
     mixed = mix(gated, halo, head, short_filter, response, tables, width)
     combined = combine(projected, before, short_filter, mixed, width)
     if paired:
-        out_full = lax.all_gather(after(w_out, near[1]), "context", axis=0, tiled=True)
+        out_other = lax.all_gather(after(near_out, gated), "groups", axis=0, tiled=True)
         out_peer = to_core(after(w_out, tail))
-        part = lambda i: lax.dynamic_slice(out_full, ((c ^ i) * out_rows, 0), (out_rows, channels))
-        sets = [w_out, out_peer, part(2), part(3)]
+        sets = [w_out, out_peer, out_other, None]
     else:
         sets = [lax.all_gather(w_out, "context", axis=0, tiled=True)]
 
@@ -468,9 +470,11 @@
         ).astype(bf16)
 
     results, firsts, seconds = [], [], []
-    for n, rows_out in enumerate(sets):
-        if paired and n == 2:
-            combined = after(combined, firsts[1])
+    for n in range(len(sets)):
+        if n == 2:
+            sets[2] = after(sets[2], combined, *firsts[:1])
+            sets[3] = to_core(sets[2])
+        rows_out = sets[n]
         partial = product(rows_out)
         combined = after(combined, partial)
 
@@ -484,8 +488,6 @@
             far_pair = block(jnp.where(z < 2, 2, 0), 2)
             firsts.append(send(far_pair, {0: 1, 3: 2}))
             got = plus(far_pair, firsts[-1])
-            if n >= 2:
-                got = after(got, seconds[n - 2])
             got = send(got, {1: 2, 2: 1})
             seconds.append(got)
             low, high = got[:length], got[length:]

time: 248 us -> 245 us (0.988)
  waiting for transfers between devices: 105 us -> 116 us
  other arithmetic: 12.7 us -> 4.51 us
  starting transfers between devices: 62.3 us -> 58.5 us
    all_gather x1, waiting for transfers between devices: 0.01 us -> 7.05 us  [local(): lax.all_gather(after(near_out, gated), 'groups', axis=0, tiled=True)]
    convert_element_type x8, other arithmetic: 9.33 us -> 2.32 us  [plus(): return total.astype(bf16)]
    ppermute x28 -> x30, waiting for transfers between devices: 103 us -> 108 us  [move(): return lax.ppermute(value, axes, pairs)]
    ppermute x28 -> x30, starting transfers between devices: 62.2 us -> 58.4 us  [move(): return lax.ppermute(value, axes, pairs)]
    dynamic_slice x4, local copies, waits for them, and re-layouts: 3.5 us -> 0.17 us  [block(): lax.dynamic_slice(partial, (index * length, 0), (blocks * length, partial...]
  transfers between devices with their start and end apart: 30 -> 32, of which waited for: 13 -> 13; matrix products, arithmetic and copies ran while one was open for 11% -> 8% of each run, Pallas kernels for 12% -> 11%
where the time goes in v8:
time: 245 us; the launch traced here: 244 us
  waiting for transfers between devices  116 us (47%)
  starting transfers between devices  58.5 us (24%)
  Pallas kernels  32.4 us (13%)
  between operations  13.8 us (6%)
  matrix products  11.7 us (5%)
  local copies, waits for them, and re-layouts  7.61 us (3%)
  other arithmetic  4.51 us (2%)
    ppermute x30, waiting for transfers between devices, move(): return lax.ppermute(value, axes, pairs)  108 us
    ppermute x30, starting transfers between devices, move(): return lax.ppermute(value, axes, pairs)  58.4 us
    pallas_call x1, Pallas kernels, gate(): pl.pallas_call(functools.partial(gate_kernel, kinds_of(one), kinds_of(two...  16.5 us
    dot_general x4, matrix products, product(): lax.dot_general(combined, rows_out, (((1,), (1,)), ((), ())), preferred_e...  11.7 us
    all_gather x1, waiting for transfers between devices, local(): lax.all_gather(after(near_out, gated), 'groups', axis=0, tiled=True)  7.05 us
    pallas_call x1, Pallas kernels, mix(): pl.pallas_call(mix_kernel, grid=(channels // width,), in_specs=[col(slab)...  5.37 us
  transfers between devices with their start and end apart: 32, of which 13 were waited for; matrix products, arithmetic and copies ran while one was open for 8% of the time, Pallas kernels for 11%

profile of v8, /device:TPU:0, one launch (start us, length us, event | category | flops | bytes accessed | tf_op | source)
XLA Modules:
  0.0 244.2 jit_solution(18091063711591277489)
XLA Ops:
  6.5 0.5 collective-permute-start
  7.0 1.3 dynamic-slice_bitcast_fusion.2
  8.3 2.0 norm.1
  10.4 2.7 %collective-permute-start.1 = (bf16[512,1024]{1,0:T(8,128)(2,1)S(1)}, bf16[512,1024]{1,0:T(8,128)(2,1)S(1)}, u32[]{:S(2)}, u32[]{:S(2)}) collective-permute-start(bf16[512,1024]{1,0:T(8,128)(2,1)S(1)} %dynamic-slice_bitcast_fusion.2), channel_id=1, source_target_pairs={{0,8},{1,9},{2,10},{3,11},{4,12},{5,13},{6,14},{7,15},{8,0},{9,1},... | collective-permute-start | bytes 3145736 | tf_op jit(solution)/shard_map/ppermute | solution.py:383
  13.1 1.7 dynamic-slice_bitcast_fusion
  14.9 21.9 %collective-permute-done.1.rest_2_ = bf16[512,1024]{1,0:T(8,128)(2,1)S(1)} collective-permute-done((bf16[512,1024]{1,0:T(8,128)(2,1)S(1)}, bf16[512,1024]{1,0:T(8,128)(2,1)S(1)}, u32[]{:S(2)}, u32[]{:S(2)}) %collective-permute-start.1) | collective-permute-done | bytes 1048608 | tf_op jit(solution)/shard_map/ppermute | solution.py:383
  36.8 1.7 collective-permute-start.5
  38.5 1.5 collective-permute-start.3
  40.1 2.3 respond.1.response_ref
  42.3 19.4 %collective-permute-done.5.rest_8_ = bf16[512,1024]{1,0:T(8,128)(2,1)S(1)} collective-permute-done((bf16[512,1024]{1,0:T(8,128)(2,1)S(1)}, bf16[512,1024]{1,0:T(8,128)(2,1)S(1)}, u32[]{:S(2)}, u32[]{:S(2)}) %collective-permute-start.5) | collective-permute-done | bytes 1048608 | tf_op jit(solution)/shard_map/ppermute | solution.py:383
  61.8 1.4 collective-permute-start.8
  63.2 1.5 collective-permute-start.7
  64.7 0.5 collective-permute-start.6
  65.3 20.9 %collective-permute-done.8.rest_14_ = bf16[512,1024]{1,0:T(8,128)(2,1)} collective-permute-done((bf16[512,1024]{1,0:T(8,128)(2,1)S(1)}, bf16[512,1024]{1,0:T(8,128)(2,1)}, u32[]{:S(2)}, u32[]{:S(2)}) %collective-permute-start.8) | collective-permute-done | bytes 1048608 | tf_op jit(solution)/shard_map/ppermute | solution.py:383
  86.2 0.8 collective-permute-done.7.rest_10_
  86.9 2.2 constant_dynamic-slice_fusion.4
  89.2 1.0 collective-permute-start.12
  90.3 1.1 copy-done.9
  91.3 1.5 collective-permute-start.11
  92.9 0.8 all-gather.3.cloned.1.call-done.x_ref
  93.7 16.5 %gate.1 = (bf16[512,1024]{1,0:T(8,128)(2,1)}, bf16[2,16,1024]{2,1,0:T(8,128)(2,1)}, bf16[160,1024]{1,0:T(8,128)(2,1)}, f32[512,1024]{1,0:T(8,128)S(1)}) custom-call(s32[6]{0:T(128)S(1)} %stack.33.at_ref, bf16[512,4096]{1,0:T(8,128)(2,1)} %all-gather.3.cloned.1.call-done.x_ref, f32[3,3,1024]{2,1,0:T(4,128)S(1)} %copy-done.3, bf16[3,1024,1024]{2,1,0:T(8,128)(2,1)} %bitcast.25, ...), custom_call_target="tpu_custom_call" | custom-call | tf_op jit(solution)/shard_map/gate/pallas_call | solution.py:180
  110.2 1.8 collective-permute-start.13
  112.0 3.2 %collective-permute-done.12 = bf16[512,1024]{1,0:T(8,128)(2,1)} collective-permute-done((bf16[512,1024]{1,0:T(8,128)(2,1)}, bf16[512,1024]{1,0:T(8,128)(2,1)}, u32[]{:S(2)}, u32[]{:S(2)}) %collective-permute-start.12) | collective-permute-done | bytes 1048608 | tf_op jit(solution)/shard_map/ppermute | solution.py:383
  115.2 2.0 collective-permute-done.11.rest_0_
  117.2 0.8 collective-permute-start.14
  118.1 2.4 collective-permute-done.14.rest_1_
  120.5 1.0 copy-done.10
  121.5 4.3 %query.1 = (bf16[512,1024]{1,0:T(8,128)(2,1)S(1)}, bf16[16,1024]{1,0:T(8,128)(2,1)}) custom-call(s32[2]{0:T(128)S(1)} %pad_add_fusion.at_ref, bf16[512,4096]{1,0:T(8,128)(2,1)} %all-gather.3.cloned.1.call-done.x_ref, f32[512,1024]{1,0:T(8,128)S(1)} %get-tuple-element.34.sum_ref, bf16[512,1024]{1,0:T(8,128)(2,1)} %collective-permute-done.11.rest_0_, ...), custom_call_target="tpu_custom_call" | custom-call | tf_op jit(solution)/shard_map/query/pallas_call | solution.py:224
  125.9 0.4 collective-permute-start.16
  126.3 2.2 collective-permute-start.15
  128.6 5.4 %mix.1.mixed_ref = f32[512,1024]{1,0:T(8,128)S(1)} custom-call(bf16[512,1024]{1,0:T(8,128)(2,1)} %get-tuple-element.41.gated_ref, bf16[160,1024]{1,0:T(8,128)(2,1)} %copy-done.11, bf16[2,16,1024]{2,1,0:T(8,128)(2,1)} %get-tuple-element.42.head_ref, f32[3,3,1024]{2,1,0:T(4,128)S(1)} %copy-done.3, f32[3,128,1024]{2,1,0:T(8,128)} %respond.1.response_ref, ...), custom_call_target="tpu_custom_call" | custom-call | tf_op jit(solution)/shard_map/mix/pallas_call | solution.py:344
  134.0 1.9 combine.1
  135.9 3.1 %convolution_convert_fusion.3 = bf16[512,1024]{1,0:T(8,128)(2,1)S(1)} fusion(bf16[512,1024]{1,0:T(8,128)(2,1)S(1)} %combine.1, bf16[1024,1024]{1,0:T(8,128)(2,1)} %param.15), kind=kOutput, calls=%fused_computation.3 | convolution fusion | flops 1074266112 | bytes 4194304 | tf_op jit(solution)/shard_map/dot_general | solution.py:468
  139.0 3.7 %collective-permute-start.17 = (bf16[256,1024]{1,0:T(8,128)(2,1)S(1)}, bf16[256,1024]{1,0:T(8,128)(2,1)}, u32[]{:S(2)}, u32[]{:S(2)}) collective-permute-start(bf16[256,1024]{1,0:T(8,128)(2,1)S(1)} %constant_dynamic-slice_fusion.3), channel_id=1, source_target_pairs={{0,1},{3,2},{4,5},{7,6},{8,9},{11,10},{12,13},{15,14},{16,17},{19,... | collective-permute-start | bytes 1572872 | tf_op jit(solution)/shard_map/ppermute | solution.py:383
  142.8 2.9 %convolution_convert_fusion.2 = bf16[512,1024]{1,0:T(8,128)(2,1)S(1)} fusion(bf16[512,1024]{1,0:T(8,128)(2,1)S(1)} %combine.1, bf16[1024,1024]{1,0:T(8,128)(2,1)} %collective-permute-done.16), kind=kOutput, calls=%fused_computation.2 | convolution fusion | flops 1074266112 | bytes 4194304 | tf_op jit(solution)/shard_map/dot_general | solution.py:468
  145.6 7.9 %collective-permute-done.17 = bf16[256,1024]{1,0:T(8,128)(2,1)} collective-permute-done((bf16[256,1024]{1,0:T(8,128)(2,1)S(1)}, bf16[256,1024]{1,0:T(8,128)(2,1)}, u32[]{:S(2)}, u32[]{:S(2)}) %collective-permute-start.17) | collective-permute-done | bytes 524320 | tf_op jit(solution)/shard_map/ppermute | solution.py:383
  153.5 7.0 %all-gather.5.cloned.1.call-done = bf16[1024,1024]{1,0:T(8,128)(2,1)} async-done(((bf16[512,1024]{1,0:T(8,128)(2,1)}), bf16[1024,1024]{1,0:T(8,128)(2,1)}) %all-gather.5.cloned.1.call-update) | async-done | bytes 2097168 | tf_op jit(solution)/shard_map/all_gather | solution.py:455
  160.6 2.9 %convolution_convert_fusion.1 = bf16[512,1024]{1,0:T(8,128)(2,1)S(1)} fusion(bf16[512,1024]{1,0:T(8,128)(2,1)S(1)} %combine.1, bf16[1024,1024]{1,0:T(8,128)(2,1)} %all-gather.5.cloned.1.call-done), kind=kOutput, calls=%fused_computation.1 | convolution fusion | flops 1074266112 | bytes 4194304 | tf_op jit(solution)/shard_map/dot_general | solution.py:468
  163.5 3.4 %collective-permute-start.22 = (bf16[256,1024]{1,0:T(8,128)(2,1)S(1)}, bf16[256,1024]{1,0:T(8,128)(2,1)S(1)}, u32[]{:S(2)}, u32[]{:S(2)}) collective-permute-start(bf16[256,1024]{1,0:T(8,128)(2,1)S(1)} %constant_dynamic-slice_fusion.1), channel_id=1, source_target_pairs={{0,1},{3,2},{4,5},{7,6},{8,9},{11,10},{12,13},{15,14},{16,17},{19,... | collective-permute-start | bytes 1572872 | tf_op jit(solution)/shard_map/ppermute | solution.py:383
  167.0 1.3 collective-permute-start.25
  168.3 2.9 %convolution_convert_fusion = bf16[512,1024]{1,0:T(8,128)(2,1)S(1)} fusion(bf16[512,1024]{1,0:T(8,128)(2,1)S(1)} %combine.1, bf16[1024,1024]{1,0:T(8,128)(2,1)} %collective-permute-done.18), kind=kOutput, calls=%fused_computation | convolution fusion | flops 1074266112 | bytes 4194304 | tf_op jit(solution)/shard_map/dot_general | solution.py:468
  171.3 1.3 collective-permute-start.19
  172.6 1.2 add_convert_fusion
  173.8 0.7 collective-permute-start.28
  174.5 15.8 %collective-permute-done.25 = bf16[256,1024]{1,0:T(8,128)(2,1)S(1)} collective-permute-done((bf16[256,1024]{1,0:T(8,128)(2,1)S(1)}, bf16[256,1024]{1,0:T(8,128)(2,1)S(1)}, u32[]{:S(2)}, u32[]{:S(2)}) %collective-permute-start.25) | collective-permute-done | bytes 524320 | tf_op jit(solution)/shard_map/ppermute | solution.py:383
  190.4 0.2 add_convert_fusion.1
  190.6 0.7 collective-permute-start.26
  191.3 0.2 add_convert_fusion.2
  191.5 0.7 collective-permute-start.23
  192.2 9.0 %collective-permute-done.19 = bf16[256,1024]{1,0:T(8,128)(2,1)S(1)} collective-permute-done((bf16[256,1024]{1,0:T(8,128)(2,1)S(1)}, bf16[256,1024]{1,0:T(8,128)(2,1)S(1)}, u32[]{:S(2)}, u32[]{:S(2)}) %collective-permute-start.19) | collective-permute-done | bytes 524320 | tf_op jit(solution)/shard_map/ppermute | solution.py:383
  201.2 0.2 add_convert_fusion.3
  201.4 0.7 collective-permute-start.20
  202.1 0.1 add_convert_fusion.5
  202.3 5.2 %collective-permute-start.29 = (bf16[128,1024]{1,0:T(8,128)(2,1)S(1)}, bf16[128,1024]{1,0:T(8,128)(2,1)S(1)}, u32[]{:S(2)}, u32[]{:S(2)}) collective-permute-start(bf16[128,1024]{1,0:T(8,128)(2,1)S(1)} %add_convert_fusion.5), channel_id=1, source_target_pairs={{0,1},{1,0},{2,3},{3,2},{4,5},{5,4},{6,7},{7,6},{8,9},{9,8},{10,11... | collective-permute-start | bytes 786440 | tf_op jit(solution)/shard_map/ppermute | solution.py:383
  207.6 2.4 collective-permute-start.27
  210.0 0.1 add_convert_fusion.9
  210.1 11.1 %collective-permute-start.24 = (bf16[128,1024]{1,0:T(8,128)(2,1)S(1)}, bf16[128,1024]{1,0:T(8,128)(2,1)S(1)}, u32[]{:S(2)}, u32[]{:S(2)}) collective-permute-start(bf16[128,1024]{1,0:T(8,128)(2,1)S(1)} %add_convert_fusion.9), channel_id=1, source_target_pairs={{0,1},{1,0},{2,3},{3,2},{4,5},{5,4},{6,7},{7,6},{8,9},{9,8},{10,11... | collective-permute-start | bytes 786440 | tf_op jit(solution)/shard_map/ppermute | solution.py:383
  221.2 0.1 add_convert_fusion.11
  221.4 9.4 %collective-permute-start.21 = (bf16[128,1024]{1,0:T(8,128)(2,1)S(1)}, bf16[128,1024]{1,0:T(8,128)(2,1)S(1)}, u32[]{:S(2)}, u32[]{:S(2)}) collective-permute-start(bf16[128,1024]{1,0:T(8,128)(2,1)S(1)} %add_convert_fusion.11), channel_id=1, source_target_pairs={{0,1},{1,0},{2,3},{3,2},{4,5},{5,4},{6,7},{7,6},{8,9},{9,8},{10,11... | collective-permute-start | bytes 786440 | tf_op jit(solution)/shard_map/ppermute | solution.py:383
  230.8 0.4 broadcast_select_fusion.3
  231.2 4.4 %collective-permute-done.21 = bf16[128,1024]{1,0:T(8,128)(2,1)S(1)} collective-permute-done((bf16[128,1024]{1,0:T(8,128)(2,1)S(1)}, bf16[128,1024]{1,0:T(8,128)(2,1)S(1)}, u32[]{:S(2)}, u32[]{:S(2)}) %collective-permute-start.21) | collective-permute-done | bytes 262176 | tf_op jit(solution)/shard_map/ppermute | solution.py:383
  235.7 0.4 broadcast_select_fusion.5
  236.1 0.2 broadcast_select_fusion.1
  236.3 1.0 pad_maximum_fusion
  (62 shorter events, 0.7 us)
Async XLA Ops:
  6.5 1.8 copy-start
  6.5 1.8 copy-start.12
  6.5 87.1 %all-gather.3.cloned.1.call-start = ((), (), s32[]{:S(2)}) async-start(), calls=%async_computation | async-start | bytes 5242880 | tf_op jit(solution)/shard_map/all_gather | solution.py:441
  6.5 56.7 %collective-permute-start = (bf16[3,1024,1024]{2,1,0:T(8,128)(2,1)}, bf16[3,1024,1024]{2,1,0:T(8,128)(2,1)}, u32[]{:S(2)}, u32[]{:S(2)}) collective-permute-start(bf16[3,1024,1024]{2,1,0:T(8,128)(2,1)} %bitcast.23), channel_id=1, source_target_pairs={{0,4},{1,5},{2,6},{3,7},{4,0},{5,1},{6,2},{7,3},{8,12},{9,13},{10,... | collective-permute-start | bytes 18874376 | tf_op jit(solution)/shard_map/ppermute | solution.py:383
  10.3 29.7 %copy-start.1 = (f32[128,1024]{1,0:T(8,128)S(1)}, f32[128,1024]{1,0:T(8,128)}, u32[]{:S(2)}) copy-start(f32[128,1024]{1,0:T(8,128)} %filter_ref.1) | copy-start | bytes 1572868
  10.3 29.7 %copy-start.2 = (bf16[256,256]{1,0:T(8,128)(2,1)S(1)}, bf16[256,256]{1,0:T(8,128)(2,1)}, u32[]{:S(2)}) copy-start(bf16[256,256]{1,0:T(8,128)(2,1)} %constant.50.clone.fwd_ref) | copy-start | bytes 393220
  10.3 29.7 %copy-start.5 = (f32[1024]{0:T(1024)S(1)}, f32[1024]{0:T(1024)}, u32[]{:S(2)}) copy-start(f32[1024]{0:T(1024)} %param.14) | copy-start | bytes 12292
  10.3 150.2 %all-gather.5.cloned.1.call-start = ((), (), s32[]{:S(2)}) async-start(), calls=%async_computation.1 | async-start | bytes 3145728 | tf_op jit(solution)/shard_map/all_gather | solution.py:455
  10.4 26.4 %collective-permute-start.1 = (bf16[512,1024]{1,0:T(8,128)(2,1)S(1)}, bf16[512,1024]{1,0:T(8,128)(2,1)S(1)}, u32[]{:S(2)}, u32[]{:S(2)}) collective-permute-start(bf16[512,1024]{1,0:T(8,128)(2,1)S(1)} %dynamic-slice_bitcast_fusion.2), channel_id=1, source_target_pairs={{0,8},{1,9},{2,10},{3,11},{4,12},{5,13},{6,14},{7,15},{8,0},{9,1},... | collective-permute-start | bytes 3145736 | tf_op jit(solution)/shard_map/ppermute | solution.py:383
  36.8 52.4 %copy-start.6 = (bf16[512,1024]{1,0:T(8,128)(2,1)}, bf16[512,1024]{1,0:T(8,128)(2,1)S(1)}, u32[]{:S(2)}) copy-start(bf16[512,1024]{1,0:T(8,128)(2,1)S(1)} %collective-permute-done.1.rest_2_) | copy-start | bytes 3145732
  36.8 25.0 %collective-permute-start.5 = (bf16[512,1024]{1,0:T(8,128)(2,1)S(1)}, bf16[512,1024]{1,0:T(8,128)(2,1)S(1)}, u32[]{:S(2)}, u32[]{:S(2)}) collective-permute-start(bf16[512,1024]{1,0:T(8,128)(2,1)S(1)} %get-tuple-element.30), channel_id=1, source_target_pairs={{0,8},{1,9},{2,10},{3,11},{4,12},{5,13},{6,14},{7,15},{8,0},{9,1},... | collective-permute-start | bytes 3145736 | tf_op jit(solution)/shard_map/ppermute | solution.py:383
  38.5 24.7 %collective-permute-start.3 = (bf16[512,1024]{1,0:T(8,128)(2,1)S(1)}, bf16[512,1024]{1,0:T(8,128)(2,1)}, u32[]{:S(2)}, u32[]{:S(2)}) collective-permute-start(bf16[512,1024]{1,0:T(8,128)(2,1)S(1)} %collective-permute-done.1.rest_2_), channel_id=1, source_target_pairs={{0,16},{1,17},{2,18},{3,19},{4,20},{5,21},{6,22},{7,23},{8,24},{9,... | collective-permute-start | bytes 3145736 | tf_op jit(solution)/shard_map/ppermute | solution.py:383
  40.1 53.6 %copy-start.3 = (f32[3,3,1024]{2,1,0:T(4,128)S(1)}, f32[3,3,1024]{2,1,0:T(4,128)}, u32[]{:S(2)}) copy-start(f32[3,3,1024]{2,1,0:T(4,128)} %taps_ref.2) | copy-start | bytes 110596
  61.8 31.0 %copy-start.7 = (bf16[512,1024]{1,0:T(8,128)(2,1)}, bf16[512,1024]{1,0:T(8,128)(2,1)S(1)}, u32[]{:S(2)}) copy-start(bf16[512,1024]{1,0:T(8,128)(2,1)S(1)} %collective-permute-done.5.rest_8_) | copy-start | bytes 3145732
  61.8 24.4 %collective-permute-start.8 = (bf16[512,1024]{1,0:T(8,128)(2,1)S(1)}, bf16[512,1024]{1,0:T(8,128)(2,1)}, u32[]{:S(2)}, u32[]{:S(2)}) collective-permute-start(bf16[512,1024]{1,0:T(8,128)(2,1)S(1)} %get-tuple-element.32), channel_id=1, source_target_pairs={{0,8},{1,9},{2,10},{3,11},{4,12},{5,13},{6,14},{7,15},{8,0},{9,1},... | collective-permute-start | bytes 3145736 | tf_op jit(solution)/shard_map/ppermute | solution.py:383
  63.2 23.7 %collective-permute-start.7 = (bf16[512,1024]{1,0:T(8,128)(2,1)S(1)}, bf16[512,1024]{1,0:T(8,128)(2,1)}, u32[]{:S(2)}, u32[]{:S(2)}) collective-permute-start(bf16[512,1024]{1,0:T(8,128)(2,1)S(1)} %collective-permute-done.5.rest_8_), channel_id=1, source_target_pairs={{0,16},{1,17},{2,18},{3,19},{4,20},{5,21},{6,22},{7,23},{8,24},{9,... | collective-permute-start | bytes 3145736 | tf_op jit(solution)/shard_map/ppermute | solution.py:383
  64.7 24.5 %collective-permute-start.2 = (bf16[512,1024]{1,0:T(8,128)(2,1)S(1)}, bf16[512,1024]{1,0:T(8,128)(2,1)S(1)}, u32[]{:S(2)}, u32[]{:S(2)}) collective-permute-start(bf16[512,1024]{1,0:T(8,128)(2,1)S(1)} %collective-permute-done.1.rest_2_), channel_id=1, source_target_pairs={{0,4},{1,5},{2,6},{3,7},{4,0},{5,1},{6,2},{7,3},{8,12},{9,13},{10,... | collective-permute-start | bytes 3145736 | tf_op jit(solution)/shard_map/ppermute | solution.py:383
  64.7 25.5 %collective-permute-start.6 = (bf16[512,1024]{1,0:T(8,128)(2,1)S(1)}, bf16[512,1024]{1,0:T(8,128)(2,1)S(1)}, u32[]{:S(2)}, u32[]{:S(2)}) collective-permute-start(bf16[512,1024]{1,0:T(8,128)(2,1)S(1)} %collective-permute-done.5.rest_8_), channel_id=1, source_target_pairs={{0,4},{1,5},{2,6},{3,7},{4,0},{5,1},{6,2},{7,3},{8,12},{9,13},{10,... | collective-permute-start | bytes 3145736 | tf_op jit(solution)/shard_map/ppermute | solution.py:383
  65.2 27.7 %collective-permute-start.4 = (bf16[512,1024]{1,0:T(8,128)(2,1)}, bf16[512,1024]{1,0:T(8,128)(2,1)}, u32[]{:S(2)}, u32[]{:S(2)}) collective-permute-start(bf16[512,1024]{1,0:T(8,128)(2,1)} %collective-permute-done.3.rest_4_), channel_id=1, source_target_pairs={{0,4},{1,5},{2,6},{3,7},{4,0},{5,1},{6,2},{7,3},{8,12},{9,13},{10,... | collective-permute-start | bytes 3145736 | tf_op jit(solution)/shard_map/ppermute | solution.py:383
  86.2 6.8 %collective-permute-start.10 = (bf16[512,1024]{1,0:T(8,128)(2,1)}, bf16[512,1024]{1,0:T(8,128)(2,1)}, u32[]{:S(2)}, u32[]{:S(2)}) collective-permute-start(bf16[512,1024]{1,0:T(8,128)(2,1)} %collective-permute-done.8.rest_14_), channel_id=1, source_target_pairs={{0,4},{1,5},{2,6},{3,7},{4,0},{5,1},{6,2},{7,3},{8,12},{9,13},{10,... | collective-permute-start | bytes 3145736 | tf_op jit(solution)/shard_map/ppermute | solution.py:383
  86.9 6.7 %collective-permute-start.9 = (bf16[512,1024]{1,0:T(8,128)(2,1)}, bf16[512,1024]{1,0:T(8,128)(2,1)}, u32[]{:S(2)}, u32[]{:S(2)}) collective-permute-start(bf16[512,1024]{1,0:T(8,128)(2,1)} %collective-permute-done.7.rest_10_), channel_id=1, source_target_pairs={{0,4},{1,5},{2,6},{3,7},{4,0},{5,1},{6,2},{7,3},{8,12},{9,13},{10,... | collective-permute-start | bytes 3145736 | tf_op jit(solution)/shard_map/ppermute | solution.py:383
  89.2 1.1 copy-start.8
  89.2 26.0 %collective-permute-start.12 = (bf16[512,1024]{1,0:T(8,128)(2,1)}, bf16[512,1024]{1,0:T(8,128)(2,1)}, u32[]{:S(2)}, u32[]{:S(2)}) collective-permute-start(bf16[512,1024]{1,0:T(8,128)(2,1)} %constant_dynamic-slice_fusion.4), channel_id=1, source_target_pairs={{0,8},{1,9},{2,10},{3,11},{4,12},{5,13},{6,14},{7,15},{8,0},{9,1},... | collective-permute-start | bytes 3145736 | tf_op jit(solution)/shard_map/ppermute | solution.py:383
  90.2 1.1 copy-start.9
  91.3 25.9 %collective-permute-start.11 = (bf16[512,1024]{1,0:T(8,128)(2,1)}, bf16[512,1024]{1,0:T(8,128)(2,1)}, u32[]{:S(2)}, u32[]{:S(2)}) collective-permute-start(bf16[512,1024]{1,0:T(8,128)(2,1)} %collective-permute-done.8.rest_14_), channel_id=1, source_target_pairs={{0,16},{1,17},{2,18},{3,19},{4,20},{5,21},{6,22},{7,23},{8,24},{9,... | collective-permute-start | bytes 3145736 | tf_op jit(solution)/shard_map/ppermute | solution.py:383
  110.2 7.0 %collective-permute-start.13 = (bf16[160,1024]{1,0:T(8,128)(2,1)}, bf16[160,1024]{1,0:T(8,128)(2,1)S(1)}, u32[]{:S(2)}, u32[]{:S(2)}) collective-permute-start(bf16[160,1024]{1,0:T(8,128)(2,1)} %get-tuple-element.37), channel_id=1, source_target_pairs={{0,4},{1,5},{2,6},{3,7},{4,8},{5,9},{6,10},{7,11},{8,12},{9,13},{1... | collective-permute-start | bytes 983048 | tf_op jit(solution)/shard_map/ppermute | solution.py:383
  117.2 3.4 %copy-start.11 = (bf16[160,1024]{1,0:T(8,128)(2,1)}, bf16[160,1024]{1,0:T(8,128)(2,1)S(1)}, u32[]{:S(2)}) copy-start(bf16[160,1024]{1,0:T(8,128)(2,1)S(1)} %collective-permute-done.13.halo_ref) | copy-start | bytes 983044
  117.2 3.3 %collective-permute-start.14 = (bf16[512,1024]{1,0:T(8,128)(2,1)}, bf16[512,1024]{1,0:T(8,128)(2,1)S(1)}, u32[]{:S(2)}, u32[]{:S(2)}) collective-permute-start(bf16[512,1024]{1,0:T(8,128)(2,1)} %collective-permute-done.11.rest_0_), channel_id=1, source_target_pairs={{0,4},{1,5},{2,6},{3,7},{4,0},{5,1},{6,2},{7,3},{8,12},{9,13},{10,... | collective-permute-start | bytes 3145736 | tf_op jit(solution)/shard_map/ppermute | solution.py:383
  120.5 1.0 copy-start.10
  121.5 7.0 %copy-start.4 = (bf16[128,768]{1,0:T(8,128)(2,1)S(1)}, bf16[128,768]{1,0:T(8,128)(2,1)}, u32[]{:S(2)}) copy-start(bf16[128,768]{1,0:T(8,128)(2,1)} %constant.51.clone.inv_ref) | copy-start | bytes 589828
  125.9 16.9 %collective-permute-start.16 = (bf16[1024,1024]{1,0:T(8,128)(2,1)}, bf16[1024,1024]{1,0:T(8,128)(2,1)}, u32[]{:S(2)}, u32[]{:S(2)}) collective-permute-start(bf16[1024,1024]{1,0:T(8,128)(2,1)} %param.15), channel_id=1, source_target_pairs={{0,4},{1,5},{2,6},{3,7},{4,0},{5,1},{6,2},{7,3},{8,12},{9,13},{10,... | collective-permute-start | bytes 6291464 | tf_op jit(solution)/shard_map/ppermute | solution.py:383
  126.3 7.6 %collective-permute-start.15 = (bf16[16,1024]{1,0:T(8,128)(2,1)}, bf16[16,1024]{1,0:T(8,128)(2,1)S(1)}, u32[]{:S(2)}, u32[]{:S(2)}) collective-permute-start(bf16[16,1024]{1,0:T(8,128)(2,1)} %get-tuple-element.40), channel_id=1, source_target_pairs={{0,4},{1,5},{2,6},{3,7},{4,8},{5,9},{6,10},{7,11},{8,12},{9,13},{1... | collective-permute-start | bytes 98312 | tf_op jit(solution)/shard_map/ppermute | solution.py:383
  139.0 14.5 %collective-permute-start.17 = (bf16[256,1024]{1,0:T(8,128)(2,1)S(1)}, bf16[256,1024]{1,0:T(8,128)(2,1)}, u32[]{:S(2)}, u32[]{:S(2)}) collective-permute-start(bf16[256,1024]{1,0:T(8,128)(2,1)S(1)} %constant_dynamic-slice_fusion.3), channel_id=1, source_target_pairs={{0,1},{3,2},{4,5},{7,6},{8,9},{11,10},{12,13},{15,14},{16,17},{19,... | collective-permute-start | bytes 1572872 | tf_op jit(solution)/shard_map/ppermute | solution.py:383
  160.6 7.7 %collective-permute-start.18 = (bf16[1024,1024]{1,0:T(8,128)(2,1)}, bf16[1024,1024]{1,0:T(8,128)(2,1)}, u32[]{:S(2)}, u32[]{:S(2)}) collective-permute-start(bf16[1024,1024]{1,0:T(8,128)(2,1)} %all-gather.5.cloned.1.call-done), channel_id=1, source_target_pairs={{0,4},{1,5},{2,6},{3,7},{4,0},{5,1},{6,2},{7,3},{8,12},{9,13},{10,... | collective-permute-start | bytes 6291464 | tf_op jit(solution)/shard_map/ppermute | solution.py:383
  163.5 27.8 %collective-permute-start.22 = (bf16[256,1024]{1,0:T(8,128)(2,1)S(1)}, bf16[256,1024]{1,0:T(8,128)(2,1)S(1)}, u32[]{:S(2)}, u32[]{:S(2)}) collective-permute-start(bf16[256,1024]{1,0:T(8,128)(2,1)S(1)} %constant_dynamic-slice_fusion.1), channel_id=1, source_target_pairs={{0,1},{3,2},{4,5},{7,6},{8,9},{11,10},{12,13},{15,14},{16,17},{19,... | collective-permute-start | bytes 1572872 | tf_op jit(solution)/shard_map/ppermute | solution.py:383
  167.0 23.4 %collective-permute-start.25 = (bf16[256,1024]{1,0:T(8,128)(2,1)S(1)}, bf16[256,1024]{1,0:T(8,128)(2,1)S(1)}, u32[]{:S(2)}, u32[]{:S(2)}) collective-permute-start(bf16[256,1024]{1,0:T(8,128)(2,1)S(1)} %constant_dynamic-slice_fusion), channel_id=1, source_target_pairs={{0,1},{3,2},{4,5},{7,6},{8,9},{11,10},{12,13},{15,14},{16,17},{19,... | collective-permute-start | bytes 1572872 | tf_op jit(solution)/shard_map/ppermute | solution.py:383
  171.3 29.9 %collective-permute-start.19 = (bf16[256,1024]{1,0:T(8,128)(2,1)S(1)}, bf16[256,1024]{1,0:T(8,128)(2,1)S(1)}, u32[]{:S(2)}, u32[]{:S(2)}) collective-permute-start(bf16[256,1024]{1,0:T(8,128)(2,1)S(1)} %constant_dynamic-slice_fusion.2), channel_id=1, source_target_pairs={{0,1},{3,2},{4,5},{7,6},{8,9},{11,10},{12,13},{15,14},{16,17},{19,... | collective-permute-start | bytes 1572872 | tf_op jit(solution)/shard_map/ppermute | solution.py:383
  173.8 28.3 %collective-permute-start.28 = (bf16[256,1024]{1,0:T(8,128)(2,1)S(1)}, bf16[256,1024]{1,0:T(8,128)(2,1)S(1)}, u32[]{:S(2)}, u32[]{:S(2)}) collective-permute-start(bf16[256,1024]{1,0:T(8,128)(2,1)S(1)} %add_convert_fusion), channel_id=1, source_target_pairs={{1,2},{2,1},{5,6},{6,5},{9,10},{10,9},{13,14},{14,13},{17,18},{18,... | collective-permute-start | bytes 1572872 | tf_op jit(solution)/shard_map/ppermute | solution.py:383
  190.6 16.9 %collective-permute-start.26 = (bf16[256,1024]{1,0:T(8,128)(2,1)S(1)}, bf16[256,1024]{1,0:T(8,128)(2,1)S(1)}, u32[]{:S(2)}, u32[]{:S(2)}) collective-permute-start(bf16[256,1024]{1,0:T(8,128)(2,1)S(1)} %add_convert_fusion.1), channel_id=1, source_target_pairs={{1,2},{2,1},{5,6},{6,5},{9,10},{10,9},{13,14},{14,13},{17,18},{18,... | collective-permute-start | bytes 1572872 | tf_op jit(solution)/shard_map/ppermute | solution.py:383
  191.5 18.5 %collective-permute-start.23 = (bf16[256,1024]{1,0:T(8,128)(2,1)S(1)}, bf16[256,1024]{1,0:T(8,128)(2,1)S(1)}, u32[]{:S(2)}, u32[]{:S(2)}) collective-permute-start(bf16[256,1024]{1,0:T(8,128)(2,1)S(1)} %add_convert_fusion.2), channel_id=1, source_target_pairs={{1,2},{2,1},{5,6},{6,5},{9,10},{10,9},{13,14},{14,13},{17,18},{18,... | collective-permute-start | bytes 1572872 | tf_op jit(solution)/shard_map/ppermute | solution.py:383
  201.4 19.8 %collective-permute-start.20 = (bf16[256,1024]{1,0:T(8,128)(2,1)S(1)}, bf16[256,1024]{1,0:T(8,128)(2,1)S(1)}, u32[]{:S(2)}, u32[]{:S(2)}) collective-permute-start(bf16[256,1024]{1,0:T(8,128)(2,1)S(1)} %add_convert_fusion.3), channel_id=1, source_target_pairs={{1,2},{2,1},{5,6},{6,5},{9,10},{10,9},{13,14},{14,13},{17,18},{18,... | collective-permute-start | bytes 1572872 | tf_op jit(solution)/shard_map/ppermute | solution.py:383
  202.3 28.5 %collective-permute-start.29 = (bf16[128,1024]{1,0:T(8,128)(2,1)S(1)}, bf16[128,1024]{1,0:T(8,128)(2,1)S(1)}, u32[]{:S(2)}, u32[]{:S(2)}) collective-permute-start(bf16[128,1024]{1,0:T(8,128)(2,1)S(1)} %add_convert_fusion.5), channel_id=1, source_target_pairs={{0,1},{1,0},{2,3},{3,2},{4,5},{5,4},{6,7},{7,6},{8,9},{9,8},{10,11... | collective-permute-start | bytes 786440 | tf_op jit(solution)/shard_map/ppermute | solution.py:383
  207.6 23.1 %collective-permute-start.27 = (bf16[128,1024]{1,0:T(8,128)(2,1)S(1)}, bf16[128,1024]{1,0:T(8,128)(2,1)S(1)}, u32[]{:S(2)}, u32[]{:S(2)}) collective-permute-start(bf16[128,1024]{1,0:T(8,128)(2,1)S(1)} %add_convert_fusion.7), channel_id=1, source_target_pairs={{0,1},{1,0},{2,3},{3,2},{4,5},{5,4},{6,7},{7,6},{8,9},{9,8},{10,11... | collective-permute-start | bytes 786440 | tf_op jit(solution)/shard_map/ppermute | solution.py:383
  210.1 21.1 %collective-permute-start.24 = (bf16[128,1024]{1,0:T(8,128)(2,1)S(1)}, bf16[128,1024]{1,0:T(8,128)(2,1)S(1)}, u32[]{:S(2)}, u32[]{:S(2)}) collective-permute-start(bf16[128,1024]{1,0:T(8,128)(2,1)S(1)} %add_convert_fusion.9), channel_id=1, source_target_pairs={{0,1},{1,0},{2,3},{3,2},{4,5},{5,4},{6,7},{7,6},{8,9},{9,8},{10,11... | collective-permute-start | bytes 786440 | tf_op jit(solution)/shard_map/ppermute | solution.py:383
  221.4 14.3 %collective-permute-start.21 = (bf16[128,1024]{1,0:T(8,128)(2,1)S(1)}, bf16[128,1024]{1,0:T(8,128)(2,1)S(1)}, u32[]{:S(2)}, u32[]{:S(2)}) collective-permute-start(bf16[128,1024]{1,0:T(8,128)(2,1)S(1)} %add_convert_fusion.11), channel_id=1, source_target_pairs={{0,1},{1,0},{2,3},{3,2},{4,5},{5,4},{6,7},{7,6},{8,9},{9,8},{10,11... | collective-permute-start | bytes 786440 | tf_op jit(solution)/shard_map/ppermute | solution.py:383
Sparse Core Ops, SparseCore 0:
  10.4 83.1 all-gather.2
  126.4 34.0 all-gather.4

commit v9 on v8

--- a/solution.py
+++ b/solution.py
@@ -472,8 +472,8 @@
     results, firsts, seconds = [], [], []
     for n in range(len(sets)):
         if n == 2:
-            sets[2] = after(sets[2], combined, *firsts[:1])
-            sets[3] = to_core(sets[2])
+            sets[2] = after(sets[2], firsts[1])
+            sets[3] = to_core(after(sets[2], seconds[0]))
         rows_out = sets[n]
         partial = product(rows_out)
         combined = after(combined, partial)

time: 245 us -> 241 us (0.984)
  waiting for transfers between devices: 116 us -> 106 us
  other arithmetic: 4.51 us -> 9.65 us
  local copies, waits for them, and re-layouts: 7.61 us -> 10.9 us
    ppermute x30, waiting for transfers between devices: 108 us -> 100 us  [move(): return lax.ppermute(value, axes, pairs)]
    convert_element_type x8, other arithmetic: 2.32 us -> 6.47 us  [plus(): return total.astype(bf16)]
    dynamic_slice x4, local copies, waits for them, and re-layouts: 0.17 us -> 2.69 us  [block(): lax.dynamic_slice(partial, (index * length, 0), (blocks * length, partial...]
  transfers between devices with their start and end apart: 32 -> 32, of which waited for: 13 -> 16; matrix products, arithmetic and copies ran while one was open for 8% -> 11% of each run, Pallas kernels for 11% -> 12%
where the time goes in v9:
time: 241 us
  waiting for transfers between devices  106 us (44%)
  starting transfers between devices  57.5 us (24%)
  Pallas kernels  32.4 us (13%)
  between operations  13.8 us (6%)
  local copies, waits for them, and re-layouts  10.9 us (5%)
  matrix products  10.1 us (4%)
  other arithmetic  9.65 us (4%)
    ppermute x30, waiting for transfers between devices, move(): return lax.ppermute(value, axes, pairs)  100 us
    ppermute x30, starting transfers between devices, move(): return lax.ppermute(value, axes, pairs)  57.5 us
    pallas_call x1, Pallas kernels, gate(): pl.pallas_call(functools.partial(gate_kernel, kinds_of(one), kinds_of(two...  16.5 us
    dot_general x4, matrix products, product(): lax.dot_general(combined, rows_out, (((1,), (1,)), ((), ())), preferred_e...  10.1 us
    convert_element_type x8, other arithmetic, plus(): return total.astype(bf16)  6.47 us
    all_gather x1, waiting for transfers between devices, local(): lax.all_gather(after(near_out, gated), 'groups', axis=0, tiled=True)  5.64 us
    pallas_call x1, Pallas kernels, mix(): pl.pallas_call(mix_kernel, grid=(channels // width,), in_specs=[col(slab)...  5.37 us
  transfers between devices with their start and end apart: 32, of which 16 were waited for; matrix products, arithmetic and copies ran while one was open for 11% of the time, Pallas kernels for 12%

profile of v9, /device:TPU:0, one launch (start us, length us, event | category | flops | bytes accessed | tf_op | source)
XLA Modules:
  0.0 240.6 jit_solution(6459627766688997701)
XLA Ops:
  6.5 0.5 collective-permute-start
  7.0 1.3 dynamic-slice_bitcast_fusion.2
  8.3 2.0 norm.1
  10.4 2.7 %collective-permute-start.1 = (bf16[512,1024]{1,0:T(8,128)(2,1)S(1)}, bf16[512,1024]{1,0:T(8,128)(2,1)S(1)}, u32[]{:S(2)}, u32[]{:S(2)}) collective-permute-start(bf16[512,1024]{1,0:T(8,128)(2,1)S(1)} %dynamic-slice_bitcast_fusion.2), channel_id=1, source_target_pairs={{0,8},{1,9},{2,10},{3,11},{4,12},{5,13},{6,14},{7,15},{8,0},{9,1},... | collective-permute-start | bytes 3145736 | tf_op jit(solution)/shard_map/ppermute | solution.py:383
  13.1 1.7 dynamic-slice_bitcast_fusion
  14.9 21.9 %collective-permute-done.1.rest_2_ = bf16[512,1024]{1,0:T(8,128)(2,1)S(1)} collective-permute-done((bf16[512,1024]{1,0:T(8,128)(2,1)S(1)}, bf16[512,1024]{1,0:T(8,128)(2,1)S(1)}, u32[]{:S(2)}, u32[]{:S(2)}) %collective-permute-start.1) | collective-permute-done | bytes 1048608 | tf_op jit(solution)/shard_map/ppermute | solution.py:383
  36.8 1.7 collective-permute-start.5
  38.5 1.5 collective-permute-start.3
  40.1 2.3 respond.1.response_ref
  42.3 19.5 %collective-permute-done.5.rest_8_ = bf16[512,1024]{1,0:T(8,128)(2,1)S(1)} collective-permute-done((bf16[512,1024]{1,0:T(8,128)(2,1)S(1)}, bf16[512,1024]{1,0:T(8,128)(2,1)S(1)}, u32[]{:S(2)}, u32[]{:S(2)}) %collective-permute-start.5) | collective-permute-done | bytes 1048608 | tf_op jit(solution)/shard_map/ppermute | solution.py:383
  61.8 1.4 collective-permute-start.8
  63.2 1.6 collective-permute-start.7
  64.8 0.5 collective-permute-start.6
  65.3 20.7 %collective-permute-done.8.rest_14_ = bf16[512,1024]{1,0:T(8,128)(2,1)S(1)} collective-permute-done((bf16[512,1024]{1,0:T(8,128)(2,1)S(1)}, bf16[512,1024]{1,0:T(8,128)(2,1)S(1)}, u32[]{:S(2)}, u32[]{:S(2)}) %collective-permute-start.8) | collective-permute-done | bytes 1048608 | tf_op jit(solution)/shard_map/ppermute | solution.py:383
  86.1 0.8 collective-permute-done.7.rest_10_
  86.9 2.7 %constant_dynamic-slice_fusion.4 = bf16[512,1024]{1,0:T(8,128)(2,1)} fusion(bf16[1024,1024]{1,0:T(8,128)(2,1)} %param.15, s32[]{:T(128)S(6)} %select_n.117), kind=kLoop, calls=%fused_computation.32 | loop fusion | bytes 2097156 | tf_op jit(solution)/shard_map/dynamic_slice | solution.py:420
  89.6 1.0 collective-permute-start.12
  90.7 1.1 copy-done.16
  91.8 1.5 collective-permute-start.11
  93.7 16.5 %gate.1 = (bf16[512,1024]{1,0:T(8,128)(2,1)}, bf16[2,16,1024]{2,1,0:T(8,128)(2,1)}, bf16[160,1024]{1,0:T(8,128)(2,1)}, f32[512,1024]{1,0:T(8,128)S(1)}) custom-call(s32[6]{0:T(128)S(1)} %stack.33.at_ref, bf16[512,4096]{1,0:T(8,128)(2,1)} %all-gather.3.cloned.1.call-done.x_ref, f32[3,3,1024]{2,1,0:T(4,128)S(1)} %copy-done.3, bf16[3,1024,1024]{2,1,0:T(8,128)(2,1)} %bitcast.25, ...), custom_call_target="tpu_custom_call" | custom-call | tf_op jit(solution)/shard_map/gate/pallas_call | solution.py:180
  110.2 2.5 %collective-permute-start.13 = (bf16[160,1024]{1,0:T(8,128)(2,1)}, bf16[160,1024]{1,0:T(8,128)(2,1)}, u32[]{:S(2)}, u32[]{:S(2)}) collective-permute-start(bf16[160,1024]{1,0:T(8,128)(2,1)} %get-tuple-element.38), channel_id=1, source_target_pairs={{0,4},{1,5},{2,6},{3,7},{4,8},{5,9},{6,10},{7,11},{8,12},{9,13},{1... | collective-permute-start | bytes 983048 | tf_op jit(solution)/shard_map/ppermute | solution.py:383
  112.7 2.5 %collective-permute-done.12 = bf16[512,1024]{1,0:T(8,128)(2,1)} collective-permute-done((bf16[512,1024]{1,0:T(8,128)(2,1)}, bf16[512,1024]{1,0:T(8,128)(2,1)}, u32[]{:S(2)}, u32[]{:S(2)}) %collective-permute-start.12) | collective-permute-done | bytes 1048608 | tf_op jit(solution)/shard_map/ppermute | solution.py:383
  115.2 1.9 collective-permute-done.11.rest_0_
  117.1 1.0 collective-permute-start.14
  118.2 2.4 %collective-permute-done.14.rest_1_ = bf16[512,1024]{1,0:T(8,128)(2,1)S(1)} collective-permute-done((bf16[512,1024]{1,0:T(8,128)(2,1)}, bf16[512,1024]{1,0:T(8,128)(2,1)S(1)}, u32[]{:S(2)}, u32[]{:S(2)}) %collective-permute-start.14) | collective-permute-done | bytes 1048608 | tf_op jit(solution)/shard_map/ppermute | solution.py:383
  120.6 1.0 copy-done.17
  121.6 4.3 %query.1 = (bf16[512,1024]{1,0:T(8,128)(2,1)S(1)}, bf16[16,1024]{1,0:T(8,128)(2,1)}) custom-call(s32[2]{0:T(128)S(1)} %pad_add_fusion.at_ref, bf16[512,4096]{1,0:T(8,128)(2,1)} %all-gather.3.cloned.1.call-done.x_ref, f32[512,1024]{1,0:T(8,128)S(1)} %get-tuple-element.35.sum_ref, bf16[512,1024]{1,0:T(8,128)(2,1)} %collective-permute-done.11.rest_0_, ...), custom_call_target="tpu_custom_call" | custom-call | tf_op jit(solution)/shard_map/query/pallas_call | solution.py:224
  126.4 2.2 collective-permute-start.15
  128.6 5.4 %mix.1.mixed_ref = f32[512,1024]{1,0:T(8,128)S(1)} custom-call(bf16[512,1024]{1,0:T(8,128)(2,1)} %get-tuple-element.42.gated_ref, bf16[160,1024]{1,0:T(8,128)(2,1)} %collective-permute-done.13.halo_ref, bf16[2,16,1024]{2,1,0:T(8,128)(2,1)} %get-tuple-element.43.head_ref, f32[3,3,1024]{2,1,0:T(4,128)S(1)} %copy-done.3, f32[3,128,1024]{2,1,0:T(8,128)} %respond.1.response_ref, ...), custom_call_target="tpu_custom_call" | custom-call | tf_op jit(solution)/shard_map/mix/pallas_call | solution.py:344
  134.0 1.9 combine.1
  136.0 3.1 %convolution_convert_fusion.3 = bf16[512,1024]{1,0:T(8,128)(2,1)S(1)} fusion(bf16[512,1024]{1,0:T(8,128)(2,1)S(1)} %combine.1, bf16[1024,1024]{1,0:T(8,128)(2,1)} %param.15), kind=kOutput, calls=%fused_computation.3 | convolution fusion | flops 1074266112 | bytes 4194304 | tf_op jit(solution)/shard_map/dot_general | solution.py:468
  139.1 2.8 %collective-permute-start.18 = (bf16[256,1024]{1,0:T(8,128)(2,1)S(1)}, bf16[256,1024]{1,0:T(8,128)(2,1)S(1)}, u32[]{:S(2)}, u32[]{:S(2)}) collective-permute-start(bf16[256,1024]{1,0:T(8,128)(2,1)S(1)} %constant_dynamic-slice_fusion.2), channel_id=1, source_target_pairs={{0,1},{3,2},{4,5},{7,6},{8,9},{11,10},{12,13},{15,14},{16,17},{19,... | collective-permute-start | bytes 1572872 | tf_op jit(solution)/shard_map/ppermute | solution.py:383
  141.9 2.9 %convolution_convert_fusion.2 = bf16[512,1024]{1,0:T(8,128)(2,1)S(1)} fusion(bf16[512,1024]{1,0:T(8,128)(2,1)S(1)} %combine.1, bf16[1024,1024]{1,0:T(8,128)(2,1)} %collective-permute-done.16), kind=kOutput, calls=%fused_computation.2 | convolution fusion | flops 1074266112 | bytes 4194304 | tf_op jit(solution)/shard_map/dot_general | solution.py:468
  144.8 0.8 constant_dynamic-slice_fusion.3
  145.6 2.1 collective-permute-start.17
  147.7 5.0 %collective-permute-done.18 = bf16[256,1024]{1,0:T(8,128)(2,1)S(1)} collective-permute-done((bf16[256,1024]{1,0:T(8,128)(2,1)S(1)}, bf16[256,1024]{1,0:T(8,128)(2,1)S(1)}, u32[]{:S(2)}, u32[]{:S(2)}) %collective-permute-start.18) | collective-permute-done | bytes 524320 | tf_op jit(solution)/shard_map/ppermute | solution.py:383
  152.7 1.0 add_convert_fusion.3
  153.7 1.4 collective-permute-start.19
  155.1 5.6 %all-gather.5.cloned.1.call-done = bf16[1024,1024]{1,0:T(8,128)(2,1)} async-done(((bf16[512,1024]{1,0:T(8,128)(2,1)}), bf16[1024,1024]{1,0:T(8,128)(2,1)}) %all-gather.5.cloned.1.call-update) | async-done | bytes 2097168 | tf_op jit(solution)/shard_map/all_gather | solution.py:455
  160.8 3.3 %collective-permute-done.17 = bf16[256,1024]{1,0:T(8,128)(2,1)} collective-permute-done((bf16[256,1024]{1,0:T(8,128)(2,1)}, bf16[256,1024]{1,0:T(8,128)(2,1)}, u32[]{:S(2)}, u32[]{:S(2)}) %collective-permute-start.17) | collective-permute-done | bytes 524320 | tf_op jit(solution)/shard_map/ppermute | solution.py:383
  164.0 1.6 collective-permute-start.20
  165.6 2.9 %convolution_convert_fusion.1 = bf16[512,1024]{1,0:T(8,128)(2,1)S(1)} fusion(bf16[512,1024]{1,0:T(8,128)(2,1)S(1)} %combine.1, bf16[1024,1024]{1,0:T(8,128)(2,1)} %all-gather.5.cloned.1.call-done), kind=kOutput, calls=%fused_computation.1 | convolution fusion | flops 1074266112 | bytes 4194304 | tf_op jit(solution)/shard_map/dot_general | solution.py:468
  168.5 0.9 constant_dynamic-slice_fusion
  169.4 10.1 %collective-permute-start.24 = (bf16[256,1024]{1,0:T(8,128)(2,1)}, bf16[256,1024]{1,0:T(8,128)(2,1)}, u32[]{:S(2)}, u32[]{:S(2)}) collective-permute-start(bf16[256,1024]{1,0:T(8,128)(2,1)} %constant_dynamic-slice_fusion), channel_id=1, source_target_pairs={{0,1},{3,2},{4,5},{7,6},{8,9},{11,10},{12,13},{15,14},{16,17},{19,... | collective-permute-start | bytes 1572872 | tf_op jit(solution)/shard_map/ppermute | solution.py:383
  179.5 1.3 convolution_convert_fusion
  180.8 0.9 constant_dynamic-slice_fusion.1
  182.0 2.1 collective-permute-start.21
  184.0 1.3 add_convert_fusion
  185.4 0.7 collective-permute-start.27
  186.1 5.2 %collective-permute-done.24 = bf16[256,1024]{1,0:T(8,128)(2,1)} collective-permute-done((bf16[256,1024]{1,0:T(8,128)(2,1)}, bf16[256,1024]{1,0:T(8,128)(2,1)}, u32[]{:S(2)}, u32[]{:S(2)}) %collective-permute-start.24) | collective-permute-done | bytes 524320 | tf_op jit(solution)/shard_map/ppermute | solution.py:383
  191.3 1.4 add_convert_fusion.1
  192.7 0.8 collective-permute-start.25
  193.5 8.0 %collective-permute-done.21 = bf16[256,1024]{1,0:T(8,128)(2,1)} collective-permute-done((bf16[256,1024]{1,0:T(8,128)(2,1)}, bf16[256,1024]{1,0:T(8,128)(2,1)}, u32[]{:S(2)}, u32[]{:S(2)}) %collective-permute-start.21) | collective-permute-done | bytes 524320 | tf_op jit(solution)/shard_map/ppermute | solution.py:383
  201.6 1.2 add_convert_fusion.2
  202.8 0.7 collective-permute-start.22
  203.5 1.2 add_convert_fusion.5
  204.7 5.2 %collective-permute-start.29 = (bf16[128,1024]{1,0:T(8,128)(2,1)S(1)}, bf16[128,1024]{1,0:T(8,128)(2,1)S(1)}, u32[]{:S(2)}, u32[]{:S(2)}) collective-permute-start(bf16[128,1024]{1,0:T(8,128)(2,1)S(1)} %add_convert_fusion.5), channel_id=1, source_target_pairs={{0,1},{1,0},{2,3},{3,2},{4,5},{5,4},{6,7},{7,6},{8,9},{9,8},{10,11... | collective-permute-start | bytes 786440 | tf_op jit(solution)/shard_map/ppermute | solution.py:383
  210.3 2.1 collective-permute-start.26
  212.4 9.1 %collective-permute-start.23 = (bf16[128,1024]{1,0:T(8,128)(2,1)S(1)}, bf16[128,1024]{1,0:T(8,128)(2,1)S(1)}, u32[]{:S(2)}, u32[]{:S(2)}) collective-permute-start(bf16[128,1024]{1,0:T(8,128)(2,1)S(1)} %add_convert_fusion.11), channel_id=1, source_target_pairs={{0,1},{1,0},{2,3},{3,2},{4,5},{5,4},{6,7},{7,6},{8,9},{9,8},{10,11... | collective-permute-start | bytes 786440 | tf_op jit(solution)/shard_map/ppermute | solution.py:383
  221.6 1.1 collective-permute-done.28
  222.7 1.4 broadcast_select_fusion.3
  224.2 4.2 %collective-permute-done.26 = bf16[128,1024]{1,0:T(8,128)(2,1)S(1)} collective-permute-done((bf16[128,1024]{1,0:T(8,128)(2,1)S(1)}, bf16[128,1024]{1,0:T(8,128)(2,1)S(1)}, u32[]{:S(2)}, u32[]{:S(2)}) %collective-permute-start.26) | collective-permute-done | bytes 262176 | tf_op jit(solution)/shard_map/ppermute | solution.py:383
  228.4 3.7 %collective-permute-done.23 = bf16[128,1024]{1,0:T(8,128)(2,1)S(1)} collective-permute-done((bf16[128,1024]{1,0:T(8,128)(2,1)S(1)}, bf16[128,1024]{1,0:T(8,128)(2,1)S(1)}, u32[]{:S(2)}, u32[]{:S(2)}) %collective-permute-start.23) | collective-permute-done | bytes 262176 | tf_op jit(solution)/shard_map/ppermute | solution.py:383
  232.7 1.1 pad_maximum_fusion
  (74 shorter events, 2.5 us)
Async XLA Ops:
  6.5 1.8 copy-start
  6.5 1.8 copy-start.18
  6.5 87.1 %all-gather.3.cloned.1.call-start = ((), (), s32[]{:S(2)}) async-start(), calls=%async_computation | async-start | bytes 5242880 | tf_op jit(solution)/shard_map/all_gather | solution.py:441
  6.5 56.7 %collective-permute-start = (bf16[3,1024,1024]{2,1,0:T(8,128)(2,1)}, bf16[3,1024,1024]{2,1,0:T(8,128)(2,1)}, u32[]{:S(2)}, u32[]{:S(2)}) collective-permute-start(bf16[3,1024,1024]{2,1,0:T(8,128)(2,1)} %bitcast.23), channel_id=1, source_target_pairs={{0,4},{1,5},{2,6},{3,7},{4,0},{5,1},{6,2},{7,3},{8,12},{9,13},{10,... | collective-permute-start | bytes 18874376 | tf_op jit(solution)/shard_map/ppermute | solution.py:383
  10.3 29.7 %copy-start.1 = (f32[128,1024]{1,0:T(8,128)S(1)}, f32[128,1024]{1,0:T(8,128)}, u32[]{:S(2)}) copy-start(f32[128,1024]{1,0:T(8,128)} %filter_ref.1) | copy-start | bytes 1572868
  10.3 29.7 %copy-start.2 = (bf16[256,256]{1,0:T(8,128)(2,1)S(1)}, bf16[256,256]{1,0:T(8,128)(2,1)}, u32[]{:S(2)}) copy-start(bf16[256,256]{1,0:T(8,128)(2,1)} %constant.50.clone.fwd_ref) | copy-start | bytes 393220
  10.3 29.7 %copy-start.5 = (f32[1024]{0:T(1024)S(1)}, f32[1024]{0:T(1024)}, u32[]{:S(2)}) copy-start(f32[1024]{0:T(1024)} %param.14) | copy-start | bytes 12292
  10.3 150.4 %all-gather.5.cloned.1.call-start = ((), (), s32[]{:S(2)}) async-start(), calls=%async_computation.1 | async-start | bytes 3145728 | tf_op jit(solution)/shard_map/all_gather | solution.py:455
  10.4 26.4 %collective-permute-start.1 = (bf16[512,1024]{1,0:T(8,128)(2,1)S(1)}, bf16[512,1024]{1,0:T(8,128)(2,1)S(1)}, u32[]{:S(2)}, u32[]{:S(2)}) collective-permute-start(bf16[512,1024]{1,0:T(8,128)(2,1)S(1)} %dynamic-slice_bitcast_fusion.2), channel_id=1, source_target_pairs={{0,8},{1,9},{2,10},{3,11},{4,12},{5,13},{6,14},{7,15},{8,0},{9,1},... | collective-permute-start | bytes 3145736 | tf_op jit(solution)/shard_map/ppermute | solution.py:383
  36.8 52.8 %copy-start.10 = (bf16[512,1024]{1,0:T(8,128)(2,1)}, bf16[512,1024]{1,0:T(8,128)(2,1)S(1)}, u32[]{:S(2)}) copy-start(bf16[512,1024]{1,0:T(8,128)(2,1)S(1)} %collective-permute-done.1.rest_2_) | copy-start | bytes 3145732
  36.8 25.0 %collective-permute-start.5 = (bf16[512,1024]{1,0:T(8,128)(2,1)S(1)}, bf16[512,1024]{1,0:T(8,128)(2,1)S(1)}, u32[]{:S(2)}, u32[]{:S(2)}) collective-permute-start(bf16[512,1024]{1,0:T(8,128)(2,1)S(1)} %get-tuple-element.31), channel_id=1, source_target_pairs={{0,8},{1,9},{2,10},{3,11},{4,12},{5,13},{6,14},{7,15},{8,0},{9,1},... | collective-permute-start | bytes 3145736 | tf_op jit(solution)/shard_map/ppermute | solution.py:383
  38.5 24.7 %collective-permute-start.3 = (bf16[512,1024]{1,0:T(8,128)(2,1)S(1)}, bf16[512,1024]{1,0:T(8,128)(2,1)S(1)}, u32[]{:S(2)}, u32[]{:S(2)}) collective-permute-start(bf16[512,1024]{1,0:T(8,128)(2,1)S(1)} %collective-permute-done.1.rest_2_), channel_id=1, source_target_pairs={{0,16},{1,17},{2,18},{3,19},{4,20},{5,21},{6,22},{7,23},{8,24},{9,... | collective-permute-start | bytes 3145736 | tf_op jit(solution)/shard_map/ppermute | solution.py:383
  40.1 53.6 %copy-start.3 = (f32[3,3,1024]{2,1,0:T(4,128)S(1)}, f32[3,3,1024]{2,1,0:T(4,128)}, u32[]{:S(2)}) copy-start(f32[3,3,1024]{2,1,0:T(4,128)} %taps_ref.2) | copy-start | bytes 110596
  61.8 28.9 %copy-start.12 = (bf16[512,1024]{1,0:T(8,128)(2,1)}, bf16[512,1024]{1,0:T(8,128)(2,1)S(1)}, u32[]{:S(2)}) copy-start(bf16[512,1024]{1,0:T(8,128)(2,1)S(1)} %collective-permute-done.5.rest_8_) | copy-start | bytes 3145732
  61.8 24.3 %collective-permute-start.8 = (bf16[512,1024]{1,0:T(8,128)(2,1)S(1)}, bf16[512,1024]{1,0:T(8,128)(2,1)S(1)}, u32[]{:S(2)}, u32[]{:S(2)}) collective-permute-start(bf16[512,1024]{1,0:T(8,128)(2,1)S(1)} %get-tuple-element.33), channel_id=1, source_target_pairs={{0,8},{1,9},{2,10},{3,11},{4,12},{5,13},{6,14},{7,15},{8,0},{9,1},... | collective-permute-start | bytes 3145736 | tf_op jit(solution)/shard_map/ppermute | solution.py:383
  63.2 30.5 %copy-start.13 = (bf16[512,1024]{1,0:T(8,128)(2,1)}, bf16[512,1024]{1,0:T(8,128)(2,1)S(1)}, u32[]{:S(2)}) copy-start(bf16[512,1024]{1,0:T(8,128)(2,1)S(1)} %collective-permute-done.3.rest_4_) | copy-start | bytes 3145732
  63.2 23.7 %collective-permute-start.7 = (bf16[512,1024]{1,0:T(8,128)(2,1)S(1)}, bf16[512,1024]{1,0:T(8,128)(2,1)S(1)}, u32[]{:S(2)}, u32[]{:S(2)}) collective-permute-start(bf16[512,1024]{1,0:T(8,128)(2,1)S(1)} %collective-permute-done.5.rest_8_), channel_id=1, source_target_pairs={{0,16},{1,17},{2,18},{3,19},{4,20},{5,21},{6,22},{7,23},{8,24},{9,... | collective-permute-start | bytes 3145736 | tf_op jit(solution)/shard_map/ppermute | solution.py:383
  64.8 24.8 %collective-permute-start.2 = (bf16[512,1024]{1,0:T(8,128)(2,1)S(1)}, bf16[512,1024]{1,0:T(8,128)(2,1)S(1)}, u32[]{:S(2)}, u32[]{:S(2)}) collective-permute-start(bf16[512,1024]{1,0:T(8,128)(2,1)S(1)} %collective-permute-done.1.rest_2_), channel_id=1, source_target_pairs={{0,4},{1,5},{2,6},{3,7},{4,0},{5,1},{6,2},{7,3},{8,12},{9,13},{10,... | collective-permute-start | bytes 3145736 | tf_op jit(solution)/shard_map/ppermute | solution.py:383
  64.8 25.8 %collective-permute-start.6 = (bf16[512,1024]{1,0:T(8,128)(2,1)S(1)}, bf16[512,1024]{1,0:T(8,128)(2,1)S(1)}, u32[]{:S(2)}, u32[]{:S(2)}) collective-permute-start(bf16[512,1024]{1,0:T(8,128)(2,1)S(1)} %collective-permute-done.5.rest_8_), channel_id=1, source_target_pairs={{0,4},{1,5},{2,6},{3,7},{4,0},{5,1},{6,2},{7,3},{8,12},{9,13},{10,... | collective-permute-start | bytes 3145736 | tf_op jit(solution)/shard_map/ppermute | solution.py:383
  65.3 28.0 %collective-permute-start.4 = (bf16[512,1024]{1,0:T(8,128)(2,1)S(1)}, bf16[512,1024]{1,0:T(8,128)(2,1)}, u32[]{:S(2)}, u32[]{:S(2)}) collective-permute-start(bf16[512,1024]{1,0:T(8,128)(2,1)S(1)} %collective-permute-done.3.rest_4_), channel_id=1, source_target_pairs={{0,4},{1,5},{2,6},{3,7},{4,0},{5,1},{6,2},{7,3},{8,12},{9,13},{10,... | collective-permute-start | bytes 3145736 | tf_op jit(solution)/shard_map/ppermute | solution.py:383
  86.1 7.6 %copy-start.11 = (bf16[512,1024]{1,0:T(8,128)(2,1)}, bf16[512,1024]{1,0:T(8,128)(2,1)S(1)}, u32[]{:S(2)}) copy-start(bf16[512,1024]{1,0:T(8,128)(2,1)S(1)} %collective-permute-done.8.rest_14_) | copy-start | bytes 3145732
  86.1 7.3 %collective-permute-start.10 = (bf16[512,1024]{1,0:T(8,128)(2,1)S(1)}, bf16[512,1024]{1,0:T(8,128)(2,1)}, u32[]{:S(2)}, u32[]{:S(2)}) collective-permute-start(bf16[512,1024]{1,0:T(8,128)(2,1)S(1)} %collective-permute-done.8.rest_14_), channel_id=1, source_target_pairs={{0,4},{1,5},{2,6},{3,7},{4,0},{5,1},{6,2},{7,3},{8,12},{9,13},{10,... | collective-permute-start | bytes 3145736 | tf_op jit(solution)/shard_map/ppermute | solution.py:383
  86.9 6.8 %copy-start.14 = (bf16[512,1024]{1,0:T(8,128)(2,1)}, bf16[512,1024]{1,0:T(8,128)(2,1)S(1)}, u32[]{:S(2)}) copy-start(bf16[512,1024]{1,0:T(8,128)(2,1)S(1)} %collective-permute-done.7.rest_10_) | copy-start | bytes 3145732
  86.9 6.8 %collective-permute-start.9 = (bf16[512,1024]{1,0:T(8,128)(2,1)S(1)}, bf16[512,1024]{1,0:T(8,128)(2,1)}, u32[]{:S(2)}, u32[]{:S(2)}) collective-permute-start(bf16[512,1024]{1,0:T(8,128)(2,1)S(1)} %collective-permute-done.7.rest_10_), channel_id=1, source_target_pairs={{0,4},{1,5},{2,6},{3,7},{4,0},{5,1},{6,2},{7,3},{8,12},{9,13},{10,... | collective-permute-start | bytes 3145736 | tf_op jit(solution)/shard_map/ppermute | solution.py:383
  89.6 1.1 copy-start.15
  89.6 25.6 %collective-permute-start.12 = (bf16[512,1024]{1,0:T(8,128)(2,1)}, bf16[512,1024]{1,0:T(8,128)(2,1)}, u32[]{:S(2)}, u32[]{:S(2)}) collective-permute-start(bf16[512,1024]{1,0:T(8,128)(2,1)} %constant_dynamic-slice_fusion.4), channel_id=1, source_target_pairs={{0,8},{1,9},{2,10},{3,11},{4,12},{5,13},{6,14},{7,15},{8,0},{9,1},... | collective-permute-start | bytes 3145736 | tf_op jit(solution)/shard_map/ppermute | solution.py:383
  90.7 1.1 copy-start.16
  91.8 25.3 %collective-permute-start.11 = (bf16[512,1024]{1,0:T(8,128)(2,1)S(1)}, bf16[512,1024]{1,0:T(8,128)(2,1)}, u32[]{:S(2)}, u32[]{:S(2)}) collective-permute-start(bf16[512,1024]{1,0:T(8,128)(2,1)S(1)} %collective-permute-done.8.rest_14_), channel_id=1, source_target_pairs={{0,16},{1,17},{2,18},{3,19},{4,20},{5,21},{6,22},{7,23},{8,24},{9,... | collective-permute-start | bytes 3145736 | tf_op jit(solution)/shard_map/ppermute | solution.py:383
  110.2 6.8 %collective-permute-start.13 = (bf16[160,1024]{1,0:T(8,128)(2,1)}, bf16[160,1024]{1,0:T(8,128)(2,1)}, u32[]{:S(2)}, u32[]{:S(2)}) collective-permute-start(bf16[160,1024]{1,0:T(8,128)(2,1)} %get-tuple-element.38), channel_id=1, source_target_pairs={{0,4},{1,5},{2,6},{3,7},{4,8},{5,9},{6,10},{7,11},{8,12},{9,13},{1... | collective-permute-start | bytes 983048 | tf_op jit(solution)/shard_map/ppermute | solution.py:383
  117.1 3.5 %collective-permute-start.14 = (bf16[512,1024]{1,0:T(8,128)(2,1)}, bf16[512,1024]{1,0:T(8,128)(2,1)S(1)}, u32[]{:S(2)}, u32[]{:S(2)}) collective-permute-start(bf16[512,1024]{1,0:T(8,128)(2,1)} %collective-permute-done.11.rest_0_), channel_id=1, source_target_pairs={{0,4},{1,5},{2,6},{3,7},{4,0},{5,1},{6,2},{7,3},{8,12},{9,13},{10,... | collective-permute-start | bytes 3145736 | tf_op jit(solution)/shard_map/ppermute | solution.py:383
  120.6 1.0 copy-start.17
  121.6 7.0 %copy-start.4 = (bf16[128,768]{1,0:T(8,128)(2,1)S(1)}, bf16[128,768]{1,0:T(8,128)(2,1)}, u32[]{:S(2)}) copy-start(bf16[128,768]{1,0:T(8,128)(2,1)} %constant.51.clone.inv_ref) | copy-start | bytes 589828
  125.9 16.0 %collective-permute-start.16 = (bf16[1024,1024]{1,0:T(8,128)(2,1)}, bf16[1024,1024]{1,0:T(8,128)(2,1)}, u32[]{:S(2)}, u32[]{:S(2)}) collective-permute-start(bf16[1024,1024]{1,0:T(8,128)(2,1)} %param.15), channel_id=1, source_target_pairs={{0,4},{1,5},{2,6},{3,7},{4,0},{5,1},{6,2},{7,3},{8,12},{9,13},{10,... | collective-permute-start | bytes 6291464 | tf_op jit(solution)/shard_map/ppermute | solution.py:383
  126.4 7.6 %collective-permute-start.15 = (bf16[16,1024]{1,0:T(8,128)(2,1)}, bf16[16,1024]{1,0:T(8,128)(2,1)S(1)}, u32[]{:S(2)}, u32[]{:S(2)}) collective-permute-start(bf16[16,1024]{1,0:T(8,128)(2,1)} %get-tuple-element.41), channel_id=1, source_target_pairs={{0,4},{1,5},{2,6},{3,7},{4,8},{5,9},{6,10},{7,11},{8,12},{9,13},{1... | collective-permute-start | bytes 98312 | tf_op jit(solution)/shard_map/ppermute | solution.py:383
  139.1 13.6 %collective-permute-start.18 = (bf16[256,1024]{1,0:T(8,128)(2,1)S(1)}, bf16[256,1024]{1,0:T(8,128)(2,1)S(1)}, u32[]{:S(2)}, u32[]{:S(2)}) collective-permute-start(bf16[256,1024]{1,0:T(8,128)(2,1)S(1)} %constant_dynamic-slice_fusion.2), channel_id=1, source_target_pairs={{0,1},{3,2},{4,5},{7,6},{8,9},{11,10},{12,13},{15,14},{16,17},{19,... | collective-permute-start | bytes 1572872 | tf_op jit(solution)/shard_map/ppermute | solution.py:383
  145.6 18.4 %collective-permute-start.17 = (bf16[256,1024]{1,0:T(8,128)(2,1)}, bf16[256,1024]{1,0:T(8,128)(2,1)}, u32[]{:S(2)}, u32[]{:S(2)}) collective-permute-start(bf16[256,1024]{1,0:T(8,128)(2,1)} %constant_dynamic-slice_fusion.3), channel_id=1, source_target_pairs={{0,1},{3,2},{4,5},{7,6},{8,9},{11,10},{12,13},{15,14},{16,17},{19,... | collective-permute-start | bytes 1572872 | tf_op jit(solution)/shard_map/ppermute | solution.py:383
  153.7 10.3 %collective-permute-start.19 = (bf16[256,1024]{1,0:T(8,128)(2,1)}, bf16[256,1024]{1,0:T(8,128)(2,1)}, u32[]{:S(2)}, u32[]{:S(2)}) collective-permute-start(bf16[256,1024]{1,0:T(8,128)(2,1)} %add_convert_fusion.3), channel_id=1, source_target_pairs={{1,2},{2,1},{5,6},{6,5},{9,10},{10,9},{13,14},{14,13},{17,18},{18,... | collective-permute-start | bytes 1572872 | tf_op jit(solution)/shard_map/ppermute | solution.py:383
  164.0 15.5 %collective-permute-start.20 = (bf16[1024,1024]{1,0:T(8,128)(2,1)}, bf16[1024,1024]{1,0:T(8,128)(2,1)S(1)}, u32[]{:S(2)}, u32[]{:S(2)}) collective-permute-start(bf16[1024,1024]{1,0:T(8,128)(2,1)} %all-gather.5.cloned.1.call-done), channel_id=1, source_target_pairs={{0,4},{1,5},{2,6},{3,7},{4,0},{5,1},{6,2},{7,3},{8,12},{9,13},{10,... | collective-permute-start | bytes 6291464 | tf_op jit(solution)/shard_map/ppermute | solution.py:383
  168.5 12.3 %copy-start.6 = (bf16[512,1024]{1,0:T(8,128)(2,1)}, bf16[512,1024]{1,0:T(8,128)(2,1)S(1)}, u32[]{:S(2)}) copy-start(bf16[512,1024]{1,0:T(8,128)(2,1)S(1)} %convolution_convert_fusion.1) | copy-start | bytes 3145732
  169.4 21.9 %collective-permute-start.24 = (bf16[256,1024]{1,0:T(8,128)(2,1)}, bf16[256,1024]{1,0:T(8,128)(2,1)}, u32[]{:S(2)}, u32[]{:S(2)}) collective-permute-start(bf16[256,1024]{1,0:T(8,128)(2,1)} %constant_dynamic-slice_fusion), channel_id=1, source_target_pairs={{0,1},{3,2},{4,5},{7,6},{8,9},{11,10},{12,13},{15,14},{16,17},{19,... | collective-permute-start | bytes 1572872 | tf_op jit(solution)/shard_map/ppermute | solution.py:383
  180.8 1.1 copy-start.8
  182.0 19.6 %collective-permute-start.21 = (bf16[256,1024]{1,0:T(8,128)(2,1)}, bf16[256,1024]{1,0:T(8,128)(2,1)}, u32[]{:S(2)}, u32[]{:S(2)}) collective-permute-start(bf16[256,1024]{1,0:T(8,128)(2,1)} %constant_dynamic-slice_fusion.1), channel_id=1, source_target_pairs={{0,1},{3,2},{4,5},{7,6},{8,9},{11,10},{12,13},{15,14},{16,17},{19,... | collective-permute-start | bytes 1572872 | tf_op jit(solution)/shard_map/ppermute | solution.py:383
  184.0 17.5 %copy-start.9 = (bf16[512,1024]{1,0:T(8,128)(2,1)S(1)}, bf16[512,1024]{1,0:T(8,128)(2,1)}, u32[]{:S(2)}) copy-start(bf16[512,1024]{1,0:T(8,128)(2,1)} %copy-done.8) | copy-start | bytes 3145732
  185.4 24.5 %collective-permute-start.27 = (bf16[256,1024]{1,0:T(8,128)(2,1)S(1)}, bf16[256,1024]{1,0:T(8,128)(2,1)S(1)}, u32[]{:S(2)}, u32[]{:S(2)}) collective-permute-start(bf16[256,1024]{1,0:T(8,128)(2,1)S(1)} %add_convert_fusion), channel_id=1, source_target_pairs={{1,2},{2,1},{5,6},{6,5},{9,10},{10,9},{13,14},{14,13},{17,18},{18,... | collective-permute-start | bytes 1572872 | tf_op jit(solution)/shard_map/ppermute | solution.py:383
  192.7 17.4 %copy-start.7 = (bf16[512,1024]{1,0:T(8,128)(2,1)S(1)}, bf16[512,1024]{1,0:T(8,128)(2,1)}, u32[]{:S(2)}) copy-start(bf16[512,1024]{1,0:T(8,128)(2,1)} %copy-done.6) | copy-start | bytes 3145732
  192.7 17.4 %collective-permute-start.25 = (bf16[256,1024]{1,0:T(8,128)(2,1)S(1)}, bf16[256,1024]{1,0:T(8,128)(2,1)S(1)}, u32[]{:S(2)}, u32[]{:S(2)}) collective-permute-start(bf16[256,1024]{1,0:T(8,128)(2,1)S(1)} %add_convert_fusion.1), channel_id=1, source_target_pairs={{1,2},{2,1},{5,6},{6,5},{9,10},{10,9},{13,14},{14,13},{17,18},{18,... | collective-permute-start | bytes 1572872 | tf_op jit(solution)/shard_map/ppermute | solution.py:383
  202.8 9.5 %collective-permute-start.22 = (bf16[256,1024]{1,0:T(8,128)(2,1)S(1)}, bf16[256,1024]{1,0:T(8,128)(2,1)S(1)}, u32[]{:S(2)}, u32[]{:S(2)}) collective-permute-start(bf16[256,1024]{1,0:T(8,128)(2,1)S(1)} %add_convert_fusion.2), channel_id=1, source_target_pairs={{1,2},{2,1},{5,6},{6,5},{9,10},{10,9},{13,14},{14,13},{17,18},{18,... | collective-permute-start | bytes 1572872 | tf_op jit(solution)/shard_map/ppermute | solution.py:383
  204.7 16.9 %collective-permute-start.29 = (bf16[128,1024]{1,0:T(8,128)(2,1)S(1)}, bf16[128,1024]{1,0:T(8,128)(2,1)S(1)}, u32[]{:S(2)}, u32[]{:S(2)}) collective-permute-start(bf16[128,1024]{1,0:T(8,128)(2,1)S(1)} %add_convert_fusion.5), channel_id=1, source_target_pairs={{0,1},{1,0},{2,3},{3,2},{4,5},{5,4},{6,7},{7,6},{8,9},{9,8},{10,11... | collective-permute-start | bytes 786440 | tf_op jit(solution)/shard_map/ppermute | solution.py:383
  210.0 12.7 %collective-permute-start.28 = (bf16[128,1024]{1,0:T(8,128)(2,1)S(1)}, bf16[128,1024]{1,0:T(8,128)(2,1)S(1)}, u32[]{:S(2)}, u32[]{:S(2)}) collective-permute-start(bf16[128,1024]{1,0:T(8,128)(2,1)S(1)} %add_convert_fusion.7), channel_id=1, source_target_pairs={{0,1},{1,0},{2,3},{3,2},{4,5},{5,4},{6,7},{7,6},{8,9},{9,8},{10,11... | collective-permute-start | bytes 786440 | tf_op jit(solution)/shard_map/ppermute | solution.py:383
  210.3 18.1 %collective-permute-start.26 = (bf16[128,1024]{1,0:T(8,128)(2,1)S(1)}, bf16[128,1024]{1,0:T(8,128)(2,1)S(1)}, u32[]{:S(2)}, u32[]{:S(2)}) collective-permute-start(bf16[128,1024]{1,0:T(8,128)(2,1)S(1)} %add_convert_fusion.9), channel_id=1, source_target_pairs={{0,1},{1,0},{2,3},{3,2},{4,5},{5,4},{6,7},{7,6},{8,9},{9,8},{10,11... | collective-permute-start | bytes 786440 | tf_op jit(solution)/shard_map/ppermute | solution.py:383
  212.4 19.6 %collective-permute-start.23 = (bf16[128,1024]{1,0:T(8,128)(2,1)S(1)}, bf16[128,1024]{1,0:T(8,128)(2,1)S(1)}, u32[]{:S(2)}, u32[]{:S(2)}) collective-permute-start(bf16[128,1024]{1,0:T(8,128)(2,1)S(1)} %add_convert_fusion.11), channel_id=1, source_target_pairs={{0,1},{1,0},{2,3},{3,2},{4,5},{5,4},{6,7},{7,6},{8,9},{9,8},{10,11... | collective-permute-start | bytes 786440 | tf_op jit(solution)/shard_map/ppermute | solution.py:383
Sparse Core Ops, SparseCore 0:
  10.4 83.1 all-gather.2
  126.5 34.2 all-gather.4

commit v10 on v7

--- a/solution.py
+++ b/solution.py
@@ -443,8 +443,8 @@
     halo = to_next(edges)
     late = pieces[0][-1:]
     if paired:
-        late.append((to_core(after(far[0], gated)), None, (c ^ 3) * rows + other_half))
-    projected, tail = query(gathered, late, after(total, halo), width)
+        late.append((to_core(after(far[0], halo)), None, (c ^ 3) * rows + other_half))
+    projected, tail = query(gathered, late, total, width)
     before = to_next(tail)
     mixed = mix(gated, halo, head, short_filter, response, tables, width)
     combined = combine(projected, before, short_filter, mixed, width)
@@ -467,10 +467,8 @@
             combined, rows_out, (((1,), (1,)), ((), ())), preferred_element_type=f32
         ).astype(bf16)
 
-    results, firsts, seconds = [], [], []
-    for n, rows_out in enumerate(sets):
-        if paired and n == 2:
-            combined = after(combined, firsts[1])
+    results = []
+    for rows_out in sets:
         partial = product(rows_out)
         combined = after(combined, partial)
 
@@ -482,12 +480,8 @@
 
         if count == 4:
             far_pair = block(jnp.where(z < 2, 2, 0), 2)
-            firsts.append(send(far_pair, {0: 1, 3: 2}))
-            got = plus(far_pair, firsts[-1])
-            if n >= 2:
-                got = after(got, seconds[n - 2])
+            got = plus(far_pair, send(far_pair, {0: 1, 3: 2}))
             got = send(got, {1: 2, 2: 1})
-            seconds.append(got)
             low, high = got[:length], got[length:]
             odd = z % 2 == 1
             got_own = jnp.where(odd, high, low)

time: 248 us -> 233 us (0.940)
  starting transfers between devices: 62.3 us -> 54 us
  other arithmetic: 12.7 us -> 5.54 us
    ppermute x28, starting transfers between devices: 62.2 us -> 54 us  [move(): return lax.ppermute(value, axes, pairs)]
    convert_element_type x8, other arithmetic: 9.33 us -> 3.35 us  [plus(): return total.astype(bf16)]
  transfers between devices with their start and end apart: 30 -> 30, of which waited for: 13 -> 12; matrix products, arithmetic and copies ran while one was open for 11% -> 8% of each run, Pallas kernels for 12% -> 13%
where the time goes in v10:
time: 233 us; the launch traced here: 232 us
  waiting for transfers between devices  107 us (46%)
  starting transfers between devices  54 us (23%)
  Pallas kernels  32.7 us (14%)
  between operations  13.8 us (6%)
  matrix products  11.5 us (5%)
  local copies, waits for them, and re-layouts  7.51 us (3%)
  other arithmetic  5.54 us (2%)
    ppermute x28, waiting for transfers between devices, move(): return lax.ppermute(value, axes, pairs)  105 us
    ppermute x28, starting transfers between devices, move(): return lax.ppermute(value, axes, pairs)  54 us
    pallas_call x1, Pallas kernels, gate(): pl.pallas_call(functools.partial(gate_kernel, kinds_of(one), kinds_of(two...  16.9 us
    dot_general x4, matrix products, product(): lax.dot_general(combined, rows_out, (((1,), (1,)), ((), ())), preferred_e...  11.5 us
    pallas_call x1, Pallas kernels, mix(): pl.pallas_call(mix_kernel, grid=(channels // width,), in_specs=[col(slab)...  5.37 us
  transfers between devices with their start and end apart: 30, of which 12 were waited for; matrix products, arithmetic and copies ran while one was open for 8% of the time, Pallas kernels for 13%

profile of v10, /device:TPU:0, one launch (start us, length us, event | category | flops | bytes accessed | tf_op | source)
XLA Modules:
  0.0 231.7 jit_solution(414503405200905605)
XLA Ops:
  6.5 1.4 dynamic-slice_bitcast_fusion.2
  8.0 0.1 copy-done
  8.1 1.9 norm.1
  10.1 3.0 %collective-permute-start.1 = (bf16[512,1024]{1,0:T(8,128)(2,1)S(1)}, bf16[512,1024]{1,0:T(8,128)(2,1)S(1)}, u32[]{:S(2)}, u32[]{:S(2)}) collective-permute-start(bf16[512,1024]{1,0:T(8,128)(2,1)S(1)} %dynamic-slice_bitcast_fusion.2), channel_id=1, source_target_pairs={{0,8},{1,9},{2,10},{3,11},{4,12},{5,13},{6,14},{7,15},{8,0},{9,1},... | collective-permute-start | bytes 3145736 | tf_op jit(solution)/shard_map/ppermute | solution.py:383
  13.1 23.2 %collective-permute-done.1.rest_2_ = bf16[512,1024]{1,0:T(8,128)(2,1)S(1)} collective-permute-done((bf16[512,1024]{1,0:T(8,128)(2,1)S(1)}, bf16[512,1024]{1,0:T(8,128)(2,1)S(1)}, u32[]{:S(2)}, u32[]{:S(2)}) %collective-permute-start.1) | collective-permute-done | bytes 1048608 | tf_op jit(solution)/shard_map/ppermute | solution.py:383
  36.4 2.1 dynamic-slice_bitcast_fusion
  38.6 1.8 collective-permute-start.5
  40.4 1.5 collective-permute-start.3
  41.9 2.3 respond.1.response_ref
  44.2 19.6 %collective-permute-done.5.rest_8_ = bf16[512,1024]{1,0:T(8,128)(2,1)S(1)} collective-permute-done((bf16[512,1024]{1,0:T(8,128)(2,1)S(1)}, bf16[512,1024]{1,0:T(8,128)(2,1)S(1)}, u32[]{:S(2)}, u32[]{:S(2)}) %collective-permute-start.5) | collective-permute-done | bytes 1048608 | tf_op jit(solution)/shard_map/ppermute | solution.py:383
  63.8 1.7 collective-permute-start.8
  65.5 1.5 collective-permute-start.7
  67.0 0.5 collective-permute-start.6
  67.6 20.6 %collective-permute-done.8.rest_14_ = bf16[512,1024]{1,0:T(8,128)(2,1)S(1)} collective-permute-done((bf16[512,1024]{1,0:T(8,128)(2,1)S(1)}, bf16[512,1024]{1,0:T(8,128)(2,1)S(1)}, u32[]{:S(2)}, u32[]{:S(2)}) %collective-permute-start.8) | collective-permute-done | bytes 1048608 | tf_op jit(solution)/shard_map/ppermute | solution.py:383
  88.2 1.6 collective-permute-done.7.rest_10_
  89.8 1.0 copy-done.10
  90.7 1.5 collective-permute-start.11
  92.4 1.3 all-gather.3.cloned.1.call-done.x_ref
  93.7 16.9 %gate.1 = (bf16[512,1024]{1,0:T(8,128)(2,1)}, bf16[2,16,1024]{2,1,0:T(8,128)(2,1)}, bf16[160,1024]{1,0:T(8,128)(2,1)}, f32[512,1024]{1,0:T(8,128)S(1)}) custom-call(s32[6]{0:T(128)S(1)} %stack.33.at_ref, bf16[512,4096]{1,0:T(8,128)(2,1)} %all-gather.3.cloned.1.call-done.x_ref, f32[3,3,1024]{2,1,0:T(4,128)S(1)} %copy-done.3, bf16[3,1024,1024]{2,1,0:T(8,128)(2,1)} %bitcast.23, ...), custom_call_target="tpu_custom_call" | custom-call | tf_op jit(solution)/shard_map/gate/pallas_call | solution.py:180
  110.6 1.6 collective-permute-start.12
  112.1 4.2 %collective-permute-done.11.rest_0_ = bf16[512,1024]{1,0:T(8,128)(2,1)S(1)} collective-permute-done((bf16[512,1024]{1,0:T(8,128)(2,1)S(1)}, bf16[512,1024]{1,0:T(8,128)(2,1)S(1)}, u32[]{:S(2)}, u32[]{:S(2)}) %collective-permute-start.11) | collective-permute-done | bytes 1048608 | tf_op jit(solution)/shard_map/ppermute | solution.py:383
  116.3 8.9 %collective-permute-start.13 = (bf16[512,1024]{1,0:T(8,128)(2,1)S(1)}, bf16[512,1024]{1,0:T(8,128)(2,1)S(1)}, u32[]{:S(2)}, u32[]{:S(2)}) collective-permute-start(bf16[512,1024]{1,0:T(8,128)(2,1)S(1)} %collective-permute-done.11.rest_0_), channel_id=1, source_target_pairs={{0,4},{1,5},{2,6},{3,7},{4,0},{5,1},{6,2},{7,3},{8,12},{9,13},{10,... | collective-permute-start | bytes 3145736 | tf_op jit(solution)/shard_map/ppermute | solution.py:383
  125.3 2.2 collective-permute-done.13.rest_1_
  127.5 1.0 copy-done.11
  128.5 4.3 %query.1 = (bf16[512,1024]{1,0:T(8,128)(2,1)S(1)}, bf16[16,1024]{1,0:T(8,128)(2,1)}) custom-call(s32[2]{0:T(128)S(1)} %pad_add_fusion.at_ref, bf16[512,4096]{1,0:T(8,128)(2,1)} %all-gather.3.cloned.1.call-done.x_ref, f32[512,1024]{1,0:T(8,128)S(1)} %get-tuple-element.32.sum_ref, bf16[512,1024]{1,0:T(8,128)(2,1)} %copy-done.9, bf16[512,1024]{1,0:T(8,128)(2,1)} %copy-done.11), custom_call_target="tpu_custom_call" | custom-call | tf_op jit(solution)/shard_map/query/pallas_call | solution.py:224
  132.8 0.4 collective-permute-start.15
  133.3 2.2 collective-permute-start.14
  135.6 5.4 %mix.1.mixed_ref = f32[512,1024]{1,0:T(8,128)S(1)} custom-call(bf16[512,1024]{1,0:T(8,128)(2,1)} %get-tuple-element.38.gated_ref, bf16[160,1024]{1,0:T(8,128)(2,1)} %copy-done.12, bf16[2,16,1024]{2,1,0:T(8,128)(2,1)} %get-tuple-element.39.head_ref, f32[3,3,1024]{2,1,0:T(4,128)S(1)} %copy-done.3, f32[3,128,1024]{2,1,0:T(8,128)} %respond.1.response_ref, ...), custom_call_target="tpu_custom_call" | custom-call | tf_op jit(solution)/shard_map/mix/pallas_call | solution.py:344
  140.9 1.9 combine.1
  142.9 2.9 %convolution_convert_fusion.1 = bf16[512,1024]{1,0:T(8,128)(2,1)S(1)} fusion(bf16[512,1024]{1,0:T(8,128)(2,1)S(1)} %combine.1, bf16[1024,1024]{1,0:T(8,128)(2,1)} %param.15), kind=kOutput, calls=%fused_computation.7 | convolution fusion | flops 1074266112 | bytes 4194304 | tf_op jit(solution)/shard_map/dot_general | solution.py:466
  145.8 0.8 constant_dynamic-slice_fusion
  146.6 3.4 %collective-permute-start.25 = (bf16[256,1024]{1,0:T(8,128)(2,1)}, bf16[256,1024]{1,0:T(8,128)(2,1)}, u32[]{:S(2)}, u32[]{:S(2)}) collective-permute-start(bf16[256,1024]{1,0:T(8,128)(2,1)} %constant_dynamic-slice_fusion), channel_id=1, source_target_pairs={{0,1},{3,2},{4,5},{7,6},{8,9},{11,10},{12,13},{15,14},{16,17},{19,... | collective-permute-start | bytes 1572872 | tf_op jit(solution)/shard_map/ppermute | solution.py:383
  150.0 2.9 %convolution_convert_fusion = bf16[512,1024]{1,0:T(8,128)(2,1)S(1)} fusion(bf16[512,1024]{1,0:T(8,128)(2,1)S(1)} %combine.1, bf16[1024,1024]{1,0:T(8,128)(2,1)} %collective-permute-done.15), kind=kOutput, calls=%fused_computation.6 | convolution fusion | flops 1074266112 | bytes 4194304 | tf_op jit(solution)/shard_map/dot_general | solution.py:466
  152.9 0.8 constant_dynamic-slice_fusion.1
  153.7 2.1 collective-permute-start.22
  155.8 2.9 %fusion.4 = bf16[512,1024]{1,0:T(8,128)(2,1)S(1)} fusion(bf16[512,1024]{1,0:T(8,128)(2,1)S(1)} %combine.1, bf16[4096,1024]{1,0:T(8,128)(2,1)} %all-gather.5.cloned.1.call-done, s32[]{:T(128)S(6)} %select_n.123), kind=kOutput, calls=%fused_computation.4 | convolution fusion | flops 1074266112 | bytes 4194308 | tf_op jit(solution)/shard_map/dot_general | solution.py:466
  158.7 1.3 collective-permute-start.19
  160.1 2.9 %fusion.7 = bf16[512,1024]{1,0:T(8,128)(2,1)S(1)} fusion(bf16[512,1024]{1,0:T(8,128)(2,1)S(1)} %combine.1, bf16[4096,1024]{1,0:T(8,128)(2,1)} %all-gather.5.cloned.1.call-done, s32[]{:T(128)S(6)} %select_n.124), kind=kOutput, calls=%fused_computation.5 | convolution fusion | flops 1074266112 | bytes 4194308 | tf_op jit(solution)/shard_map/dot_general | solution.py:466
  163.0 1.3 collective-permute-start.16
  164.3 1.2 add_convert_fusion
  165.6 0.7 collective-permute-start.26
  166.3 5.3 %collective-permute-done.22 = bf16[256,1024]{1,0:T(8,128)(2,1)} collective-permute-done((bf16[256,1024]{1,0:T(8,128)(2,1)}, bf16[256,1024]{1,0:T(8,128)(2,1)}, u32[]{:S(2)}, u32[]{:S(2)}) %collective-permute-start.22) | collective-permute-done | bytes 524320 | tf_op jit(solution)/shard_map/ppermute | solution.py:383
  171.6 1.2 add_convert_fusion.1
  172.8 0.7 collective-permute-start.23
  173.5 9.2 %collective-permute-done.19 = bf16[256,1024]{1,0:T(8,128)(2,1)S(1)} collective-permute-done((bf16[256,1024]{1,0:T(8,128)(2,1)S(1)}, bf16[256,1024]{1,0:T(8,128)(2,1)S(1)}, u32[]{:S(2)}, u32[]{:S(2)}) %collective-permute-start.19) | collective-permute-done | bytes 524320 | tf_op jit(solution)/shard_map/ppermute | solution.py:383
  182.7 0.2 add_convert_fusion.2
  182.9 0.7 collective-permute-start.20
  183.6 10.3 %collective-permute-done.16 = bf16[256,1024]{1,0:T(8,128)(2,1)S(1)} collective-permute-done((bf16[256,1024]{1,0:T(8,128)(2,1)S(1)}, bf16[256,1024]{1,0:T(8,128)(2,1)S(1)}, u32[]{:S(2)}, u32[]{:S(2)}) %collective-permute-start.16) | collective-permute-done | bytes 524320 | tf_op jit(solution)/shard_map/ppermute | solution.py:383
  193.9 0.2 add_convert_fusion.3
  194.1 0.7 collective-permute-start.17
  194.8 0.1 add_convert_fusion.5
  195.0 5.1 %collective-permute-start.27 = (bf16[128,1024]{1,0:T(8,128)(2,1)S(1)}, bf16[128,1024]{1,0:T(8,128)(2,1)S(1)}, u32[]{:S(2)}, u32[]{:S(2)}) collective-permute-start(bf16[128,1024]{1,0:T(8,128)(2,1)S(1)} %add_convert_fusion.5), channel_id=1, source_target_pairs={{0,1},{1,0},{2,3},{3,2},{4,5},{5,4},{6,7},{7,6},{8,9},{9,8},{10,11... | collective-permute-start | bytes 786440 | tf_op jit(solution)/shard_map/ppermute | solution.py:383
  200.1 0.1 add_convert_fusion.7
  200.2 0.1 collective-permute-start.24
  200.3 0.1 add_convert_fusion.9
  200.4 2.1 collective-permute-start.21
  202.5 0.1 add_convert_fusion.11
  202.6 11.0 %collective-permute-start.18 = (bf16[128,1024]{1,0:T(8,128)(2,1)S(1)}, bf16[128,1024]{1,0:T(8,128)(2,1)S(1)}, u32[]{:S(2)}, u32[]{:S(2)}) collective-permute-start(bf16[128,1024]{1,0:T(8,128)(2,1)S(1)} %add_convert_fusion.11), channel_id=1, source_target_pairs={{0,1},{1,0},{2,3},{3,2},{4,5},{5,4},{6,7},{7,6},{8,9},{9,8},{10,11... | collective-permute-start | bytes 786440 | tf_op jit(solution)/shard_map/ppermute | solution.py:383
  213.6 0.4 broadcast_select_fusion.3
  214.0 3.6 %collective-permute-done.21 = bf16[128,1024]{1,0:T(8,128)(2,1)S(1)} collective-permute-done((bf16[128,1024]{1,0:T(8,128)(2,1)S(1)}, bf16[128,1024]{1,0:T(8,128)(2,1)S(1)}, u32[]{:S(2)}, u32[]{:S(2)}) %collective-permute-start.21) | collective-permute-done | bytes 262176 | tf_op jit(solution)/shard_map/ppermute | solution.py:383
  217.6 5.6 %collective-permute-done.18 = bf16[128,1024]{1,0:T(8,128)(2,1)S(1)} collective-permute-done((bf16[128,1024]{1,0:T(8,128)(2,1)S(1)}, bf16[128,1024]{1,0:T(8,128)(2,1)S(1)}, u32[]{:S(2)}, u32[]{:S(2)}) %collective-permute-start.18) | collective-permute-done | bytes 262176 | tf_op jit(solution)/shard_map/ppermute | solution.py:383
  223.2 0.4 broadcast_select_fusion.5
  223.6 0.2 broadcast_select_fusion.1
  223.9 1.0 pad_maximum_fusion
  (59 shorter events, 0.6 us)
Async XLA Ops:
  6.5 1.6 copy-start
  6.5 1.4 copy-start.13
  6.5 87.1 %all-gather.3.cloned.1.call-start = ((), (), s32[]{:S(2)}) async-start(), calls=%async_computation | async-start | bytes 5242880 | tf_op jit(solution)/shard_map/all_gather | solution.py:438
  10.0 145.8 %all-gather.5.cloned.1.call-start = ((), (), s32[]{:S(2)}) async-start(), calls=%async_computation.1 | async-start | bytes 10485760 | tf_op jit(solution)/shard_map/all_gather | solution.py:452
  10.1 26.2 %collective-permute-start.1 = (bf16[512,1024]{1,0:T(8,128)(2,1)S(1)}, bf16[512,1024]{1,0:T(8,128)(2,1)S(1)}, u32[]{:S(2)}, u32[]{:S(2)}) collective-permute-start(bf16[512,1024]{1,0:T(8,128)(2,1)S(1)} %dynamic-slice_bitcast_fusion.2), channel_id=1, source_target_pairs={{0,8},{1,9},{2,10},{3,11},{4,12},{5,13},{6,14},{7,15},{8,0},{9,1},... | collective-permute-start | bytes 3145736 | tf_op jit(solution)/shard_map/ppermute | solution.py:383
  36.3 30.8 %copy-start.6 = (bf16[512,1024]{1,0:T(8,128)(2,1)}, bf16[512,1024]{1,0:T(8,128)(2,1)S(1)}, u32[]{:S(2)}) copy-start(bf16[512,1024]{1,0:T(8,128)(2,1)S(1)} %collective-permute-done.1.rest_2_) | copy-start | bytes 3145732
  36.3 5.6 %copy-start.1 = (f32[128,1024]{1,0:T(8,128)S(1)}, f32[128,1024]{1,0:T(8,128)}, u32[]{:S(2)}) copy-start(f32[128,1024]{1,0:T(8,128)} %filter_ref.1) | copy-start | bytes 1572868
  36.3 5.6 %copy-start.2 = (bf16[256,256]{1,0:T(8,128)(2,1)S(1)}, bf16[256,256]{1,0:T(8,128)(2,1)}, u32[]{:S(2)}) copy-start(bf16[256,256]{1,0:T(8,128)(2,1)} %constant.52.clone.fwd_ref) | copy-start | bytes 393220
  36.3 5.6 %copy-start.5 = (f32[1024]{0:T(1024)S(1)}, f32[1024]{0:T(1024)}, u32[]{:S(2)}) copy-start(f32[1024]{0:T(1024)} %param.14) | copy-start | bytes 12292
  36.3 29.2 %collective-permute-start = (bf16[3,1024,1024]{2,1,0:T(8,128)(2,1)}, bf16[3,1024,1024]{2,1,0:T(8,128)(2,1)}, u32[]{:S(2)}, u32[]{:S(2)}) collective-permute-start(bf16[3,1024,1024]{2,1,0:T(8,128)(2,1)} %bitcast.21), channel_id=1, source_target_pairs={{0,4},{1,5},{2,6},{3,7},{4,0},{5,1},{6,2},{7,3},{8,12},{9,13},{10,... | collective-permute-start | bytes 18874376 | tf_op jit(solution)/shard_map/ppermute | solution.py:383
  38.6 55.1 %copy-start.3 = (f32[3,3,1024]{2,1,0:T(4,128)S(1)}, f32[3,3,1024]{2,1,0:T(4,128)}, u32[]{:S(2)}) copy-start(f32[3,3,1024]{2,1,0:T(4,128)} %taps_ref.2) | copy-start | bytes 110596
  38.6 25.2 %collective-permute-start.5 = (bf16[512,1024]{1,0:T(8,128)(2,1)S(1)}, bf16[512,1024]{1,0:T(8,128)(2,1)S(1)}, u32[]{:S(2)}, u32[]{:S(2)}) collective-permute-start(bf16[512,1024]{1,0:T(8,128)(2,1)S(1)} %get-tuple-element.28), channel_id=1, source_target_pairs={{0,8},{1,9},{2,10},{3,11},{4,12},{5,13},{6,14},{7,15},{8,0},{9,1},... | collective-permute-start | bytes 3145736 | tf_op jit(solution)/shard_map/ppermute | solution.py:383
  40.4 25.1 %collective-permute-start.3 = (bf16[512,1024]{1,0:T(8,128)(2,1)S(1)}, bf16[512,1024]{1,0:T(8,128)(2,1)}, u32[]{:S(2)}, u32[]{:S(2)}) collective-permute-start(bf16[512,1024]{1,0:T(8,128)(2,1)S(1)} %collective-permute-done.1.rest_2_), channel_id=1, source_target_pairs={{0,16},{1,17},{2,18},{3,19},{4,20},{5,21},{6,22},{7,23},{8,24},{9,... | collective-permute-start | bytes 3145736 | tf_op jit(solution)/shard_map/ppermute | solution.py:383
  63.8 29.9 %copy-start.7 = (bf16[512,1024]{1,0:T(8,128)(2,1)}, bf16[512,1024]{1,0:T(8,128)(2,1)S(1)}, u32[]{:S(2)}) copy-start(bf16[512,1024]{1,0:T(8,128)(2,1)S(1)} %collective-permute-done.5.rest_8_) | copy-start | bytes 3145732
  63.8 24.4 %collective-permute-start.8 = (bf16[512,1024]{1,0:T(8,128)(2,1)S(1)}, bf16[512,1024]{1,0:T(8,128)(2,1)S(1)}, u32[]{:S(2)}, u32[]{:S(2)}) collective-permute-start(bf16[512,1024]{1,0:T(8,128)(2,1)S(1)} %get-tuple-element.30), channel_id=1, source_target_pairs={{0,8},{1,9},{2,10},{3,11},{4,12},{5,13},{6,14},{7,15},{8,0},{9,1},... | collective-permute-start | bytes 3145736 | tf_op jit(solution)/shard_map/ppermute | solution.py:383
  65.5 24.2 %collective-permute-start.7 = (bf16[512,1024]{1,0:T(8,128)(2,1)S(1)}, bf16[512,1024]{1,0:T(8,128)(2,1)}, u32[]{:S(2)}, u32[]{:S(2)}) collective-permute-start(bf16[512,1024]{1,0:T(8,128)(2,1)S(1)} %collective-permute-done.5.rest_8_), channel_id=1, source_target_pairs={{0,16},{1,17},{2,18},{3,19},{4,20},{5,21},{6,22},{7,23},{8,24},{9,... | collective-permute-start | bytes 3145736 | tf_op jit(solution)/shard_map/ppermute | solution.py:383
  67.0 22.7 %collective-permute-start.2 = (bf16[512,1024]{1,0:T(8,128)(2,1)S(1)}, bf16[512,1024]{1,0:T(8,128)(2,1)S(1)}, u32[]{:S(2)}, u32[]{:S(2)}) collective-permute-start(bf16[512,1024]{1,0:T(8,128)(2,1)S(1)} %collective-permute-done.1.rest_2_), channel_id=1, source_target_pairs={{0,4},{1,5},{2,6},{3,7},{4,0},{5,1},{6,2},{7,3},{8,12},{9,13},{10,... | collective-permute-start | bytes 3145736 | tf_op jit(solution)/shard_map/ppermute | solution.py:383
  67.0 25.3 %collective-permute-start.6 = (bf16[512,1024]{1,0:T(8,128)(2,1)S(1)}, bf16[512,1024]{1,0:T(8,128)(2,1)}, u32[]{:S(2)}, u32[]{:S(2)}) collective-permute-start(bf16[512,1024]{1,0:T(8,128)(2,1)S(1)} %collective-permute-done.5.rest_8_), channel_id=1, source_target_pairs={{0,4},{1,5},{2,6},{3,7},{4,0},{5,1},{6,2},{7,3},{8,12},{9,13},{10,... | collective-permute-start | bytes 3145736 | tf_op jit(solution)/shard_map/ppermute | solution.py:383
  67.6 24.8 %collective-permute-start.4 = (bf16[512,1024]{1,0:T(8,128)(2,1)}, bf16[512,1024]{1,0:T(8,128)(2,1)}, u32[]{:S(2)}, u32[]{:S(2)}) collective-permute-start(bf16[512,1024]{1,0:T(8,128)(2,1)} %collective-permute-done.3.rest_4_), channel_id=1, source_target_pairs={{0,4},{1,5},{2,6},{3,7},{4,0},{5,1},{6,2},{7,3},{8,12},{9,13},{10,... | collective-permute-start | bytes 3145736 | tf_op jit(solution)/shard_map/ppermute | solution.py:383
  88.2 5.5 %copy-start.8 = (bf16[512,1024]{1,0:T(8,128)(2,1)}, bf16[512,1024]{1,0:T(8,128)(2,1)S(1)}, u32[]{:S(2)}) copy-start(bf16[512,1024]{1,0:T(8,128)(2,1)S(1)} %collective-permute-done.8.rest_14_) | copy-start | bytes 3145732
  88.2 4.2 %collective-permute-start.10 = (bf16[512,1024]{1,0:T(8,128)(2,1)S(1)}, bf16[512,1024]{1,0:T(8,128)(2,1)}, u32[]{:S(2)}, u32[]{:S(2)}) collective-permute-start(bf16[512,1024]{1,0:T(8,128)(2,1)S(1)} %collective-permute-done.8.rest_14_), channel_id=1, source_target_pairs={{0,4},{1,5},{2,6},{3,7},{4,0},{5,1},{6,2},{7,3},{8,12},{9,13},{10,... | collective-permute-start | bytes 3145736 | tf_op jit(solution)/shard_map/ppermute | solution.py:383
  89.7 3.9 %collective-permute-start.9 = (bf16[512,1024]{1,0:T(8,128)(2,1)}, bf16[512,1024]{1,0:T(8,128)(2,1)}, u32[]{:S(2)}, u32[]{:S(2)}) collective-permute-start(bf16[512,1024]{1,0:T(8,128)(2,1)} %collective-permute-done.7.rest_10_), channel_id=1, source_target_pairs={{0,4},{1,5},{2,6},{3,7},{4,0},{5,1},{6,2},{7,3},{8,12},{9,13},{10,... | collective-permute-start | bytes 3145736 | tf_op jit(solution)/shard_map/ppermute | solution.py:383
  89.7 1.0 copy-start.10
  90.7 25.6 %collective-permute-start.11 = (bf16[512,1024]{1,0:T(8,128)(2,1)S(1)}, bf16[512,1024]{1,0:T(8,128)(2,1)S(1)}, u32[]{:S(2)}, u32[]{:S(2)}) collective-permute-start(bf16[512,1024]{1,0:T(8,128)(2,1)S(1)} %collective-permute-done.8.rest_14_), channel_id=1, source_target_pairs={{0,16},{1,17},{2,18},{3,19},{4,20},{5,21},{6,22},{7,23},{8,24},{9,... | collective-permute-start | bytes 3145736 | tf_op jit(solution)/shard_map/ppermute | solution.py:383
  110.6 5.8 %collective-permute-start.12 = (bf16[160,1024]{1,0:T(8,128)(2,1)}, bf16[160,1024]{1,0:T(8,128)(2,1)S(1)}, u32[]{:S(2)}, u32[]{:S(2)}) collective-permute-start(bf16[160,1024]{1,0:T(8,128)(2,1)} %get-tuple-element.34), channel_id=1, source_target_pairs={{0,4},{1,5},{2,6},{3,7},{4,8},{5,9},{6,10},{7,11},{8,12},{9,13},{1... | collective-permute-start | bytes 983048 | tf_op jit(solution)/shard_map/ppermute | solution.py:383
  116.3 11.2 %copy-start.9 = (bf16[512,1024]{1,0:T(8,128)(2,1)}, bf16[512,1024]{1,0:T(8,128)(2,1)S(1)}, u32[]{:S(2)}) copy-start(bf16[512,1024]{1,0:T(8,128)(2,1)S(1)} %collective-permute-done.11.rest_0_) | copy-start | bytes 3145732
  116.3 19.2 %copy-start.12 = (bf16[160,1024]{1,0:T(8,128)(2,1)}, bf16[160,1024]{1,0:T(8,128)(2,1)S(1)}, u32[]{:S(2)}) copy-start(bf16[160,1024]{1,0:T(8,128)(2,1)S(1)} %collective-permute-done.12.halo_ref) | copy-start | bytes 983044
  116.3 11.2 %collective-permute-start.13 = (bf16[512,1024]{1,0:T(8,128)(2,1)S(1)}, bf16[512,1024]{1,0:T(8,128)(2,1)S(1)}, u32[]{:S(2)}, u32[]{:S(2)}) collective-permute-start(bf16[512,1024]{1,0:T(8,128)(2,1)S(1)} %collective-permute-done.11.rest_0_), channel_id=1, source_target_pairs={{0,4},{1,5},{2,6},{3,7},{4,0},{5,1},{6,2},{7,3},{8,12},{9,13},{10,... | collective-permute-start | bytes 3145736 | tf_op jit(solution)/shard_map/ppermute | solution.py:383
  127.5 1.0 copy-start.11
  128.5 7.0 %copy-start.4 = (bf16[128,768]{1,0:T(8,128)(2,1)S(1)}, bf16[128,768]{1,0:T(8,128)(2,1)}, u32[]{:S(2)}) copy-start(bf16[128,768]{1,0:T(8,128)(2,1)} %constant.53.clone.inv_ref) | copy-start | bytes 589828
  132.8 17.2 %collective-permute-start.15 = (bf16[1024,1024]{1,0:T(8,128)(2,1)}, bf16[1024,1024]{1,0:T(8,128)(2,1)}, u32[]{:S(2)}, u32[]{:S(2)}) collective-permute-start(bf16[1024,1024]{1,0:T(8,128)(2,1)} %param.15), channel_id=1, source_target_pairs={{0,4},{1,5},{2,6},{3,7},{4,0},{5,1},{6,2},{7,3},{8,12},{9,13},{10,... | collective-permute-start | bytes 6291464 | tf_op jit(solution)/shard_map/ppermute | solution.py:383
  133.3 7.7 %collective-permute-start.14 = (bf16[16,1024]{1,0:T(8,128)(2,1)}, bf16[16,1024]{1,0:T(8,128)(2,1)S(1)}, u32[]{:S(2)}, u32[]{:S(2)}) collective-permute-start(bf16[16,1024]{1,0:T(8,128)(2,1)} %get-tuple-element.37), channel_id=1, source_target_pairs={{0,4},{1,5},{2,6},{3,7},{4,8},{5,9},{6,10},{7,11},{8,12},{9,13},{1... | collective-permute-start | bytes 98312 | tf_op jit(solution)/shard_map/ppermute | solution.py:383
  146.6 17.7 %collective-permute-start.25 = (bf16[256,1024]{1,0:T(8,128)(2,1)}, bf16[256,1024]{1,0:T(8,128)(2,1)}, u32[]{:S(2)}, u32[]{:S(2)}) collective-permute-start(bf16[256,1024]{1,0:T(8,128)(2,1)} %constant_dynamic-slice_fusion), channel_id=1, source_target_pairs={{0,1},{3,2},{4,5},{7,6},{8,9},{11,10},{12,13},{15,14},{16,17},{19,... | collective-permute-start | bytes 1572872 | tf_op jit(solution)/shard_map/ppermute | solution.py:383
  153.7 17.9 %collective-permute-start.22 = (bf16[256,1024]{1,0:T(8,128)(2,1)}, bf16[256,1024]{1,0:T(8,128)(2,1)}, u32[]{:S(2)}, u32[]{:S(2)}) collective-permute-start(bf16[256,1024]{1,0:T(8,128)(2,1)} %constant_dynamic-slice_fusion.1), channel_id=1, source_target_pairs={{0,1},{3,2},{4,5},{7,6},{8,9},{11,10},{12,13},{15,14},{16,17},{19,... | collective-permute-start | bytes 1572872 | tf_op jit(solution)/shard_map/ppermute | solution.py:383
  158.7 24.0 %collective-permute-start.19 = (bf16[256,1024]{1,0:T(8,128)(2,1)S(1)}, bf16[256,1024]{1,0:T(8,128)(2,1)S(1)}, u32[]{:S(2)}, u32[]{:S(2)}) collective-permute-start(bf16[256,1024]{1,0:T(8,128)(2,1)S(1)} %constant_dynamic-slice_fusion.2), channel_id=1, source_target_pairs={{0,1},{3,2},{4,5},{7,6},{8,9},{11,10},{12,13},{15,14},{16,17},{19,... | collective-permute-start | bytes 1572872 | tf_op jit(solution)/shard_map/ppermute | solution.py:383
  163.0 30.9 %collective-permute-start.16 = (bf16[256,1024]{1,0:T(8,128)(2,1)S(1)}, bf16[256,1024]{1,0:T(8,128)(2,1)S(1)}, u32[]{:S(2)}, u32[]{:S(2)}) collective-permute-start(bf16[256,1024]{1,0:T(8,128)(2,1)S(1)} %constant_dynamic-slice_fusion.3), channel_id=1, source_target_pairs={{0,1},{3,2},{4,5},{7,6},{8,9},{11,10},{12,13},{15,14},{16,17},{19,... | collective-permute-start | bytes 1572872 | tf_op jit(solution)/shard_map/ppermute | solution.py:383
  165.6 29.3 %collective-permute-start.26 = (bf16[256,1024]{1,0:T(8,128)(2,1)S(1)}, bf16[256,1024]{1,0:T(8,128)(2,1)S(1)}, u32[]{:S(2)}, u32[]{:S(2)}) collective-permute-start(bf16[256,1024]{1,0:T(8,128)(2,1)S(1)} %add_convert_fusion), channel_id=1, source_target_pairs={{1,2},{2,1},{5,6},{6,5},{9,10},{10,9},{13,14},{14,13},{17,18},{18,... | collective-permute-start | bytes 1572872 | tf_op jit(solution)/shard_map/ppermute | solution.py:383
  172.8 27.3 %collective-permute-start.23 = (bf16[256,1024]{1,0:T(8,128)(2,1)S(1)}, bf16[256,1024]{1,0:T(8,128)(2,1)S(1)}, u32[]{:S(2)}, u32[]{:S(2)}) collective-permute-start(bf16[256,1024]{1,0:T(8,128)(2,1)S(1)} %add_convert_fusion.1), channel_id=1, source_target_pairs={{1,2},{2,1},{5,6},{6,5},{9,10},{10,9},{13,14},{14,13},{17,18},{18,... | collective-permute-start | bytes 1572872 | tf_op jit(solution)/shard_map/ppermute | solution.py:383
  182.9 17.4 %collective-permute-start.20 = (bf16[256,1024]{1,0:T(8,128)(2,1)S(1)}, bf16[256,1024]{1,0:T(8,128)(2,1)S(1)}, u32[]{:S(2)}, u32[]{:S(2)}) collective-permute-start(bf16[256,1024]{1,0:T(8,128)(2,1)S(1)} %add_convert_fusion.2), channel_id=1, source_target_pairs={{1,2},{2,1},{5,6},{6,5},{9,10},{10,9},{13,14},{14,13},{17,18},{18,... | collective-permute-start | bytes 1572872 | tf_op jit(solution)/shard_map/ppermute | solution.py:383
  194.1 8.3 %collective-permute-start.17 = (bf16[256,1024]{1,0:T(8,128)(2,1)S(1)}, bf16[256,1024]{1,0:T(8,128)(2,1)S(1)}, u32[]{:S(2)}, u32[]{:S(2)}) collective-permute-start(bf16[256,1024]{1,0:T(8,128)(2,1)S(1)} %add_convert_fusion.3), channel_id=1, source_target_pairs={{1,2},{2,1},{5,6},{6,5},{9,10},{10,9},{13,14},{14,13},{17,18},{18,... | collective-permute-start | bytes 1572872 | tf_op jit(solution)/shard_map/ppermute | solution.py:383
  195.0 18.6 %collective-permute-start.27 = (bf16[128,1024]{1,0:T(8,128)(2,1)S(1)}, bf16[128,1024]{1,0:T(8,128)(2,1)S(1)}, u32[]{:S(2)}, u32[]{:S(2)}) collective-permute-start(bf16[128,1024]{1,0:T(8,128)(2,1)S(1)} %add_convert_fusion.5), channel_id=1, source_target_pairs={{0,1},{1,0},{2,3},{3,2},{4,5},{5,4},{6,7},{7,6},{8,9},{9,8},{10,11... | collective-permute-start | bytes 786440 | tf_op jit(solution)/shard_map/ppermute | solution.py:383
  200.2 13.4 %collective-permute-start.24 = (bf16[128,1024]{1,0:T(8,128)(2,1)S(1)}, bf16[128,1024]{1,0:T(8,128)(2,1)S(1)}, u32[]{:S(2)}, u32[]{:S(2)}) collective-permute-start(bf16[128,1024]{1,0:T(8,128)(2,1)S(1)} %add_convert_fusion.7), channel_id=1, source_target_pairs={{0,1},{1,0},{2,3},{3,2},{4,5},{5,4},{6,7},{7,6},{8,9},{9,8},{10,11... | collective-permute-start | bytes 786440 | tf_op jit(solution)/shard_map/ppermute | solution.py:383
  200.4 17.2 %collective-permute-start.21 = (bf16[128,1024]{1,0:T(8,128)(2,1)S(1)}, bf16[128,1024]{1,0:T(8,128)(2,1)S(1)}, u32[]{:S(2)}, u32[]{:S(2)}) collective-permute-start(bf16[128,1024]{1,0:T(8,128)(2,1)S(1)} %add_convert_fusion.9), channel_id=1, source_target_pairs={{0,1},{1,0},{2,3},{3,2},{4,5},{5,4},{6,7},{7,6},{8,9},{9,8},{10,11... | collective-permute-start | bytes 786440 | tf_op jit(solution)/shard_map/ppermute | solution.py:383
  202.6 20.6 %collective-permute-start.18 = (bf16[128,1024]{1,0:T(8,128)(2,1)S(1)}, bf16[128,1024]{1,0:T(8,128)(2,1)S(1)}, u32[]{:S(2)}, u32[]{:S(2)}) collective-permute-start(bf16[128,1024]{1,0:T(8,128)(2,1)S(1)} %add_convert_fusion.11), channel_id=1, source_target_pairs={{0,1},{1,0},{2,3},{3,2},{4,5},{5,4},{6,7},{7,6},{8,9},{9,8},{10,11... | collective-permute-start | bytes 786440 | tf_op jit(solution)/shard_map/ppermute | solution.py:383
Sparse Core Ops, SparseCore 0:
  10.2 83.4 all-gather.2
  95.2 56.8 all-gather.4

commit v11 on v5

--- a/solution.py
+++ b/solution.py
@@ -421,8 +421,10 @@
             combined, rows_out, (((1,), (1,)), ((), ())), preferred_element_type=f32
         ).astype(bf16)
 
-    results, firsts = [], []
-    for rows_out in sets:
+    results, firsts, seconds = [], [], []
+    for n, rows_out in enumerate(sets):
+        if paired and n == 2:
+            combined = after(combined, firsts[0])
         partial = product(rows_out)
         combined = after(combined, partial)
 
@@ -436,7 +438,10 @@
             far_pair = block(jnp.where(z < 2, 2, 0), 2)
             firsts.append(send(far_pair, {0: 1, 3: 2}))
             got = plus(far_pair, firsts[-1])
+            if n >= 2:
+                got = after(got, seconds[n - 2])
             got = send(got, {1: 2, 2: 1})
+            seconds.append(got)
             low, high = got[:length], got[length:]
             odd = z % 2 == 1
             got_own = jnp.where(odd, high, low)

time: 231 us -> 239 us (1.035)
  other arithmetic: 5.47 us -> 11.3 us
  waiting for transfers between devices: 97.7 us -> 103 us
  starting transfers between devices: 59.5 us -> 55.4 us
    ppermute x28, waiting for transfers between devices: 90.3 us -> 101 us  [move(): return lax.ppermute(value, axes, pairs)]
    all_gather x1, waiting for transfers between devices: 5.29 us -> 0.01 us  [local(): lax.all_gather(after(w_out, near[1]), 'context', axis=0, tiled=True)]
    convert_element_type x8, other arithmetic: 3.36 us -> 8.03 us  [plus(): return total.astype(bf16)]
    ppermute x28, starting transfers between devices: 59.4 us -> 55.4 us  [move(): return lax.ppermute(value, axes, pairs)]
  transfers between devices with their start and end apart: 30 -> 30, of which waited for: 11 -> 12; matrix products, arithmetic and copies ran while one was open for 9% -> 11% of each run, Pallas kernels for 14% -> 13%
where the time goes in v11:
time: 239 us; the launch traced here: 238 us
  waiting for transfers between devices  103 us (43%)
  starting transfers between devices  55.4 us (23%)
  Pallas kernels  33.5 us (14%)
  between operations  13.8 us (6%)
  matrix products  11.5 us (5%)
  other arithmetic  11.3 us (5%)
  local copies, waits for them, and re-layouts  9.5 us (4%)
    ppermute x28, waiting for transfers between devices, move(): return lax.ppermute(value, axes, pairs)  101 us
    ppermute x28, starting transfers between devices, move(): return lax.ppermute(value, axes, pairs)  55.4 us
    pallas_call x1, Pallas kernels, gate(): pl.pallas_call(functools.partial(gate_kernel, kinds_of(one), kinds_of(two...  15 us
    dot_general x4, matrix products, product(): lax.dot_general(combined, rows_out, (((1,), (1,)), ((), ())), preferred_e...  11.5 us
    pallas_call x1, Pallas kernels, query(): pl.pallas_call(functools.partial(query_kernel, kinds_of(pieces), width),...  8.86 us
    convert_element_type x8, other arithmetic, plus(): return total.astype(bf16)  8.03 us
    pallas_call x1, Pallas kernels, mix(): pl.pallas_call(mix_kernel, grid=(channels // width,), in_specs=[col(slab)...  5.39 us
  transfers between devices with their start and end apart: 30, of which 12 were waited for; matrix products, arithmetic and copies ran while one was open for 11% of the time, Pallas kernels for 13%

profile of v11, /device:TPU:0, one launch (start us, length us, event | category | flops | bytes accessed | tf_op | source)
XLA Modules:
  0.0 238.3 jit_solution(11386674349880616769)
XLA Ops:
  6.5 1.4 dynamic-slice_bitcast_fusion.2
  8.0 0.1 copy-done
  8.1 1.9 norm.1
  10.1 3.0 %collective-permute-start.1 = (bf16[512,1024]{1,0:T(8,128)(2,1)S(1)}, bf16[512,1024]{1,0:T(8,128)(2,1)S(1)}, u32[]{:S(2)}, u32[]{:S(2)}) collective-permute-start(bf16[512,1024]{1,0:T(8,128)(2,1)S(1)} %dynamic-slice_bitcast_fusion.2), channel_id=1, source_target_pairs={{0,8},{1,9},{2,10},{3,11},{4,12},{5,13},{6,14},{7,15},{8,0},{9,1},... | collective-permute-start | bytes 3145736 | tf_op jit(solution)/shard_map/ppermute | solution.py:342
  13.1 23.2 %collective-permute-done.1.rest_2_ = bf16[512,1024]{1,0:T(8,128)(2,1)S(1)} collective-permute-done((bf16[512,1024]{1,0:T(8,128)(2,1)S(1)}, bf16[512,1024]{1,0:T(8,128)(2,1)S(1)}, u32[]{:S(2)}, u32[]{:S(2)}) %collective-permute-start.1) | collective-permute-done | bytes 1048608 | tf_op jit(solution)/shard_map/ppermute | solution.py:342
  36.4 2.1 dynamic-slice_bitcast_fusion
  38.6 1.8 collective-permute-start.5
  40.4 1.5 collective-permute-start.3
  41.9 2.3 respond.1.response_ref
  44.2 19.6 %collective-permute-done.5.rest_8_ = bf16[512,1024]{1,0:T(8,128)(2,1)} collective-permute-done((bf16[512,1024]{1,0:T(8,128)(2,1)S(1)}, bf16[512,1024]{1,0:T(8,128)(2,1)}, u32[]{:S(2)}, u32[]{:S(2)}) %collective-permute-start.5) | collective-permute-done | bytes 1048608 | tf_op jit(solution)/shard_map/ppermute | solution.py:342
  63.9 1.7 collective-permute-start.8
  65.6 1.5 collective-permute-start.7
  67.1 0.5 collective-permute-start.6
  67.7 20.5 %collective-permute-done.8.rest_2_ = bf16[512,1024]{1,0:T(8,128)(2,1)S(1)} collective-permute-done((bf16[512,1024]{1,0:T(8,128)(2,1)S(1)}, bf16[512,1024]{1,0:T(8,128)(2,1)S(1)}, u32[]{:S(2)}, u32[]{:S(2)}) %collective-permute-start.8) | collective-permute-done | bytes 1048608 | tf_op jit(solution)/shard_map/ppermute | solution.py:342
  88.2 1.8 collective-permute-done.7.rest_10_
  90.0 1.5 collective-permute-start.13
  91.6 2.1 all-gather.3.cloned.1.call-done.x_ref
  93.7 0.9 slice.36
  94.6 15.0 %gate.1 = (bf16[512,1024]{1,0:T(8,128)(2,1)}, bf16[2,16,1024]{2,1,0:T(8,128)(2,1)}, bf16[160,1024]{1,0:T(8,128)(2,1)}) custom-call(s32[6]{0:T(128)S(1)} %stack.34.at_ref, bf16[512,4096]{1,0:T(8,128)(2,1)} %all-gather.3.cloned.1.call-done.x_ref, f32[3,3,1024]{2,1,0:T(4,128)S(1)} %copy-done.3, bf16[3,1024,1024]{2,1,0:T(8,128)(2,1)} %bitcast.23, ...), custom_call_target="tpu_custom_call" | custom-call | tf_op jit(solution)/shard_map/gate/pallas_call | solution.py:170
  109.6 1.5 collective-permute-start.10
  111.1 1.9 collective-permute-start.12
  113.1 2.5 %collective-permute-done.13.rest_4_ = bf16[512,1024]{1,0:T(8,128)(2,1)S(1)} collective-permute-done((bf16[512,1024]{1,0:T(8,128)(2,1)S(1)}, bf16[512,1024]{1,0:T(8,128)(2,1)S(1)}, u32[]{:S(2)}, u32[]{:S(2)}) %collective-permute-start.13) | collective-permute-done | bytes 1048608 | tf_op jit(solution)/shard_map/ppermute | solution.py:342
  115.5 2.1 collective-permute-start.14
  117.7 3.1 %collective-permute-start.11 = (bf16[160,1024]{1,0:T(8,128)(2,1)}, bf16[160,1024]{1,0:T(8,128)(2,1)}, u32[]{:S(2)}, u32[]{:S(2)}) collective-permute-start(bf16[160,1024]{1,0:T(8,128)(2,1)} %get-tuple-element.37), channel_id=1, source_target_pairs={{0,4},{1,5},{2,6},{3,7},{4,8},{5,9},{6,10},{7,11},{8,12},{9,13},{1... | collective-permute-start | bytes 983048 | tf_op jit(solution)/shard_map/ppermute | solution.py:342
  120.8 0.7 collective-permute-done.14.rest_5_
  121.5 0.3 copy-done.14
  121.8 8.9 %query.1.query_ref = f32[512,1024]{1,0:T(8,128)S(1)} custom-call(s32[6]{0:T(128)S(1)} %stack.34.at_ref, bf16[512,4096]{1,0:T(8,128)(2,1)} %all-gather.3.cloned.1.call-done.x_ref, bf16[16,4096]{1,0:T(8,128)(2,1)} %copy-done.15, f32[3,3,1024]{2,1,0:T(4,128)S(1)} %copy-done.3, bf16[3,1024,1024]{2,1,0:T(8,128)(2,1)} %bitcast.25, ...), custom_call_target="tpu_custom_call" | custom-call | tf_op jit(solution)/shard_map/query/pallas_call | solution.py:209
  130.7 5.4 %mix.1 = bf16[512,1024]{1,0:T(8,128)(2,1)S(1)} custom-call(bf16[512,1024]{1,0:T(8,128)(2,1)} %get-tuple-element.34.gated_ref, bf16[160,1024]{1,0:T(8,128)(2,1)} %collective-permute-done.11.halo_ref, bf16[2,16,1024]{2,1,0:T(8,128)(2,1)} %get-tuple-element.38.head_ref, f32[3,3,1024]{2,1,0:T(4,128)S(1)} %copy-done.3, f32[3,128,1024]{2,1,0:T(8,128)} %respond.1.response_ref, ...), custom_call_target="tpu_custom_call" | custom-call | tf_op jit(solution)/shard_map/mix/pallas_call | solution.py:302
  136.1 2.9 %convolution_convert_fusion.1 = bf16[512,1024]{1,0:T(8,128)(2,1)S(1)} fusion(bf16[512,1024]{1,0:T(8,128)(2,1)S(1)} %mix.1, bf16[1024,1024]{1,0:T(8,128)(2,1)} %param.15), kind=kOutput, calls=%fused_computation.7 | convolution fusion | flops 1074266112 | bytes 4194304 | tf_op jit(solution)/shard_map/dot_general | solution.py:420
  139.0 1.5 collective-permute-start.16
  140.5 9.8 %collective-permute-done.16 = bf16[256,1024]{1,0:T(8,128)(2,1)S(1)} collective-permute-done((bf16[256,1024]{1,0:T(8,128)(2,1)S(1)}, bf16[256,1024]{1,0:T(8,128)(2,1)S(1)}, u32[]{:S(2)}, u32[]{:S(2)}) %collective-permute-start.16) | collective-permute-done | bytes 524320 | tf_op jit(solution)/shard_map/ppermute | solution.py:342
  150.3 1.0 add_convert_fusion
  151.3 1.5 collective-permute-start.23
  152.8 2.9 %convolution_convert_fusion = bf16[512,1024]{1,0:T(8,128)(2,1)S(1)} fusion(bf16[512,1024]{1,0:T(8,128)(2,1)S(1)} %mix.1, bf16[1024,1024]{1,0:T(8,128)(2,1)} %collective-permute-done.15), kind=kOutput, calls=%fused_computation.6 | convolution fusion | flops 1074266112 | bytes 4194304 | tf_op jit(solution)/shard_map/dot_general | solution.py:420
  155.7 1.0 copy-done.8
  156.6 0.8 constant_dynamic-slice_fusion.1
  157.4 7.8 %collective-permute-start.18 = (bf16[256,1024]{1,0:T(8,128)(2,1)}, bf16[256,1024]{1,0:T(8,128)(2,1)}, u32[]{:S(2)}, u32[]{:S(2)}) collective-permute-start(bf16[256,1024]{1,0:T(8,128)(2,1)} %constant_dynamic-slice_fusion.1), channel_id=1, source_target_pairs={{0,1},{3,2},{4,5},{7,6},{8,9},{11,10},{12,13},{15,14},{16,17},{19,... | collective-permute-start | bytes 1572872 | tf_op jit(solution)/shard_map/ppermute | solution.py:342
  165.2 2.9 %fusion.4 = bf16[512,1024]{1,0:T(8,128)(2,1)S(1)} fusion(bf16[512,1024]{1,0:T(8,128)(2,1)S(1)} %mix.1, bf16[4096,1024]{1,0:T(8,128)(2,1)} %all-gather.5.cloned.1.call-done, s32[]{:T(128)S(6)} %select_n.125), kind=kOutput, calls=%fused_computation.4 | convolution fusion | flops 1074266112 | bytes 4194308 | tf_op jit(solution)/shard_map/dot_general | solution.py:420
  168.1 0.9 constant_dynamic-slice_fusion
  169.0 2.2 collective-permute-start.22
  171.2 2.9 %fusion.7 = bf16[512,1024]{1,0:T(8,128)(2,1)S(1)} fusion(bf16[512,1024]{1,0:T(8,128)(2,1)S(1)} %mix.1, bf16[4096,1024]{1,0:T(8,128)(2,1)} %all-gather.5.cloned.1.call-done, s32[]{:T(128)S(6)} %select_n.126), kind=kOutput, calls=%fused_computation.5 | convolution fusion | flops 1074266112 | bytes 4194308 | tf_op jit(solution)/shard_map/dot_general | solution.py:420
  174.1 1.0 copy-done.6
  175.1 0.8 constant_dynamic-slice_fusion.2
  175.9 2.2 collective-permute-start.17
  178.1 2.0 add_convert_fusion.2
  180.1 1.4 collective-permute-start.19
  181.6 6.3 %collective-permute-done.22 = bf16[256,1024]{1,0:T(8,128)(2,1)} collective-permute-done((bf16[256,1024]{1,0:T(8,128)(2,1)}, bf16[256,1024]{1,0:T(8,128)(2,1)}, u32[]{:S(2)}, u32[]{:S(2)}) %collective-permute-start.22) | collective-permute-done | bytes 524320 | tf_op jit(solution)/shard_map/ppermute | solution.py:342
  187.9 1.2 add_convert_fusion.1
  189.1 0.7 collective-permute-start.24
  189.8 9.3 %collective-permute-done.17 = bf16[256,1024]{1,0:T(8,128)(2,1)} collective-permute-done((bf16[256,1024]{1,0:T(8,128)(2,1)}, bf16[256,1024]{1,0:T(8,128)(2,1)}, u32[]{:S(2)}, u32[]{:S(2)}) %collective-permute-start.17) | collective-permute-done | bytes 524320 | tf_op jit(solution)/shard_map/ppermute | solution.py:342
  199.1 1.2 add_convert_fusion.3
  200.3 0.7 collective-permute-start.20
  201.0 1.2 add_convert_fusion.5
  202.2 3.8 %collective-permute-start.27 = (bf16[128,1024]{1,0:T(8,128)(2,1)S(1)}, bf16[128,1024]{1,0:T(8,128)(2,1)S(1)}, u32[]{:S(2)}, u32[]{:S(2)}) collective-permute-start(bf16[128,1024]{1,0:T(8,128)(2,1)S(1)} %add_convert_fusion.5), channel_id=1, source_target_pairs={{0,1},{1,0},{2,3},{3,2},{4,5},{5,4},{6,7},{7,6},{8,9},{9,8},{10,11... | collective-permute-start | bytes 786440 | tf_op jit(solution)/shard_map/ppermute | solution.py:342
  206.0 1.2 add_convert_fusion.7
  207.2 0.1 add_convert_fusion.9
  207.4 2.1 collective-permute-start.25
  209.6 11.0 %collective-permute-start.21 = (bf16[128,1024]{1,0:T(8,128)(2,1)S(1)}, bf16[128,1024]{1,0:T(8,128)(2,1)S(1)}, u32[]{:S(2)}, u32[]{:S(2)}) collective-permute-start(bf16[128,1024]{1,0:T(8,128)(2,1)S(1)} %add_convert_fusion.11), channel_id=1, source_target_pairs={{0,1},{1,0},{2,3},{3,2},{4,5},{5,4},{6,7},{7,6},{8,9},{9,8},{10,11... | collective-permute-start | bytes 786440 | tf_op jit(solution)/shard_map/ppermute | solution.py:342
  220.6 1.6 broadcast_select_fusion.3
  222.2 2.1 collective-permute-done.25
  224.4 5.3 %collective-permute-done.21 = bf16[128,1024]{1,0:T(8,128)(2,1)S(1)} collective-permute-done((bf16[128,1024]{1,0:T(8,128)(2,1)S(1)}, bf16[128,1024]{1,0:T(8,128)(2,1)S(1)}, u32[]{:S(2)}, u32[]{:S(2)}) %collective-permute-start.21) | collective-permute-done | bytes 262176 | tf_op jit(solution)/shard_map/ppermute | solution.py:342
  229.7 0.4 broadcast_select_fusion.5
  230.1 0.2 broadcast_select_fusion.1
  230.4 1.1 pad_maximum_fusion
  (64 shorter events, 0.7 us)
Async XLA Ops:
  6.5 1.6 copy-start
  6.5 1.4 copy-start.16
  6.5 87.1 %all-gather.3.cloned.1.call-start = ((), (), s32[]{:S(2)}) async-start(), calls=%async_computation | async-start | bytes 5242880 | tf_op jit(solution)/shard_map/all_gather | solution.py:395
  10.0 155.2 %all-gather.5.cloned.1.call-start = ((), (), s32[]{:S(2)}) async-start(), calls=%async_computation.1 | async-start | bytes 10485760 | tf_op jit(solution)/shard_map/all_gather | solution.py:406
  10.1 26.2 %collective-permute-start.1 = (bf16[512,1024]{1,0:T(8,128)(2,1)S(1)}, bf16[512,1024]{1,0:T(8,128)(2,1)S(1)}, u32[]{:S(2)}, u32[]{:S(2)}) collective-permute-start(bf16[512,1024]{1,0:T(8,128)(2,1)S(1)} %dynamic-slice_bitcast_fusion.2), channel_id=1, source_target_pairs={{0,8},{1,9},{2,10},{3,11},{4,12},{5,13},{6,14},{7,15},{8,0},{9,1},... | collective-permute-start | bytes 3145736 | tf_op jit(solution)/shard_map/ppermute | solution.py:342
  36.3 30.9 %copy-start.12 = (bf16[512,1024]{1,0:T(8,128)(2,1)}, bf16[512,1024]{1,0:T(8,128)(2,1)S(1)}, u32[]{:S(2)}) copy-start(bf16[512,1024]{1,0:T(8,128)(2,1)S(1)} %collective-permute-done.1.rest_2_) | copy-start | bytes 3145732
  36.3 5.6 %copy-start.1 = (f32[128,1024]{1,0:T(8,128)S(1)}, f32[128,1024]{1,0:T(8,128)}, u32[]{:S(2)}) copy-start(f32[128,1024]{1,0:T(8,128)} %filter_ref.1) | copy-start | bytes 1572868
  36.3 5.6 %copy-start.2 = (bf16[256,256]{1,0:T(8,128)(2,1)S(1)}, bf16[256,256]{1,0:T(8,128)(2,1)}, u32[]{:S(2)}) copy-start(bf16[256,256]{1,0:T(8,128)(2,1)} %constant.52.clone.fwd_ref) | copy-start | bytes 393220
  36.3 5.6 %copy-start.5 = (f32[1024]{0:T(1024)S(1)}, f32[1024]{0:T(1024)}, u32[]{:S(2)}) copy-start(f32[1024]{0:T(1024)} %param.14) | copy-start | bytes 12292
  36.3 29.3 %collective-permute-start = (bf16[3,1024,1024]{2,1,0:T(8,128)(2,1)}, bf16[3,1024,1024]{2,1,0:T(8,128)(2,1)}, u32[]{:S(2)}, u32[]{:S(2)}) collective-permute-start(bf16[3,1024,1024]{2,1,0:T(8,128)(2,1)} %bitcast.21), channel_id=1, source_target_pairs={{0,4},{1,5},{2,6},{3,7},{4,0},{5,1},{6,2},{7,3},{8,12},{9,13},{10,... | collective-permute-start | bytes 18874376 | tf_op jit(solution)/shard_map/ppermute | solution.py:342
  38.6 56.1 %copy-start.3 = (f32[3,3,1024]{2,1,0:T(4,128)S(1)}, f32[3,3,1024]{2,1,0:T(4,128)}, u32[]{:S(2)}) copy-start(f32[3,3,1024]{2,1,0:T(4,128)} %short_ref.1) | copy-start | bytes 110596
  38.6 25.3 %collective-permute-start.5 = (bf16[512,1024]{1,0:T(8,128)(2,1)S(1)}, bf16[512,1024]{1,0:T(8,128)(2,1)}, u32[]{:S(2)}, u32[]{:S(2)}) collective-permute-start(bf16[512,1024]{1,0:T(8,128)(2,1)S(1)} %get-tuple-element.30), channel_id=1, source_target_pairs={{0,8},{1,9},{2,10},{3,11},{4,12},{5,13},{6,14},{7,15},{8,0},{9,1},... | collective-permute-start | bytes 3145736 | tf_op jit(solution)/shard_map/ppermute | solution.py:342
  40.4 25.2 %collective-permute-start.3 = (bf16[512,1024]{1,0:T(8,128)(2,1)S(1)}, bf16[512,1024]{1,0:T(8,128)(2,1)}, u32[]{:S(2)}, u32[]{:S(2)}) collective-permute-start(bf16[512,1024]{1,0:T(8,128)(2,1)S(1)} %collective-permute-done.1.rest_2_), channel_id=1, source_target_pairs={{0,16},{1,17},{2,18},{3,19},{4,20},{5,21},{6,22},{7,23},{8,24},{9,... | collective-permute-start | bytes 3145736 | tf_op jit(solution)/shard_map/ppermute | solution.py:342
  63.9 24.3 %collective-permute-start.8 = (bf16[512,1024]{1,0:T(8,128)(2,1)S(1)}, bf16[512,1024]{1,0:T(8,128)(2,1)S(1)}, u32[]{:S(2)}, u32[]{:S(2)}) collective-permute-start(bf16[512,1024]{1,0:T(8,128)(2,1)S(1)} %get-tuple-element.32), channel_id=1, source_target_pairs={{0,8},{1,9},{2,10},{3,11},{4,12},{5,13},{6,14},{7,15},{8,0},{9,1},... | collective-permute-start | bytes 3145736 | tf_op jit(solution)/shard_map/ppermute | solution.py:342
  65.6 24.3 %collective-permute-start.7 = (bf16[512,1024]{1,0:T(8,128)(2,1)}, bf16[512,1024]{1,0:T(8,128)(2,1)}, u32[]{:S(2)}, u32[]{:S(2)}) collective-permute-start(bf16[512,1024]{1,0:T(8,128)(2,1)} %collective-permute-done.5.rest_8_), channel_id=1, source_target_pairs={{0,16},{1,17},{2,18},{3,19},{4,20},{5,21},{6,22},{7,23},{8,24},{9,... | collective-permute-start | bytes 3145736 | tf_op jit(solution)/shard_map/ppermute | solution.py:342
  67.1 27.4 %collective-permute-start.2 = (bf16[512,1024]{1,0:T(8,128)(2,1)S(1)}, bf16[512,1024]{1,0:T(8,128)(2,1)}, u32[]{:S(2)}, u32[]{:S(2)}) collective-permute-start(bf16[512,1024]{1,0:T(8,128)(2,1)S(1)} %collective-permute-done.1.rest_2_), channel_id=1, source_target_pairs={{0,4},{1,5},{2,6},{3,7},{4,0},{5,1},{6,2},{7,3},{8,12},{9,13},{10,... | collective-permute-start | bytes 3145736 | tf_op jit(solution)/shard_map/ppermute | solution.py:342
  67.1 27.4 %collective-permute-start.6 = (bf16[512,1024]{1,0:T(8,128)(2,1)}, bf16[512,1024]{1,0:T(8,128)(2,1)}, u32[]{:S(2)}, u32[]{:S(2)}) collective-permute-start(bf16[512,1024]{1,0:T(8,128)(2,1)} %collective-permute-done.5.rest_8_), channel_id=1, source_target_pairs={{0,4},{1,5},{2,6},{3,7},{4,0},{5,1},{6,2},{7,3},{8,12},{9,13},{10,... | collective-permute-start | bytes 3145736 | tf_op jit(solution)/shard_map/ppermute | solution.py:342
  67.7 26.9 %collective-permute-start.4 = (bf16[512,1024]{1,0:T(8,128)(2,1)}, bf16[512,1024]{1,0:T(8,128)(2,1)}, u32[]{:S(2)}, u32[]{:S(2)}) collective-permute-start(bf16[512,1024]{1,0:T(8,128)(2,1)} %collective-permute-done.3.rest_4_), channel_id=1, source_target_pairs={{0,4},{1,5},{2,6},{3,7},{4,0},{5,1},{6,2},{7,3},{8,12},{9,13},{10,... | collective-permute-start | bytes 3145736 | tf_op jit(solution)/shard_map/ppermute | solution.py:342
  88.2 22.9 %copy-start.11 = (bf16[512,1024]{1,0:T(8,128)(2,1)}, bf16[512,1024]{1,0:T(8,128)(2,1)S(1)}, u32[]{:S(2)}) copy-start(bf16[512,1024]{1,0:T(8,128)(2,1)S(1)} %collective-permute-done.8.rest_2_) | copy-start | bytes 3145732
  90.0 4.7 %collective-permute-start.9 = (bf16[512,1024]{1,0:T(8,128)(2,1)}, bf16[512,1024]{1,0:T(8,128)(2,1)}, u32[]{:S(2)}, u32[]{:S(2)}) collective-permute-start(bf16[512,1024]{1,0:T(8,128)(2,1)} %collective-permute-done.7.rest_10_), channel_id=1, source_target_pairs={{0,4},{1,5},{2,6},{3,7},{4,0},{5,1},{6,2},{7,3},{8,12},{9,13},{10,... | collective-permute-start | bytes 3145736 | tf_op jit(solution)/shard_map/ppermute | solution.py:342
  90.0 25.6 %collective-permute-start.13 = (bf16[512,1024]{1,0:T(8,128)(2,1)S(1)}, bf16[512,1024]{1,0:T(8,128)(2,1)S(1)}, u32[]{:S(2)}, u32[]{:S(2)}) collective-permute-start(bf16[512,1024]{1,0:T(8,128)(2,1)S(1)} %collective-permute-done.8.rest_2_), channel_id=1, source_target_pairs={{0,16},{1,17},{2,18},{3,19},{4,20},{5,21},{6,22},{7,23},{8,24},{9,... | collective-permute-start | bytes 3145736 | tf_op jit(solution)/shard_map/ppermute | solution.py:342
  109.6 5.9 %collective-permute-start.10 = (bf16[16,4096]{1,0:T(8,128)(2,1)S(1)}, bf16[16,4096]{1,0:T(8,128)(2,1)S(1)}, u32[]{:S(2)}, u32[]{:S(2)}) collective-permute-start(bf16[16,4096]{1,0:T(8,128)(2,1)S(1)} %slice.36), channel_id=1, source_target_pairs={{0,4},{1,5},{2,6},{3,7},{4,8},{5,9},{6,10},{7,11},{8,12},{9,13},{1... | collective-permute-start | bytes 393224 | tf_op jit(solution)/shard_map/ppermute | solution.py:342
  111.1 9.7 %collective-permute-start.12 = (bf16[512,1024]{1,0:T(8,128)(2,1)S(1)}, bf16[512,1024]{1,0:T(8,128)(2,1)S(1)}, u32[]{:S(2)}, u32[]{:S(2)}) collective-permute-start(bf16[512,1024]{1,0:T(8,128)(2,1)S(1)} %collective-permute-done.8.rest_2_), channel_id=1, source_target_pairs={{0,4},{1,5},{2,6},{3,7},{4,0},{5,1},{6,2},{7,3},{8,12},{9,13},{10,... | collective-permute-start | bytes 3145736 | tf_op jit(solution)/shard_map/ppermute | solution.py:342
  115.5 6.0 %copy-start.13 = (bf16[512,1024]{1,0:T(8,128)(2,1)}, bf16[512,1024]{1,0:T(8,128)(2,1)S(1)}, u32[]{:S(2)}) copy-start(bf16[512,1024]{1,0:T(8,128)(2,1)S(1)} %collective-permute-done.13.rest_4_) | copy-start | bytes 3145732
  115.5 6.0 %copy-start.15 = (bf16[16,4096]{1,0:T(8,128)(2,1)}, bf16[16,4096]{1,0:T(8,128)(2,1)S(1)}, u32[]{:S(2)}) copy-start(bf16[16,4096]{1,0:T(8,128)(2,1)S(1)} %collective-permute-done.10.before_ref) | copy-start | bytes 393220
  115.5 6.0 %collective-permute-start.14 = (bf16[512,1024]{1,0:T(8,128)(2,1)S(1)}, bf16[512,1024]{1,0:T(8,128)(2,1)}, u32[]{:S(2)}, u32[]{:S(2)}) collective-permute-start(bf16[512,1024]{1,0:T(8,128)(2,1)S(1)} %collective-permute-done.13.rest_4_), channel_id=1, source_target_pairs={{0,4},{1,5},{2,6},{3,7},{4,0},{5,1},{6,2},{7,3},{8,12},{9,13},{10,... | collective-permute-start | bytes 3145736 | tf_op jit(solution)/shard_map/ppermute | solution.py:342
  117.7 35.1 %collective-permute-start.15 = (bf16[1024,1024]{1,0:T(8,128)(2,1)}, bf16[1024,1024]{1,0:T(8,128)(2,1)}, u32[]{:S(2)}, u32[]{:S(2)}) collective-permute-start(bf16[1024,1024]{1,0:T(8,128)(2,1)} %param.15), channel_id=1, source_target_pairs={{0,4},{1,5},{2,6},{3,7},{4,0},{5,1},{6,2},{7,3},{8,12},{9,13},{10,... | collective-permute-start | bytes 6291464 | tf_op jit(solution)/shard_map/ppermute | solution.py:342
  117.7 13.0 %collective-permute-start.11 = (bf16[160,1024]{1,0:T(8,128)(2,1)}, bf16[160,1024]{1,0:T(8,128)(2,1)}, u32[]{:S(2)}, u32[]{:S(2)}) collective-permute-start(bf16[160,1024]{1,0:T(8,128)(2,1)} %get-tuple-element.37), channel_id=1, source_target_pairs={{0,4},{1,5},{2,6},{3,7},{4,8},{5,9},{6,10},{7,11},{8,12},{9,13},{1... | collective-permute-start | bytes 983048 | tf_op jit(solution)/shard_map/ppermute | solution.py:342
  120.8 9.9 %copy-start.4 = (bf16[128,768]{1,0:T(8,128)(2,1)S(1)}, bf16[128,768]{1,0:T(8,128)(2,1)}, u32[]{:S(2)}) copy-start(bf16[128,768]{1,0:T(8,128)(2,1)} %constant.53.clone.inv_ref) | copy-start | bytes 589828
  120.8 1.0 copy-start.14
  139.0 11.3 %collective-permute-start.16 = (bf16[256,1024]{1,0:T(8,128)(2,1)S(1)}, bf16[256,1024]{1,0:T(8,128)(2,1)S(1)}, u32[]{:S(2)}, u32[]{:S(2)}) collective-permute-start(bf16[256,1024]{1,0:T(8,128)(2,1)S(1)} %constant_dynamic-slice_fusion.3), channel_id=1, source_target_pairs={{0,1},{3,2},{4,5},{7,6},{8,9},{11,10},{12,13},{15,14},{16,17},{19,... | collective-permute-start | bytes 1572872 | tf_op jit(solution)/shard_map/ppermute | solution.py:342
  151.3 37.8 %collective-permute-start.23 = (bf16[256,1024]{1,0:T(8,128)(2,1)}, bf16[256,1024]{1,0:T(8,128)(2,1)}, u32[]{:S(2)}, u32[]{:S(2)}) collective-permute-start(bf16[256,1024]{1,0:T(8,128)(2,1)} %add_convert_fusion), channel_id=1, source_target_pairs={{1,2},{2,1},{5,6},{6,5},{9,10},{10,9},{13,14},{14,13},{17,18},{18,... | collective-permute-start | bytes 1572872 | tf_op jit(solution)/shard_map/ppermute | solution.py:342
  155.7 1.0 copy-start.8
  157.4 20.7 %collective-permute-start.18 = (bf16[256,1024]{1,0:T(8,128)(2,1)}, bf16[256,1024]{1,0:T(8,128)(2,1)}, u32[]{:S(2)}, u32[]{:S(2)}) collective-permute-start(bf16[256,1024]{1,0:T(8,128)(2,1)} %constant_dynamic-slice_fusion.1), channel_id=1, source_target_pairs={{0,1},{3,2},{4,5},{7,6},{8,9},{11,10},{12,13},{15,14},{16,17},{19,... | collective-permute-start | bytes 1572872 | tf_op jit(solution)/shard_map/ppermute | solution.py:342
  169.0 9.2 %copy-start.9 = (bf16[512,1024]{1,0:T(8,128)(2,1)S(1)}, bf16[512,1024]{1,0:T(8,128)(2,1)}, u32[]{:S(2)}) copy-start(bf16[512,1024]{1,0:T(8,128)(2,1)} %copy-done.8) | copy-start | bytes 3145732
  169.0 18.9 %collective-permute-start.22 = (bf16[256,1024]{1,0:T(8,128)(2,1)}, bf16[256,1024]{1,0:T(8,128)(2,1)}, u32[]{:S(2)}, u32[]{:S(2)}) collective-permute-start(bf16[256,1024]{1,0:T(8,128)(2,1)} %constant_dynamic-slice_fusion), channel_id=1, source_target_pairs={{0,1},{3,2},{4,5},{7,6},{8,9},{11,10},{12,13},{15,14},{16,17},{19,... | collective-permute-start | bytes 1572872 | tf_op jit(solution)/shard_map/ppermute | solution.py:342
  174.1 1.0 copy-start.6
  175.9 23.2 %copy-start.7 = (bf16[512,1024]{1,0:T(8,128)(2,1)S(1)}, bf16[512,1024]{1,0:T(8,128)(2,1)}, u32[]{:S(2)}) copy-start(bf16[512,1024]{1,0:T(8,128)(2,1)} %copy-done.6) | copy-start | bytes 3145732
  175.9 23.2 %collective-permute-start.17 = (bf16[256,1024]{1,0:T(8,128)(2,1)}, bf16[256,1024]{1,0:T(8,128)(2,1)}, u32[]{:S(2)}, u32[]{:S(2)}) collective-permute-start(bf16[256,1024]{1,0:T(8,128)(2,1)} %constant_dynamic-slice_fusion.2), channel_id=1, source_target_pairs={{0,1},{3,2},{4,5},{7,6},{8,9},{11,10},{12,13},{15,14},{16,17},{19,... | collective-permute-start | bytes 1572872 | tf_op jit(solution)/shard_map/ppermute | solution.py:342
  180.1 20.2 %collective-permute-start.19 = (bf16[256,1024]{1,0:T(8,128)(2,1)}, bf16[256,1024]{1,0:T(8,128)(2,1)}, u32[]{:S(2)}, u32[]{:S(2)}) collective-permute-start(bf16[256,1024]{1,0:T(8,128)(2,1)} %add_convert_fusion.2), channel_id=1, source_target_pairs={{1,2},{2,1},{5,6},{6,5},{9,10},{10,9},{13,14},{14,13},{17,18},{18,... | collective-permute-start | bytes 1572872 | tf_op jit(solution)/shard_map/ppermute | solution.py:342
  181.6 24.4 %copy-start.10 = (bf16[512,1024]{1,0:T(8,128)(2,1)S(1)}, bf16[512,1024]{1,0:T(8,128)(2,1)}, u32[]{:S(2)}) copy-start(bf16[512,1024]{1,0:T(8,128)(2,1)} %copy-done.8) | copy-start | bytes 3145732
  189.1 18.1 %collective-permute-start.24 = (bf16[256,1024]{1,0:T(8,128)(2,1)S(1)}, bf16[256,1024]{1,0:T(8,128)(2,1)S(1)}, u32[]{:S(2)}, u32[]{:S(2)}) collective-permute-start(bf16[256,1024]{1,0:T(8,128)(2,1)S(1)} %add_convert_fusion.1), channel_id=1, source_target_pairs={{1,2},{2,1},{5,6},{6,5},{9,10},{10,9},{13,14},{14,13},{17,18},{18,... | collective-permute-start | bytes 1572872 | tf_op jit(solution)/shard_map/ppermute | solution.py:342
  200.3 9.1 %collective-permute-start.20 = (bf16[256,1024]{1,0:T(8,128)(2,1)S(1)}, bf16[256,1024]{1,0:T(8,128)(2,1)S(1)}, u32[]{:S(2)}, u32[]{:S(2)}) collective-permute-start(bf16[256,1024]{1,0:T(8,128)(2,1)S(1)} %add_convert_fusion.3), channel_id=1, source_target_pairs={{1,2},{2,1},{5,6},{6,5},{9,10},{10,9},{13,14},{14,13},{17,18},{18,... | collective-permute-start | bytes 1572872 | tf_op jit(solution)/shard_map/ppermute | solution.py:342
  202.2 18.4 %collective-permute-start.27 = (bf16[128,1024]{1,0:T(8,128)(2,1)S(1)}, bf16[128,1024]{1,0:T(8,128)(2,1)S(1)}, u32[]{:S(2)}, u32[]{:S(2)}) collective-permute-start(bf16[128,1024]{1,0:T(8,128)(2,1)S(1)} %add_convert_fusion.5), channel_id=1, source_target_pairs={{0,1},{1,0},{2,3},{3,2},{4,5},{5,4},{6,7},{7,6},{8,9},{9,8},{10,11... | collective-permute-start | bytes 786440 | tf_op jit(solution)/shard_map/ppermute | solution.py:342
  207.1 13.5 %collective-permute-start.26 = (bf16[128,1024]{1,0:T(8,128)(2,1)S(1)}, bf16[128,1024]{1,0:T(8,128)(2,1)S(1)}, u32[]{:S(2)}, u32[]{:S(2)}) collective-permute-start(bf16[128,1024]{1,0:T(8,128)(2,1)S(1)} %add_convert_fusion.7), channel_id=1, source_target_pairs={{0,1},{1,0},{2,3},{3,2},{4,5},{5,4},{6,7},{7,6},{8,9},{9,8},{10,11... | collective-permute-start | bytes 786440 | tf_op jit(solution)/shard_map/ppermute | solution.py:342
  207.4 17.0 %collective-permute-start.25 = (bf16[128,1024]{1,0:T(8,128)(2,1)S(1)}, bf16[128,1024]{1,0:T(8,128)(2,1)S(1)}, u32[]{:S(2)}, u32[]{:S(2)}) collective-permute-start(bf16[128,1024]{1,0:T(8,128)(2,1)S(1)} %add_convert_fusion.9), channel_id=1, source_target_pairs={{0,1},{1,0},{2,3},{3,2},{4,5},{5,4},{6,7},{7,6},{8,9},{9,8},{10,11... | collective-permute-start | bytes 786440 | tf_op jit(solution)/shard_map/ppermute | solution.py:342
  209.6 20.1 %collective-permute-start.21 = (bf16[128,1024]{1,0:T(8,128)(2,1)S(1)}, bf16[128,1024]{1,0:T(8,128)(2,1)S(1)}, u32[]{:S(2)}, u32[]{:S(2)}) collective-permute-start(bf16[128,1024]{1,0:T(8,128)(2,1)S(1)} %add_convert_fusion.11), channel_id=1, source_target_pairs={{0,1},{1,0},{2,3},{3,2},{4,5},{5,4},{6,7},{7,6},{8,9},{9,8},{10,11... | collective-permute-start | bytes 786440 | tf_op jit(solution)/shard_map/ppermute | solution.py:342
Sparse Core Ops, SparseCore 0:
  10.2 83.4 all-gather.2
  95.2 57.8 all-gather.4
